TPU v7x, 128 devices: a whole 4x4x4 slice. The times are simulated.
128 devices in a mesh: row: 16 (over y, x), col: 8 (over z, core).
Axes of the slice: x: 4, y: 4, z: 4, core: 2. Of those that a mesh axis runs over, the one named last changes fastest.
Arguments:
- src_points: bfloat16 [16384, 256], P('row'), may hold values from -32 to 32, as said below
- tgt_points: bfloat16 [32768, 256], P(('col', 'row')), may hold values from -32 to 32, as said below
- log_src_mass: float32 [16384], P('row'), may hold values from -3 to 3
- log_tgt_mass: float32 [32768], P('col'), may hold values from -3 to 3
Outputs:
- src_potential: float32 [16384], P('row')
- tgt_potential: float32 [32768], P('col')
- mean_potentials: float32 [], replicated
Inputs may be any that keep to these rules, and one draw needn't show every extreme that they name: `src_points`: point coordinates. `tgt_points`: point coordinates.
All inputs are finite; a program needn't handle non-finite values.
Results may differ from a plain program's by a relative error of at most 0.0003.
Values may be sent and summed in bfloat16 or wider, within the bound.
No kernel may reach another device: no remote copies, remote signals or barrier semaphores. Data moves between devices by JAX's collectives and lax.ppermute only.
A program may use at most 64 MiB of HBM per device.

v0:
```python
import jax
import jax.numpy as jnp
from jax import lax
from jax.sharding import Mesh
from jax.sharding import PartitionSpec as P

ITERS = 3
ROW = ("row_0", "row_1")
COL = ("col_0", "col_1")
ROW_COL = ("row_0", "row_1", "col_0", "col_1")
COL_ROW = ("col_0", "col_1", "row_0", "row_1")


entropy_weight = 0.1


def from_everyone(value, axis):
    peers = lax.axis_size(axis)
    return lax.all_to_all(
        jnp.broadcast_to(value[None], (peers, *value.shape)), axis, 0, 0, tiled=True
    )


def laid_out(tiles, dim):
    shape = list(tiles.shape[1:])
    shape[dim] *= tiles.shape[0]
    return jnp.moveaxis(tiles, 0, dim).reshape(shape)


def gathered_copies(value, axis, dim):
    tiles = from_everyone(value, axis)
    return laid_out(tiles, dim)


def collected_together(value, axis):
    leaves = jax.tree.leaves(value)
    sequence = sorted(range(len(leaves)), key=lambda k: -leaves[k].size)
    width = (1, *leaves[sequence[0]].shape)[-1]
    lines = [
        jnp.pad(leaves[k].reshape(-1), (0, -leaves[k].size % width)).reshape(-1, width)
        for k in sequence
    ]
    both, at, found = (from_everyone(jnp.concatenate(lines), axis), 0, {})
    for k, line in zip(sequence, lines):
        section = both[:, at : at + len(line)].reshape(len(both), -1)
        found[k] = section[:, : leaves[k].size].reshape(-1, *leaves[k].shape)
        at += len(line)
    numbers = iter(range(len(leaves)))
    return jax.tree.map(lambda _: found[next(numbers)], value)


def once_a_type(value, axis):
    leaves, found = (jax.tree.leaves(value), {})
    for leading, a in enumerate(leaves):
        if leading not in found:
            alike = [k for k, b in enumerate(leaves) if b.dtype == a.dtype]
            got = (
                collected_together([leaves[k] for k in alike], axis)
                if len(alike) > 1
                else [from_everyone(a, axis)]
            )
            for k, b in zip(alike, got):
                found[k] = b
    numbers = iter(range(len(leaves)))
    return jax.tree.map(lambda _: found[next(numbers)], value)


def folded_in_pairs(pieces, combine):
    while len(jax.tree.leaves(pieces)[0]) > 1:
        pieces = jax.vmap(combine)(
            *(jax.tree.map(lambda part: part[side::2], pieces) for side in (0, 1))
        )
    return jax.tree.map(lambda part: part[0], pieces)


def combined_all(value, axis, combine):
    pieces = once_a_type(value, axis)
    return folded_in_pairs(pieces, combine)


def joined_all(value, axis, combine):
    pieces = collected_together(value, axis)
    return folded_in_pairs(pieces, combine)


def over_axes(value, axes):
    for axis in axes:
        value = lax.psum(value, axis)
    return value


def cost_block(points_a, squares_a, points_b, squares_b):
    product = lax.dot_general(
        points_a, points_b, (((1,), (1,)), ((), ())), preferred_element_type=jnp.float32
    )
    return (squares_a[:, None] + squares_b[None, :] - 2.0 * product) / points_a.shape[1]


def combine(early, later):
    top = jnp.maximum(early[0], later[0])
    return (top, early[1] * jnp.exp(early[0] - top) + later[1] * jnp.exp(later[0] - top))


def body(src_points, tgt_points, log_src_mass, log_tgt_mass):
    targets = gathered_copies(tgt_points, ROW, 0)
    sqy = jnp.sum(targets.astype(jnp.float32) ** 2, axis=1)
    count = src_points.shape[0]
    block = min(256, count)
    blocks = count // block
    src_blocks = src_points.reshape(blocks, block, -1)
    sq_blocks = jnp.sum(src_points.astype(jnp.float32) ** 2, axis=1).reshape(blocks, block)
    mass_blocks = log_src_mass.reshape(blocks, block)
    width_tgt = targets.shape[0]
    tgt_potential = jnp.zeros((width_tgt,), jnp.float32)
    src_potential = jnp.zeros((count,), jnp.float32)
    for step in range(ITERS):

        def row_terms(points, squares):
            cost = cost_block(points, squares, targets, sqy)
            return log_tgt_mass[None, :] + (tgt_potential[None, :] - cost) / entropy_weight

        def row_pair(item):
            terms = row_terms(item[0], item[1])
            top = jnp.max(terms, axis=1)
            return (top, jnp.sum(jnp.exp(terms - top[:, None]), axis=1))

        top, total = lax.map(row_pair, (src_blocks, sq_blocks))
        top, total = combined_all((top.reshape(-1), total.reshape(-1)), COL, combine)
        src_potential = -entropy_weight * (top + jnp.log(total))
        pot_blocks = src_potential.reshape(blocks, block)

        def col_terms(points, squares, mass, pot):
            cost = cost_block(points, squares, targets, sqy)
            return mass[:, None] + (pot[:, None] - cost) / entropy_weight

        def pair_step(carry, item):
            terms = col_terms(item[0], item[1], item[2], item[3])
            block_top = jnp.max(terms, axis=0)
            block_sum = jnp.sum(jnp.exp(terms - block_top[None, :]), axis=0)
            return (combine(carry, (block_top, block_sum)), None)

        start = (
            jnp.full((width_tgt,), -jnp.inf, jnp.float32),
            jnp.zeros((width_tgt,), jnp.float32),
        )
        inputs = (src_blocks, sq_blocks, mass_blocks, pot_blocks)
        (top, total), unused = lax.scan(pair_step, start, inputs)
        top, total = joined_all((top, total), ROW, combine)
        tgt_potential = -entropy_weight * (top + jnp.log(total))
    sources_all = count * lax.axis_size(ROW)
    targets_all = width_tgt * lax.axis_size(COL)
    local = jnp.sum(src_potential) / (sources_all * lax.axis_size(COL)) + jnp.sum(tgt_potential) / (
        targets_all * lax.axis_size(ROW)
    )
    mean_potentials = over_axes(local, ROW_COL)
    return (src_potential, tgt_potential, mean_potentials)


def solution(mesh):
    finer = Mesh(mesh.devices.reshape(4, 4, 4, 2), ("row_0", "row_1", "col_0", "col_1"))
    placed = (P(ROW, None), P(COL_ROW, None), P(ROW), P(COL))
    return jax.shard_map(
        body, mesh=finer, in_specs=placed, out_specs=(P(ROW), P(COL), P()), check_vma=False
    )
```

profile of v0, /device:TPU:1, one launch (start us, length us, event | category | flops | bytes accessed | tf_op | source)
XLA Modules:
  0.0 220.8 jit_solution(14711009485905905026)
XLA Ops:
  3.2 7.6 %all-to-all-start = ((bf16[16,256,256]{2,1,0:T(8,128)(2,1)}), bf16[16,256,256]{2,1,0:T(8,128)(2,1)S(1)}, u32[]{:S(2)}, u32[]{:S(2)}) async-start(bf16[16,256,256]{2,1,0:T(8,128)(2,1)} %broadcast_in_dim.47), calls=%async_computation | async-start | bytes 4194304 | tf_op jit(solution)/shard_map/all_to_all | solution.py:19
  11.0 30.2 %all-to-all-done = bf16[16,256,256]{2,1,0:T(8,128)(2,1)S(1)} async-done(((bf16[16,256,256]{2,1,0:T(8,128)(2,1)}), bf16[16,256,256]{2,1,0:T(8,128)(2,1)S(1)}, u32[]{:S(2)}, u32[]{:S(2)}) %all-to-all-start) | async-done | bytes 2097184 | tf_op jit(solution)/shard_map/all_to_all | solution.py:19
  41.9 9.3 %while.75 = (s32[]{:T(128)}, f32[4,256]{1,0:T(4,128)S(1)}, f32[4,256]{1,0:T(4,128)S(1)}, f32[4096]{0:T(1024)S(1)}, f32[4,256]{1,0:T(4,128)S(1)}, /*index=5*/f32[...) while((s32[]{:T(128)}, f32[4,256]{1,0:T(4,128)S(1)}, ...), condition=%wide.region_5.6_spmd, body=%wide.region_2.5_spmd.sunk | while | flops 547356160 | bytes 10659957 | solution.py:127
  51.9 7.4 %all-to-all-start.1 = ((f32[8,2,1024]{2,1,0:T(2,128)}), f32[8,2,1024]{2,1,0:T(2,128)S(1)}, u32[]{:S(2)}, u32[]{:S(2)}) async-start(f32[8,2,1024]{2,1,0:T(2,128)} %broadcast_in_dim.48), calls=%async_computation.1 | async-start | bytes 131072 | tf_op jit(solution)/shard_map/all_to_all | solution.py:19
  59.4 4.8 %all-to-all-done.1 = f32[8,2,1024]{2,1,0:T(2,128)S(1)} async-done(((f32[8,2,1024]{2,1,0:T(2,128)}), f32[8,2,1024]{2,1,0:T(2,128)S(1)}, u32[]{:S(2)}, u32[]{:S(2)}) %all-to-all-start.1) | async-done | bytes 65568 | tf_op jit(solution)/shard_map/all_to_all | solution.py:19
  64.6 8.5 %while.78 = (s32[]{:T(128)}, f32[4096]{0:T(1024)S(1)}, f32[4096]{0:T(1024)S(1)}, f32[4,256]{1,0:T(4,128)S(1)}, f32[4,256]{1,0:T(4,128)S(1)}, /*index=5*/f32[4,25...) while((s32[]{:T(128)}, f32[4096]{0:T(1024)S(1)}, ...), condition=%wide.region_9.10_spmd.clone, body=%wide.region_6.9_spmd.clone.sunk | while | flops 547381248 | bytes 10790019 | solution.py:147
  74.1 3.6 %all-to-all-start.2 = ((f32[16,2,4096]{2,1,0:T(2,128)}), f32[16,2,4096]{2,1,0:T(2,128)S(1)}, u32[]{:S(2)}, u32[]{:S(2)}) async-start(f32[16,2,4096]{2,1,0:T(2,128)} %broadcast_in_dim.49), calls=%async_computation.2 | async-start | bytes 1048576 | tf_op jit(solution)/shard_map/all_to_all | solution.py:19
  77.7 10.5 %all-to-all-done.2 = f32[16,2,4096]{2,1,0:T(2,128)S(1)} async-done(((f32[16,2,4096]{2,1,0:T(2,128)}), f32[16,2,4096]{2,1,0:T(2,128)S(1)}, u32[]{:S(2)}, u32[]{:S(2)}) %all-to-all-start.2) | async-done | bytes 524320 | tf_op jit(solution)/shard_map/all_to_all | solution.py:19
  90.8 9.4 %while.76 = (s32[]{:T(128)}, f32[4,256]{1,0:T(4,128)S(1)}, f32[4,256]{1,0:T(4,128)S(1)}, f32[4096]{0:T(1024)S(1)}, f32[4096]{0:T(1024)S(1)}, /*index=5*/f32[4,25...) while((s32[]{:T(128)}, f32[4,256]{1,0:T(4,128)S(1)}, ...), condition=%wide.region_13.14_spmd, body=%wide.region_10.13_spmd.sunk | while | flops 547356160 | bytes 10676349 | solution.py:127
  100.8 5.2 %all-to-all-start.3 = ((f32[8,2,1024]{2,1,0:T(2,128)}), f32[8,2,1024]{2,1,0:T(2,128)S(1)}, u32[]{:S(2)}, u32[]{:S(2)}) async-start(f32[8,2,1024]{2,1,0:T(2,128)} %broadcast_in_dim.50), calls=%async_computation.3 | async-start | bytes 131072 | tf_op jit(solution)/shard_map/all_to_all | solution.py:19
  106.0 4.9 %all-to-all-done.3 = f32[8,2,1024]{2,1,0:T(2,128)S(1)} async-done(((f32[8,2,1024]{2,1,0:T(2,128)}), f32[8,2,1024]{2,1,0:T(2,128)S(1)}, u32[]{:S(2)}, u32[]{:S(2)}) %all-to-all-start.3) | async-done | bytes 65568 | tf_op jit(solution)/shard_map/all_to_all | solution.py:19
  111.3 8.5 %while.79 = (s32[]{:T(128)}, f32[4096]{0:T(1024)S(1)}, f32[4096]{0:T(1024)S(1)}, f32[4,256]{1,0:T(4,128)S(1)}, f32[4,256]{1,0:T(4,128)S(1)}, /*index=5*/f32[4,25...) while((s32[]{:T(128)}, f32[4096]{0:T(1024)S(1)}, ...), condition=%wide.region_17.18_spmd.clone, body=%wide.region_14.17_spmd.clone.sunk | while | flops 547381248 | bytes 10790019 | solution.py:147
  120.8 3.6 %all-to-all-start.4 = ((f32[16,2,4096]{2,1,0:T(2,128)}), f32[16,2,4096]{2,1,0:T(2,128)S(1)}, u32[]{:S(2)}, u32[]{:S(2)}) async-start(f32[16,2,4096]{2,1,0:T(2,128)} %broadcast_in_dim.56), calls=%async_computation.4 | async-start | bytes 1048576 | tf_op jit(solution)/shard_map/all_to_all | solution.py:19
  124.4 10.5 %all-to-all-done.4 = f32[16,2,4096]{2,1,0:T(2,128)S(1)} async-done(((f32[16,2,4096]{2,1,0:T(2,128)}), f32[16,2,4096]{2,1,0:T(2,128)S(1)}, u32[]{:S(2)}, u32[]{:S(2)}) %all-to-all-start.4) | async-done | bytes 524320 | tf_op jit(solution)/shard_map/all_to_all | solution.py:19
  137.5 9.4 %while.77 = (s32[]{:T(128)}, f32[4,256]{1,0:T(4,128)S(1)}, f32[4,256]{1,0:T(4,128)S(1)}, f32[4096]{0:T(1024)S(1)}, f32[4096]{0:T(1024)S(1)}, /*index=5*/f32[4,25...) while((s32[]{:T(128)}, f32[4,256]{1,0:T(4,128)S(1)}, ...), condition=%wide.region_21.22_spmd, body=%wide.region_18.21_spmd.sunk | while | flops 547356160 | bytes 10676349 | solution.py:127
  147.6 5.2 %all-to-all-start.5 = ((f32[8,2,1024]{2,1,0:T(2,128)}), f32[8,2,1024]{2,1,0:T(2,128)S(1)}, u32[]{:S(2)}, u32[]{:S(2)}) async-start(f32[8,2,1024]{2,1,0:T(2,128)} %broadcast_in_dim.57), calls=%async_computation.5 | async-start | bytes 131072 | tf_op jit(solution)/shard_map/all_to_all | solution.py:19
  152.7 4.9 %all-to-all-done.5 = f32[8,2,1024]{2,1,0:T(2,128)S(1)} async-done(((f32[8,2,1024]{2,1,0:T(2,128)}), f32[8,2,1024]{2,1,0:T(2,128)S(1)}, u32[]{:S(2)}, u32[]{:S(2)}) %all-to-all-start.5) | async-done | bytes 65568 | tf_op jit(solution)/shard_map/all_to_all | solution.py:19
  160.3 8.4 %while.80 = (s32[]{:T(128)}, f32[4096]{0:T(1024)S(1)}, f32[4096]{0:T(1024)S(1)}, f32[4,256]{1,0:T(4,128)S(1)}, f32[4,256]{1,0:T(4,128)S(1)}, /*index=5*/f32[4,25...) while((s32[]{:T(128)}, f32[4096]{0:T(1024)S(1)}, ...), condition=%wide.region_25.26_spmd.clone, body=%wide.region_22.25_spmd.clone.sunk | while | flops 547381248 | bytes 10790019 | solution.py:147
  169.8 3.6 %all-to-all-start.6 = ((f32[16,2,4096]{2,1,0:T(2,128)}), f32[16,2,4096]{2,1,0:T(2,128)S(1)}, u32[]{:S(2)}, u32[]{:S(2)}) async-start(f32[16,2,4096]{2,1,0:T(2,128)} %broadcast_in_dim.58), calls=%async_computation.6 | async-start | bytes 1048576 | tf_op jit(solution)/shard_map/all_to_all | solution.py:19
  174.0 9.9 %all-to-all-done.6 = f32[16,2,4096]{2,1,0:T(2,128)S(1)} async-done(((f32[16,2,4096]{2,1,0:T(2,128)}), f32[16,2,4096]{2,1,0:T(2,128)S(1)}, u32[]{:S(2)}, u32[]{:S(2)}) %all-to-all-start.6) | async-done | bytes 524320 | tf_op jit(solution)/shard_map/all_to_all | solution.py:19
  188.3 7.2 %psum.28 = f32[]{:T(128)} all-reduce(f32[]{:T(128)S(6)} %add.300), channel_id=1, replica_groups=mesh['row_0'=4,'row_1'=4,'col_0'=4,'col_1'=2] {'row_0'}, use_global_device_ids=true, to_apply=%region_28.29 | all-reduce | flops 1 | bytes 8 | tf_op jit(solution)/shard_map/psum | solution.py:88
  195.5 7.4 %psum.29 = f32[]{:T(128)} all-reduce(f32[]{:T(128)} %psum.28), channel_id=1, replica_groups=mesh['row_0'=4,'row_1'=4,'col_0'=4,'col_1'=2] {'row_1'}, use_global_device_ids=true, to_apply=%region_29.30 | all-reduce | flops 1 | bytes 8 | tf_op jit(solution)/shard_map/psum | solution.py:88
  202.9 7.5 %psum.30 = f32[]{:T(128)} all-reduce(f32[]{:T(128)} %psum.29), channel_id=1, replica_groups=mesh['row_0'=4,'row_1'=4,'col_0'=4,'col_1'=2] {'col_0'}, use_global_device_ids=true, to_apply=%region_30.31 | all-reduce | flops 1 | bytes 8 | tf_op jit(solution)/shard_map/psum | solution.py:88
  210.4 10.4 %psum.31 = f32[]{:T(128)} all-reduce(f32[]{:T(128)} %psum.30), channel_id=1, replica_groups=mesh['row_0'=4,'row_1'=4,'col_0'=4,'col_1'=2] {'col_1'}, use_global_device_ids=true, to_apply=%region_31.32 | all-reduce | flops 1 | bytes 8 | tf_op jit(solution)/shard_map/psum | solution.py:88
  (264 shorter events, 72.9 us)
Async XLA Ops:
  0.6 10.1 %copy-start = (bf16[1024,256]{1,0:T(8,128)(2,1)S(1)}, bf16[1024,256]{1,0:T(8,128)(2,1)}, u32[]{:S(2)}) copy-start(bf16[1024,256]{1,0:T(8,128)(2,1)} %param.16) | copy-start | bytes 1572868
  0.6 41.3 %copy-start.2 = (f32[4096]{0:T(1024)S(1)}, f32[4096]{0:T(1024)}, u32[]{:S(2)}) copy-start(f32[4096]{0:T(1024)} %param.19) | copy-start | bytes 49156
  3.2 38.1 %all-to-all-start = ((bf16[16,256,256]{2,1,0:T(8,128)(2,1)}), bf16[16,256,256]{2,1,0:T(8,128)(2,1)S(1)}, u32[]{:S(2)}, u32[]{:S(2)}) async-start(bf16[16,256,256]{2,1,0:T(8,128)(2,1)} %broadcast_in_dim.47), calls=%async_computation | async-start | bytes 4194304 | tf_op jit(solution)/shard_map/all_to_all | solution.py:19
  41.9 17.4 %copy-start.1 = (f32[1024]{0:T(1024)S(1)}, f32[1024]{0:T(1024)}, u32[]{:S(2)}) copy-start(f32[1024]{0:T(1024)} %param.18) | copy-start | bytes 12292
  51.9 12.3 %all-to-all-start.1 = ((f32[8,2,1024]{2,1,0:T(2,128)}), f32[8,2,1024]{2,1,0:T(2,128)S(1)}, u32[]{:S(2)}, u32[]{:S(2)}) async-start(f32[8,2,1024]{2,1,0:T(2,128)} %broadcast_in_dim.48), calls=%async_computation.1 | async-start | bytes 131072 | tf_op jit(solution)/shard_map/all_to_all | solution.py:19
  74.1 14.1 %all-to-all-start.2 = ((f32[16,2,4096]{2,1,0:T(2,128)}), f32[16,2,4096]{2,1,0:T(2,128)S(1)}, u32[]{:S(2)}, u32[]{:S(2)}) async-start(f32[16,2,4096]{2,1,0:T(2,128)} %broadcast_in_dim.49), calls=%async_computation.2 | async-start | bytes 1048576 | tf_op jit(solution)/shard_map/all_to_all | solution.py:19
  100.8 10.1 %all-to-all-start.3 = ((f32[8,2,1024]{2,1,0:T(2,128)}), f32[8,2,1024]{2,1,0:T(2,128)S(1)}, u32[]{:S(2)}, u32[]{:S(2)}) async-start(f32[8,2,1024]{2,1,0:T(2,128)} %broadcast_in_dim.50), calls=%async_computation.3 | async-start | bytes 131072 | tf_op jit(solution)/shard_map/all_to_all | solution.py:19
  120.8 14.1 %all-to-all-start.4 = ((f32[16,2,4096]{2,1,0:T(2,128)}), f32[16,2,4096]{2,1,0:T(2,128)S(1)}, u32[]{:S(2)}, u32[]{:S(2)}) async-start(f32[16,2,4096]{2,1,0:T(2,128)} %broadcast_in_dim.56), calls=%async_computation.4 | async-start | bytes 1048576 | tf_op jit(solution)/shard_map/all_to_all | solution.py:19
  147.6 10.0 %all-to-all-start.5 = ((f32[8,2,1024]{2,1,0:T(2,128)}), f32[8,2,1024]{2,1,0:T(2,128)S(1)}, u32[]{:S(2)}, u32[]{:S(2)}) async-start(f32[8,2,1024]{2,1,0:T(2,128)} %broadcast_in_dim.57), calls=%async_computation.5 | async-start | bytes 131072 | tf_op jit(solution)/shard_map/all_to_all | solution.py:19
  169.8 14.1 %all-to-all-start.6 = ((f32[16,2,4096]{2,1,0:T(2,128)}), f32[16,2,4096]{2,1,0:T(2,128)S(1)}, u32[]{:S(2)}, u32[]{:S(2)}) async-start(f32[16,2,4096]{2,1,0:T(2,128)} %broadcast_in_dim.58), calls=%async_computation.6 | async-start | bytes 1048576 | tf_op jit(solution)/shard_map/all_to_all | solution.py:19
where the time goes:
time: 222 us; the launch traced here: 221 us
  waiting for transfers between devices  75.8 us (34%)
  starting transfers between devices  36.1 us (16%)
  matrix products  35.4 us (16%)
  blocking collectives  32.4 us (15%)
  other arithmetic  21 us (9%)
  local copies, waits for them, and re-layouts  16.5 us (7%)
  between operations  2.76 us (1%)
    all_to_all x7, waiting for transfers between devices, from_everyone(): lax.all_to_all(jnp.broadcast_to(value[None], (peers, *value.shape)), axis...  75.8 us
    all_to_all x7, starting transfers between devices, from_everyone(): lax.all_to_all(jnp.broadcast_to(value[None], (peers, *value.shape)), axis...  36.1 us
    dot_general x24, matrix products, cost_block(): lax.dot_general(points_a, points_b, (((1,), (1,)), ((), ())), preferred_e...  35.4 us
    psum x4, blocking collectives, over_axes(): value = lax.psum(value, axis)  32.4 us
    reduce_sum x12, other arithmetic, row_pair(): return (top, jnp.sum(jnp.exp(terms - top[:, None]), axis=1))  8.61 us
    broadcast_in_dim x7, local copies, waits for them, and re-layouts, from_everyone(): jnp.broadcast_to(value[None], (peers, *value.shape))  7.4 us
    reduce_sum x12, other arithmetic, pair_step(): block_sum = jnp.sum(jnp.exp(terms - block_top[None, :]), axis=0)  7.15 us
  transfers between devices with their start and end apart: 7, of which 7 were waited for; matrix products, arithmetic and copies ran while one was open for 0% of the time, Pallas kernels for 0%

commit v1 on v0

v1 whole, which is shorter than its diff:
```python
import math

import jax
import jax.numpy as jnp
from jax import lax
from jax.experimental import pallas as pl
from jax.experimental.pallas import tpu as pltpu
from jax.sharding import Mesh
from jax.sharding import PartitionSpec as P

ROW = ("row_0", "row_1")
COL = ("col_0", "col_1")
COL_ROW = ("col_0", "col_1", "row_0", "row_1")

EPS = 0.1
WIDTH = 256
NATS = 2.0 / (WIDTH * EPS)
BITS = NATS * math.log2(math.e)
LOG2E = math.log2(math.e)
VMEM_LIMIT = 24 * 1024 * 1024
LANES = 128
STEP = 64

VMEM = pl.BlockSpec(memory_space=pltpu.VMEM)
SMEM = pl.BlockSpec(memory_space=pltpu.SMEM)


def call(kernel, outs, ins, scratch, aliases=None):
    return pl.pallas_call(
        kernel,
        out_shape=outs,
        in_specs=ins,
        out_specs=jax.tree.map(lambda _: VMEM, outs),
        scratch_shapes=scratch,
        input_output_aliases=aliases or {},
        compiler_params=pltpu.CompilerParams(vmem_limit_bytes=VMEM_LIMIT),
    )


def f32(*shape):
    return jax.ShapeDtypeStruct(shape, jnp.float32)


def spread(dense, wide_ref):
    for b in range(dense.shape[0]):
        square = jnp.broadcast_to(dense[b : b + 1, :], (LANES, LANES))
        wide_ref[b * LANES : (b + 1) * LANES, :] = square.T


def terms_kernel(place, x_ref, *refs):
    pieces, (mass_ref, t_ref, out_ref, top_ref, sum_ref) = refs[:8], refs[8:]
    rows = x_ref.shape[0]
    top_ref[...] = jnp.full(top_ref.shape, -jnp.inf, jnp.float32)
    for k in range(8):
        half, shift = k // 4, k % 4
        for m in range(2):
            points = pieces[k][m * 256 : (m + 1) * 256, :]
            squares = points.astype(jnp.float32) ** 2
            squares = squares[:, :LANES] + squares[:, LANES:]
            product = lax.dot_general(
                x_ref[...], points, (((1,), (1,)), ((), ())), preferred_element_type=jnp.float32
            )
            both = None
            for side in range(2):
                inner = 2 * m + side
                shift_y, shift_x = (shift, inner) if half == 0 else (inner, shift)
                at_y = lax.rem(place[0] + (4 - shift_y), 4)
                at_x = lax.rem(place[1] + (4 - shift_x), 4)
                tile = 2 * (4 * at_y + at_x) + half
                square = squares[side * LANES : (side + 1) * LANES, :].T
                bias = (
                    mass_ref[pl.ds(tile, 1), :] / NATS
                    - jnp.sum(square, axis=0, keepdims=True) * 0.5
                )
                terms = product[:, side * LANES : (side + 1) * LANES] + bias
                t_ref[:, pl.ds(pl.multiple_of(tile * LANES, LANES), LANES)] = terms
                both = terms if both is None else jnp.maximum(both, terms)
            top_ref[...] = jnp.maximum(top_ref[...], both)

    def rows_step(r, unused):
        at = pl.ds(pl.multiple_of(r * STEP, STEP), STEP)
        top = jnp.max(top_ref[at, :], axis=1, keepdims=True)
        total = jnp.zeros((STEP, LANES), jnp.float32)
        for t in range(t_ref.shape[1] // LANES):
            total += jnp.exp2((t_ref[at, t * LANES : (t + 1) * LANES] - top) * BITS)
        top_ref[at, :] = jnp.broadcast_to(top, (STEP, LANES))
        sum_ref[at, :] = total
        return unused

    lax.fori_loop(0, rows // STEP, rows_step, 0)
    for b in range(rows // LANES):
        at = slice(b * LANES, (b + 1) * LANES)
        total = jnp.sum(sum_ref[at, :].T, axis=0, keepdims=True)
        top = top_ref[at, :].T[:1, :]
        out_ref[b : b + 1, :] = top * NATS + jnp.log(total)


def column_kernel(t_ref, lse_ref, mass_ref, out_ref, wide_ref):
    rows, columns = t_ref.shape
    spread((mass_ref[...] - lse_ref[...]) / NATS, wide_ref)
    block = 4 * LANES

    def tile(r, c, t):
        at = pl.ds(pl.multiple_of(r * STEP, STEP), STEP)
        column = pl.ds(pl.multiple_of(c * block + t * LANES, LANES), LANES)
        return (t_ref[at, column] + wide_ref[at, :]).reshape(STEP // 8, 8, LANES)

    for c in range(columns // block):

        def top_step(r, tops):
            return tuple(jnp.maximum(top, jnp.max(tile(r, c, t), axis=0)) for t, top in enumerate(tops))

        start = tuple(jnp.full((8, LANES), -jnp.inf, jnp.float32) for _ in range(4))
        tops = lax.fori_loop(0, rows // STEP, top_step, start)
        tops = [jnp.max(top, axis=0, keepdims=True) for top in tops]
        wide = [jnp.broadcast_to(top, (8, LANES))[None] for top in tops]

        def sum_step(r, totals):
            return tuple(
                total + jnp.sum(jnp.exp2((tile(r, c, t) - wide[t]) * BITS), axis=0)
                for t, total in enumerate(totals)
            )

        start = tuple(jnp.zeros((8, LANES), jnp.float32) for _ in range(4))
        totals = lax.fori_loop(0, rows // STEP, sum_step, start)
        for t in range(4):
            total = jnp.sum(totals[t], axis=0, keepdims=True)
            out_ref[c * 4 + t : c * 4 + t + 1, :] = tops[t] * NATS + jnp.log(total)


def plan_kernel(t_ref, row_ref, column_ref, plan_ref, out_ref, wide_ref, sum_ref):
    rows, columns = t_ref.shape
    spread(row_ref[...], wide_ref)

    def rows_step(r, unused):
        at = pl.ds(pl.multiple_of(r * STEP, STEP), STEP)
        total = jnp.zeros((STEP, LANES), jnp.float32)
        own = wide_ref[at, :]
        for t in range(columns // LANES):
            column = slice(t * LANES, (t + 1) * LANES)
            value = jnp.exp2(t_ref[at, column] * BITS + own + column_ref[t : t + 1, :])
            plan_ref[at, column] = value
            total += value
        sum_ref[at, :] = total
        return unused

    lax.fori_loop(0, rows // STEP, rows_step, 0)
    for b in range(rows // LANES):
        at = slice(b * LANES, (b + 1) * LANES)
        out_ref[b : b + 1, :] = jnp.sum(sum_ref[at, :].T, axis=0, keepdims=True)


def row_sums_kernel(plan_ref, scale_ref, out_ref, sum_ref):
    rows, columns = plan_ref.shape

    def rows_step(r, unused):
        at = pl.ds(pl.multiple_of(r * STEP, STEP), STEP)
        total = jnp.zeros((STEP, LANES), jnp.float32)
        for t in range(columns // LANES):
            total += plan_ref[at, t * LANES : (t + 1) * LANES] * scale_ref[t : t + 1, :]
        sum_ref[at, :] = total
        return unused

    lax.fori_loop(0, rows // STEP, rows_step, 0)
    for b in range(rows // LANES):
        at = slice(b * LANES, (b + 1) * LANES)
        out_ref[b : b + 1, :] = jnp.sum(sum_ref[at, :].T, axis=0, keepdims=True)


def column_sums_kernel(plan_ref, scale_ref, out_ref, wide_ref):
    rows, columns = plan_ref.shape
    spread(scale_ref[...], wide_ref)
    tiles = columns // LANES
    per = 16
    for c in range(0, tiles, per):

        def rows_step(r, totals):
            at = pl.ds(pl.multiple_of(r * STEP, STEP), STEP)
            own = wide_ref[at, :]
            return tuple(
                total
                + jnp.sum(
                    (plan_ref[at, (c + t) * LANES : (c + t + 1) * LANES] * own).reshape(
                        STEP // 8, 8, LANES
                    ),
                    axis=0,
                )
                for t, total in enumerate(totals)
            )

        start = tuple(jnp.zeros((8, LANES), jnp.float32) for _ in range(per))
        totals = lax.fori_loop(0, rows // STEP, rows_step, start)
        for t in range(per):
            out_ref[c + t : c + t + 1, :] = jnp.sum(totals[t], axis=0, keepdims=True)


def shifted(value, axis):
    n = lax.axis_size(axis)
    return [value] + [
        lax.ppermute(value, axis, [(i, (i + k) % n) for i in range(n)]) for k in range(1, n)
    ]


def add_all(parts):
    total = parts[0]
    for part in parts[1:]:
        total = total + part
    return total


def lse_all(parts):
    top = parts[0]
    for part in parts[1:]:
        top = jnp.maximum(top, part)
    return top + jnp.log(add_all([jnp.exp(part - top) for part in parts]))


def over(value, axes, combine):
    for axis in axes:
        value = combine(shifted(value, axis))
    return value


def gather_targets(points):
    half = points.shape[0] // 2
    first = jnp.concatenate(shifted(points[:half], "row_1"))
    second = jnp.concatenate(shifted(points[half:], "row_0"))
    return shifted(first, "row_0") + shifted(second, "row_1")


def body(src_points, tgt_points, log_src_mass, log_tgt_mass):
    rows, columns = src_points.shape[0], log_tgt_mass.shape[0]
    row_tiles, column_tiles = rows // LANES, columns // LANES
    src_mass = log_src_mass.reshape(row_tiles, LANES)
    tgt_mass = log_tgt_mass.reshape(column_tiles, LANES)
    place = jnp.stack([lax.axis_index("row_0"), lax.axis_index("row_1")]).astype(jnp.int32)
    wide = pltpu.VMEM((rows, LANES), jnp.float32)
    big = pltpu.VMEM((rows, columns), jnp.float32)

    def resident(value):
        return pltpu.with_memory_space_constraint(value, pltpu.VMEM)

    pieces = gather_targets(tgt_points)
    terms, lse = call(
        terms_kernel, (big, f32(row_tiles, LANES)), [SMEM] + [VMEM] * 10, [wide, wide]
    )(place, src_points, *pieces, tgt_mass)
    src_lse = over(lse, ("col_1", "col_0"), lse_all)
    lse = call(column_kernel, f32(column_tiles, LANES), [VMEM] * 3, [wide])(
        resident(terms), src_lse, src_mass
    )
    tgt_lse = over(lse, ("row_1", "row_0"), lse_all)
    plan, sums = call(
        plan_kernel, (big, f32(row_tiles, LANES)), [VMEM] * 3, [wide, wide], {0: 0}
    )(resident(terms), (src_mass - src_lse) * LOG2E, (tgt_mass - tgt_lse) * LOG2E)
    plan = resident(plan)
    src_mass_lin, tgt_mass_lin = jnp.exp(src_mass), jnp.exp(tgt_mass)
    col_call = call(column_sums_kernel, f32(column_tiles, LANES), [VMEM] * 2, [wide])
    row_call = call(row_sums_kernel, f32(row_tiles, LANES), [VMEM] * 2, [wide])
    src_sums = over(sums, ("col_1", "col_0"), add_all)
    tgt_sums = over(col_call(plan, src_mass_lin / src_sums), ("row_1", "row_0"), add_all)
    src_sums = over(row_call(plan, tgt_mass_lin / tgt_sums), ("col_1", "col_0"), add_all)
    tgt_sums = over(col_call(plan, src_mass_lin / src_sums), ("row_1", "row_0"), add_all)
    squares = jnp.sum(src_points.astype(jnp.float32) ** 2, axis=1).reshape(row_tiles, LANES)
    src_potential = -EPS * (src_lse + jnp.log(src_sums) - src_mass - squares / (WIDTH * EPS))
    tgt_potential = -EPS * (tgt_lse + jnp.log(tgt_sums) - 2.0 * tgt_mass)
    peers_row, peers_col = lax.axis_size(ROW), lax.axis_size(COL)
    src_mean = jnp.sum(src_potential) / (rows * peers_row)
    src_mean = over(jnp.full((8, LANES), src_mean), ("row_1", "row_0"), add_all)
    tgt_mean = jnp.sum(tgt_potential) / (columns * peers_col)
    tgt_mean = over(jnp.full((8, LANES), tgt_mean), ("col_1", "col_0"), add_all)
    mean_potentials = (src_mean + tgt_mean)[0, 0]
    return (src_potential.reshape(-1), tgt_potential.reshape(-1), mean_potentials)


def solution(mesh):
    finer = Mesh(mesh.devices.reshape(4, 4, 4, 2), ("row_0", "row_1", "col_0", "col_1"))
    placed = (P(ROW, None), P(COL_ROW, None), P(ROW), P(COL))
    return jax.shard_map(
        body, mesh=finer, in_specs=placed, out_specs=(P(ROW), P(COL), P()), check_vma=False
    )
```

time: 222 us -> 157 us (0.71)
  starting transfers between devices: 36.1 us -> 84.4 us
  waiting for transfers between devices: 75.8 us -> 32 us
  matrix products: 35.4 us -> 0 us
  blocking collectives: 32.4 us -> 0 us
  Pallas kernels: 0 us -> 28.5 us
  other arithmetic: 21 us -> 3.6 us
  local copies, waits for them, and re-layouts: 16.5 us -> 3.85 us
    ppermute x0 -> x52, starting transfers between devices: none -> 84.4 us  [shifted(): lax.ppermute(value, axis, [(i, (i + k) % n) for i in range(n)])]
    all_to_all x7 -> x0, waiting for transfers between devices: 75.8 us -> none  [from_everyone(): lax.all_to_all(jnp.broadcast_to(value[None], (peers, *value.shape)), axis...]
    all_to_all x7 -> x0, starting transfers between devices: 36.1 us -> none  [from_everyone(): lax.all_to_all(jnp.broadcast_to(value[None], (peers, *value.shape)), axis...]
    dot_general x24 -> x0, matrix products: 35.4 us -> none  [cost_block(): lax.dot_general(points_a, points_b, (((1,), (1,)), ((), ())), preferred_e...]
    psum x4 -> x0, blocking collectives: 32.4 us -> none  [over_axes(): value = lax.psum(value, axis)]
    ppermute x0 -> x52, waiting for transfers between devices: none -> 32 us  [shifted(): lax.ppermute(value, axis, [(i, (i + k) % n) for i in range(n)])]
    pallas_call x0 -> x6, Pallas kernels: none -> 28.5 us  [the longest x1 8.85 us: body(): call(terms_kernel, (big, f32(row_tiles, LANES)), [SMEM] + [VMEM] * 10, [w...]
    reduce_sum x28 -> x3, other arithmetic: 19.7 us -> 2.64 us  [the longest x1 1.22 us: body(): tgt_mean = jnp.sum(tgt_potential) / (columns * peers_col)]
  transfers between devices with their start and end apart: 7 -> 52, of which waited for: 7 -> 37; matrix products, arithmetic and copies ran while one was open for 0% -> 1% of each run, Pallas kernels for 0% -> 0%
where the time goes in v1:
time: 157 us; the launch traced here: 154 us
  starting transfers between devices  84.4 us (54%)
  waiting for transfers between devices  32 us (20%)
  Pallas kernels  28.5 us (18%)
  local copies, waits for them, and re-layouts  3.85 us (2%)
  other arithmetic  3.6 us (2%)
  between operations  2.12 us (1%)
    ppermute x52, starting transfers between devices, shifted(): lax.ppermute(value, axis, [(i, (i + k) % n) for i in range(n)])  84.4 us
    ppermute x52, waiting for transfers between devices, shifted(): lax.ppermute(value, axis, [(i, (i + k) % n) for i in range(n)])  32 us
    pallas_call x1, Pallas kernels, body(): call(terms_kernel, (big, f32(row_tiles, LANES)), [SMEM] + [VMEM] * 10, [w...  8.85 us
    pallas_call x1, Pallas kernels, body(): call(plan_kernel, (big, f32(row_tiles, LANES)), [VMEM] * 3, [wide, wide],...  7.52 us
    pallas_call x1, Pallas kernels, body(): call(column_kernel, f32(column_tiles, LANES), [VMEM] * 3, [wide])  6.94 us
    pallas_call x2, Pallas kernels, body(): col_call(plan, src_mass_lin / src_sums)  3.34 us
  transfers between devices with their start and end apart: 52, of which 37 were waited for; matrix products, arithmetic and copies ran while one was open for 1% of the time, Pallas kernels for 0%

profile of v1, /device:TPU:1, one launch (start us, length us, event | category | flops | bytes accessed | tf_op | source)
XLA Modules:
  0.0 154.4 jit_solution(14833438015982906028)
XLA Ops:
  1.5 2.2 %collective-permute-start.6 = (bf16[128,256]{1,0:T(8,128)(2,1)S(1)}, bf16[128,256]{1,0:T(8,128)(2,1)S(1)}, u32[]{:S(2)}, u32[]{:S(2)}) collective-permute-start(bf16[128,256]{1,0:T(8,128)(2,1)S(1)} %get-tuple-element.20), channel_id=1, source_target_pairs={{0,32},{32,64},{64,96},{96,0},{1,33},{33,65},{65,97},{97,1},{2,34}... | collective-permute-start | bytes 196616 | tf_op jit(solution)/shard_map/ppermute | solution.py:200
  3.7 2.6 %collective-permute-start.7 = (bf16[128,256]{1,0:T(8,128)(2,1)S(1)}, bf16[128,256]{1,0:T(8,128)(2,1)S(1)}, u32[]{:S(2)}, u32[]{:S(2)}) collective-permute-start(bf16[128,256]{1,0:T(8,128)(2,1)S(1)} %get-tuple-element.20), channel_id=1, source_target_pairs={{0,64},{32,96},{64,0},{96,32},{1,65},{33,97},{65,1},{97,33},{2,66}... | collective-permute-start | bytes 196616 | tf_op jit(solution)/shard_map/ppermute | solution.py:200
  9.8 2.8 %collective-permute-start.10 = (bf16[512,256]{1,0:T(8,128)(2,1)S(1)}, bf16[512,256]{1,0:T(8,128)(2,1)S(1)}, u32[]{:S(2)}, u32[]{:S(2)}) collective-permute-start(bf16[512,256]{1,0:T(8,128)(2,1)S(1)} %pad_maximum_fusion.1.refs_4_), channel_id=1, source_target_pairs={{0,16},{8,24},{16,0},{24,8},{1,17},{9,25},{17,1},{25,9},{2,18},{10... | collective-permute-start | bytes 786440 | tf_op jit(solution)/shard_map/ppermute | solution.py:200
  16.2 2.3 %collective-permute-done = bf16[128,256]{1,0:T(8,128)(2,1)S(1)} collective-permute-done((bf16[128,256]{1,0:T(8,128)(2,1)S(1)}, bf16[128,256]{1,0:T(8,128)(2,1)S(1)}, u32[]{:S(2)}, u32[]{:S(2)}) %collective-permute-start) | collective-permute-done | bytes 65568 | tf_op jit(solution)/shard_map/ppermute | solution.py:200
  20.1 3.2 %collective-permute-start.4 = (bf16[512,256]{1,0:T(8,128)(2,1)S(1)}, bf16[512,256]{1,0:T(8,128)(2,1)S(1)}, u32[]{:S(2)}, u32[]{:S(2)}) collective-permute-start(bf16[512,256]{1,0:T(8,128)(2,1)S(1)} %pad_maximum_fusion.refs_0_), channel_id=1, source_target_pairs={{0,64},{32,96},{64,0},{96,32},{1,65},{33,97},{65,1},{97,33},{2,66}... | collective-permute-start | bytes 786440 | tf_op jit(solution)/shard_map/ppermute | solution.py:200
  23.4 3.0 %collective-permute-done.11.refs_7_ = bf16[512,256]{1,0:T(8,128)(2,1)S(1)} collective-permute-done((bf16[512,256]{1,0:T(8,128)(2,1)S(1)}, bf16[512,256]{1,0:T(8,128)(2,1)S(1)}, u32[]{:S(2)}, u32[]{:S(2)}) %collective-permute-start.11) | collective-permute-done | bytes 262176 | tf_op jit(solution)/shard_map/ppermute | solution.py:200
  26.8 3.0 %collective-permute-done.4.refs_2_ = bf16[512,256]{1,0:T(8,128)(2,1)S(1)} collective-permute-done((bf16[512,256]{1,0:T(8,128)(2,1)S(1)}, bf16[512,256]{1,0:T(8,128)(2,1)S(1)}, u32[]{:S(2)}, u32[]{:S(2)}) %collective-permute-start.4) | collective-permute-done | bytes 262176 | tf_op jit(solution)/shard_map/ppermute | solution.py:200
  32.0 8.8 %shard_map.67 = (f32[1024,4096]{1,0:T(8,128)S(1)}, f32[8,128]{1,0:T(8,128)S(1)}) custom-call(s32[2]{0:T(128)S(1)} %pad_add_fusion.place, bf16[1024,256]{1,0:T(8,128)(2,1)S(1)} %copy-done, bf16[512,256]{1,0:T(8,128)(2,1)S(1)} %pad_maximum_fusion.refs_0_, bf16[512,256]{1,0:T(8,128)(2,1)S(1)} %collective-permute-done.3.refs_1_, ...), custom_call_target="tpu_custom_call" | custom-call | tf_op jit(solution)/shard_map/pallas_call | solution.py:244
  40.8 6.8 %collective-permute-start.12 = (f32[8,128]{1,0:T(8,128)S(1)}, f32[8,128]{1,0:T(8,128)S(1)}, u32[]{:S(2)}, u32[]{:S(2)}) collective-permute-start(f32[8,128]{1,0:T(8,128)S(1)} %get-tuple-element.7), channel_id=1, source_target_pairs={{0,1},{1,0},{2,3},{3,2},{4,5},{5,4},{6,7},{7,6},{8,9},{9,8},{10,11... | collective-permute-start | bytes 12296 | tf_op jit(solution)/shard_map/ppermute | solution.py:200
  50.2 3.3 %collective-permute-start.14 = (f32[8,128]{1,0:T(8,128)S(1)}, f32[8,128]{1,0:T(8,128)S(1)}, u32[]{:S(2)}, u32[]{:S(2)}) collective-permute-start(f32[8,128]{1,0:T(8,128)S(1)} %log_add_fusion.3), channel_id=1, source_target_pairs={{0,4},{2,6},{4,0},{6,2},{1,5},{3,7},{5,1},{7,3},{8,12},{10,14},{12... | collective-permute-start | bytes 12296 | tf_op jit(solution)/shard_map/ppermute | solution.py:200
  57.4 6.9 %shard_map.68 = f32[32,128]{1,0:T(8,128)S(1)} custom-call(f32[1024,4096]{1,0:T(8,128)S(1)} %get-tuple-element.8.t_ref, f32[8,128]{1,0:T(8,128)S(1)} %get-tuple-element.19.lse_ref, f32[8,128]{1,0:T(8,128)S(1)} %bitcast.22), custom_call_target="tpu_custom_call" | custom-call | tf_op jit(solution)/shard_map/pallas_call | solution.py:248
  64.8 2.4 %collective-permute-start.17 = (f32[32,128]{1,0:T(8,128)S(1)}, f32[32,128]{1,0:T(8,128)S(1)}, u32[]{:S(2)}, u32[]{:S(2)}) collective-permute-start(f32[32,128]{1,0:T(8,128)S(1)} %shard_map.68), channel_id=1, source_target_pairs={{0,16},{8,24},{16,0},{24,8},{1,17},{9,25},{17,1},{25,9},{2,18},{10... | collective-permute-start | bytes 49160 | tf_op jit(solution)/shard_map/ppermute | solution.py:200
  70.4 3.0 %collective-permute-start.20 = (f32[32,128]{1,0:T(8,128)S(1)}, f32[32,128]{1,0:T(8,128)S(1)}, u32[]{:S(2)}, u32[]{:S(2)}) collective-permute-start(f32[32,128]{1,0:T(8,128)S(1)} %log_add_fusion.1), channel_id=1, source_target_pairs={{0,64},{32,96},{64,0},{96,32},{1,65},{33,97},{65,1},{97,33},{2,66}... | collective-permute-start | bytes 49160 | tf_op jit(solution)/shard_map/ppermute | solution.py:200
  76.0 7.5 %shard_map.69 = (f32[1024,4096]{1,0:T(8,128)S(1)}, f32[8,128]{1,0:T(8,128)S(1)}) custom-call(f32[1024,4096]{1,0:T(8,128)S(1)} %get-tuple-element.8.t_ref, f32[8,128]{1,0:T(8,128)S(1)} %get-tuple-element.18.row_ref, f32[32,128]{1,0:T(8,128)S(1)} %get-tuple-element.16.column_ref), custom_call_target="tpu_custom_call", output_to_operand_aliasing={{0}: (0, {})} | custom-call | tf_op jit(solution)/shard_map/pallas_call | solution.py:252
  83.5 5.6 %collective-permute-start.22 = (f32[8,128]{1,0:T(8,128)S(1)}, f32[8,128]{1,0:T(8,128)S(1)}, u32[]{:S(2)}, u32[]{:S(2)}) collective-permute-start(f32[8,128]{1,0:T(8,128)S(1)} %get-tuple-element.10), channel_id=1, source_target_pairs={{0,1},{1,0},{2,3},{3,2},{4,5},{5,4},{6,7},{7,6},{8,9},{9,8},{10,11... | collective-permute-start | bytes 12296 | tf_op jit(solution)/shard_map/ppermute | solution.py:200
  89.9 3.1 %collective-permute-start.24 = (f32[8,128]{1,0:T(8,128)S(1)}, f32[8,128]{1,0:T(8,128)S(1)}, u32[]{:S(2)}, u32[]{:S(2)}) collective-permute-start(f32[8,128]{1,0:T(8,128)S(1)} %add.155), channel_id=1, source_target_pairs={{0,4},{2,6},{4,0},{6,2},{1,5},{3,7},{5,1},{7,3},{8,12},{10,14},{12... | collective-permute-start | bytes 12296 | tf_op jit(solution)/shard_map/ppermute | solution.py:200
  97.7 3.1 %collective-permute-start.27 = (f32[32,128]{1,0:T(8,128)S(1)}, f32[32,128]{1,0:T(8,128)S(1)}, u32[]{:S(2)}, u32[]{:S(2)}) collective-permute-start(f32[32,128]{1,0:T(8,128)S(1)} %shard_map.70), channel_id=1, source_target_pairs={{0,16},{8,24},{16,0},{24,8},{1,17},{9,25},{17,1},{25,9},{2,18},{10... | collective-permute-start | bytes 49160 | tf_op jit(solution)/shard_map/ppermute | solution.py:200
  103.8 2.1 %collective-permute-start.30 = (f32[32,128]{1,0:T(8,128)S(1)}, f32[32,128]{1,0:T(8,128)S(1)}, u32[]{:S(2)}, u32[]{:S(2)}) collective-permute-start(f32[32,128]{1,0:T(8,128)S(1)} %add_add_fusion.1), channel_id=1, source_target_pairs={{0,64},{32,96},{64,0},{96,32},{1,65},{33,97},{65,1},{97,33},{2,66}... | collective-permute-start | bytes 49160 | tf_op jit(solution)/shard_map/ppermute | solution.py:200
  110.4 5.3 %collective-permute-start.32 = (f32[8,128]{1,0:T(8,128)S(1)}, f32[8,128]{1,0:T(8,128)S(1)}, u32[]{:S(2)}, u32[]{:S(2)}) collective-permute-start(f32[8,128]{1,0:T(8,128)S(1)} %shard_map.71), channel_id=1, source_target_pairs={{0,1},{1,0},{2,3},{3,2},{4,5},{5,4},{6,7},{7,6},{8,9},{9,8},{10,11... | collective-permute-start | bytes 12296 | tf_op jit(solution)/shard_map/ppermute | solution.py:200
  116.6 2.4 %collective-permute-start.34 = (f32[8,128]{1,0:T(8,128)S(1)}, f32[8,128]{1,0:T(8,128)S(1)}, u32[]{:S(2)}, u32[]{:S(2)}) collective-permute-start(f32[8,128]{1,0:T(8,128)S(1)} %add.165), channel_id=1, source_target_pairs={{0,4},{2,6},{4,0},{6,2},{1,5},{3,7},{5,1},{7,3},{8,12},{10,14},{12... | collective-permute-start | bytes 12296 | tf_op jit(solution)/shard_map/ppermute | solution.py:200
  130.6 2.4 %collective-permute-start.40 = (f32[32,128]{1,0:T(8,128)S(1)}, f32[32,128]{1,0:T(8,128)S(1)}, u32[]{:S(2)}, u32[]{:S(2)}) collective-permute-start(f32[32,128]{1,0:T(8,128)S(1)} %add_add_fusion), channel_id=1, source_target_pairs={{0,64},{32,96},{64,0},{96,32},{1,65},{33,97},{65,1},{97,33},{2,66}... | collective-permute-start | bytes 49160 | tf_op jit(solution)/shard_map/ppermute | solution.py:200
  135.0 2.5 %collective-permute-start.43 = (f32[8,128]{1,0:T(8,128)S(1)}, f32[8,128]{1,0:T(8,128)S(1)}, u32[]{:S(2)}, u32[]{:S(2)}) collective-permute-start(f32[8,128]{1,0:T(8,128)S(1)} %broadcast_in_dim.6), channel_id=1, source_target_pairs={{0,16},{8,24},{16,0},{24,8},{1,17},{9,25},{17,1},{25,9},{2,18},{10... | collective-permute-start | bytes 12296 | tf_op jit(solution)/shard_map/ppermute | solution.py:200
  139.4 4.6 %collective-permute-start.48 = (f32[8,128]{1,0:T(8,128)S(1)}, f32[8,128]{1,0:T(8,128)S(1)}, u32[]{:S(2)}, u32[]{:S(2)}) collective-permute-start(f32[8,128]{1,0:T(8,128)S(1)} %broadcast_in_dim.7), channel_id=1, source_target_pairs={{0,1},{1,0},{2,3},{3,2},{4,5},{5,4},{6,7},{7,6},{8,9},{9,8},{10,11... | collective-permute-start | bytes 12296 | tf_op jit(solution)/shard_map/ppermute | solution.py:200
  149.0 2.4 %collective-permute-start.50 = (f32[8,128]{1,0:T(8,128)S(1)}, f32[8,128]{1,0:T(8,128)S(1)}, u32[]{:S(2)}, u32[]{:S(2)}) collective-permute-start(f32[8,128]{1,0:T(8,128)S(1)} %broadcast_add_fusion), channel_id=1, source_target_pairs={{0,4},{2,6},{4,0},{6,2},{1,5},{3,7},{5,1},{7,3},{8,12},{10,14},{12... | collective-permute-start | bytes 12296 | tf_op jit(solution)/shard_map/ppermute | solution.py:200
  (118 shorter events, 60.7 us)
Async XLA Ops:
  1.5 5.9 %collective-permute-start.6 = (bf16[128,256]{1,0:T(8,128)(2,1)S(1)}, bf16[128,256]{1,0:T(8,128)(2,1)S(1)}, u32[]{:S(2)}, u32[]{:S(2)}) collective-permute-start(bf16[128,256]{1,0:T(8,128)(2,1)S(1)} %get-tuple-element.20), channel_id=1, source_target_pairs={{0,32},{32,64},{64,96},{96,0},{1,33},{33,65},{65,97},{97,1},{2,34}... | collective-permute-start | bytes 196616 | tf_op jit(solution)/shard_map/ppermute | solution.py:200
  3.7 5.2 %collective-permute-start.7 = (bf16[128,256]{1,0:T(8,128)(2,1)S(1)}, bf16[128,256]{1,0:T(8,128)(2,1)S(1)}, u32[]{:S(2)}, u32[]{:S(2)}) collective-permute-start(bf16[128,256]{1,0:T(8,128)(2,1)S(1)} %get-tuple-element.20), channel_id=1, source_target_pairs={{0,64},{32,96},{64,0},{96,32},{1,65},{33,97},{65,1},{97,33},{2,66}... | collective-permute-start | bytes 196616 | tf_op jit(solution)/shard_map/ppermute | solution.py:200
  9.8 13.5 %collective-permute-start.10 = (bf16[512,256]{1,0:T(8,128)(2,1)S(1)}, bf16[512,256]{1,0:T(8,128)(2,1)S(1)}, u32[]{:S(2)}, u32[]{:S(2)}) collective-permute-start(bf16[512,256]{1,0:T(8,128)(2,1)S(1)} %pad_maximum_fusion.1.refs_4_), channel_id=1, source_target_pairs={{0,16},{8,24},{16,0},{24,8},{1,17},{9,25},{17,1},{25,9},{2,18},{10... | collective-permute-start | bytes 786440 | tf_op jit(solution)/shard_map/ppermute | solution.py:200
  12.6 5.9 %collective-permute-start = (bf16[128,256]{1,0:T(8,128)(2,1)S(1)}, bf16[128,256]{1,0:T(8,128)(2,1)S(1)}, u32[]{:S(2)}, u32[]{:S(2)}) collective-permute-start(bf16[128,256]{1,0:T(8,128)(2,1)S(1)} %get-tuple-element.21), channel_id=1, source_target_pairs={{0,8},{8,16},{16,24},{24,0},{1,9},{9,17},{17,25},{25,1},{2,10},{10... | collective-permute-start | bytes 196616 | tf_op jit(solution)/shard_map/ppermute | solution.py:200
  12.9 7.0 %collective-permute-start.1 = (bf16[128,256]{1,0:T(8,128)(2,1)S(1)}, bf16[128,256]{1,0:T(8,128)(2,1)S(1)}, u32[]{:S(2)}, u32[]{:S(2)}) collective-permute-start(bf16[128,256]{1,0:T(8,128)(2,1)S(1)} %get-tuple-element.21), channel_id=1, source_target_pairs={{0,16},{8,24},{16,0},{24,8},{1,17},{9,25},{17,1},{25,9},{2,18},{10... | collective-permute-start | bytes 196616 | tf_op jit(solution)/shard_map/ppermute | solution.py:200
  14.6 5.3 %collective-permute-start.2 = (bf16[128,256]{1,0:T(8,128)(2,1)S(1)}, bf16[128,256]{1,0:T(8,128)(2,1)S(1)}, u32[]{:S(2)}, u32[]{:S(2)}) collective-permute-start(bf16[128,256]{1,0:T(8,128)(2,1)S(1)} %get-tuple-element.21), channel_id=1, source_target_pairs={{0,24},{8,0},{16,8},{24,16},{1,25},{9,1},{17,9},{25,17},{2,26},{10... | collective-permute-start | bytes 196616 | tf_op jit(solution)/shard_map/ppermute | solution.py:200
  15.3 11.1 %collective-permute-start.11 = (bf16[512,256]{1,0:T(8,128)(2,1)S(1)}, bf16[512,256]{1,0:T(8,128)(2,1)S(1)}, u32[]{:S(2)}, u32[]{:S(2)}) collective-permute-start(bf16[512,256]{1,0:T(8,128)(2,1)S(1)} %pad_maximum_fusion.1.refs_4_), channel_id=1, source_target_pairs={{0,24},{8,0},{16,8},{24,16},{1,25},{9,1},{17,9},{25,17},{2,26},{10... | collective-permute-start | bytes 786440 | tf_op jit(solution)/shard_map/ppermute | solution.py:200
  18.5 7.9 %collective-permute-start.9 = (bf16[512,256]{1,0:T(8,128)(2,1)S(1)}, bf16[512,256]{1,0:T(8,128)(2,1)S(1)}, u32[]{:S(2)}, u32[]{:S(2)}) collective-permute-start(bf16[512,256]{1,0:T(8,128)(2,1)S(1)} %pad_maximum_fusion.1.refs_4_), channel_id=1, source_target_pairs={{0,8},{8,16},{16,24},{24,0},{1,9},{9,17},{17,25},{25,1},{2,10},{10... | collective-permute-start | bytes 786440 | tf_op jit(solution)/shard_map/ppermute | solution.py:200
  20.0 6.8 %collective-permute-start.3 = (bf16[512,256]{1,0:T(8,128)(2,1)S(1)}, bf16[512,256]{1,0:T(8,128)(2,1)S(1)}, u32[]{:S(2)}, u32[]{:S(2)}) collective-permute-start(bf16[512,256]{1,0:T(8,128)(2,1)S(1)} %pad_maximum_fusion.refs_0_), channel_id=1, source_target_pairs={{0,32},{32,64},{64,96},{96,0},{1,33},{33,65},{65,97},{97,1},{2,34}... | collective-permute-start | bytes 786440 | tf_op jit(solution)/shard_map/ppermute | solution.py:200
  20.1 9.8 %collective-permute-start.4 = (bf16[512,256]{1,0:T(8,128)(2,1)S(1)}, bf16[512,256]{1,0:T(8,128)(2,1)S(1)}, u32[]{:S(2)}, u32[]{:S(2)}) collective-permute-start(bf16[512,256]{1,0:T(8,128)(2,1)S(1)} %pad_maximum_fusion.refs_0_), channel_id=1, source_target_pairs={{0,64},{32,96},{64,0},{96,32},{1,65},{33,97},{65,1},{97,33},{2,66}... | collective-permute-start | bytes 786440 | tf_op jit(solution)/shard_map/ppermute | solution.py:200
  23.3 7.0 %collective-permute-start.5 = (bf16[512,256]{1,0:T(8,128)(2,1)S(1)}, bf16[512,256]{1,0:T(8,128)(2,1)S(1)}, u32[]{:S(2)}, u32[]{:S(2)}) collective-permute-start(bf16[512,256]{1,0:T(8,128)(2,1)S(1)} %pad_maximum_fusion.refs_0_), channel_id=1, source_target_pairs={{0,96},{32,0},{64,32},{96,64},{1,97},{33,1},{65,33},{97,65},{2,98}... | collective-permute-start | bytes 786440 | tf_op jit(solution)/shard_map/ppermute | solution.py:200
  40.8 7.7 %collective-permute-start.12 = (f32[8,128]{1,0:T(8,128)S(1)}, f32[8,128]{1,0:T(8,128)S(1)}, u32[]{:S(2)}, u32[]{:S(2)}) collective-permute-start(f32[8,128]{1,0:T(8,128)S(1)} %get-tuple-element.7), channel_id=1, source_target_pairs={{0,1},{1,0},{2,3},{3,2},{4,5},{5,4},{6,7},{7,6},{8,9},{9,8},{10,11... | collective-permute-start | bytes 12296 | tf_op jit(solution)/shard_map/ppermute | solution.py:200
  48.5 5.7 %collective-permute-start.13 = (f32[8,128]{1,0:T(8,128)S(1)}, f32[8,128]{1,0:T(8,128)S(1)}, u32[]{:S(2)}, u32[]{:S(2)}) collective-permute-start(f32[8,128]{1,0:T(8,128)S(1)} %log_add_fusion.3), channel_id=1, source_target_pairs={{0,2},{2,4},{4,6},{6,0},{1,3},{3,5},{5,7},{7,1},{8,10},{10,12},{12... | collective-permute-start | bytes 12296 | tf_op jit(solution)/shard_map/ppermute | solution.py:200
  83.5 6.4 %collective-permute-start.22 = (f32[8,128]{1,0:T(8,128)S(1)}, f32[8,128]{1,0:T(8,128)S(1)}, u32[]{:S(2)}, u32[]{:S(2)}) collective-permute-start(f32[8,128]{1,0:T(8,128)S(1)} %get-tuple-element.10), channel_id=1, source_target_pairs={{0,1},{1,0},{2,3},{3,2},{4,5},{5,4},{6,7},{7,6},{8,9},{9,8},{10,11... | collective-permute-start | bytes 12296 | tf_op jit(solution)/shard_map/ppermute | solution.py:200
  110.4 6.1 %collective-permute-start.32 = (f32[8,128]{1,0:T(8,128)S(1)}, f32[8,128]{1,0:T(8,128)S(1)}, u32[]{:S(2)}, u32[]{:S(2)}) collective-permute-start(f32[8,128]{1,0:T(8,128)S(1)} %shard_map.71), channel_id=1, source_target_pairs={{0,1},{1,0},{2,3},{3,2},{4,5},{5,4},{6,7},{7,6},{8,9},{9,8},{10,11... | collective-permute-start | bytes 12296 | tf_op jit(solution)/shard_map/ppermute | solution.py:200
  129.5 8.0 %collective-permute-start.39 = (f32[32,128]{1,0:T(8,128)S(1)}, f32[32,128]{1,0:T(8,128)S(1)}, u32[]{:S(2)}, u32[]{:S(2)}) collective-permute-start(f32[32,128]{1,0:T(8,128)S(1)} %add_add_fusion), channel_id=1, source_target_pairs={{0,32},{32,64},{64,96},{96,0},{1,33},{33,65},{65,97},{97,1},{2,34}... | collective-permute-start | bytes 49160 | tf_op jit(solution)/shard_map/ppermute | solution.py:200
  130.6 6.9 %collective-permute-start.40 = (f32[32,128]{1,0:T(8,128)S(1)}, f32[32,128]{1,0:T(8,128)S(1)}, u32[]{:S(2)}, u32[]{:S(2)}) collective-permute-start(f32[32,128]{1,0:T(8,128)S(1)} %add_add_fusion), channel_id=1, source_target_pairs={{0,64},{32,96},{64,0},{96,32},{1,65},{33,97},{65,1},{97,33},{2,66}... | collective-permute-start | bytes 49160 | tf_op jit(solution)/shard_map/ppermute | solution.py:200
  133.8 10.3 %collective-permute-start.42 = (f32[8,128]{1,0:T(8,128)S(1)}, f32[8,128]{1,0:T(8,128)S(1)}, u32[]{:S(2)}, u32[]{:S(2)}) collective-permute-start(f32[8,128]{1,0:T(8,128)S(1)} %broadcast_in_dim.6), channel_id=1, source_target_pairs={{0,8},{8,16},{16,24},{24,0},{1,9},{9,17},{17,25},{25,1},{2,10},{10... | collective-permute-start | bytes 12296 | tf_op jit(solution)/shard_map/ppermute | solution.py:200
  135.0 9.1 %collective-permute-start.43 = (f32[8,128]{1,0:T(8,128)S(1)}, f32[8,128]{1,0:T(8,128)S(1)}, u32[]{:S(2)}, u32[]{:S(2)}) collective-permute-start(f32[8,128]{1,0:T(8,128)S(1)} %broadcast_in_dim.6), channel_id=1, source_target_pairs={{0,16},{8,24},{16,0},{24,8},{1,17},{9,25},{17,1},{25,9},{2,18},{10... | collective-permute-start | bytes 12296 | tf_op jit(solution)/shard_map/ppermute | solution.py:200
  137.5 6.6 %collective-permute-start.44 = (f32[8,128]{1,0:T(8,128)S(1)}, f32[8,128]{1,0:T(8,128)S(1)}, u32[]{:S(2)}, u32[]{:S(2)}) collective-permute-start(f32[8,128]{1,0:T(8,128)S(1)} %broadcast_in_dim.6), channel_id=1, source_target_pairs={{0,24},{8,0},{16,8},{24,16},{1,25},{9,1},{17,9},{25,17},{2,26},{10... | collective-permute-start | bytes 12296 | tf_op jit(solution)/shard_map/ppermute | solution.py:200
  139.4 8.9 %collective-permute-start.48 = (f32[8,128]{1,0:T(8,128)S(1)}, f32[8,128]{1,0:T(8,128)S(1)}, u32[]{:S(2)}, u32[]{:S(2)}) collective-permute-start(f32[8,128]{1,0:T(8,128)S(1)} %broadcast_in_dim.7), channel_id=1, source_target_pairs={{0,1},{1,0},{2,3},{3,2},{4,5},{5,4},{6,7},{7,6},{8,9},{9,8},{10,11... | collective-permute-start | bytes 12296 | tf_op jit(solution)/shard_map/ppermute | solution.py:200
  144.1 7.4 %collective-permute-start.45 = (f32[8,128]{1,0:T(8,128)S(1)}, f32[8,128]{1,0:T(8,128)S(1)}, u32[]{:S(2)}, u32[]{:S(2)}) collective-permute-start(f32[8,128]{1,0:T(8,128)S(1)} %add_add_fusion.3), channel_id=1, source_target_pairs={{0,32},{32,64},{64,96},{96,0},{1,33},{33,65},{65,97},{97,1},{2,34}... | collective-permute-start | bytes 12296 | tf_op jit(solution)/shard_map/ppermute | solution.py:200
  145.9 5.8 %collective-permute-start.46 = (f32[8,128]{1,0:T(8,128)S(1)}, f32[8,128]{1,0:T(8,128)S(1)}, u32[]{:S(2)}, u32[]{:S(2)}) collective-permute-start(f32[8,128]{1,0:T(8,128)S(1)} %add_add_fusion.3), channel_id=1, source_target_pairs={{0,64},{32,96},{64,0},{96,32},{1,65},{33,97},{65,1},{97,33},{2,66}... | collective-permute-start | bytes 12296 | tf_op jit(solution)/shard_map/ppermute | solution.py:200
  146.4 5.3 %collective-permute-start.47 = (f32[8,128]{1,0:T(8,128)S(1)}, f32[8,128]{1,0:T(8,128)S(1)}, u32[]{:S(2)}, u32[]{:S(2)}) collective-permute-start(f32[8,128]{1,0:T(8,128)S(1)} %add_add_fusion.3), channel_id=1, source_target_pairs={{0,96},{32,0},{64,32},{96,64},{1,97},{33,1},{65,33},{97,65},{2,98}... | collective-permute-start | bytes 12296 | tf_op jit(solution)/shard_map/ppermute | solution.py:200
  (32 other events, 131.1 us)

commit v2 on v0

v2 whole, which is shorter than its diff:
```python
import itertools
import math

import jax
import jax.numpy as jnp
from jax import lax
from jax.experimental import pallas as pl
from jax.experimental.pallas import tpu as pltpu
from jax.sharding import Mesh
from jax.sharding import PartitionSpec as P

ROW = ("row_0", "row_1")
COL = ("col_0", "col_1")
COL_ROW = ("col_0", "col_1", "row_0", "row_1")

EPS = 0.1
WIDTH = 256
NATS = 2.0 / (WIDTH * EPS)
BITS = NATS * math.log2(math.e)
LOG2E = math.log2(math.e)
VMEM_LIMIT = 24 * 1024 * 1024
LANES = 128
STEP = 64
HUGE = 3.0e38

VMEM = pl.BlockSpec(memory_space=pltpu.VMEM)
SMEM = pl.BlockSpec(memory_space=pltpu.SMEM)


def call(kernel, outs, ins, scratch, aliases=None):
    return pl.pallas_call(
        kernel,
        out_shape=outs,
        in_specs=ins,
        out_specs=jax.tree.map(lambda _: VMEM, outs),
        scratch_shapes=scratch,
        input_output_aliases=aliases or {},
        compiler_params=pltpu.CompilerParams(vmem_limit_bytes=VMEM_LIMIT),
    )


def f32(*shape):
    return jax.ShapeDtypeStruct(shape, jnp.float32)


def spread(dense, wide_ref):
    for b in range(dense.shape[0]):
        square = jnp.broadcast_to(dense[b : b + 1, :], (LANES, LANES))
        wide_ref[b * LANES : (b + 1) * LANES, :] = square.T


def collapse(wide_ref):
    lines = [
        jnp.sum(wide_ref[b * LANES : (b + 1) * LANES, :].T, axis=0, keepdims=True)
        for b in range(wide_ref.shape[0] // LANES)
    ]
    return jnp.concatenate(lines, axis=0)


def collapse_top(wide_ref):
    lines = [
        wide_ref[b * LANES : (b + 1) * LANES, :].T[:1, :]
        for b in range(wide_ref.shape[0] // LANES)
    ]
    return jnp.concatenate(lines, axis=0)


def add_all(parts):
    total = parts[0]
    for part in parts[1:]:
        total = total + part
    return total


def lse_all(parts):
    top = parts[0]
    for part in parts[1:]:
        top = jnp.maximum(top, part)
    return top + jnp.log(add_all([jnp.exp(part - top) for part in parts]))


def at_rows(r):
    return pl.ds(pl.multiple_of(r * STEP, STEP), STEP)


def lane_tile(t):
    return slice(t * LANES, (t + 1) * LANES)


def target_block(place, shift, inner):
    first_core = place[2] == 0
    shift_y = jnp.where(first_core, shift, inner)
    shift_x = jnp.where(first_core, inner, shift)
    return 4 * lax.rem(place[0] + 4 - shift_y, 4) + lax.rem(place[1] + 4 - shift_x, 4)


def chunk_terms(x_ref, points, mass_ref, block):
    squares = points.astype(jnp.float32) ** 2
    squares = squares[:, :LANES] + squares[:, LANES:]
    product = lax.dot_general(
        x_ref[...], points, (((1,), (1,)), ((), ())), preferred_element_type=jnp.float32
    )
    found = []
    for side in range(2):
        square = squares[side * LANES : (side + 1) * LANES, :].T
        mass = mass_ref[pl.ds(2 * block + side, 1), :]
        bias = mass / NATS - jnp.sum(square, axis=0, keepdims=True) * 0.5
        found.append(product[:, lane_tile(side)] + bias)
    return found


def block_columns(block, side):
    return pl.ds(pl.multiple_of(block * 256 + side * LANES, LANES), LANES)


def first_terms_kernel(place, x_ref, points_ref, mass_ref, t_ref, top_ref, sum_ref):
    rows = x_ref.shape[0]
    blocks = [target_block(place, 0, m) for m in range(4)]
    for m in range(4):
        both = chunk_terms(x_ref, points_ref[m * 256 : (m + 1) * 256, :], mass_ref, blocks[m])
        for side in range(2):
            t_ref[:, block_columns(blocks[m], side)] = both[side]
        top = jnp.maximum(both[0], both[1])
        top_ref[...] = top if m == 0 else jnp.maximum(top_ref[...], top)

    def rows_step(r, unused):
        at = at_rows(r)
        top = jnp.max(top_ref[at, :], axis=1, keepdims=True)
        total = jnp.zeros((STEP, LANES), jnp.float32)
        for m in range(4):
            for side in range(2):
                terms = t_ref[at, block_columns(blocks[m], side)]
                total += jnp.exp2((terms - top) * BITS)
        top_ref[at, :] = jnp.broadcast_to(top, (STEP, LANES))
        sum_ref[at, :] = total
        return unused

    lax.fori_loop(0, rows // STEP, rows_step, 0)


def terms_kernel(place, x_ref, old_ref, first_top_ref, first_sum_ref, *refs):
    pieces, (mass_ref, t_ref, out_ref, top_ref, sum_ref) = refs[:3], refs[3:]
    rows, columns = t_ref.shape
    sum_ref[...] = first_sum_ref[...]
    for k in range(3):

        def chunk_step(m, unused):
            block = target_block(place, k + 1, m)
            points = pieces[k][pl.ds(pl.multiple_of(m * 256, 256), 256), :]
            both = chunk_terms(x_ref, points, mass_ref, block)
            top = first_top_ref[...]
            total = sum_ref[...]
            for side in range(2):
                t_ref[:, block_columns(block, side)] = both[side]
                total += jnp.exp2((both[side] - top) * BITS)
            sum_ref[...] = total
            return unused

        lax.fori_loop(0, 4, chunk_step, 0)
    total = collapse(sum_ref)
    out_ref[...] = collapse_top(first_top_ref) * NATS + jnp.log(total)

    @pl.when(jnp.logical_not(jnp.max(total) < HUGE))
    def exact():
        def rows_step(r, unused):
            at = at_rows(r)
            top = jnp.full((STEP, LANES), -jnp.inf, jnp.float32)
            for t in range(columns // LANES):
                top = jnp.maximum(top, t_ref[at, lane_tile(t)])
            top = jnp.max(top, axis=1, keepdims=True)
            total = jnp.zeros((STEP, LANES), jnp.float32)
            for t in range(columns // LANES):
                total += jnp.exp2((t_ref[at, lane_tile(t)] - top) * BITS)
            top_ref[at, :] = jnp.broadcast_to(top, (STEP, LANES))
            sum_ref[at, :] = total
            return unused

        lax.fori_loop(0, rows // STEP, rows_step, 0)
        out_ref[...] = collapse_top(top_ref) * NATS + jnp.log(collapse(sum_ref))


def column_kernel(t_ref, *refs):
    parts, (mass_ref, out_ref, lse_ref, wide_ref) = refs[:4], refs[4:]
    rows, columns = t_ref.shape
    lse = lse_all([part[...] for part in parts])
    lse_ref[...] = lse
    spread((mass_ref[...] - lse) / NATS, wide_ref)
    per = 4

    def group(value):
        return value.reshape(STEP // 8, 8, LANES)

    def sums(c, tops):
        wide = [jnp.broadcast_to(top, (STEP, LANES)) for top in tops]

        def sum_step(r, totals):
            at = at_rows(r)
            own = wide_ref[at, :]
            return tuple(
                total
                + jnp.sum(
                    group(jnp.exp2((t_ref[at, lane_tile(c + t)] + own - wide[t]) * BITS)), axis=0
                )
                for t, total in enumerate(totals)
            )

        start = tuple(jnp.zeros((8, LANES), jnp.float32) for _ in range(per))
        totals = lax.fori_loop(0, rows // STEP, sum_step, start)
        for t in range(per):
            total = jnp.sum(totals[t], axis=0, keepdims=True)
            out_ref[c + t : c + t + 1, :] = tops[t] * NATS + jnp.log(total)

    for c in range(0, columns // LANES, per):
        tops = [
            jnp.max(t_ref[:STEP, lane_tile(c + t)] + wide_ref[:STEP, :], axis=0, keepdims=True)
            for t in range(per)
        ]
        sums(c, tops)

    @pl.when(jnp.logical_not(jnp.max(out_ref[...]) < HUGE))
    def exact():
        for c in range(0, columns // LANES, per):

            def top_step(r, tops):
                at = at_rows(r)
                return tuple(
                    jnp.maximum(top, jnp.max(group(t_ref[at, lane_tile(c + t)] + wide_ref[at, :]), axis=0))
                    for t, top in enumerate(tops)
                )

            start = tuple(jnp.full((8, LANES), -jnp.inf, jnp.float32) for _ in range(per))
            tops = lax.fori_loop(0, rows // STEP, top_step, start)
            sums(c, [jnp.max(top, axis=0, keepdims=True) for top in tops])


def plan_kernel(t_ref, *refs):
    parts, refs = refs[:4], refs[4:]
    tgt_mass_ref, src_lse_ref, src_mass_ref, plan_ref, out_ref, lse_ref = refs[:6]
    wide_ref, sum_ref, line_ref = refs[6:]
    rows, columns = t_ref.shape
    lse = lse_all([part[...] for part in parts])
    lse_ref[...] = lse
    line_ref[...] = (tgt_mass_ref[...] - lse) * LOG2E
    spread((src_mass_ref[...] - src_lse_ref[...]) * LOG2E, wide_ref)
    per = 4

    def rows_step(r, unused):
        at = at_rows(r)
        total = jnp.zeros((STEP, LANES), jnp.float32)
        own = wide_ref[at, :]
        for c in range(0, columns // LANES, per):
            terms = [t_ref[at, lane_tile(c + t)] for t in range(per)]
            values = [
                jnp.exp2(terms[t] * BITS + own + line_ref[c + t : c + t + 1, :]) for t in range(per)
            ]
            for t in range(per):
                plan_ref[at, lane_tile(c + t)] = values[t]
                total += values[t]
        sum_ref[at, :] = total
        return unused

    lax.fori_loop(0, rows // STEP, rows_step, 0)
    out_ref[...] = collapse(sum_ref)


def row_sums_kernel(plan_ref, *refs):
    parts, (mass_ref, out_ref, sum_ref, line_ref) = refs[:4], refs[4:]
    rows, columns = plan_ref.shape
    line_ref[...] = jnp.exp(mass_ref[...]) / add_all([part[...] for part in parts])

    def rows_step(r, unused):
        at = at_rows(r)
        total = jnp.zeros((STEP, LANES), jnp.float32)
        for t in range(columns // LANES):
            total += plan_ref[at, lane_tile(t)] * line_ref[t : t + 1, :]
        sum_ref[at, :] = total
        return unused

    lax.fori_loop(0, rows // STEP, rows_step, 0)
    out_ref[...] = collapse(sum_ref)


def column_sums(plan_ref, scale, out_ref, wide_ref):
    rows, columns = plan_ref.shape
    spread(scale, wide_ref)
    per = 16
    for c in range(0, columns // LANES, per):

        def rows_step(r, totals):
            at = at_rows(r)
            own = wide_ref[at, :]
            return tuple(
                total
                + jnp.sum(
                    (plan_ref[at, lane_tile(c + t)] * own).reshape(STEP // 8, 8, LANES), axis=0
                )
                for t, total in enumerate(totals)
            )

        start = tuple(jnp.zeros((8, LANES), jnp.float32) for _ in range(per))
        totals = lax.fori_loop(0, rows // STEP, rows_step, start)
        for t in range(per):
            out_ref[c + t : c + t + 1, :] = jnp.sum(totals[t], axis=0, keepdims=True)


def column_sums_kernel(plan_ref, *refs):
    parts, (mass_ref, out_ref, wide_ref) = refs[:4], refs[4:]
    scale = jnp.exp(mass_ref[...]) / add_all([part[...] for part in parts])
    column_sums(plan_ref, scale, out_ref, wide_ref)


def last_column_sums_kernel(plan_ref, *refs):
    parts, (mass_ref, lse_ref, squares_ref, out_ref, potential_ref, wide_ref) = refs[:4], refs[4:]
    sums = add_all([part[...] for part in parts])
    mass = mass_ref[...]
    column_sums(plan_ref, jnp.exp(mass) / sums, out_ref, wide_ref)
    squares = squares_ref[...] / (WIDTH * EPS)
    potential = -EPS * (lse_ref[...] + jnp.log(sums) - mass - squares)
    potential_ref[...] = potential
    tiles = plan_ref.shape[1] // LANES
    out_ref[tiles:, :] = jnp.broadcast_to(jnp.sum(potential), (8, LANES))


def last_kernel(*refs):
    parts, (mass_ref, lse_ref, potential_ref, own_ref, other_ref) = refs[:4], refs[4:]
    tiles = mass_ref.shape[0]
    sums = add_all([part[...] for part in parts])
    potential = -EPS * (lse_ref[...] + jnp.log(sums[:tiles]) - 2.0 * mass_ref[...])
    potential_ref[...] = potential
    own_ref[...] = jnp.broadcast_to(jnp.sum(potential), (8, LANES))
    other_ref[...] = sums[tiles:]


def shifted(value, axis):
    n = lax.axis_size(axis)
    return [value] + [
        lax.ppermute(value, axis, [(i, (i + k) % n) for i in range(n)]) for k in range(1, n)
    ]


ALL = ("row_0", "row_1", "col_0", "col_1")
SIZES = (4, 4, 4, 2)


def number(y, x, z, core):
    return ((y % 4 * 4 + x % 4) * 4 + z) * 2 + core


def turned(value, stage):
    found = [value]
    for k in range(1, 4):
        pairs = []
        for y, x, z, core in itertools.product(*map(range, SIZES)):
            along_y = (core + stage) % 2
            to = number(y + k * along_y, x + k * (1 - along_y), z, core)
            pairs.append((number(y, x, z, core), to))
        found.append(lax.ppermute(value, ALL, pairs))
    return found


def body(src_points, tgt_points, log_src_mass, log_tgt_mass):
    rows, columns = src_points.shape[0], log_tgt_mass.shape[0]
    row_tiles, column_tiles = rows // LANES, columns // LANES
    src_mass = log_src_mass.reshape(row_tiles, LANES)
    tgt_mass = log_tgt_mass.reshape(column_tiles, LANES)
    place = jnp.stack([lax.axis_index(name) for name in ("row_0", "row_1", "col_1")])
    place = place.astype(jnp.int32)
    wide = pltpu.VMEM((rows, LANES), jnp.float32)
    big = pltpu.VMEM((rows, columns), jnp.float32)
    line = pltpu.VMEM((column_tiles, LANES), jnp.float32)
    by_row, by_column = f32(row_tiles, LANES), f32(column_tiles, LANES)

    def resident(value):
        return pltpu.with_memory_space_constraint(value, pltpu.VMEM)

    def over_col(value, combine):
        return shifted(combine(shifted(value, "col_1")), "col_0")

    def over_row(value, combine):
        return shifted(combine(shifted(value, "row_1")), "row_0")

    first = jnp.concatenate(turned(tgt_points, 0))
    pieces = turned(first, 1)[1:]
    terms, top, sums = call(first_terms_kernel, (big, wide, wide), [SMEM] + [VMEM] * 3, [])(
        place, src_points, first, tgt_mass
    )
    terms, lse = call(terms_kernel, (big, by_row), [SMEM] + [VMEM] * 8, [wide, wide], {2: 0})(
        place, src_points, resident(terms), resident(top), resident(sums), *pieces, tgt_mass
    )
    parts = over_col(lse, lse_all)
    lse, src_lse = call(column_kernel, (by_column, by_row), [VMEM] * 6, [wide])(
        resident(terms), *parts, src_mass
    )
    parts = over_row(lse, lse_all)
    plan, sums, tgt_lse = call(
        plan_kernel, (big, by_row, by_column), [VMEM] * 8, [wide, wide, line], {0: 0}
    )(resident(terms), *parts, tgt_mass, src_lse, src_mass)
    plan = resident(plan)
    parts = over_col(sums, add_all)
    sums = call(column_sums_kernel, by_column, [VMEM] * 6, [wide])(plan, *parts, src_mass)
    parts = over_row(sums, add_all)
    sums = call(row_sums_kernel, by_row, [VMEM] * 6, [wide, line])(plan, *parts, tgt_mass)
    parts = over_col(sums, add_all)
    squares = jnp.sum(src_points.astype(jnp.float32) ** 2, axis=1).reshape(row_tiles, LANES)
    sums, src_potential = call(
        last_column_sums_kernel, (f32(column_tiles + 8, LANES), by_row), [VMEM] * 8, [wide]
    )(plan, *parts, src_mass, src_lse, squares)
    parts = over_row(sums, add_all)
    tile = f32(8, LANES)
    tgt_potential, tgt_sum, src_sum = call(last_kernel, (by_column, tile, tile), [VMEM] * 6, [])(
        *parts, tgt_mass, tgt_lse
    )
    tgt_sum = add_all(over_col(tgt_sum, add_all))
    sources_all, targets_all = rows * lax.axis_size(ROW), columns * lax.axis_size(COL)
    mean_potentials = (src_sum / sources_all + tgt_sum / targets_all)[0, 0]
    return (src_potential.reshape(-1), tgt_potential.reshape(-1), mean_potentials)


def solution(mesh):
    finer = Mesh(mesh.devices.reshape(4, 4, 4, 2), ("row_0", "row_1", "col_0", "col_1"))
    placed = (P(ROW, None), P(COL_ROW, None), P(ROW), P(COL))
    return jax.shard_map(
        body, mesh=finer, in_specs=placed, out_specs=(P(ROW), P(COL), P()), check_vma=False
    )
```

time: 222 us -> 132 us (0.59)
  waiting for transfers between devices: 75.8 us -> 31 us
  matrix products: 35.4 us -> 0 us
  starting transfers between devices: 36.1 us -> 70 us
  blocking collectives: 32.4 us -> 0 us
  Pallas kernels: 0 us -> 25.9 us
  other arithmetic: 21 us -> 0.36 us
  local copies, waits for them, and re-layouts: 16.5 us -> 3.26 us
    all_to_all x7 -> x0, waiting for transfers between devices: 75.8 us -> none  [from_everyone(): lax.all_to_all(jnp.broadcast_to(value[None], (peers, *value.shape)), axis...]
    ppermute x0 -> x40, starting transfers between devices: none -> 70 us  [the longest x34 59.2 us: shifted(): lax.ppermute(value, axis, [(i, (i + k) % n) for i in range(n)])]
    all_to_all x7 -> x0, starting transfers between devices: 36.1 us -> none  [from_everyone(): lax.all_to_all(jnp.broadcast_to(value[None], (peers, *value.shape)), axis...]
    dot_general x24 -> x0, matrix products: 35.4 us -> none  [cost_block(): lax.dot_general(points_a, points_b, (((1,), (1,)), ((), ())), preferred_e...]
    psum x4 -> x0, blocking collectives: 32.4 us -> none  [over_axes(): value = lax.psum(value, axis)]
    ppermute x0 -> x40, waiting for transfers between devices: none -> 31 us  [the longest x34 22.9 us: shifted(): lax.ppermute(value, axis, [(i, (i + k) % n) for i in range(n)])]
    pallas_call x0 -> x8, Pallas kernels: none -> 25.9 us  [the longest x1 6.61 us: body(): call(terms_kernel, (big, by_row), [SMEM] + [VMEM] * 8, [wide, wide], {2: 0})]
    reduce_sum x28 -> x1, other arithmetic: 19.7 us -> 0.21 us  [body(): jnp.sum(src_points.astype(jnp.float32) ** 2, axis=1)]
  transfers between devices with their start and end apart: 7 -> 40, of which waited for: 7 -> 31; matrix products, arithmetic and copies ran while one was open for 0% -> 1% of each run, Pallas kernels for 0% -> 3%
where the time goes in v2:
time: 132 us; the launch traced here: 131 us
  starting transfers between devices  70 us (53%)
  waiting for transfers between devices  31 us (23%)
  Pallas kernels  25.9 us (20%)
  local copies, waits for them, and re-layouts  3.26 us (2%)
    ppermute x34, starting transfers between devices, shifted(): lax.ppermute(value, axis, [(i, (i + k) % n) for i in range(n)])  59.2 us
    ppermute x34, waiting for transfers between devices, shifted(): lax.ppermute(value, axis, [(i, (i + k) % n) for i in range(n)])  22.9 us
    ppermute x6, starting transfers between devices, turned(): found.append(lax.ppermute(value, ALL, pairs))  10.8 us
    ppermute x6, waiting for transfers between devices, turned(): found.append(lax.ppermute(value, ALL, pairs))  8.07 us
    pallas_call x1, Pallas kernels, body(): call(terms_kernel, (big, by_row), [SMEM] + [VMEM] * 8, [wide, wide], {2: 0})  6.61 us
    pallas_call x1, Pallas kernels, body(): call(column_kernel, (by_column, by_row), [VMEM] * 6, [wide])  5.06 us
    pallas_call x1, Pallas kernels, body(): call(plan_kernel, (big, by_row, by_column), [VMEM] * 8, [wide, wide, line...  3.93 us
    pallas_call x1, Pallas kernels, body(): call(first_terms_kernel, (big, wide, wide), [SMEM] + [VMEM] * 3, [])  3.67 us
  transfers between devices with their start and end apart: 40, of which 31 were waited for; matrix products, arithmetic and copies ran while one was open for 1% of the time, Pallas kernels for 3%

profile of v2, /device:TPU:1, one launch (start us, length us, event | category | flops | bytes accessed | tf_op | source)
XLA Modules:
  0.0 131.2 jit_solution(1185857821276098905)
XLA Ops:
  0.6 2.2 %collective-permute-start = (bf16[256,256]{1,0:T(8,128)(2,1)}, bf16[256,256]{1,0:T(8,128)(2,1)S(1)}, u32[]{:S(2)}, u32[]{:S(2)}) collective-permute-start(bf16[256,256]{1,0:T(8,128)(2,1)} %param.5), channel_id=1, source_target_pairs={{0,8},{1,33},{2,10},{3,35},{4,12},{5,37},{6,14},{7,39},{8,16},{9,4... | collective-permute-start | bytes 393224 | tf_op jit(solution)/shard_map/ppermute | solution.py:357
  2.8 2.6 %collective-permute-start.1 = (bf16[256,256]{1,0:T(8,128)(2,1)}, bf16[256,256]{1,0:T(8,128)(2,1)S(1)}, u32[]{:S(2)}, u32[]{:S(2)}) collective-permute-start(bf16[256,256]{1,0:T(8,128)(2,1)} %param.5), channel_id=1, source_target_pairs={{0,16},{1,65},{2,18},{3,67},{4,20},{5,69},{6,22},{7,71},{8,24},{9,... | collective-permute-start | bytes 393224 | tf_op jit(solution)/shard_map/ppermute | solution.py:357
  7.5 2.2 %collective-permute-done.1 = bf16[256,256]{1,0:T(8,128)(2,1)S(1)} collective-permute-done((bf16[256,256]{1,0:T(8,128)(2,1)}, bf16[256,256]{1,0:T(8,128)(2,1)S(1)}, u32[]{:S(2)}, u32[]{:S(2)}) %collective-permute-start.1) | collective-permute-done | bytes 131104 | tf_op jit(solution)/shard_map/ppermute | solution.py:357
  11.1 2.5 %collective-permute-start.4 = (bf16[1024,256]{1,0:T(8,128)(2,1)S(1)}, bf16[1024,256]{1,0:T(8,128)(2,1)S(1)}, u32[]{:S(2)}, u32[]{:S(2)}) collective-permute-start(bf16[1024,256]{1,0:T(8,128)(2,1)S(1)} %constant_dynamic-update-slice_fusion.points_ref), channel_id=1, source_target_pairs={{0,64},{1,17},{2,66},{3,19},{4,68},{5,21},{6,70},{7,23},{8,72},{9,... | collective-permute-start | bytes 1572872 | tf_op jit(solution)/shard_map/ppermute | solution.py:357
  16.5 3.7 %shard_map.67 = (f32[1024,4096]{1,0:T(8,128)S(1)}, f32[1024,128]{1,0:T(8,128)S(1)}, f32[1024,128]{1,0:T(8,128)S(1)}) custom-call(s32[3]{0:T(128)S(1)} %pad_add_fusion.place, bf16[1024,256]{1,0:T(8,128)(2,1)S(1)} %copy-done, bf16[1024,256]{1,0:T(8,128)(2,1)S(1)} %constant_dynamic-update-slice_fusion.points_ref, f32[32,128]{1,0:T(8,128)S(1)} %bitcast.9), custom_call_target="tpu_custom_call" | custom-call | tf_op jit(solution)/shard_map/pallas_call | solution.py:384
  20.2 5.8 %collective-permute-done.4.refs_1_ = bf16[1024,256]{1,0:T(8,128)(2,1)S(1)} collective-permute-done((bf16[1024,256]{1,0:T(8,128)(2,1)S(1)}, bf16[1024,256]{1,0:T(8,128)(2,1)S(1)}, u32[]{:S(2)}, u32[]{:S(2)}) %collective-permute-start.4) | collective-permute-done | bytes 524320 | tf_op jit(solution)/shard_map/ppermute | solution.py:357
  26.0 6.6 %shard_map.68 = (f32[1024,4096]{1,0:T(8,128)S(1)}, f32[8,128]{1,0:T(8,128)S(1)}) custom-call(s32[3]{0:T(128)S(1)} %pad_add_fusion.place, bf16[1024,256]{1,0:T(8,128)(2,1)S(1)} %copy-done, f32[1024,4096]{1,0:T(8,128)S(1)} %get-tuple-element.18.old_ref, f32[1024,128]{1,0:T(8,128)S(1)} %get-tuple-element.19.first_top_ref, ...), custom_call_target="tpu_custom_call", output_to_operand_aliasing={{0}: (2, {})} | custom-call | tf_op jit(solution)/shard_map/pallas_call | solution.py:387
  32.6 3.0 %collective-permute-start.6 = (f32[8,128]{1,0:T(8,128)S(1)}, f32[8,128]{1,0:T(8,128)S(1)}, u32[]{:S(2)}, u32[]{:S(2)}) collective-permute-start(f32[8,128]{1,0:T(8,128)S(1)} %get-tuple-element.22), channel_id=1, source_target_pairs={{0,1},{1,0},{2,3},{3,2},{4,5},{5,4},{6,7},{7,6},{8,9},{9,8},{10,11... | collective-permute-start | bytes 12296 | tf_op jit(solution)/shard_map/ppermute | solution.py:337
  38.2 3.3 %collective-permute-start.8 = (f32[8,128]{1,0:T(8,128)S(1)}, f32[8,128]{1,0:T(8,128)S(1)}, u32[]{:S(2)}, u32[]{:S(2)}) collective-permute-start(f32[8,128]{1,0:T(8,128)S(1)} %log_add_fusion.1.refs_0_), channel_id=1, source_target_pairs={{0,4},{2,6},{4,0},{6,2},{1,5},{3,7},{5,1},{7,3},{8,12},{10,14},{12... | collective-permute-start | bytes 12296 | tf_op jit(solution)/shard_map/ppermute | solution.py:337
  43.9 5.1 %shard_map.69 = (f32[32,128]{1,0:T(8,128)S(1)}, f32[8,128]{1,0:T(8,128)S(1)}) custom-call(f32[1024,4096]{1,0:T(8,128)S(1)} %get-tuple-element.21.t_ref, f32[8,128]{1,0:T(8,128)S(1)} %log_add_fusion.1.refs_0_, f32[8,128]{1,0:T(8,128)S(1)} %collective-permute-done.7.refs_1_, f32[8,128]{1,0:T(8,128)S(1)} %collective-permute-done.8.refs_2_, ...), custom_call_target="tpu_custom_call" | custom-call | tf_op jit(solution)/shard_map/pallas_call | solution.py:391
  50.0 2.5 %collective-permute-start.11 = (f32[32,128]{1,0:T(8,128)S(1)}, f32[32,128]{1,0:T(8,128)S(1)}, u32[]{:S(2)}, u32[]{:S(2)}) collective-permute-start(f32[32,128]{1,0:T(8,128)S(1)} %get-tuple-element.23), channel_id=1, source_target_pairs={{0,16},{8,24},{16,0},{24,8},{1,17},{9,25},{17,1},{25,9},{2,18},{10... | collective-permute-start | bytes 49160 | tf_op jit(solution)/shard_map/ppermute | solution.py:337
  58.8 2.0 %collective-permute-start.15 = (f32[32,128]{1,0:T(8,128)S(1)}, f32[32,128]{1,0:T(8,128)S(1)}, u32[]{:S(2)}, u32[]{:S(2)}) collective-permute-start(f32[32,128]{1,0:T(8,128)S(1)} %log_add_fusion.refs_0_), channel_id=1, source_target_pairs={{0,96},{32,0},{64,32},{96,64},{1,97},{33,1},{65,33},{97,65},{2,98}... | collective-permute-start | bytes 49160 | tf_op jit(solution)/shard_map/ppermute | solution.py:337
  61.7 3.9 %shard_map.70 = (f32[1024,4096]{1,0:T(8,128)S(1)}, f32[8,128]{1,0:T(8,128)S(1)}, f32[32,128]{1,0:T(8,128)S(1)}) custom-call(f32[1024,4096]{1,0:T(8,128)S(1)} %get-tuple-element.21.t_ref, f32[32,128]{1,0:T(8,128)S(1)} %log_add_fusion.refs_0_, f32[32,128]{1,0:T(8,128)S(1)} %collective-permute-done.13.refs_1_, ...), custom_call_target="tpu_custom_call", output_to_operand_aliasing={{0}: (0, {})} | custom-call | tf_op jit(solution)/shard_map/pallas_call | solution.py:395
  65.6 4.9 %collective-permute-start.16 = (f32[8,128]{1,0:T(8,128)S(1)}, f32[8,128]{1,0:T(8,128)S(1)}, u32[]{:S(2)}, u32[]{:S(2)}) collective-permute-start(f32[8,128]{1,0:T(8,128)S(1)} %get-tuple-element.26), channel_id=1, source_target_pairs={{0,1},{1,0},{2,3},{3,2},{4,5},{5,4},{6,7},{7,6},{8,9},{9,8},{10,11... | collective-permute-start | bytes 12296 | tf_op jit(solution)/shard_map/ppermute | solution.py:337
  79.7 3.6 %collective-permute-start.21 = (f32[32,128]{1,0:T(8,128)S(1)}, f32[32,128]{1,0:T(8,128)S(1)}, u32[]{:S(2)}, u32[]{:S(2)}) collective-permute-start(f32[32,128]{1,0:T(8,128)S(1)} %shard_map.71), channel_id=1, source_target_pairs={{0,16},{8,24},{16,0},{24,8},{1,17},{9,25},{17,1},{25,9},{2,18},{10... | collective-permute-start | bytes 49160 | tf_op jit(solution)/shard_map/ppermute | solution.py:337
  87.0 3.6 %collective-permute-start.24 = (f32[32,128]{1,0:T(8,128)S(1)}, f32[32,128]{1,0:T(8,128)S(1)}, u32[]{:S(2)}, u32[]{:S(2)}) collective-permute-start(f32[32,128]{1,0:T(8,128)S(1)} %add_add_fusion.1.refs_0_), channel_id=1, source_target_pairs={{0,64},{32,96},{64,0},{96,32},{1,65},{33,97},{65,1},{97,33},{2,66}... | collective-permute-start | bytes 49160 | tf_op jit(solution)/shard_map/ppermute | solution.py:337
  93.2 2.1 %shard_map.72 = f32[8,128]{1,0:T(8,128)S(1)} custom-call(f32[1024,4096]{1,0:T(8,128)S(1)} %get-tuple-element.25.plan_ref, f32[32,128]{1,0:T(8,128)S(1)} %add_add_fusion.1.refs_0_, f32[32,128]{1,0:T(8,128)S(1)} %collective-permute-done.23.refs_1_, f32[32,128]{1,0:T(8,128)S(1)} %collective-permute-done.24.refs_2_, ...), custom_call_target="tpu_custom_call" | custom-call | tf_op jit(solution)/shard_map/pallas_call | solution.py:402
  95.2 5.0 %collective-permute-start.26 = (f32[8,128]{1,0:T(8,128)S(1)}, f32[8,128]{1,0:T(8,128)S(1)}, u32[]{:S(2)}, u32[]{:S(2)}) collective-permute-start(f32[8,128]{1,0:T(8,128)S(1)} %shard_map.72), channel_id=1, source_target_pairs={{0,1},{1,0},{2,3},{3,2},{4,5},{5,4},{6,7},{7,6},{8,9},{9,8},{10,11... | collective-permute-start | bytes 12296 | tf_op jit(solution)/shard_map/ppermute | solution.py:337
  101.0 2.7 %collective-permute-start.28 = (f32[8,128]{1,0:T(8,128)S(1)}, f32[8,128]{1,0:T(8,128)S(1)}, u32[]{:S(2)}, u32[]{:S(2)}) collective-permute-start(f32[8,128]{1,0:T(8,128)S(1)} %add.67.refs_0_), channel_id=1, source_target_pairs={{0,4},{2,6},{4,0},{6,2},{1,5},{3,7},{5,1},{7,3},{8,12},{10,14},{12... | collective-permute-start | bytes 12296 | tf_op jit(solution)/shard_map/ppermute | solution.py:337
  106.2 2.3 %shard_map.73 = (f32[40,128]{1,0:T(8,128)S(1)}, f32[8,128]{1,0:T(8,128)}) custom-call(f32[1024,4096]{1,0:T(8,128)S(1)} %get-tuple-element.25.plan_ref, f32[8,128]{1,0:T(8,128)S(1)} %add.67.refs_0_, f32[8,128]{1,0:T(8,128)S(1)} %collective-permute-done.27.refs_1_, f32[8,128]{1,0:T(8,128)S(1)} %collective-permute-done.28.refs_2_, ...), custom_call_target="tpu_custom_call" | custom-call | tf_op jit(solution)/shard_map/pallas_call | solution.py:405
  108.4 2.1 %collective-permute-start.31 = (f32[40,128]{1,0:T(8,128)S(1)}, f32[40,128]{1,0:T(8,128)S(1)}, u32[]{:S(2)}, u32[]{:S(2)}) collective-permute-start(f32[40,128]{1,0:T(8,128)S(1)} %get-tuple-element.28), channel_id=1, source_target_pairs={{0,16},{8,24},{16,0},{24,8},{1,17},{9,25},{17,1},{25,9},{2,18},{10... | collective-permute-start | bytes 61448 | tf_op jit(solution)/shard_map/ppermute | solution.py:337
  113.3 2.1 %collective-permute-start.34 = (f32[40,128]{1,0:T(8,128)S(1)}, f32[40,128]{1,0:T(8,128)S(1)}, u32[]{:S(2)}, u32[]{:S(2)}) collective-permute-start(f32[40,128]{1,0:T(8,128)S(1)} %add_add_fusion.refs_0_), channel_id=1, source_target_pairs={{0,64},{32,96},{64,0},{96,32},{1,65},{33,97},{65,1},{97,33},{2,66}... | collective-permute-start | bytes 61448 | tf_op jit(solution)/shard_map/ppermute | solution.py:337
  118.6 5.5 %collective-permute-start.36 = (f32[8,128]{1,0:T(8,128)S(1)}, f32[8,128]{1,0:T(8,128)S(1)}, u32[]{:S(2)}, u32[]{:S(2)}) collective-permute-start(f32[8,128]{1,0:T(8,128)S(1)} %get-tuple-element.32), channel_id=1, source_target_pairs={{0,1},{1,0},{2,3},{3,2},{4,5},{5,4},{6,7},{7,6},{8,9},{9,8},{10,11... | collective-permute-start | bytes 12296 | tf_op jit(solution)/shard_map/ppermute | solution.py:337
  125.5 2.4 %collective-permute-start.38 = (f32[8,128]{1,0:T(8,128)S(1)}, f32[8,128]{1,0:T(8,128)S(1)}, u32[]{:S(2)}, u32[]{:S(2)}) collective-permute-start(f32[8,128]{1,0:T(8,128)S(1)} %add.71), channel_id=1, source_target_pairs={{0,4},{2,6},{4,0},{6,2},{1,5},{3,7},{5,1},{7,3},{8,12},{10,14},{12... | collective-permute-start | bytes 12296 | tf_op jit(solution)/shard_map/ppermute | solution.py:337
  (87 shorter events, 49.0 us)
Async XLA Ops:
  0.6 6.8 %collective-permute-start = (bf16[256,256]{1,0:T(8,128)(2,1)}, bf16[256,256]{1,0:T(8,128)(2,1)S(1)}, u32[]{:S(2)}, u32[]{:S(2)}) collective-permute-start(bf16[256,256]{1,0:T(8,128)(2,1)} %param.5), channel_id=1, source_target_pairs={{0,8},{1,33},{2,10},{3,35},{4,12},{5,37},{6,14},{7,39},{8,16},{9,4... | collective-permute-start | bytes 393224 | tf_op jit(solution)/shard_map/ppermute | solution.py:357
  2.8 6.9 %collective-permute-start.1 = (bf16[256,256]{1,0:T(8,128)(2,1)}, bf16[256,256]{1,0:T(8,128)(2,1)S(1)}, u32[]{:S(2)}, u32[]{:S(2)}) collective-permute-start(bf16[256,256]{1,0:T(8,128)(2,1)} %param.5), channel_id=1, source_target_pairs={{0,16},{1,65},{2,18},{3,67},{4,20},{5,69},{6,22},{7,71},{8,24},{9,... | collective-permute-start | bytes 393224 | tf_op jit(solution)/shard_map/ppermute | solution.py:357
  5.5 4.3 %collective-permute-start.2 = (bf16[256,256]{1,0:T(8,128)(2,1)}, bf16[256,256]{1,0:T(8,128)(2,1)S(1)}, u32[]{:S(2)}, u32[]{:S(2)}) collective-permute-start(bf16[256,256]{1,0:T(8,128)(2,1)} %param.5), channel_id=1, source_target_pairs={{0,24},{1,97},{2,26},{3,99},{4,28},{5,101},{6,30},{7,103},{8,0},{9... | collective-permute-start | bytes 393224 | tf_op jit(solution)/shard_map/ppermute | solution.py:357
  9.8 10.4 %collective-permute-start.3 = (bf16[1024,256]{1,0:T(8,128)(2,1)S(1)}, bf16[1024,256]{1,0:T(8,128)(2,1)S(1)}, u32[]{:S(2)}, u32[]{:S(2)}) collective-permute-start(bf16[1024,256]{1,0:T(8,128)(2,1)S(1)} %constant_dynamic-update-slice_fusion.points_ref), channel_id=1, source_target_pairs={{0,32},{1,9},{2,34},{3,11},{4,36},{5,13},{6,38},{7,15},{8,40},{9,1... | collective-permute-start | bytes 1572872 | tf_op jit(solution)/shard_map/ppermute | solution.py:357
  11.1 14.9 %collective-permute-start.4 = (bf16[1024,256]{1,0:T(8,128)(2,1)S(1)}, bf16[1024,256]{1,0:T(8,128)(2,1)S(1)}, u32[]{:S(2)}, u32[]{:S(2)}) collective-permute-start(bf16[1024,256]{1,0:T(8,128)(2,1)S(1)} %constant_dynamic-update-slice_fusion.points_ref), channel_id=1, source_target_pairs={{0,64},{1,17},{2,66},{3,19},{4,68},{5,21},{6,70},{7,23},{8,72},{9,... | collective-permute-start | bytes 1572872 | tf_op jit(solution)/shard_map/ppermute | solution.py:357
  13.5 12.5 %collective-permute-start.5 = (bf16[1024,256]{1,0:T(8,128)(2,1)S(1)}, bf16[1024,256]{1,0:T(8,128)(2,1)S(1)}, u32[]{:S(2)}, u32[]{:S(2)}) collective-permute-start(bf16[1024,256]{1,0:T(8,128)(2,1)S(1)} %constant_dynamic-update-slice_fusion.points_ref), channel_id=1, source_target_pairs={{0,96},{1,25},{2,98},{3,27},{4,100},{5,29},{6,102},{7,31},{8,104},... | collective-permute-start | bytes 1572872 | tf_op jit(solution)/shard_map/ppermute | solution.py:357
  36.4 5.7 %collective-permute-start.7 = (f32[8,128]{1,0:T(8,128)S(1)}, f32[8,128]{1,0:T(8,128)S(1)}, u32[]{:S(2)}, u32[]{:S(2)}) collective-permute-start(f32[8,128]{1,0:T(8,128)S(1)} %log_add_fusion.1.refs_0_), channel_id=1, source_target_pairs={{0,2},{2,4},{4,6},{6,0},{1,3},{3,5},{5,7},{7,1},{8,10},{10,12},{12... | collective-permute-start | bytes 12296 | tf_op jit(solution)/shard_map/ppermute | solution.py:337
  38.2 4.3 %collective-permute-start.8 = (f32[8,128]{1,0:T(8,128)S(1)}, f32[8,128]{1,0:T(8,128)S(1)}, u32[]{:S(2)}, u32[]{:S(2)}) collective-permute-start(f32[8,128]{1,0:T(8,128)S(1)} %log_add_fusion.1.refs_0_), channel_id=1, source_target_pairs={{0,4},{2,6},{4,0},{6,2},{1,5},{3,7},{5,1},{7,3},{8,12},{10,14},{12... | collective-permute-start | bytes 12296 | tf_op jit(solution)/shard_map/ppermute | solution.py:337
  49.0 4.2 %collective-permute-start.10 = (f32[32,128]{1,0:T(8,128)S(1)}, f32[32,128]{1,0:T(8,128)S(1)}, u32[]{:S(2)}, u32[]{:S(2)}) collective-permute-start(f32[32,128]{1,0:T(8,128)S(1)} %get-tuple-element.23), channel_id=1, source_target_pairs={{0,8},{8,16},{16,24},{24,0},{1,9},{9,17},{17,25},{25,1},{2,10},{10... | collective-permute-start | bytes 49160 | tf_op jit(solution)/shard_map/ppermute | solution.py:337
  50.0 4.1 %collective-permute-start.11 = (f32[32,128]{1,0:T(8,128)S(1)}, f32[32,128]{1,0:T(8,128)S(1)}, u32[]{:S(2)}, u32[]{:S(2)}) collective-permute-start(f32[32,128]{1,0:T(8,128)S(1)} %get-tuple-element.23), channel_id=1, source_target_pairs={{0,16},{8,24},{16,0},{24,8},{1,17},{9,25},{17,1},{25,9},{2,18},{10... | collective-permute-start | bytes 49160 | tf_op jit(solution)/shard_map/ppermute | solution.py:337
  55.5 5.3 %collective-permute-start.13 = (f32[32,128]{1,0:T(8,128)S(1)}, f32[32,128]{1,0:T(8,128)S(1)}, u32[]{:S(2)}, u32[]{:S(2)}) collective-permute-start(f32[32,128]{1,0:T(8,128)S(1)} %log_add_fusion.refs_0_), channel_id=1, source_target_pairs={{0,32},{32,64},{64,96},{96,0},{1,33},{33,65},{65,97},{97,1},{2,34}... | collective-permute-start | bytes 49160 | tf_op jit(solution)/shard_map/ppermute | solution.py:337
  56.9 4.1 %collective-permute-start.14 = (f32[32,128]{1,0:T(8,128)S(1)}, f32[32,128]{1,0:T(8,128)S(1)}, u32[]{:S(2)}, u32[]{:S(2)}) collective-permute-start(f32[32,128]{1,0:T(8,128)S(1)} %log_add_fusion.refs_0_), channel_id=1, source_target_pairs={{0,64},{32,96},{64,0},{96,32},{1,65},{33,97},{65,1},{97,33},{2,66}... | collective-permute-start | bytes 49160 | tf_op jit(solution)/shard_map/ppermute | solution.py:337
  65.6 5.8 %collective-permute-start.16 = (f32[8,128]{1,0:T(8,128)S(1)}, f32[8,128]{1,0:T(8,128)S(1)}, u32[]{:S(2)}, u32[]{:S(2)}) collective-permute-start(f32[8,128]{1,0:T(8,128)S(1)} %get-tuple-element.26), channel_id=1, source_target_pairs={{0,1},{1,0},{2,3},{3,2},{4,5},{5,4},{6,7},{7,6},{8,9},{9,8},{10,11... | collective-permute-start | bytes 12296 | tf_op jit(solution)/shard_map/ppermute | solution.py:337
  72.5 4.0 %collective-permute-start.18 = (f32[8,128]{1,0:T(8,128)S(1)}, f32[8,128]{1,0:T(8,128)S(1)}, u32[]{:S(2)}, u32[]{:S(2)}) collective-permute-start(f32[8,128]{1,0:T(8,128)S(1)} %add.63.refs_0_), channel_id=1, source_target_pairs={{0,4},{2,6},{4,0},{6,2},{1,5},{3,7},{5,1},{7,3},{8,12},{10,14},{12... | collective-permute-start | bytes 12296 | tf_op jit(solution)/shard_map/ppermute | solution.py:337
  78.9 4.3 %collective-permute-start.20 = (f32[32,128]{1,0:T(8,128)S(1)}, f32[32,128]{1,0:T(8,128)S(1)}, u32[]{:S(2)}, u32[]{:S(2)}) collective-permute-start(f32[32,128]{1,0:T(8,128)S(1)} %shard_map.71), channel_id=1, source_target_pairs={{0,8},{8,16},{16,24},{24,0},{1,9},{9,17},{17,25},{25,1},{2,10},{10... | collective-permute-start | bytes 49160 | tf_op jit(solution)/shard_map/ppermute | solution.py:337
  79.7 4.9 %collective-permute-start.21 = (f32[32,128]{1,0:T(8,128)S(1)}, f32[32,128]{1,0:T(8,128)S(1)}, u32[]{:S(2)}, u32[]{:S(2)}) collective-permute-start(f32[32,128]{1,0:T(8,128)S(1)} %shard_map.71), channel_id=1, source_target_pairs={{0,16},{8,24},{16,0},{24,8},{1,17},{9,25},{17,1},{25,9},{2,18},{10... | collective-permute-start | bytes 49160 | tf_op jit(solution)/shard_map/ppermute | solution.py:337
  86.2 4.4 %collective-permute-start.23 = (f32[32,128]{1,0:T(8,128)S(1)}, f32[32,128]{1,0:T(8,128)S(1)}, u32[]{:S(2)}, u32[]{:S(2)}) collective-permute-start(f32[32,128]{1,0:T(8,128)S(1)} %add_add_fusion.1.refs_0_), channel_id=1, source_target_pairs={{0,32},{32,64},{64,96},{96,0},{1,33},{33,65},{65,97},{97,1},{2,34}... | collective-permute-start | bytes 49160 | tf_op jit(solution)/shard_map/ppermute | solution.py:337
  87.0 4.9 %collective-permute-start.24 = (f32[32,128]{1,0:T(8,128)S(1)}, f32[32,128]{1,0:T(8,128)S(1)}, u32[]{:S(2)}, u32[]{:S(2)}) collective-permute-start(f32[32,128]{1,0:T(8,128)S(1)} %add_add_fusion.1.refs_0_), channel_id=1, source_target_pairs={{0,64},{32,96},{64,0},{96,32},{1,65},{33,97},{65,1},{97,33},{2,66}... | collective-permute-start | bytes 49160 | tf_op jit(solution)/shard_map/ppermute | solution.py:337
  95.2 5.8 %collective-permute-start.26 = (f32[8,128]{1,0:T(8,128)S(1)}, f32[8,128]{1,0:T(8,128)S(1)}, u32[]{:S(2)}, u32[]{:S(2)}) collective-permute-start(f32[8,128]{1,0:T(8,128)S(1)} %shard_map.72), channel_id=1, source_target_pairs={{0,1},{1,0},{2,3},{3,2},{4,5},{5,4},{6,7},{7,6},{8,9},{9,8},{10,11... | collective-permute-start | bytes 12296 | tf_op jit(solution)/shard_map/ppermute | solution.py:337
  101.0 4.0 %collective-permute-start.28 = (f32[8,128]{1,0:T(8,128)S(1)}, f32[8,128]{1,0:T(8,128)S(1)}, u32[]{:S(2)}, u32[]{:S(2)}) collective-permute-start(f32[8,128]{1,0:T(8,128)S(1)} %add.67.refs_0_), channel_id=1, source_target_pairs={{0,4},{2,6},{4,0},{6,2},{1,5},{3,7},{5,1},{7,3},{8,12},{10,14},{12... | collective-permute-start | bytes 12296 | tf_op jit(solution)/shard_map/ppermute | solution.py:337
  108.4 4.1 %collective-permute-start.31 = (f32[40,128]{1,0:T(8,128)S(1)}, f32[40,128]{1,0:T(8,128)S(1)}, u32[]{:S(2)}, u32[]{:S(2)}) collective-permute-start(f32[40,128]{1,0:T(8,128)S(1)} %get-tuple-element.28), channel_id=1, source_target_pairs={{0,16},{8,24},{16,0},{24,8},{1,17},{9,25},{17,1},{25,9},{2,18},{10... | collective-permute-start | bytes 61448 | tf_op jit(solution)/shard_map/ppermute | solution.py:337
  113.3 4.2 %collective-permute-start.34 = (f32[40,128]{1,0:T(8,128)S(1)}, f32[40,128]{1,0:T(8,128)S(1)}, u32[]{:S(2)}, u32[]{:S(2)}) collective-permute-start(f32[40,128]{1,0:T(8,128)S(1)} %add_add_fusion.refs_0_), channel_id=1, source_target_pairs={{0,64},{32,96},{64,0},{96,32},{1,65},{33,97},{65,1},{97,33},{2,66}... | collective-permute-start | bytes 61448 | tf_op jit(solution)/shard_map/ppermute | solution.py:337
  118.6 6.3 %collective-permute-start.36 = (f32[8,128]{1,0:T(8,128)S(1)}, f32[8,128]{1,0:T(8,128)S(1)}, u32[]{:S(2)}, u32[]{:S(2)}) collective-permute-start(f32[8,128]{1,0:T(8,128)S(1)} %get-tuple-element.32), channel_id=1, source_target_pairs={{0,1},{1,0},{2,3},{3,2},{4,5},{5,4},{6,7},{7,6},{8,9},{9,8},{10,11... | collective-permute-start | bytes 12296 | tf_op jit(solution)/shard_map/ppermute | solution.py:337
  125.5 4.0 %collective-permute-start.38 = (f32[8,128]{1,0:T(8,128)S(1)}, f32[8,128]{1,0:T(8,128)S(1)}, u32[]{:S(2)}, u32[]{:S(2)}) collective-permute-start(f32[8,128]{1,0:T(8,128)S(1)} %add.71), channel_id=1, source_target_pairs={{0,4},{2,6},{4,0},{6,2},{1,5},{3,7},{5,1},{7,3},{8,12},{10,14},{12... | collective-permute-start | bytes 12296 | tf_op jit(solution)/shard_map/ppermute | solution.py:337
  (20 other events, 121.6 us)

commit v3 on v2

--- a/solution.py
+++ b/solution.py
@@ -1,3 +1,4 @@
+import functools
 import itertools
 import math
 
@@ -77,6 +78,15 @@
     for part in parts[1:]:
         top = jnp.maximum(top, part)
     return top + jnp.log(add_all([jnp.exp(part - top) for part in parts]))
+
+
+def copies(out_ref, value):
+    for peer in range(out_ref.shape[0]):
+        out_ref[peer] = value
+
+
+def combined(parts_ref, combine):
+    return combine([parts_ref[peer] for peer in range(parts_ref.shape[0])])
 
 
 def at_rows(r):
@@ -113,8 +123,11 @@
     return pl.ds(pl.multiple_of(block * 256 + side * LANES, LANES), LANES)
 
 
-def first_terms_kernel(place, x_ref, points_ref, mass_ref, t_ref, top_ref, sum_ref):
+def first_terms_kernel(place, x_ref, points_ref, mass_ref, t_ref, top_ref, sum_ref, squares_ref):
     rows = x_ref.shape[0]
+    squares = x_ref[...].astype(jnp.float32) ** 2
+    sum_ref[...] = squares[:, :LANES] + squares[:, LANES:]
+    squares_ref[...] = collapse(sum_ref)
     blocks = [target_block(place, 0, m) for m in range(4)]
     for m in range(4):
         both = chunk_terms(x_ref, points_ref[m * 256 : (m + 1) * 256, :], mass_ref, blocks[m])
@@ -138,27 +151,34 @@
     lax.fori_loop(0, rows // STEP, rows_step, 0)
 
 
-def terms_kernel(place, x_ref, old_ref, first_top_ref, first_sum_ref, *refs):
-    pieces, (mass_ref, t_ref, out_ref, top_ref, sum_ref) = refs[:3], refs[3:]
+def chunk_steps(k, place, x_ref, points_ref, mass_ref, top_ref, t_ref, sum_ref):
+    def chunk_step(m, unused):
+        block = target_block(place, k, m)
+        points = points_ref[pl.ds(pl.multiple_of(m * 256, 256), 256), :]
+        both = chunk_terms(x_ref, points, mass_ref, block)
+        top = top_ref[...]
+        total = sum_ref[...]
+        for side in range(2):
+            t_ref[:, block_columns(block, side)] = both[side]
+            total += jnp.exp2((both[side] - top) * BITS)
+        sum_ref[...] = total
+        return unused
+
+    lax.fori_loop(0, 4, chunk_step, 0)
+
+
+def more_terms_kernel(k, place, x_ref, old_ref, old_sum_ref, top_ref, points_ref, mass_ref, *refs):
+    t_ref, sum_ref = refs
+    chunk_steps(k, place, x_ref, points_ref, mass_ref, top_ref, t_ref, sum_ref)
+
+
+def last_terms_kernel(k, place, x_ref, old_ref, old_sum_ref, old_top_ref, points_ref, mass_ref, *refs):
+    t_ref, sum_ref, out_ref, top_ref = refs
     rows, columns = t_ref.shape
-    sum_ref[...] = first_sum_ref[...]
-    for k in range(3):
-
-        def chunk_step(m, unused):
-            block = target_block(place, k + 1, m)
-            points = pieces[k][pl.ds(pl.multiple_of(m * 256, 256), 256), :]
-            both = chunk_terms(x_ref, points, mass_ref, block)
-            top = first_top_ref[...]
-            total = sum_ref[...]
-            for side in range(2):
-                t_ref[:, block_columns(block, side)] = both[side]
-                total += jnp.exp2((both[side] - top) * BITS)
-            sum_ref[...] = total
-            return unused
-
-        lax.fori_loop(0, 4, chunk_step, 0)
+    sum_ref[...] = old_sum_ref[...]
+    chunk_steps(k, place, x_ref, points_ref, mass_ref, old_top_ref, t_ref, sum_ref)
     total = collapse(sum_ref)
-    out_ref[...] = collapse_top(first_top_ref) * NATS + jnp.log(total)
+    copies(out_ref, collapse_top(old_top_ref) * NATS + jnp.log(total))
 
     @pl.when(jnp.logical_not(jnp.max(total) < HUGE))
     def exact():
@@ -176,13 +196,12 @@
             return unused
 
         lax.fori_loop(0, rows // STEP, rows_step, 0)
-        out_ref[...] = collapse_top(top_ref) * NATS + jnp.log(collapse(sum_ref))
-
-
-def column_kernel(t_ref, *refs):
-    parts, (mass_ref, out_ref, lse_ref, wide_ref) = refs[:4], refs[4:]
+        copies(out_ref, collapse_top(top_ref) * NATS + jnp.log(collapse(sum_ref)))
+
+
+def column_kernel(t_ref, parts_ref, mass_ref, out_ref, lse_ref, wide_ref, line_ref):
     rows, columns = t_ref.shape
-    lse = lse_all([part[...] for part in parts])
+    lse = combined(parts_ref, lse_all)
     lse_ref[...] = lse
     spread((mass_ref[...] - lse) / NATS, wide_ref)
     per = 4
@@ -208,7 +227,7 @@
         totals = lax.fori_loop(0, rows // STEP, sum_step, start)
         for t in range(per):
             total = jnp.sum(totals[t], axis=0, keepdims=True)
-            out_ref[c + t : c + t + 1, :] = tops[t] * NATS + jnp.log(total)
+            line_ref[c + t : c + t + 1, :] = tops[t] * NATS + jnp.log(total)
 
     for c in range(0, columns // LANES, per):
         tops = [
@@ -217,7 +236,7 @@
         ]
         sums(c, tops)
 
-    @pl.when(jnp.logical_not(jnp.max(out_ref[...]) < HUGE))
+    @pl.when(jnp.logical_not(jnp.max(line_ref[...]) < HUGE))
     def exact():
         for c in range(0, columns // LANES, per):
 
@@ -232,13 +251,13 @@
             tops = lax.fori_loop(0, rows // STEP, top_step, start)
             sums(c, [jnp.max(top, axis=0, keepdims=True) for top in tops])
 
-
-def plan_kernel(t_ref, *refs):
-    parts, refs = refs[:4], refs[4:]
-    tgt_mass_ref, src_lse_ref, src_mass_ref, plan_ref, out_ref, lse_ref = refs[:6]
-    wide_ref, sum_ref, line_ref = refs[6:]
+    copies(out_ref, line_ref[...])
+
+
+def plan_kernel(t_ref, parts_ref, tgt_mass_ref, src_lse_ref, src_mass_ref, *refs):
+    plan_ref, out_ref, lse_ref, wide_ref, sum_ref, line_ref = refs
     rows, columns = t_ref.shape
-    lse = lse_all([part[...] for part in parts])
+    lse = combined(parts_ref, lse_all)
     lse_ref[...] = lse
     line_ref[...] = (tgt_mass_ref[...] - lse) * LOG2E
     spread((src_mass_ref[...] - src_lse_ref[...]) * LOG2E, wide_ref)
@@ -260,13 +279,12 @@
         return unused
 
     lax.fori_loop(0, rows // STEP, rows_step, 0)
-    out_ref[...] = collapse(sum_ref)
-
-
-def row_sums_kernel(plan_ref, *refs):
-    parts, (mass_ref, out_ref, sum_ref, line_ref) = refs[:4], refs[4:]
+    copies(out_ref, collapse(sum_ref))
+
+
+def row_sums_kernel(plan_ref, parts_ref, mass_ref, out_ref, sum_ref, line_ref):
     rows, columns = plan_ref.shape
-    line_ref[...] = jnp.exp(mass_ref[...]) / add_all([part[...] for part in parts])
+    line_ref[...] = jnp.exp(mass_ref[...]) / combined(parts_ref, add_all)
 
     def rows_step(r, unused):
         at = at_rows(r)
@@ -277,10 +295,10 @@
         return unused
 
     lax.fori_loop(0, rows // STEP, rows_step, 0)
-    out_ref[...] = collapse(sum_ref)
-
-
-def column_sums(plan_ref, scale, out_ref, wide_ref):
+    copies(out_ref, collapse(sum_ref))
+
+
+def column_sums(plan_ref, scale, line_ref, wide_ref):
     rows, columns = plan_ref.shape
     spread(scale, wide_ref)
     per = 16
@@ -300,42 +318,35 @@
         start = tuple(jnp.zeros((8, LANES), jnp.float32) for _ in range(per))
         totals = lax.fori_loop(0, rows // STEP, rows_step, start)
         for t in range(per):
-            out_ref[c + t : c + t + 1, :] = jnp.sum(totals[t], axis=0, keepdims=True)
-
-
-def column_sums_kernel(plan_ref, *refs):
-    parts, (mass_ref, out_ref, wide_ref) = refs[:4], refs[4:]
-    scale = jnp.exp(mass_ref[...]) / add_all([part[...] for part in parts])
-    column_sums(plan_ref, scale, out_ref, wide_ref)
-
-
-def last_column_sums_kernel(plan_ref, *refs):
-    parts, (mass_ref, lse_ref, squares_ref, out_ref, potential_ref, wide_ref) = refs[:4], refs[4:]
-    sums = add_all([part[...] for part in parts])
+            line_ref[c + t : c + t + 1, :] = jnp.sum(totals[t], axis=0, keepdims=True)
+
+
+def column_sums_kernel(plan_ref, parts_ref, mass_ref, out_ref, wide_ref, line_ref):
+    scale = jnp.exp(mass_ref[...]) / combined(parts_ref, add_all)
+    column_sums(plan_ref, scale, line_ref, wide_ref)
+    copies(out_ref, line_ref[...])
+
+
+def last_column_sums_kernel(plan_ref, parts_ref, mass_ref, lse_ref, squares_ref, *refs):
+    out_ref, potential_ref, wide_ref, line_ref = refs
+    sums = combined(parts_ref, add_all)
     mass = mass_ref[...]
-    column_sums(plan_ref, jnp.exp(mass) / sums, out_ref, wide_ref)
+    column_sums(plan_ref, jnp.exp(mass) / sums, line_ref, wide_ref)
     squares = squares_ref[...] / (WIDTH * EPS)
     potential = -EPS * (lse_ref[...] + jnp.log(sums) - mass - squares)
     potential_ref[...] = potential
     tiles = plan_ref.shape[1] // LANES
-    out_ref[tiles:, :] = jnp.broadcast_to(jnp.sum(potential), (8, LANES))
-
-
-def last_kernel(*refs):
-    parts, (mass_ref, lse_ref, potential_ref, own_ref, other_ref) = refs[:4], refs[4:]
+    line_ref[tiles:, :] = jnp.broadcast_to(jnp.sum(potential), (8, LANES))
+    copies(out_ref, line_ref[...])
+
+
+def last_kernel(parts_ref, mass_ref, lse_ref, potential_ref, own_ref, other_ref):
     tiles = mass_ref.shape[0]
-    sums = add_all([part[...] for part in parts])
+    sums = combined(parts_ref, add_all)
     potential = -EPS * (lse_ref[...] + jnp.log(sums[:tiles]) - 2.0 * mass_ref[...])
     potential_ref[...] = potential
-    own_ref[...] = jnp.broadcast_to(jnp.sum(potential), (8, LANES))
+    copies(own_ref, jnp.broadcast_to(jnp.sum(potential), (8, LANES)))
     other_ref[...] = sums[tiles:]
-
-
-def shifted(value, axis):
-    n = lax.axis_size(axis)
-    return [value] + [
-        lax.ppermute(value, axis, [(i, (i + k) % n) for i in range(n)]) for k in range(1, n)
-    ]
 
 
 ALL = ("row_0", "row_1", "col_0", "col_1")
@@ -347,15 +358,15 @@
 
 
 def turned(value, stage):
-    found = [value]
-    for k in range(1, 4):
+    found = {0: value}
+    for k in (2, 1, 3):
         pairs = []
         for y, x, z, core in itertools.product(*map(range, SIZES)):
             along_y = (core + stage) % 2
             to = number(y + k * along_y, x + k * (1 - along_y), z, core)
             pairs.append((number(y, x, z, core), to))
-        found.append(lax.ppermute(value, ALL, pairs))
-    return found
+        found[k] = lax.ppermute(value, ALL, pairs)
+    return [found[k] for k in range(4)]
 
 
 def body(src_points, tgt_points, log_src_mass, log_tgt_mass):
@@ -368,50 +379,58 @@
     wide = pltpu.VMEM((rows, LANES), jnp.float32)
     big = pltpu.VMEM((rows, columns), jnp.float32)
     line = pltpu.VMEM((column_tiles, LANES), jnp.float32)
+    longer = pltpu.VMEM((column_tiles + 8, LANES), jnp.float32)
     by_row, by_column = f32(row_tiles, LANES), f32(column_tiles, LANES)
+    peers_row, peers_col = lax.axis_size(ROW), lax.axis_size(COL)
+    rows_out, columns_out = f32(peers_col, row_tiles, LANES), f32(peers_row, column_tiles, LANES)
 
     def resident(value):
         return pltpu.with_memory_space_constraint(value, pltpu.VMEM)
 
-    def over_col(value, combine):
-        return shifted(combine(shifted(value, "col_1")), "col_0")
-
-    def over_row(value, combine):
-        return shifted(combine(shifted(value, "row_1")), "row_0")
+    def over_col(value):
+        return lax.all_to_all(value, COL, 0, 0, tiled=True)
+
+    def over_row(value):
+        return lax.all_to_all(value, ROW, 0, 0, tiled=True)
 
     first = jnp.concatenate(turned(tgt_points, 0))
-    pieces = turned(first, 1)[1:]
-    terms, top, sums = call(first_terms_kernel, (big, wide, wide), [SMEM] + [VMEM] * 3, [])(
-        place, src_points, first, tgt_mass
+    pieces = turned(first, 1)
+    terms, top, sums, squares = call(
+        first_terms_kernel, (big, wide, wide, by_row), [SMEM] + [VMEM] * 3, []
+    )(place, src_points, first, tgt_mass)
+    for k in (1, 3):
+        terms, sums = call(
+            functools.partial(more_terms_kernel, k), (big, wide), [SMEM] + [VMEM] * 6, [], {2: 0, 3: 1}
+        )(place, src_points, resident(terms), resident(sums), resident(top), pieces[k], tgt_mass)
+    terms, sums, lse = call(
+        functools.partial(last_terms_kernel, 2),
+        (big, wide, rows_out),
+        [SMEM] + [VMEM] * 6,
+        [wide],
+        {2: 0, 3: 1},
+    )(place, src_points, resident(terms), resident(sums), resident(top), pieces[2], tgt_mass)
+    lse, src_lse = call(column_kernel, (columns_out, by_row), [VMEM] * 3, [wide, line])(
+        resident(terms), over_col(lse), src_mass
     )
-    terms, lse = call(terms_kernel, (big, by_row), [SMEM] + [VMEM] * 8, [wide, wide], {2: 0})(
-        place, src_points, resident(terms), resident(top), resident(sums), *pieces, tgt_mass
+    plan, sums, tgt_lse = call(
+        plan_kernel, (big, rows_out, by_column), [VMEM] * 5, [wide, wide, line], {0: 0}
+    )(resident(terms), over_row(lse), tgt_mass, src_lse, src_mass)
+    plan = resident(plan)
+    sums = call(column_sums_kernel, columns_out, [VMEM] * 3, [wide, line])(
+        plan, over_col(sums), src_mass
     )
-    parts = over_col(lse, lse_all)
-    lse, src_lse = call(column_kernel, (by_column, by_row), [VMEM] * 6, [wide])(
-        resident(terms), *parts, src_mass
-    )
-    parts = over_row(lse, lse_all)
-    plan, sums, tgt_lse = call(
-        plan_kernel, (big, by_row, by_column), [VMEM] * 8, [wide, wide, line], {0: 0}
-    )(resident(terms), *parts, tgt_mass, src_lse, src_mass)
-    plan = resident(plan)
-    parts = over_col(sums, add_all)
-    sums = call(column_sums_kernel, by_column, [VMEM] * 6, [wide])(plan, *parts, src_mass)
-    parts = over_row(sums, add_all)
-    sums = call(row_sums_kernel, by_row, [VMEM] * 6, [wide, line])(plan, *parts, tgt_mass)
-    parts = over_col(sums, add_all)
-    squares = jnp.sum(src_points.astype(jnp.float32) ** 2, axis=1).reshape(row_tiles, LANES)
+    sums = call(row_sums_kernel, rows_out, [VMEM] * 3, [wide, line])(plan, over_row(sums), tgt_mass)
     sums, src_potential = call(
-        last_column_sums_kernel, (f32(column_tiles + 8, LANES), by_row), [VMEM] * 8, [wide]
-    )(plan, *parts, src_mass, src_lse, squares)
-    parts = over_row(sums, add_all)
-    tile = f32(8, LANES)
-    tgt_potential, tgt_sum, src_sum = call(last_kernel, (by_column, tile, tile), [VMEM] * 6, [])(
-        *parts, tgt_mass, tgt_lse
-    )
-    tgt_sum = add_all(over_col(tgt_sum, add_all))
-    sources_all, targets_all = rows * lax.axis_size(ROW), columns * lax.axis_size(COL)
+        last_column_sums_kernel,
+        (f32(peers_row, column_tiles + 8, LANES), by_row),
+        [VMEM] * 5,
+        [wide, longer],
+    )(plan, over_col(sums), src_mass, src_lse, squares)
+    tgt_potential, tgt_sum, src_sum = call(
+        last_kernel, (by_column, f32(peers_col, 8, LANES), f32(8, LANES)), [VMEM] * 3, []
+    )(over_row(sums), tgt_mass, tgt_lse)
+    tgt_sum = jnp.sum(over_col(tgt_sum), axis=0)
+    sources_all, targets_all = rows * peers_row, columns * peers_col
     mean_potentials = (src_sum / sources_all + tgt_sum / targets_all)[0, 0]
     return (src_potential.reshape(-1), tgt_potential.reshape(-1), mean_potentials)
 

time: 132 us -> 123 us (0.932)
  blocking collectives: 0 us -> 77.4 us
  starting transfers between devices: 70 us -> 10.2 us
  waiting for transfers between devices: 31 us -> 3.94 us
    all_to_all x0 -> x7, blocking collectives: none -> 77.4 us  [the longest x4 40.3 us: over_col(): return lax.all_to_all(value, COL, 0, 0, tiled=True)]
    ppermute x40 -> x6, starting transfers between devices: 70 us -> 10.2 us  [turned(): found[k] = lax.ppermute(value, ALL, pairs)]
    ppermute x40 -> x6, waiting for transfers between devices: 31 us -> 3.94 us  [turned(): found[k] = lax.ppermute(value, ALL, pairs)]
    pallas_call x8 -> x10, Pallas kernels: 25.9 us -> 26.8 us  [the longest x1 5.07 us: body(): call(column_kernel, (columns_out, by_row), [VMEM] * 3, [wide, line])]
  transfers between devices with their start and end apart: 40 -> 6, of which waited for: 31 -> 2; matrix products, arithmetic and copies ran while one was open for 1% -> 1% of each run, Pallas kernels for 3% -> 7%
where the time goes in v3:
time: 123 us; the launch traced here: 122 us
  blocking collectives  77.4 us (63%)
  Pallas kernels  26.8 us (22%)
  starting transfers between devices  10.2 us (8%)
  waiting for transfers between devices  3.94 us (3%)
  local copies, waits for them, and re-layouts  3.26 us (3%)
    all_to_all x4, blocking collectives, over_col(): return lax.all_to_all(value, COL, 0, 0, tiled=True)  40.3 us
    all_to_all x3, blocking collectives, over_row(): return lax.all_to_all(value, ROW, 0, 0, tiled=True)  37.2 us
    ppermute x6, starting transfers between devices, turned(): found[k] = lax.ppermute(value, ALL, pairs)  10.2 us
    pallas_call x1, Pallas kernels, body(): call(column_kernel, (columns_out, by_row), [VMEM] * 3, [wide, line])  5.07 us
    pallas_call x2, Pallas kernels, body(): call(functools.partial(more_terms_kernel, k), (big, wide), [SMEM] + [VMEM...  4.66 us
    ppermute x6, waiting for transfers between devices, turned(): found[k] = lax.ppermute(value, ALL, pairs)  3.94 us
    pallas_call x1, Pallas kernels, body(): call(plan_kernel, (big, rows_out, by_column), [VMEM] * 5, [wide, wide, li...  3.93 us
    pallas_call x1, Pallas kernels, body(): call(first_terms_kernel, (big, wide, wide, by_row), [SMEM] + [VMEM] * 3, [])  3.7 us
  transfers between devices with their start and end apart: 6, of which 2 were waited for; matrix products, arithmetic and copies ran while one was open for 1% of the time, Pallas kernels for 7%

profile of v3, /device:TPU:1, one launch (start us, length us, event | category | flops | bytes accessed | tf_op | source)
XLA Modules:
  0.0 122.5 jit_solution(32226883508723829)
XLA Ops:
  0.6 2.2 %collective-permute-start = (bf16[256,256]{1,0:T(8,128)(2,1)}, bf16[256,256]{1,0:T(8,128)(2,1)S(1)}, u32[]{:S(2)}, u32[]{:S(2)}) collective-permute-start(bf16[256,256]{1,0:T(8,128)(2,1)} %param.5), channel_id=1, source_target_pairs={{0,8},{1,33},{2,10},{3,35},{4,12},{5,37},{6,14},{7,39},{8,16},{9,4... | collective-permute-start | bytes 393224 | tf_op jit(solution)/shard_map/ppermute | solution.py:368
  2.8 2.6 %collective-permute-start.1 = (bf16[256,256]{1,0:T(8,128)(2,1)}, bf16[256,256]{1,0:T(8,128)(2,1)S(1)}, u32[]{:S(2)}, u32[]{:S(2)}) collective-permute-start(bf16[256,256]{1,0:T(8,128)(2,1)} %param.5), channel_id=1, source_target_pairs={{0,16},{1,65},{2,18},{3,67},{4,20},{5,69},{6,22},{7,71},{8,24},{9,... | collective-permute-start | bytes 393224 | tf_op jit(solution)/shard_map/ppermute | solution.py:368
  5.4 1.1 collective-permute-start.2
  7.5 2.2 %collective-permute-done.1 = bf16[256,256]{1,0:T(8,128)(2,1)S(1)} collective-permute-done((bf16[256,256]{1,0:T(8,128)(2,1)}, bf16[256,256]{1,0:T(8,128)(2,1)S(1)}, u32[]{:S(2)}, u32[]{:S(2)}) %collective-permute-start.1) | collective-permute-done | bytes 131104 | tf_op jit(solution)/shard_map/ppermute | solution.py:368
  9.8 1.3 %collective-permute-start.3 = (bf16[1024,256]{1,0:T(8,128)(2,1)S(1)}, bf16[1024,256]{1,0:T(8,128)(2,1)S(1)}, u32[]{:S(2)}, u32[]{:S(2)}) collective-permute-start(bf16[1024,256]{1,0:T(8,128)(2,1)S(1)} %constant_dynamic-update-slice_fusion.points_ref), channel_id=1, source_target_pairs={{0,32},{1,9},{2,34},{3,11},{4,36},{5,13},{6,38},{7,15},{8,40},{9,1... | collective-permute-start | bytes 1572872 | tf_op jit(solution)/shard_map/ppermute | solution.py:368
  11.1 1.5 %collective-permute-start.4 = (bf16[1024,256]{1,0:T(8,128)(2,1)S(1)}, bf16[1024,256]{1,0:T(8,128)(2,1)S(1)}, u32[]{:S(2)}, u32[]{:S(2)}) collective-permute-start(bf16[1024,256]{1,0:T(8,128)(2,1)S(1)} %constant_dynamic-update-slice_fusion.points_ref), channel_id=1, source_target_pairs={{0,96},{1,25},{2,98},{3,27},{4,100},{5,29},{6,102},{7,31},{8,104},... | collective-permute-start | bytes 1572872 | tf_op jit(solution)/shard_map/ppermute | solution.py:368
  12.5 1.5 %collective-permute-start.5 = (bf16[1024,256]{1,0:T(8,128)(2,1)S(1)}, bf16[1024,256]{1,0:T(8,128)(2,1)S(1)}, u32[]{:S(2)}, u32[]{:S(2)}) collective-permute-start(bf16[1024,256]{1,0:T(8,128)(2,1)S(1)} %constant_dynamic-update-slice_fusion.points_ref), channel_id=1, source_target_pairs={{0,64},{1,17},{2,66},{3,19},{4,68},{5,21},{6,70},{7,23},{8,72},{9,... | collective-permute-start | bytes 1572872 | tf_op jit(solution)/shard_map/ppermute | solution.py:368
  15.9 3.7 %shard_map.67 = (f32[1024,4096]{1,0:T(8,128)S(1)}, f32[1024,128]{1,0:T(8,128)S(1)}, f32[1024,128]{1,0:T(8,128)S(1)}, f32[8,128]{1,0:T(8,128)S(1)}) custom-call(s32[3]{0:T(128)S(1)} %pad_add_fusion.place, bf16[1024,256]{1,0:T(8,128)(2,1)S(1)} %copy-done, bf16[1024,256]{1,0:T(8,128)(2,1)S(1)} %constant_dynamic-update-slice_fusion.points_ref, f32[32,128]{1,0:T(8,128)S(1)} %bitcast.8), custom_call_target="tpu_custom_call" | custom-call | tf_op jit(solution)/shard_map/pallas_call | solution.py:398
  19.6 2.3 %shard_map.68 = (f32[1024,4096]{1,0:T(8,128)S(1)}, f32[1024,128]{1,0:T(8,128)S(1)}) custom-call(s32[3]{0:T(128)S(1)} %pad_add_fusion.place, bf16[1024,256]{1,0:T(8,128)(2,1)S(1)} %copy-done, f32[1024,4096]{1,0:T(8,128)S(1)} %get-tuple-element.23.old_ref, ...), custom_call_target="tpu_custom_call", output_to_operand_aliasing={{0}: (2, {}), {1}: (3, {})} | custom-call | tf_op jit(solution)/shard_map/pallas_call | solution.py:402
  22.0 2.3 %shard_map.69 = (f32[1024,4096]{1,0:T(8,128)S(1)}, f32[1024,128]{1,0:T(8,128)S(1)}) custom-call(s32[3]{0:T(128)S(1)} %pad_add_fusion.place, bf16[1024,256]{1,0:T(8,128)(2,1)S(1)} %copy-done, f32[1024,4096]{1,0:T(8,128)S(1)} %get-tuple-element.26.old_ref, ...), custom_call_target="tpu_custom_call", output_to_operand_aliasing={{0}: (2, {}), {1}: (3, {})} | custom-call | tf_op jit(solution)/shard_map/pallas_call | solution.py:402
  24.3 1.7 %collective-permute-done.5.points_ref = bf16[1024,256]{1,0:T(8,128)(2,1)S(1)} collective-permute-done((bf16[1024,256]{1,0:T(8,128)(2,1)S(1)}, bf16[1024,256]{1,0:T(8,128)(2,1)S(1)}, u32[]{:S(2)}, u32[]{:S(2)}) %collective-permute-start.5) | collective-permute-done | bytes 524320 | tf_op jit(solution)/shard_map/ppermute | solution.py:368
  26.0 2.8 %shard_map.70 = (f32[1024,4096]{1,0:T(8,128)S(1)}, f32[1024,128]{1,0:T(8,128)S(1)}, f32[8,8,128]{2,1,0:T(8,128)S(1)}) custom-call(s32[3]{0:T(128)S(1)} %pad_add_fusion.place, bf16[1024,256]{1,0:T(8,128)(2,1)S(1)} %copy-done, f32[1024,4096]{1,0:T(8,128)S(1)} %get-tuple-element.28.old_ref, ...), custom_call_target="tpu_custom_call", output_to_operand_aliasing={{0}: (2, {}), {1}: (3, {})} | custom-call | tf_op jit(solution)/shard_map/pallas_call | solution.py:405
  28.7 12.8 %all_to_all.35.parts_ref = f32[8,8,128]{2,1,0:T(8,128)S(1)} all-to-all(f32[8,8,128]{2,1,0:T(8,128)S(1)} %get-tuple-element.31), channel_id=1, replica_groups=mesh['row_0'=4,'row_1'=4,'col_0'=4,'col_1'=2] {'col_0','col_1'}, dimensions={0} | all-to-all | bytes 65536 | tf_op jit(solution)/shard_map/all_to_all | solution.py:391
  41.5 5.1 %shard_map.71 = (f32[16,32,128]{2,1,0:T(8,128)S(1)}, f32[8,128]{1,0:T(8,128)S(1)}) custom-call(f32[1024,4096]{1,0:T(8,128)S(1)} %get-tuple-element.30.t_ref, f32[8,8,128]{2,1,0:T(8,128)S(1)} %all_to_all.35.parts_ref, f32[8,128]{1,0:T(8,128)S(1)} %bitcast.15), custom_call_target="tpu_custom_call" | custom-call | tf_op jit(solution)/shard_map/pallas_call | solution.py:412
  46.6 16.0 %all_to_all.36.parts_ref = f32[16,32,128]{2,1,0:T(8,128)S(1)} all-to-all(f32[16,32,128]{2,1,0:T(8,128)S(1)} %get-tuple-element.32), channel_id=1, replica_groups=mesh['row_0'=4,'row_1'=4,'col_0'=4,'col_1'=2] {'row_0','row_1'}, dimensions={0} | all-to-all | bytes 524288 | tf_op jit(solution)/shard_map/all_to_all | solution.py:394
  62.6 3.9 %shard_map.72 = (f32[1024,4096]{1,0:T(8,128)S(1)}, f32[8,8,128]{2,1,0:T(8,128)S(1)}, f32[32,128]{1,0:T(8,128)S(1)}) custom-call(f32[1024,4096]{1,0:T(8,128)S(1)} %get-tuple-element.30.t_ref, f32[16,32,128]{2,1,0:T(8,128)S(1)} %all_to_all.36.parts_ref, f32[32,128]{1,0:T(8,128)S(1)} %bitcast.12, ...), custom_call_target="tpu_custom_call", output_to_operand_aliasing={{0}: (0, {})} | custom-call | tf_op jit(solution)/shard_map/pallas_call | solution.py:415
  66.5 9.2 %all_to_all.37.parts_ref = f32[8,8,128]{2,1,0:T(8,128)S(1)} all-to-all(f32[8,8,128]{2,1,0:T(8,128)S(1)} %get-tuple-element.35), channel_id=1, replica_groups=mesh['row_0'=4,'row_1'=4,'col_0'=4,'col_1'=2] {'col_0','col_1'}, dimensions={0} | all-to-all | bytes 65536 | tf_op jit(solution)/shard_map/all_to_all | solution.py:391
  75.8 1.7 %shard_map.73 = f32[16,32,128]{2,1,0:T(8,128)S(1)} custom-call(f32[1024,4096]{1,0:T(8,128)S(1)} %get-tuple-element.34.plan_ref, f32[8,8,128]{2,1,0:T(8,128)S(1)} %all_to_all.37.parts_ref, f32[8,128]{1,0:T(8,128)S(1)} %bitcast.17), custom_call_target="tpu_custom_call" | custom-call | tf_op jit(solution)/shard_map/pallas_call | solution.py:419
  77.5 10.2 %all_to_all.38.parts_ref = f32[16,32,128]{2,1,0:T(8,128)S(1)} all-to-all(f32[16,32,128]{2,1,0:T(8,128)S(1)} %shard_map.73), channel_id=1, replica_groups=mesh['row_0'=4,'row_1'=4,'col_0'=4,'col_1'=2] {'row_0','row_1'}, dimensions={0} | all-to-all | bytes 524288 | tf_op jit(solution)/shard_map/all_to_all | solution.py:394
  87.6 2.1 %shard_map.74 = f32[8,8,128]{2,1,0:T(8,128)S(1)} custom-call(f32[1024,4096]{1,0:T(8,128)S(1)} %get-tuple-element.34.plan_ref, f32[16,32,128]{2,1,0:T(8,128)S(1)} %all_to_all.38.parts_ref, f32[32,128]{1,0:T(8,128)S(1)} %bitcast.13), custom_call_target="tpu_custom_call" | custom-call | tf_op jit(solution)/shard_map/pallas_call | solution.py:422
  89.7 9.2 %all_to_all.39.parts_ref = f32[8,8,128]{2,1,0:T(8,128)S(1)} all-to-all(f32[8,8,128]{2,1,0:T(8,128)S(1)} %shard_map.74), channel_id=1, replica_groups=mesh['row_0'=4,'row_1'=4,'col_0'=4,'col_1'=2] {'col_0','col_1'}, dimensions={0} | all-to-all | bytes 65536 | tf_op jit(solution)/shard_map/all_to_all | solution.py:391
  99.0 2.3 %shard_map.75 = (f32[16,40,128]{2,1,0:T(8,128)S(1)}, f32[8,128]{1,0:T(8,128)}) custom-call(f32[1024,4096]{1,0:T(8,128)S(1)} %get-tuple-element.34.plan_ref, f32[8,8,128]{2,1,0:T(8,128)S(1)} %all_to_all.39.parts_ref, f32[8,128]{1,0:T(8,128)S(1)} %bitcast.18, f32[8,128]{1,0:T(8,128)S(1)} %get-tuple-element.33.src_lse_ref.lse_ref, ...), custom_call_target="tpu_custom_call" | custom-call | tf_op jit(solution)/shard_map/pallas_call | solution.py:423
  101.3 11.0 %all_to_all.40.parts_ref = f32[16,40,128]{2,1,0:T(8,128)S(1)} all-to-all(f32[16,40,128]{2,1,0:T(8,128)S(1)} %get-tuple-element.38), channel_id=1, replica_groups=mesh['row_0'=4,'row_1'=4,'col_0'=4,'col_1'=2] {'row_0','row_1'}, dimensions={0} | all-to-all | bytes 655360 | tf_op jit(solution)/shard_map/all_to_all | solution.py:394
  112.9 9.0 %all_to_all.41 = f32[8,8,128]{2,1,0:T(8,128)S(1)} all-to-all(f32[8,8,128]{2,1,0:T(8,128)S(1)} %get-tuple-element.42), channel_id=1, replica_groups=mesh['row_0'=4,'row_1'=4,'col_0'=4,'col_1'=2] {'col_0','col_1'}, dimensions={0} | all-to-all | bytes 65536 | tf_op jit(solution)/shard_map/all_to_all | solution.py:391
  (21 shorter events, 4.0 us)
Async XLA Ops:
  0.6 6.8 %collective-permute-start = (bf16[256,256]{1,0:T(8,128)(2,1)}, bf16[256,256]{1,0:T(8,128)(2,1)S(1)}, u32[]{:S(2)}, u32[]{:S(2)}) collective-permute-start(bf16[256,256]{1,0:T(8,128)(2,1)} %param.5), channel_id=1, source_target_pairs={{0,8},{1,33},{2,10},{3,35},{4,12},{5,37},{6,14},{7,39},{8,16},{9,4... | collective-permute-start | bytes 393224 | tf_op jit(solution)/shard_map/ppermute | solution.py:368
  2.8 6.9 %collective-permute-start.1 = (bf16[256,256]{1,0:T(8,128)(2,1)}, bf16[256,256]{1,0:T(8,128)(2,1)S(1)}, u32[]{:S(2)}, u32[]{:S(2)}) collective-permute-start(bf16[256,256]{1,0:T(8,128)(2,1)} %param.5), channel_id=1, source_target_pairs={{0,16},{1,65},{2,18},{3,67},{4,20},{5,69},{6,22},{7,71},{8,24},{9,... | collective-permute-start | bytes 393224 | tf_op jit(solution)/shard_map/ppermute | solution.py:368
  5.4 4.3 %collective-permute-start.2 = (bf16[256,256]{1,0:T(8,128)(2,1)}, bf16[256,256]{1,0:T(8,128)(2,1)S(1)}, u32[]{:S(2)}, u32[]{:S(2)}) collective-permute-start(bf16[256,256]{1,0:T(8,128)(2,1)} %param.5), channel_id=1, source_target_pairs={{0,24},{1,97},{2,26},{3,99},{4,28},{5,101},{6,30},{7,103},{8,0},{9... | collective-permute-start | bytes 393224 | tf_op jit(solution)/shard_map/ppermute | solution.py:368
  9.8 9.8 %collective-permute-start.3 = (bf16[1024,256]{1,0:T(8,128)(2,1)S(1)}, bf16[1024,256]{1,0:T(8,128)(2,1)S(1)}, u32[]{:S(2)}, u32[]{:S(2)}) collective-permute-start(bf16[1024,256]{1,0:T(8,128)(2,1)S(1)} %constant_dynamic-update-slice_fusion.points_ref), channel_id=1, source_target_pairs={{0,32},{1,9},{2,34},{3,11},{4,36},{5,13},{6,38},{7,15},{8,40},{9,1... | collective-permute-start | bytes 1572872 | tf_op jit(solution)/shard_map/ppermute | solution.py:368
  11.1 10.9 %collective-permute-start.4 = (bf16[1024,256]{1,0:T(8,128)(2,1)S(1)}, bf16[1024,256]{1,0:T(8,128)(2,1)S(1)}, u32[]{:S(2)}, u32[]{:S(2)}) collective-permute-start(bf16[1024,256]{1,0:T(8,128)(2,1)S(1)} %constant_dynamic-update-slice_fusion.points_ref), channel_id=1, source_target_pairs={{0,96},{1,25},{2,98},{3,27},{4,100},{5,29},{6,102},{7,31},{8,104},... | collective-permute-start | bytes 1572872 | tf_op jit(solution)/shard_map/ppermute | solution.py:368
  12.5 13.5 %collective-permute-start.5 = (bf16[1024,256]{1,0:T(8,128)(2,1)S(1)}, bf16[1024,256]{1,0:T(8,128)(2,1)S(1)}, u32[]{:S(2)}, u32[]{:S(2)}) collective-permute-start(bf16[1024,256]{1,0:T(8,128)(2,1)S(1)} %constant_dynamic-update-slice_fusion.points_ref), channel_id=1, source_target_pairs={{0,64},{1,17},{2,66},{3,19},{4,68},{5,21},{6,70},{7,23},{8,72},{9,... | collective-permute-start | bytes 1572872 | tf_op jit(solution)/shard_map/ppermute | solution.py:368
  14.1 1.0 copy-start
  15.2 0.7 copy-start.1
  19.6 6.4 %copy-start.2 = (f32[4096]{0:T(1024)S(1)}, f32[4096]{0:T(1024)}, u32[]{:S(2)}) copy-start(f32[4096]{0:T(1024)} %param.7) | copy-start | bytes 49156
  22.0 19.6 %copy-start.3 = (f32[1024]{0:T(1024)S(1)}, f32[1024]{0:T(1024)}, u32[]{:S(2)}) copy-start(f32[1024]{0:T(1024)} %param.6) | copy-start | bytes 12292

commit v4 on v3

--- a/solution.py
+++ b/solution.py
@@ -19,9 +19,11 @@
 NATS = 2.0 / (WIDTH * EPS)
 BITS = NATS * math.log2(math.e)
 LOG2E = math.log2(math.e)
+LN2 = math.log(2.0)
 VMEM_LIMIT = 24 * 1024 * 1024
 LANES = 128
 STEP = 64
+ROWS = 512
 HUGE = 3.0e38
 
 VMEM = pl.BlockSpec(memory_space=pltpu.VMEM)
@@ -104,23 +106,32 @@
     return 4 * lax.rem(place[0] + 4 - shift_y, 4) + lax.rem(place[1] + 4 - shift_x, 4)
 
 
-def chunk_terms(x_ref, points, mass_ref, block):
+def chunk_biases(points, mass_ref, block):
     squares = points.astype(jnp.float32) ** 2
     squares = squares[:, :LANES] + squares[:, LANES:]
-    product = lax.dot_general(
-        x_ref[...], points, (((1,), (1,)), ((), ())), preferred_element_type=jnp.float32
-    )
     found = []
     for side in range(2):
         square = squares[side * LANES : (side + 1) * LANES, :].T
         mass = mass_ref[pl.ds(2 * block + side, 1), :]
-        bias = mass / NATS - jnp.sum(square, axis=0, keepdims=True) * 0.5
-        found.append(product[:, lane_tile(side)] + bias)
+        found.append(mass * LOG2E - jnp.sum(square, axis=0, keepdims=True) * (0.5 * BITS))
     return found
 
 
-def block_columns(block, side):
-    return pl.ds(pl.multiple_of(block * 256 + side * LANES, LANES), LANES)
+def piece_product(x_ref, points_ref, r, m):
+    return lax.dot_general(
+        x_ref[r : r + ROWS, :],
+        points_ref[m * 256 : (m + 1) * 256, :],
+        (((1,), (1,)), ((), ())),
+        preferred_element_type=jnp.float32,
+    )
+
+
+def piece_blocks(k, place, points_ref, mass_ref):
+    blocks = [target_block(place, k, m) for m in range(4)]
+    biases = [
+        chunk_biases(points_ref[m * 256 : (m + 1) * 256, :], mass_ref, blocks[m]) for m in range(4)
+    ]
+    return blocks, biases
 
 
 def first_terms_kernel(place, x_ref, points_ref, mass_ref, t_ref, top_ref, sum_ref, squares_ref):
@@ -128,13 +139,16 @@
     squares = x_ref[...].astype(jnp.float32) ** 2
     sum_ref[...] = squares[:, :LANES] + squares[:, LANES:]
     squares_ref[...] = collapse(sum_ref)
-    blocks = [target_block(place, 0, m) for m in range(4)]
-    for m in range(4):
-        both = chunk_terms(x_ref, points_ref[m * 256 : (m + 1) * 256, :], mass_ref, blocks[m])
-        for side in range(2):
-            t_ref[:, block_columns(blocks[m], side)] = both[side]
-        top = jnp.maximum(both[0], both[1])
-        top_ref[...] = top if m == 0 else jnp.maximum(top_ref[...], top)
+    blocks, biases = piece_blocks(0, place, points_ref, mass_ref)
+    for r in range(0, rows, ROWS):
+        top = None
+        for m in range(4):
+            product = piece_product(x_ref, points_ref, r, m)
+            for side in range(2):
+                terms = product[:, lane_tile(side)] * BITS + biases[m][side]
+                t_ref[2 * blocks[m] + side, r : r + ROWS, :] = terms
+                top = terms if top is None else jnp.maximum(top, terms)
+        top_ref[r : r + ROWS, :] = top
 
     def rows_step(r, unused):
         at = at_rows(r)
@@ -142,8 +156,7 @@
         total = jnp.zeros((STEP, LANES), jnp.float32)
         for m in range(4):
             for side in range(2):
-                terms = t_ref[at, block_columns(blocks[m], side)]
-                total += jnp.exp2((terms - top) * BITS)
+                total += jnp.exp2(t_ref[2 * blocks[m] + side, at, :] - top)
         top_ref[at, :] = jnp.broadcast_to(top, (STEP, LANES))
         sum_ref[at, :] = total
         return unused
@@ -151,59 +164,56 @@
     lax.fori_loop(0, rows // STEP, rows_step, 0)
 
 
-def chunk_steps(k, place, x_ref, points_ref, mass_ref, top_ref, t_ref, sum_ref):
-    def chunk_step(m, unused):
-        block = target_block(place, k, m)
-        points = points_ref[pl.ds(pl.multiple_of(m * 256, 256), 256), :]
-        both = chunk_terms(x_ref, points, mass_ref, block)
-        top = top_ref[...]
-        total = sum_ref[...]
-        for side in range(2):
-            t_ref[:, block_columns(block, side)] = both[side]
-            total += jnp.exp2((both[side] - top) * BITS)
-        sum_ref[...] = total
-        return unused
-
-    lax.fori_loop(0, 4, chunk_step, 0)
+def piece_steps(k, place, x_ref, points_ref, mass_ref, top_ref, old_sum_ref, t_ref, sum_ref):
+    blocks, biases = piece_blocks(k, place, points_ref, mass_ref)
+    for r in range(0, x_ref.shape[0], ROWS):
+        top = top_ref[r : r + ROWS, :]
+        total = old_sum_ref[r : r + ROWS, :]
+        for m in range(4):
+            product = piece_product(x_ref, points_ref, r, m)
+            for side in range(2):
+                terms = product[:, lane_tile(side)] * BITS + biases[m][side]
+                t_ref[2 * blocks[m] + side, r : r + ROWS, :] = terms
+                total += jnp.exp2(terms - top)
+        sum_ref[r : r + ROWS, :] = total
 
 
 def more_terms_kernel(k, place, x_ref, old_ref, old_sum_ref, top_ref, points_ref, mass_ref, *refs):
     t_ref, sum_ref = refs
-    chunk_steps(k, place, x_ref, points_ref, mass_ref, top_ref, t_ref, sum_ref)
+    piece_steps(k, place, x_ref, points_ref, mass_ref, top_ref, old_sum_ref, t_ref, sum_ref)
 
 
 def last_terms_kernel(k, place, x_ref, old_ref, old_sum_ref, old_top_ref, points_ref, mass_ref, *refs):
     t_ref, sum_ref, out_ref, top_ref = refs
-    rows, columns = t_ref.shape
-    sum_ref[...] = old_sum_ref[...]
-    chunk_steps(k, place, x_ref, points_ref, mass_ref, old_top_ref, t_ref, sum_ref)
+    tiles, rows, _ = t_ref.shape
+    piece_steps(k, place, x_ref, points_ref, mass_ref, old_top_ref, old_sum_ref, t_ref, sum_ref)
     total = collapse(sum_ref)
-    copies(out_ref, collapse_top(old_top_ref) * NATS + jnp.log(total))
+    copies(out_ref, collapse_top(old_top_ref) * LN2 + jnp.log(total))
 
     @pl.when(jnp.logical_not(jnp.max(total) < HUGE))
     def exact():
         def rows_step(r, unused):
             at = at_rows(r)
             top = jnp.full((STEP, LANES), -jnp.inf, jnp.float32)
-            for t in range(columns // LANES):
-                top = jnp.maximum(top, t_ref[at, lane_tile(t)])
+            for t in range(tiles):
+                top = jnp.maximum(top, t_ref[t, at, :])
             top = jnp.max(top, axis=1, keepdims=True)
             total = jnp.zeros((STEP, LANES), jnp.float32)
-            for t in range(columns // LANES):
-                total += jnp.exp2((t_ref[at, lane_tile(t)] - top) * BITS)
+            for t in range(tiles):
+                total += jnp.exp2(t_ref[t, at, :] - top)
             top_ref[at, :] = jnp.broadcast_to(top, (STEP, LANES))
             sum_ref[at, :] = total
             return unused
 
         lax.fori_loop(0, rows // STEP, rows_step, 0)
-        copies(out_ref, collapse_top(top_ref) * NATS + jnp.log(collapse(sum_ref)))
+        copies(out_ref, collapse_top(top_ref) * LN2 + jnp.log(collapse(sum_ref)))
 
 
 def column_kernel(t_ref, parts_ref, mass_ref, out_ref, lse_ref, wide_ref, line_ref):
-    rows, columns = t_ref.shape
+    tiles, rows, _ = t_ref.shape
     lse = combined(parts_ref, lse_all)
     lse_ref[...] = lse
-    spread((mass_ref[...] - lse) / NATS, wide_ref)
+    spread((mass_ref[...] - lse) * LOG2E, wide_ref)
     per = 4
 
     def group(value):
@@ -218,7 +228,7 @@
             return tuple(
                 total
                 + jnp.sum(
-                    group(jnp.exp2((t_ref[at, lane_tile(c + t)] + own - wide[t]) * BITS)), axis=0
+                    group(jnp.exp2(t_ref[c + t, at, :] + own - wide[t])), axis=0
                 )
                 for t, total in enumerate(totals)
             )
@@ -227,23 +237,23 @@
         totals = lax.fori_loop(0, rows // STEP, sum_step, start)
         for t in range(per):
             total = jnp.sum(totals[t], axis=0, keepdims=True)
-            line_ref[c + t : c + t + 1, :] = tops[t] * NATS + jnp.log(total)
-
-    for c in range(0, columns // LANES, per):
+            line_ref[c + t : c + t + 1, :] = tops[t] * LN2 + jnp.log(total)
+
+    for c in range(0, tiles, per):
         tops = [
-            jnp.max(t_ref[:STEP, lane_tile(c + t)] + wide_ref[:STEP, :], axis=0, keepdims=True)
+            jnp.max(t_ref[c + t, :STEP, :] + wide_ref[:STEP, :], axis=0, keepdims=True)
             for t in range(per)
         ]
         sums(c, tops)
 
     @pl.when(jnp.logical_not(jnp.max(line_ref[...]) < HUGE))
     def exact():
-        for c in range(0, columns // LANES, per):
+        for c in range(0, tiles, per):
 
             def top_step(r, tops):
                 at = at_rows(r)
                 return tuple(
-                    jnp.maximum(top, jnp.max(group(t_ref[at, lane_tile(c + t)] + wide_ref[at, :]), axis=0))
+                    jnp.maximum(top, jnp.max(group(t_ref[c + t, at, :] + wide_ref[at, :]), axis=0))
                     for t, top in enumerate(tops)
                 )
 
@@ -256,7 +266,7 @@
 
 def plan_kernel(t_ref, parts_ref, tgt_mass_ref, src_lse_ref, src_mass_ref, *refs):
     plan_ref, out_ref, lse_ref, wide_ref, sum_ref, line_ref = refs
-    rows, columns = t_ref.shape
+    tiles, rows, _ = t_ref.shape
     lse = combined(parts_ref, lse_all)
     lse_ref[...] = lse
     line_ref[...] = (tgt_mass_ref[...] - lse) * LOG2E
@@ -267,13 +277,13 @@
         at = at_rows(r)
         total = jnp.zeros((STEP, LANES), jnp.float32)
         own = wide_ref[at, :]
-        for c in range(0, columns // LANES, per):
-            terms = [t_ref[at, lane_tile(c + t)] for t in range(per)]
+        for c in range(0, tiles, per):
+            terms = [t_ref[c + t, at, :] for t in range(per)]
             values = [
-                jnp.exp2(terms[t] * BITS + own + line_ref[c + t : c + t + 1, :]) for t in range(per)
+                jnp.exp2(terms[t] + own + line_ref[c + t : c + t + 1, :]) for t in range(per)
             ]
             for t in range(per):
-                plan_ref[at, lane_tile(c + t)] = values[t]
+                plan_ref[c + t, at, :] = values[t]
                 total += values[t]
         sum_ref[at, :] = total
         return unused
@@ -283,14 +293,14 @@
 
 
 def row_sums_kernel(plan_ref, parts_ref, mass_ref, out_ref, sum_ref, line_ref):
-    rows, columns = plan_ref.shape
+    tiles, rows, _ = plan_ref.shape
     line_ref[...] = jnp.exp(mass_ref[...]) / combined(parts_ref, add_all)
 
     def rows_step(r, unused):
         at = at_rows(r)
         total = jnp.zeros((STEP, LANES), jnp.float32)
-        for t in range(columns // LANES):
-            total += plan_ref[at, lane_tile(t)] * line_ref[t : t + 1, :]
+        for t in range(tiles):
+            total += plan_ref[t, at, :] * line_ref[t : t + 1, :]
         sum_ref[at, :] = total
         return unused
 
@@ -299,10 +309,10 @@
 
 
 def column_sums(plan_ref, scale, line_ref, wide_ref):
-    rows, columns = plan_ref.shape
+    tiles, rows, _ = plan_ref.shape
     spread(scale, wide_ref)
     per = 16
-    for c in range(0, columns // LANES, per):
+    for c in range(0, tiles, per):
 
         def rows_step(r, totals):
             at = at_rows(r)
@@ -310,7 +320,7 @@
             return tuple(
                 total
                 + jnp.sum(
-                    (plan_ref[at, lane_tile(c + t)] * own).reshape(STEP // 8, 8, LANES), axis=0
+                    (plan_ref[c + t, at, :] * own).reshape(STEP // 8, 8, LANES), axis=0
                 )
                 for t, total in enumerate(totals)
             )
@@ -335,7 +345,7 @@
     squares = squares_ref[...] / (WIDTH * EPS)
     potential = -EPS * (lse_ref[...] + jnp.log(sums) - mass - squares)
     potential_ref[...] = potential
-    tiles = plan_ref.shape[1] // LANES
+    tiles = plan_ref.shape[0]
     line_ref[tiles:, :] = jnp.broadcast_to(jnp.sum(potential), (8, LANES))
     copies(out_ref, line_ref[...])
 
@@ -377,7 +387,7 @@
     place = jnp.stack([lax.axis_index(name) for name in ("row_0", "row_1", "col_1")])
     place = place.astype(jnp.int32)
     wide = pltpu.VMEM((rows, LANES), jnp.float32)
-    big = pltpu.VMEM((rows, columns), jnp.float32)
+    big = pltpu.VMEM((column_tiles, rows, LANES), jnp.float32)
     line = pltpu.VMEM((column_tiles, LANES), jnp.float32)
     longer = pltpu.VMEM((column_tiles + 8, LANES), jnp.float32)
     by_row, by_column = f32(row_tiles, LANES), f32(column_tiles, LANES)

time: 123 us -> 120 us (0.976)
  Pallas kernels: 26.8 us -> 24 us
  waiting for transfers between devices: 3.94 us -> 5.34 us
    ppermute x6, waiting for transfers between devices: 3.94 us -> 5.34 us  [turned(): found[k] = lax.ppermute(value, ALL, pairs)]
    pallas_call x2, Pallas kernels: 4.66 us -> 3.43 us  [body(): call(functools.partial(more_terms_kernel, k), (big, wide), [SMEM] + [VMEM...]
  transfers between devices with their start and end apart: 6 -> 6, of which waited for: 2 -> 2; matrix products, arithmetic and copies ran while one was open for 1% -> 1% of each run, Pallas kernels for 7% -> 6%
where the time goes in v4:
time: 120 us
  blocking collectives  76.2 us (64%)
  Pallas kernels  24 us (20%)
  starting transfers between devices  10.2 us (8%)
  waiting for transfers between devices  5.34 us (4%)
  local copies, waits for them, and re-layouts  3.26 us (3%)
    all_to_all x4, blocking collectives, over_col(): return lax.all_to_all(value, COL, 0, 0, tiled=True)  40.3 us
    all_to_all x3, blocking collectives, over_row(): return lax.all_to_all(value, ROW, 0, 0, tiled=True)  36 us
    ppermute x6, starting transfers between devices, turned(): found[k] = lax.ppermute(value, ALL, pairs)  10.2 us
    ppermute x6, waiting for transfers between devices, turned(): found[k] = lax.ppermute(value, ALL, pairs)  5.34 us
    pallas_call x1, Pallas kernels, body(): call(column_kernel, (columns_out, by_row), [VMEM] * 3, [wide, line])  4.73 us
    pallas_call x1, Pallas kernels, body(): call(plan_kernel, (big, rows_out, by_column), [VMEM] * 5, [wide, wide, li...  3.78 us
    pallas_call x1, Pallas kernels, body(): call(first_terms_kernel, (big, wide, wide, by_row), [SMEM] + [VMEM] * 3, [])  3.52 us
    pallas_call x2, Pallas kernels, body(): call(functools.partial(more_terms_kernel, k), (big, wide), [SMEM] + [VMEM...  3.43 us
  transfers between devices with their start and end apart: 6, of which 2 were waited for; matrix products, arithmetic and copies ran while one was open for 1% of the time, Pallas kernels for 6%

profile of v4, /device:TPU:1, one launch (start us, length us, event | category | flops | bytes accessed | tf_op | source)
XLA Modules:
  0.0 119.9 jit_solution(7292179406285011711)
XLA Ops:
  0.6 2.2 %collective-permute-start = (bf16[256,256]{1,0:T(8,128)(2,1)}, bf16[256,256]{1,0:T(8,128)(2,1)S(1)}, u32[]{:S(2)}, u32[]{:S(2)}) collective-permute-start(bf16[256,256]{1,0:T(8,128)(2,1)} %param.5), channel_id=1, source_target_pairs={{0,8},{1,33},{2,10},{3,35},{4,12},{5,37},{6,14},{7,39},{8,16},{9,4... | collective-permute-start | bytes 393224 | tf_op jit(solution)/shard_map/ppermute | solution.py:378
  2.8 2.6 %collective-permute-start.1 = (bf16[256,256]{1,0:T(8,128)(2,1)}, bf16[256,256]{1,0:T(8,128)(2,1)S(1)}, u32[]{:S(2)}, u32[]{:S(2)}) collective-permute-start(bf16[256,256]{1,0:T(8,128)(2,1)} %param.5), channel_id=1, source_target_pairs={{0,16},{1,65},{2,18},{3,67},{4,20},{5,69},{6,22},{7,71},{8,24},{9,... | collective-permute-start | bytes 393224 | tf_op jit(solution)/shard_map/ppermute | solution.py:378
  5.4 1.1 collective-permute-start.2
  7.5 2.2 %collective-permute-done.1 = bf16[256,256]{1,0:T(8,128)(2,1)S(1)} collective-permute-done((bf16[256,256]{1,0:T(8,128)(2,1)}, bf16[256,256]{1,0:T(8,128)(2,1)S(1)}, u32[]{:S(2)}, u32[]{:S(2)}) %collective-permute-start.1) | collective-permute-done | bytes 131104 | tf_op jit(solution)/shard_map/ppermute | solution.py:378
  9.8 1.3 %collective-permute-start.3 = (bf16[1024,256]{1,0:T(8,128)(2,1)S(1)}, bf16[1024,256]{1,0:T(8,128)(2,1)S(1)}, u32[]{:S(2)}, u32[]{:S(2)}) collective-permute-start(bf16[1024,256]{1,0:T(8,128)(2,1)S(1)} %constant_dynamic-update-slice_fusion.points_ref), channel_id=1, source_target_pairs={{0,32},{1,9},{2,34},{3,11},{4,36},{5,13},{6,38},{7,15},{8,40},{9,1... | collective-permute-start | bytes 1572872 | tf_op jit(solution)/shard_map/ppermute | solution.py:378
  11.1 1.5 %collective-permute-start.4 = (bf16[1024,256]{1,0:T(8,128)(2,1)S(1)}, bf16[1024,256]{1,0:T(8,128)(2,1)S(1)}, u32[]{:S(2)}, u32[]{:S(2)}) collective-permute-start(bf16[1024,256]{1,0:T(8,128)(2,1)S(1)} %constant_dynamic-update-slice_fusion.points_ref), channel_id=1, source_target_pairs={{0,96},{1,25},{2,98},{3,27},{4,100},{5,29},{6,102},{7,31},{8,104},... | collective-permute-start | bytes 1572872 | tf_op jit(solution)/shard_map/ppermute | solution.py:378
  12.5 1.5 %collective-permute-start.5 = (bf16[1024,256]{1,0:T(8,128)(2,1)S(1)}, bf16[1024,256]{1,0:T(8,128)(2,1)S(1)}, u32[]{:S(2)}, u32[]{:S(2)}) collective-permute-start(bf16[1024,256]{1,0:T(8,128)(2,1)S(1)} %constant_dynamic-update-slice_fusion.points_ref), channel_id=1, source_target_pairs={{0,64},{1,17},{2,66},{3,19},{4,68},{5,21},{6,70},{7,23},{8,72},{9,... | collective-permute-start | bytes 1572872 | tf_op jit(solution)/shard_map/ppermute | solution.py:378
  15.9 3.5 %shard_map.67 = (f32[32,1024,128]{2,1,0:T(8,128)S(1)}, f32[1024,128]{1,0:T(8,128)S(1)}, f32[1024,128]{1,0:T(8,128)S(1)}, f32[8,128]{1,0:T(8,128)S(1)}) custom-call(s32[3]{0:T(128)S(1)} %pad_add_fusion.place, bf16[1024,256]{1,0:T(8,128)(2,1)S(1)} %copy-done, bf16[1024,256]{1,0:T(8,128)(2,1)S(1)} %constant_dynamic-update-slice_fusion.points_ref, ...), custom_call_target="tpu_custom_call" | custom-call | tf_op jit(solution)/shard_map/pallas_call | solution.py:408
  19.5 1.7 %shard_map.68 = (f32[32,1024,128]{2,1,0:T(8,128)S(1)}, f32[1024,128]{1,0:T(8,128)S(1)}) custom-call(s32[3]{0:T(128)S(1)} %pad_add_fusion.place, bf16[1024,256]{1,0:T(8,128)(2,1)S(1)} %copy-done, f32[32,1024,128]{2,1,0:T(8,128)S(1)} %get-tuple-element.23.old_ref, ...), custom_call_target="tpu_custom_call", output_to_operand_aliasing={{0}: (2, {}), {1}: (3, {})} | custom-call | tf_op jit(solution)/shard_map/pallas_call | solution.py:412
  21.2 1.7 %shard_map.69 = (f32[32,1024,128]{2,1,0:T(8,128)S(1)}, f32[1024,128]{1,0:T(8,128)S(1)}) custom-call(s32[3]{0:T(128)S(1)} %pad_add_fusion.place, bf16[1024,256]{1,0:T(8,128)(2,1)S(1)} %copy-done, f32[32,1024,128]{2,1,0:T(8,128)S(1)} %get-tuple-element.26.old_ref, ...), custom_call_target="tpu_custom_call", output_to_operand_aliasing={{0}: (2, {}), {1}: (3, {})} | custom-call | tf_op jit(solution)/shard_map/pallas_call | solution.py:412
  22.9 3.1 %collective-permute-done.5.points_ref = bf16[1024,256]{1,0:T(8,128)(2,1)S(1)} collective-permute-done((bf16[1024,256]{1,0:T(8,128)(2,1)S(1)}, bf16[1024,256]{1,0:T(8,128)(2,1)S(1)}, u32[]{:S(2)}, u32[]{:S(2)}) %collective-permute-start.5) | collective-permute-done | bytes 524320 | tf_op jit(solution)/shard_map/ppermute | solution.py:378
  26.0 1.9 %shard_map.70 = (f32[32,1024,128]{2,1,0:T(8,128)S(1)}, f32[1024,128]{1,0:T(8,128)S(1)}, f32[8,8,128]{2,1,0:T(8,128)S(1)}) custom-call(s32[3]{0:T(128)S(1)} %pad_add_fusion.place, bf16[1024,256]{1,0:T(8,128)(2,1)S(1)} %copy-done, f32[32,1024,128]{2,1,0:T(8,128)S(1)} %get-tuple-element.28.old_ref, ...), custom_call_target="tpu_custom_call", output_to_operand_aliasing={{0}: (2, {}), {1}: (3, {})} | custom-call | tf_op jit(solution)/shard_map/pallas_call | solution.py:415
  27.9 12.8 %all_to_all.35.parts_ref = f32[8,8,128]{2,1,0:T(8,128)S(1)} all-to-all(f32[8,8,128]{2,1,0:T(8,128)S(1)} %get-tuple-element.31), channel_id=1, replica_groups=mesh['row_0'=4,'row_1'=4,'col_0'=4,'col_1'=2] {'col_0','col_1'}, dimensions={0} | all-to-all | bytes 65536 | tf_op jit(solution)/shard_map/all_to_all | solution.py:401
  40.7 4.7 %shard_map.71 = (f32[16,32,128]{2,1,0:T(8,128)S(1)}, f32[8,128]{1,0:T(8,128)S(1)}) custom-call(f32[32,1024,128]{2,1,0:T(8,128)S(1)} %get-tuple-element.30.t_ref, f32[8,8,128]{2,1,0:T(8,128)S(1)} %all_to_all.35.parts_ref, f32[8,128]{1,0:T(8,128)S(1)} %bitcast.15), custom_call_target="tpu_custom_call" | custom-call | tf_op jit(solution)/shard_map/pallas_call | solution.py:422
  45.4 14.8 %all_to_all.36.parts_ref = f32[16,32,128]{2,1,0:T(8,128)S(1)} all-to-all(f32[16,32,128]{2,1,0:T(8,128)S(1)} %get-tuple-element.32), channel_id=1, replica_groups=mesh['row_0'=4,'row_1'=4,'col_0'=4,'col_1'=2] {'row_0','row_1'}, dimensions={0} | all-to-all | bytes 524288 | tf_op jit(solution)/shard_map/all_to_all | solution.py:404
  60.2 3.8 %shard_map.72 = (f32[32,1024,128]{2,1,0:T(8,128)S(1)}, f32[8,8,128]{2,1,0:T(8,128)S(1)}, f32[32,128]{1,0:T(8,128)S(1)}) custom-call(f32[32,1024,128]{2,1,0:T(8,128)S(1)} %get-tuple-element.30.t_ref, f32[16,32,128]{2,1,0:T(8,128)S(1)} %all_to_all.36.parts_ref, f32[32,128]{1,0:T(8,128)S(1)} %bitcast.12, ...), custom_call_target="tpu_custom_call", output_to_operand_aliasing={{0}: (0, {})} | custom-call | tf_op jit(solution)/shard_map/pallas_call | solution.py:425
  64.0 9.2 %all_to_all.37.parts_ref = f32[8,8,128]{2,1,0:T(8,128)S(1)} all-to-all(f32[8,8,128]{2,1,0:T(8,128)S(1)} %get-tuple-element.35), channel_id=1, replica_groups=mesh['row_0'=4,'row_1'=4,'col_0'=4,'col_1'=2] {'col_0','col_1'}, dimensions={0} | all-to-all | bytes 65536 | tf_op jit(solution)/shard_map/all_to_all | solution.py:401
  73.3 1.7 %shard_map.73 = f32[16,32,128]{2,1,0:T(8,128)S(1)} custom-call(f32[32,1024,128]{2,1,0:T(8,128)S(1)} %get-tuple-element.34.plan_ref, f32[8,8,128]{2,1,0:T(8,128)S(1)} %all_to_all.37.parts_ref, f32[8,128]{1,0:T(8,128)S(1)} %bitcast.17), custom_call_target="tpu_custom_call" | custom-call | tf_op jit(solution)/shard_map/pallas_call | solution.py:429
  74.9 10.2 %all_to_all.38.parts_ref = f32[16,32,128]{2,1,0:T(8,128)S(1)} all-to-all(f32[16,32,128]{2,1,0:T(8,128)S(1)} %shard_map.73), channel_id=1, replica_groups=mesh['row_0'=4,'row_1'=4,'col_0'=4,'col_1'=2] {'row_0','row_1'}, dimensions={0} | all-to-all | bytes 524288 | tf_op jit(solution)/shard_map/all_to_all | solution.py:404
  85.1 2.1 %shard_map.74 = f32[8,8,128]{2,1,0:T(8,128)S(1)} custom-call(f32[32,1024,128]{2,1,0:T(8,128)S(1)} %get-tuple-element.34.plan_ref, f32[16,32,128]{2,1,0:T(8,128)S(1)} %all_to_all.38.parts_ref, f32[32,128]{1,0:T(8,128)S(1)} %bitcast.13), custom_call_target="tpu_custom_call" | custom-call | tf_op jit(solution)/shard_map/pallas_call | solution.py:432
  87.2 9.2 %all_to_all.39.parts_ref = f32[8,8,128]{2,1,0:T(8,128)S(1)} all-to-all(f32[8,8,128]{2,1,0:T(8,128)S(1)} %shard_map.74), channel_id=1, replica_groups=mesh['row_0'=4,'row_1'=4,'col_0'=4,'col_1'=2] {'col_0','col_1'}, dimensions={0} | all-to-all | bytes 65536 | tf_op jit(solution)/shard_map/all_to_all | solution.py:401
  96.4 2.3 %shard_map.75 = (f32[16,40,128]{2,1,0:T(8,128)S(1)}, f32[8,128]{1,0:T(8,128)}) custom-call(f32[32,1024,128]{2,1,0:T(8,128)S(1)} %get-tuple-element.34.plan_ref, f32[8,8,128]{2,1,0:T(8,128)S(1)} %all_to_all.39.parts_ref, f32[8,128]{1,0:T(8,128)S(1)} %bitcast.18, f32[8,128]{1,0:T(8,128)S(1)} %get-tuple-element.33.src_lse_ref.lse_ref, ...), custom_call_target="tpu_custom_call" | custom-call | tf_op jit(solution)/shard_map/pallas_call | solution.py:433
  98.7 11.0 %all_to_all.40.parts_ref = f32[16,40,128]{2,1,0:T(8,128)S(1)} all-to-all(f32[16,40,128]{2,1,0:T(8,128)S(1)} %get-tuple-element.38), channel_id=1, replica_groups=mesh['row_0'=4,'row_1'=4,'col_0'=4,'col_1'=2] {'row_0','row_1'}, dimensions={0} | all-to-all | bytes 655360 | tf_op jit(solution)/shard_map/all_to_all | solution.py:404
  110.3 9.0 %all_to_all.41 = f32[8,8,128]{2,1,0:T(8,128)S(1)} all-to-all(f32[8,8,128]{2,1,0:T(8,128)S(1)} %get-tuple-element.42), channel_id=1, replica_groups=mesh['row_0'=4,'row_1'=4,'col_0'=4,'col_1'=2] {'col_0','col_1'}, dimensions={0} | all-to-all | bytes 65536 | tf_op jit(solution)/shard_map/all_to_all | solution.py:401
  (21 shorter events, 4.0 us)
Async XLA Ops:
  0.6 6.8 %collective-permute-start = (bf16[256,256]{1,0:T(8,128)(2,1)}, bf16[256,256]{1,0:T(8,128)(2,1)S(1)}, u32[]{:S(2)}, u32[]{:S(2)}) collective-permute-start(bf16[256,256]{1,0:T(8,128)(2,1)} %param.5), channel_id=1, source_target_pairs={{0,8},{1,33},{2,10},{3,35},{4,12},{5,37},{6,14},{7,39},{8,16},{9,4... | collective-permute-start | bytes 393224 | tf_op jit(solution)/shard_map/ppermute | solution.py:378
  2.8 6.9 %collective-permute-start.1 = (bf16[256,256]{1,0:T(8,128)(2,1)}, bf16[256,256]{1,0:T(8,128)(2,1)S(1)}, u32[]{:S(2)}, u32[]{:S(2)}) collective-permute-start(bf16[256,256]{1,0:T(8,128)(2,1)} %param.5), channel_id=1, source_target_pairs={{0,16},{1,65},{2,18},{3,67},{4,20},{5,69},{6,22},{7,71},{8,24},{9,... | collective-permute-start | bytes 393224 | tf_op jit(solution)/shard_map/ppermute | solution.py:378
  5.4 4.3 %collective-permute-start.2 = (bf16[256,256]{1,0:T(8,128)(2,1)}, bf16[256,256]{1,0:T(8,128)(2,1)S(1)}, u32[]{:S(2)}, u32[]{:S(2)}) collective-permute-start(bf16[256,256]{1,0:T(8,128)(2,1)} %param.5), channel_id=1, source_target_pairs={{0,24},{1,97},{2,26},{3,99},{4,28},{5,101},{6,30},{7,103},{8,0},{9... | collective-permute-start | bytes 393224 | tf_op jit(solution)/shard_map/ppermute | solution.py:378
  9.8 9.7 %collective-permute-start.3 = (bf16[1024,256]{1,0:T(8,128)(2,1)S(1)}, bf16[1024,256]{1,0:T(8,128)(2,1)S(1)}, u32[]{:S(2)}, u32[]{:S(2)}) collective-permute-start(bf16[1024,256]{1,0:T(8,128)(2,1)S(1)} %constant_dynamic-update-slice_fusion.points_ref), channel_id=1, source_target_pairs={{0,32},{1,9},{2,34},{3,11},{4,36},{5,13},{6,38},{7,15},{8,40},{9,1... | collective-permute-start | bytes 1572872 | tf_op jit(solution)/shard_map/ppermute | solution.py:378
  11.1 10.1 %collective-permute-start.4 = (bf16[1024,256]{1,0:T(8,128)(2,1)S(1)}, bf16[1024,256]{1,0:T(8,128)(2,1)S(1)}, u32[]{:S(2)}, u32[]{:S(2)}) collective-permute-start(bf16[1024,256]{1,0:T(8,128)(2,1)S(1)} %constant_dynamic-update-slice_fusion.points_ref), channel_id=1, source_target_pairs={{0,96},{1,25},{2,98},{3,27},{4,100},{5,29},{6,102},{7,31},{8,104},... | collective-permute-start | bytes 1572872 | tf_op jit(solution)/shard_map/ppermute | solution.py:378
  12.5 13.5 %collective-permute-start.5 = (bf16[1024,256]{1,0:T(8,128)(2,1)S(1)}, bf16[1024,256]{1,0:T(8,128)(2,1)S(1)}, u32[]{:S(2)}, u32[]{:S(2)}) collective-permute-start(bf16[1024,256]{1,0:T(8,128)(2,1)S(1)} %constant_dynamic-update-slice_fusion.points_ref), channel_id=1, source_target_pairs={{0,64},{1,17},{2,66},{3,19},{4,68},{5,21},{6,70},{7,23},{8,72},{9,... | collective-permute-start | bytes 1572872 | tf_op jit(solution)/shard_map/ppermute | solution.py:378
  14.1 1.0 copy-start
  15.2 0.7 copy-start.1
  19.4 6.6 %copy-start.2 = (f32[4096]{0:T(1024)S(1)}, f32[4096]{0:T(1024)}, u32[]{:S(2)}) copy-start(f32[4096]{0:T(1024)} %param.7) | copy-start | bytes 49156
  21.2 19.5 %copy-start.3 = (f32[1024]{0:T(1024)S(1)}, f32[1024]{0:T(1024)}, u32[]{:S(2)}) copy-start(f32[1024]{0:T(1024)} %param.6) | copy-start | bytes 12292

commit v5 on v4

--- a/solution.py
+++ b/solution.py
@@ -89,6 +89,10 @@
 
 def combined(parts_ref, combine):
     return combine([parts_ref[peer] for peer in range(parts_ref.shape[0])])
+
+
+def values(refs):
+    return [ref[...] for ref in refs]
 
 
 def at_rows(r):
@@ -188,7 +192,7 @@
     tiles, rows, _ = t_ref.shape
     piece_steps(k, place, x_ref, points_ref, mass_ref, old_top_ref, old_sum_ref, t_ref, sum_ref)
     total = collapse(sum_ref)
-    copies(out_ref, collapse_top(old_top_ref) * LN2 + jnp.log(total))
+    out_ref[...] = collapse_top(old_top_ref) * LN2 + jnp.log(total)
 
     @pl.when(jnp.logical_not(jnp.max(total) < HUGE))
     def exact():
@@ -206,12 +210,13 @@
             return unused
 
         lax.fori_loop(0, rows // STEP, rows_step, 0)
-        copies(out_ref, collapse_top(top_ref) * LN2 + jnp.log(collapse(sum_ref)))
-
-
-def column_kernel(t_ref, parts_ref, mass_ref, out_ref, lse_ref, wide_ref, line_ref):
+        out_ref[...] = collapse_top(top_ref) * LN2 + jnp.log(collapse(sum_ref))
+
+
+def column_kernel(t_ref, *refs):
+    parts, (mass_ref, out_ref, lse_ref, wide_ref, line_ref) = refs[:4], refs[4:]
     tiles, rows, _ = t_ref.shape
-    lse = combined(parts_ref, lse_all)
+    lse = lse_all(values(parts))
     lse_ref[...] = lse
     spread((mass_ref[...] - lse) * LOG2E, wide_ref)
     per = 4
@@ -289,7 +294,7 @@
         return unused
 
     lax.fori_loop(0, rows // STEP, rows_step, 0)
-    copies(out_ref, collapse(sum_ref))
+    out_ref[...] = collapse(sum_ref)
 
 
 def row_sums_kernel(plan_ref, parts_ref, mass_ref, out_ref, sum_ref, line_ref):
@@ -305,7 +310,7 @@
         return unused
 
     lax.fori_loop(0, rows // STEP, rows_step, 0)
-    copies(out_ref, collapse(sum_ref))
+    out_ref[...] = collapse(sum_ref)
 
 
 def column_sums(plan_ref, scale, line_ref, wide_ref):
@@ -331,15 +336,17 @@
             line_ref[c + t : c + t + 1, :] = jnp.sum(totals[t], axis=0, keepdims=True)
 
 
-def column_sums_kernel(plan_ref, parts_ref, mass_ref, out_ref, wide_ref, line_ref):
-    scale = jnp.exp(mass_ref[...]) / combined(parts_ref, add_all)
+def column_sums_kernel(plan_ref, *refs):
+    parts, (mass_ref, out_ref, wide_ref, line_ref) = refs[:4], refs[4:]
+    scale = jnp.exp(mass_ref[...]) / add_all(values(parts))
     column_sums(plan_ref, scale, line_ref, wide_ref)
     copies(out_ref, line_ref[...])
 
 
-def last_column_sums_kernel(plan_ref, parts_ref, mass_ref, lse_ref, squares_ref, *refs):
-    out_ref, potential_ref, wide_ref, line_ref = refs
-    sums = combined(parts_ref, add_all)
+def last_column_sums_kernel(plan_ref, *refs):
+    parts, (mass_ref, lse_ref, squares_ref) = refs[:4], refs[4:7]
+    out_ref, potential_ref, wide_ref, line_ref = refs[7:]
+    sums = add_all(values(parts))
     mass = mass_ref[...]
     column_sums(plan_ref, jnp.exp(mass) / sums, line_ref, wide_ref)
     squares = squares_ref[...] / (WIDTH * EPS)
@@ -355,7 +362,7 @@
     sums = combined(parts_ref, add_all)
     potential = -EPS * (lse_ref[...] + jnp.log(sums[:tiles]) - 2.0 * mass_ref[...])
     potential_ref[...] = potential
-    copies(own_ref, jnp.broadcast_to(jnp.sum(potential), (8, LANES)))
+    own_ref[...] = jnp.broadcast_to(jnp.sum(potential), (8, LANES))
     other_ref[...] = sums[tiles:]
 
 
@@ -377,6 +384,13 @@
             pairs.append((number(y, x, z, core), to))
         found[k] = lax.ppermute(value, ALL, pairs)
     return [found[k] for k in range(4)]
+
+
+def crossed(value, k):
+    pairs = []
+    for y, x, z, core in itertools.product(*map(range, SIZES)):
+        pairs.append((number(y, x, z, core), number(y, x, (z + k) % 4, 1 - core)))
+    return lax.ppermute(value, ALL, pairs)
 
 
 def body(src_points, tgt_points, log_src_mass, log_tgt_mass):
@@ -392,13 +406,14 @@
     longer = pltpu.VMEM((column_tiles + 8, LANES), jnp.float32)
     by_row, by_column = f32(row_tiles, LANES), f32(column_tiles, LANES)
     peers_row, peers_col = lax.axis_size(ROW), lax.axis_size(COL)
-    rows_out, columns_out = f32(peers_col, row_tiles, LANES), f32(peers_row, column_tiles, LANES)
+    columns_out = f32(peers_row, column_tiles, LANES)
 
     def resident(value):
         return pltpu.with_memory_space_constraint(value, pltpu.VMEM)
 
-    def over_col(value):
-        return lax.all_to_all(value, COL, 0, 0, tiled=True)
+    def over_col(value, combine):
+        both = combine([value, lax.ppermute(value, "col_1", [(0, 1), (1, 0)])])
+        return [both] + [crossed(both, k) for k in (2, 1, 3)]
 
     def over_row(value):
         return lax.all_to_all(value, ROW, 0, 0, tiled=True)
@@ -414,32 +429,32 @@
         )(place, src_points, resident(terms), resident(sums), resident(top), pieces[k], tgt_mass)
     terms, sums, lse = call(
         functools.partial(last_terms_kernel, 2),
-        (big, wide, rows_out),
+        (big, wide, by_row),
         [SMEM] + [VMEM] * 6,
         [wide],
         {2: 0, 3: 1},
     )(place, src_points, resident(terms), resident(sums), resident(top), pieces[2], tgt_mass)
-    lse, src_lse = call(column_kernel, (columns_out, by_row), [VMEM] * 3, [wide, line])(
-        resident(terms), over_col(lse), src_mass
+    lse, src_lse = call(column_kernel, (columns_out, by_row), [VMEM] * 6, [wide, line])(
+        resident(terms), *over_col(lse, lse_all), src_mass
     )
     plan, sums, tgt_lse = call(
-        plan_kernel, (big, rows_out, by_column), [VMEM] * 5, [wide, wide, line], {0: 0}
+        plan_kernel, (big, by_row, by_column), [VMEM] * 5, [wide, wide, line], {0: 0}
     )(resident(terms), over_row(lse), tgt_mass, src_lse, src_mass)
     plan = resident(plan)
-    sums = call(column_sums_kernel, columns_out, [VMEM] * 3, [wide, line])(
-        plan, over_col(sums), src_mass
+    sums = call(column_sums_kernel, columns_out, [VMEM] * 6, [wide, line])(
+        plan, *over_col(sums, add_all), src_mass
     )
-    sums = call(row_sums_kernel, rows_out, [VMEM] * 3, [wide, line])(plan, over_row(sums), tgt_mass)
+    sums = call(row_sums_kernel, by_row, [VMEM] * 3, [wide, line])(plan, over_row(sums), tgt_mass)
     sums, src_potential = call(
         last_column_sums_kernel,
         (f32(peers_row, column_tiles + 8, LANES), by_row),
-        [VMEM] * 5,
+        [VMEM] * 8,
         [wide, longer],
-    )(plan, over_col(sums), src_mass, src_lse, squares)
+    )(plan, *over_col(sums, add_all), src_mass, src_lse, squares)
     tgt_potential, tgt_sum, src_sum = call(
-        last_kernel, (by_column, f32(peers_col, 8, LANES), f32(8, LANES)), [VMEM] * 3, []
+        last_kernel, (by_column, f32(8, LANES), f32(8, LANES)), [VMEM] * 3, []
     )(over_row(sums), tgt_mass, tgt_lse)
-    tgt_sum = jnp.sum(over_col(tgt_sum), axis=0)
+    tgt_sum = add_all(over_col(tgt_sum, add_all))
     sources_all, targets_all = rows * peers_row, columns * peers_col
     mean_potentials = (src_sum / sources_all + tgt_sum / targets_all)[0, 0]
     return (src_potential.reshape(-1), tgt_potential.reshape(-1), mean_potentials)

time: 120 us -> 119 us (level)
  blocking collectives: 76.2 us -> 38.1 us
  starting transfers between devices: 10.2 us -> 36.8 us
  waiting for transfers between devices: 5.34 us -> 15.7 us
    all_to_all x4 -> x0, blocking collectives: 40.3 us -> none  [over_col(): return lax.all_to_all(value, COL, 0, 0, tiled=True)]
    ppermute x0 -> x16, starting transfers between devices: none -> 26.7 us  [the longest x12 19.3 us: crossed(): return lax.ppermute(value, ALL, pairs)]
    ppermute x0 -> x16, waiting for transfers between devices: none -> 10.4 us  [the longest x12 7.07 us: crossed(): return lax.ppermute(value, ALL, pairs)]
    all_to_all x3, blocking collectives: 36 us -> 38.1 us  [over_row(): return lax.all_to_all(value, ROW, 0, 0, tiled=True)]
    unnamed x11 -> x9, local copies, waits for them, and re-layouts: 2.74 us -> 2.73 us
  transfers between devices with their start and end apart: 6 -> 22, of which waited for: 2 -> 16; matrix products, arithmetic and copies ran while one was open for 1% -> 1% of each run, Pallas kernels for 6% -> 6%
where the time goes in v5:
time: 119 us
  blocking collectives  38.1 us (32%)
  starting transfers between devices  36.8 us (31%)
  Pallas kernels  24 us (20%)
  waiting for transfers between devices  15.7 us (13%)
  local copies, waits for them, and re-layouts  3.26 us (3%)
    all_to_all x3, blocking collectives, over_row(): return lax.all_to_all(value, ROW, 0, 0, tiled=True)  38.1 us
    ppermute x12, starting transfers between devices, crossed(): return lax.ppermute(value, ALL, pairs)  19.3 us
    ppermute x6, starting transfers between devices, turned(): found[k] = lax.ppermute(value, ALL, pairs)  10.2 us
    ppermute x4, starting transfers between devices, over_col(): both = combine([value, lax.ppermute(value, 'col_1', [(0, 1), (1, 0)])])  7.33 us
    ppermute x12, waiting for transfers between devices, crossed(): return lax.ppermute(value, ALL, pairs)  7.07 us
    ppermute x6, waiting for transfers between devices, turned(): found[k] = lax.ppermute(value, ALL, pairs)  5.34 us
    pallas_call x1, Pallas kernels, body(): call(column_kernel, (columns_out, by_row), [VMEM] * 6, [wide, line])  4.73 us
    pallas_call x1, Pallas kernels, body(): call(plan_kernel, (big, by_row, by_column), [VMEM] * 5, [wide, wide, line...  3.77 us
  transfers between devices with their start and end apart: 22, of which 16 were waited for; matrix products, arithmetic and copies ran while one was open for 1% of the time, Pallas kernels for 6%

profile of v5, /device:TPU:1, one launch (start us, length us, event | category | flops | bytes accessed | tf_op | source)
XLA Modules:
  0.0 118.7 jit_solution(6977152464425635133)
XLA Ops:
  0.6 2.2 %collective-permute-start = (bf16[256,256]{1,0:T(8,128)(2,1)}, bf16[256,256]{1,0:T(8,128)(2,1)S(1)}, u32[]{:S(2)}, u32[]{:S(2)}) collective-permute-start(bf16[256,256]{1,0:T(8,128)(2,1)} %param.5), channel_id=1, source_target_pairs={{0,8},{1,33},{2,10},{3,35},{4,12},{5,37},{6,14},{7,39},{8,16},{9,4... | collective-permute-start | bytes 393224 | tf_op jit(solution)/shard_map/ppermute | solution.py:385
  2.8 2.6 %collective-permute-start.1 = (bf16[256,256]{1,0:T(8,128)(2,1)}, bf16[256,256]{1,0:T(8,128)(2,1)S(1)}, u32[]{:S(2)}, u32[]{:S(2)}) collective-permute-start(bf16[256,256]{1,0:T(8,128)(2,1)} %param.5), channel_id=1, source_target_pairs={{0,16},{1,65},{2,18},{3,67},{4,20},{5,69},{6,22},{7,71},{8,24},{9,... | collective-permute-start | bytes 393224 | tf_op jit(solution)/shard_map/ppermute | solution.py:385
  7.5 2.2 %collective-permute-done.1 = bf16[256,256]{1,0:T(8,128)(2,1)S(1)} collective-permute-done((bf16[256,256]{1,0:T(8,128)(2,1)}, bf16[256,256]{1,0:T(8,128)(2,1)S(1)}, u32[]{:S(2)}, u32[]{:S(2)}) %collective-permute-start.1) | collective-permute-done | bytes 131104 | tf_op jit(solution)/shard_map/ppermute | solution.py:385
  12.5 1.5 %collective-permute-start.5 = (bf16[1024,256]{1,0:T(8,128)(2,1)S(1)}, bf16[1024,256]{1,0:T(8,128)(2,1)S(1)}, u32[]{:S(2)}, u32[]{:S(2)}) collective-permute-start(bf16[1024,256]{1,0:T(8,128)(2,1)S(1)} %constant_dynamic-update-slice_fusion.points_ref), channel_id=1, source_target_pairs={{0,64},{1,17},{2,66},{3,19},{4,68},{5,21},{6,70},{7,23},{8,72},{9,... | collective-permute-start | bytes 1572872 | tf_op jit(solution)/shard_map/ppermute | solution.py:385
  15.9 3.5 %shard_map.67 = (f32[32,1024,128]{2,1,0:T(8,128)S(1)}, f32[1024,128]{1,0:T(8,128)S(1)}, f32[1024,128]{1,0:T(8,128)S(1)}, f32[8,128]{1,0:T(8,128)S(1)}) custom-call(s32[3]{0:T(128)S(1)} %pad_add_fusion.place, bf16[1024,256]{1,0:T(8,128)(2,1)S(1)} %copy-done, bf16[1024,256]{1,0:T(8,128)(2,1)S(1)} %constant_dynamic-update-slice_fusion.points_ref, ...), custom_call_target="tpu_custom_call" | custom-call | tf_op jit(solution)/shard_map/pallas_call | solution.py:423
  19.4 1.7 %shard_map.68 = (f32[32,1024,128]{2,1,0:T(8,128)S(1)}, f32[1024,128]{1,0:T(8,128)S(1)}) custom-call(s32[3]{0:T(128)S(1)} %pad_add_fusion.place, bf16[1024,256]{1,0:T(8,128)(2,1)S(1)} %copy-done, f32[32,1024,128]{2,1,0:T(8,128)S(1)} %get-tuple-element.23.old_ref, ...), custom_call_target="tpu_custom_call", output_to_operand_aliasing={{0}: (2, {}), {1}: (3, {})} | custom-call | tf_op jit(solution)/shard_map/pallas_call | solution.py:427
  21.2 1.7 %shard_map.69 = (f32[32,1024,128]{2,1,0:T(8,128)S(1)}, f32[1024,128]{1,0:T(8,128)S(1)}) custom-call(s32[3]{0:T(128)S(1)} %pad_add_fusion.place, bf16[1024,256]{1,0:T(8,128)(2,1)S(1)} %copy-done, f32[32,1024,128]{2,1,0:T(8,128)S(1)} %get-tuple-element.26.old_ref, ...), custom_call_target="tpu_custom_call", output_to_operand_aliasing={{0}: (2, {}), {1}: (3, {})} | custom-call | tf_op jit(solution)/shard_map/pallas_call | solution.py:427
  22.9 3.1 %collective-permute-done.5.points_ref = bf16[1024,256]{1,0:T(8,128)(2,1)S(1)} collective-permute-done((bf16[1024,256]{1,0:T(8,128)(2,1)S(1)}, bf16[1024,256]{1,0:T(8,128)(2,1)S(1)}, u32[]{:S(2)}, u32[]{:S(2)}) %collective-permute-start.5) | collective-permute-done | bytes 524320 | tf_op jit(solution)/shard_map/ppermute | solution.py:385
  26.0 1.9 %shard_map.70 = (f32[32,1024,128]{2,1,0:T(8,128)S(1)}, f32[1024,128]{1,0:T(8,128)S(1)}, f32[8,128]{1,0:T(8,128)S(1)}) custom-call(s32[3]{0:T(128)S(1)} %pad_add_fusion.place, bf16[1024,256]{1,0:T(8,128)(2,1)S(1)} %copy-done, f32[32,1024,128]{2,1,0:T(8,128)S(1)} %get-tuple-element.28.old_ref, ...), custom_call_target="tpu_custom_call", output_to_operand_aliasing={{0}: (2, {}), {1}: (3, {})} | custom-call | tf_op jit(solution)/shard_map/pallas_call | solution.py:430
  27.9 3.0 %collective-permute-start.6 = (f32[8,128]{1,0:T(8,128)S(1)}, f32[8,128]{1,0:T(8,128)S(1)}, u32[]{:S(2)}, u32[]{:S(2)}) collective-permute-start(f32[8,128]{1,0:T(8,128)S(1)} %get-tuple-element.31), channel_id=1, source_target_pairs={{0,1},{1,0},{2,3},{3,2},{4,5},{5,4},{6,7},{7,6},{8,9},{9,8},{10,11... | collective-permute-start | bytes 12296 | tf_op jit(solution)/shard_map/ppermute | solution.py:415
  31.8 3.9 %collective-permute-start.7 = (f32[8,128]{1,0:T(8,128)S(1)}, f32[8,128]{1,0:T(8,128)S(1)}, u32[]{:S(2)}, u32[]{:S(2)}) collective-permute-start(f32[8,128]{1,0:T(8,128)S(1)} %log_add_fusion.refs_0_), channel_id=1, source_target_pairs={{0,5},{1,4},{2,7},{3,6},{4,1},{5,0},{6,3},{7,2},{8,13},{9,12},{10,... | collective-permute-start | bytes 12296 | tf_op jit(solution)/shard_map/ppermute | solution.py:393
  36.5 2.2 %collective-permute-start.9 = (f32[8,128]{1,0:T(8,128)S(1)}, f32[8,128]{1,0:T(8,128)S(1)}, u32[]{:S(2)}, u32[]{:S(2)}) collective-permute-start(f32[8,128]{1,0:T(8,128)S(1)} %log_add_fusion.refs_0_), channel_id=1, source_target_pairs={{0,7},{1,6},{2,1},{3,0},{4,3},{5,2},{6,5},{7,4},{8,15},{9,14},{10,... | collective-permute-start | bytes 12296 | tf_op jit(solution)/shard_map/ppermute | solution.py:393
  39.9 4.7 %shard_map.71 = (f32[16,32,128]{2,1,0:T(8,128)S(1)}, f32[8,128]{1,0:T(8,128)S(1)}) custom-call(f32[32,1024,128]{2,1,0:T(8,128)S(1)} %get-tuple-element.30.t_ref, f32[8,128]{1,0:T(8,128)S(1)} %log_add_fusion.refs_0_, f32[8,128]{1,0:T(8,128)S(1)} %collective-permute-done.7.refs_1_, f32[8,128]{1,0:T(8,128)S(1)} %collective-permute-done.8.refs_2_, ...), custom_call_target="tpu_custom_call" | custom-call | tf_op jit(solution)/shard_map/pallas_call | solution.py:437
  44.7 15.5 %all_to_all.15.parts_ref = f32[16,32,128]{2,1,0:T(8,128)S(1)} all-to-all(f32[16,32,128]{2,1,0:T(8,128)S(1)} %get-tuple-element.32), channel_id=1, replica_groups=mesh['row_0'=4,'row_1'=4,'col_0'=4,'col_1'=2] {'row_0','row_1'}, dimensions={0} | all-to-all | bytes 524288 | tf_op jit(solution)/shard_map/all_to_all | solution.py:419
  60.2 3.8 %shard_map.72 = (f32[32,1024,128]{2,1,0:T(8,128)S(1)}, f32[8,128]{1,0:T(8,128)S(1)}, f32[32,128]{1,0:T(8,128)S(1)}) custom-call(f32[32,1024,128]{2,1,0:T(8,128)S(1)} %get-tuple-element.30.t_ref, f32[16,32,128]{2,1,0:T(8,128)S(1)} %all_to_all.15.parts_ref, f32[32,128]{1,0:T(8,128)S(1)} %bitcast.12, ...), custom_call_target="tpu_custom_call", output_to_operand_aliasing={{0}: (0, {})} | custom-call | tf_op jit(solution)/shard_map/pallas_call | solution.py:440
  67.6 2.2 %collective-permute-start.12 = (f32[8,128]{1,0:T(8,128)S(1)}, f32[8,128]{1,0:T(8,128)S(1)}, u32[]{:S(2)}, u32[]{:S(2)}) collective-permute-start(f32[8,128]{1,0:T(8,128)S(1)} %add.29.refs_0_), channel_id=1, source_target_pairs={{0,3},{1,2},{2,5},{3,4},{4,7},{5,6},{6,1},{7,0},{8,11},{9,10},{10,... | collective-permute-start | bytes 12296 | tf_op jit(solution)/shard_map/ppermute | solution.py:393
  72.8 1.7 %shard_map.73 = f32[16,32,128]{2,1,0:T(8,128)S(1)} custom-call(f32[32,1024,128]{2,1,0:T(8,128)S(1)} %get-tuple-element.34.plan_ref, f32[8,128]{1,0:T(8,128)S(1)} %add.29.refs_0_, f32[8,128]{1,0:T(8,128)S(1)} %collective-permute-done.11.refs_1_, f32[8,128]{1,0:T(8,128)S(1)} %collective-permute-done.12.refs_2_, f32[8,128]{1,0:T(8,128)S(1)} %collective-permute-done.13.refs_3_, ...), custom_call_target="tpu_custom_call" | custom-call | tf_op jit(solution)/shard_map/pallas_call | solution.py:444
  74.5 11.1 %all_to_all.16.parts_ref = f32[16,32,128]{2,1,0:T(8,128)S(1)} all-to-all(f32[16,32,128]{2,1,0:T(8,128)S(1)} %shard_map.73), channel_id=1, replica_groups=mesh['row_0'=4,'row_1'=4,'col_0'=4,'col_1'=2] {'row_0','row_1'}, dimensions={0} | all-to-all | bytes 524288 | tf_op jit(solution)/shard_map/all_to_all | solution.py:419
  85.6 2.1 %shard_map.74 = f32[8,128]{1,0:T(8,128)S(1)} custom-call(f32[32,1024,128]{2,1,0:T(8,128)S(1)} %get-tuple-element.34.plan_ref, f32[16,32,128]{2,1,0:T(8,128)S(1)} %all_to_all.16.parts_ref, f32[32,128]{1,0:T(8,128)S(1)} %bitcast.13), custom_call_target="tpu_custom_call" | custom-call | tf_op jit(solution)/shard_map/pallas_call | solution.py:447
  90.7 1.8 %collective-permute-start.16 = (f32[8,128]{1,0:T(8,128)S(1)}, f32[8,128]{1,0:T(8,128)S(1)}, u32[]{:S(2)}, u32[]{:S(2)}) collective-permute-start(f32[8,128]{1,0:T(8,128)S(1)} %add.30.refs_0_), channel_id=1, source_target_pairs={{0,3},{1,2},{2,5},{3,4},{4,7},{5,6},{6,1},{7,0},{8,11},{9,10},{10,... | collective-permute-start | bytes 12296 | tf_op jit(solution)/shard_map/ppermute | solution.py:393
  95.5 2.3 %shard_map.75 = (f32[16,40,128]{2,1,0:T(8,128)S(1)}, f32[8,128]{1,0:T(8,128)}) custom-call(f32[32,1024,128]{2,1,0:T(8,128)S(1)} %get-tuple-element.34.plan_ref, f32[8,128]{1,0:T(8,128)S(1)} %add.30.refs_0_, f32[8,128]{1,0:T(8,128)S(1)} %collective-permute-done.15.refs_1_, f32[8,128]{1,0:T(8,128)S(1)} %collective-permute-done.16.refs_2_, ...), custom_call_target="tpu_custom_call" | custom-call | tf_op jit(solution)/shard_map/pallas_call | solution.py:448
  97.8 11.5 %all_to_all.17.parts_ref = f32[16,40,128]{2,1,0:T(8,128)S(1)} all-to-all(f32[16,40,128]{2,1,0:T(8,128)S(1)} %get-tuple-element.38), channel_id=1, replica_groups=mesh['row_0'=4,'row_1'=4,'col_0'=4,'col_1'=2] {'row_0','row_1'}, dimensions={0} | all-to-all | bytes 655360 | tf_op jit(solution)/shard_map/all_to_all | solution.py:419
  109.9 1.5 %collective-permute-start.18 = (f32[8,128]{1,0:T(8,128)S(1)}, f32[8,128]{1,0:T(8,128)S(1)}, u32[]{:S(2)}, u32[]{:S(2)}) collective-permute-start(f32[8,128]{1,0:T(8,128)S(1)} %get-tuple-element.42), channel_id=1, source_target_pairs={{0,1},{1,0},{2,3},{3,2},{4,5},{5,4},{6,7},{7,6},{8,9},{9,8},{10,11... | collective-permute-start | bytes 12296 | tf_op jit(solution)/shard_map/ppermute | solution.py:415
  113.6 1.5 %collective-permute-start.20 = (f32[8,128]{1,0:T(8,128)S(1)}, f32[8,128]{1,0:T(8,128)S(1)}, u32[]{:S(2)}, u32[]{:S(2)}) collective-permute-start(f32[8,128]{1,0:T(8,128)S(1)} %add.31), channel_id=1, source_target_pairs={{0,3},{1,2},{2,5},{3,4},{4,7},{5,6},{6,1},{7,0},{8,11},{9,10},{10,... | collective-permute-start | bytes 12296 | tf_op jit(solution)/shard_map/ppermute | solution.py:393
  (50 shorter events, 28.7 us)
Async XLA Ops:
  0.6 6.8 %collective-permute-start = (bf16[256,256]{1,0:T(8,128)(2,1)}, bf16[256,256]{1,0:T(8,128)(2,1)S(1)}, u32[]{:S(2)}, u32[]{:S(2)}) collective-permute-start(bf16[256,256]{1,0:T(8,128)(2,1)} %param.5), channel_id=1, source_target_pairs={{0,8},{1,33},{2,10},{3,35},{4,12},{5,37},{6,14},{7,39},{8,16},{9,4... | collective-permute-start | bytes 393224 | tf_op jit(solution)/shard_map/ppermute | solution.py:385
  2.8 6.9 %collective-permute-start.1 = (bf16[256,256]{1,0:T(8,128)(2,1)}, bf16[256,256]{1,0:T(8,128)(2,1)S(1)}, u32[]{:S(2)}, u32[]{:S(2)}) collective-permute-start(bf16[256,256]{1,0:T(8,128)(2,1)} %param.5), channel_id=1, source_target_pairs={{0,16},{1,65},{2,18},{3,67},{4,20},{5,69},{6,22},{7,71},{8,24},{9,... | collective-permute-start | bytes 393224 | tf_op jit(solution)/shard_map/ppermute | solution.py:385
  5.4 4.3 %collective-permute-start.2 = (bf16[256,256]{1,0:T(8,128)(2,1)}, bf16[256,256]{1,0:T(8,128)(2,1)S(1)}, u32[]{:S(2)}, u32[]{:S(2)}) collective-permute-start(bf16[256,256]{1,0:T(8,128)(2,1)} %param.5), channel_id=1, source_target_pairs={{0,24},{1,97},{2,26},{3,99},{4,28},{5,101},{6,30},{7,103},{8,0},{9... | collective-permute-start | bytes 393224 | tf_op jit(solution)/shard_map/ppermute | solution.py:385
  9.8 9.7 %collective-permute-start.3 = (bf16[1024,256]{1,0:T(8,128)(2,1)S(1)}, bf16[1024,256]{1,0:T(8,128)(2,1)S(1)}, u32[]{:S(2)}, u32[]{:S(2)}) collective-permute-start(bf16[1024,256]{1,0:T(8,128)(2,1)S(1)} %constant_dynamic-update-slice_fusion.points_ref), channel_id=1, source_target_pairs={{0,32},{1,9},{2,34},{3,11},{4,36},{5,13},{6,38},{7,15},{8,40},{9,1... | collective-permute-start | bytes 1572872 | tf_op jit(solution)/shard_map/ppermute | solution.py:385
  11.1 10.1 %collective-permute-start.4 = (bf16[1024,256]{1,0:T(8,128)(2,1)S(1)}, bf16[1024,256]{1,0:T(8,128)(2,1)S(1)}, u32[]{:S(2)}, u32[]{:S(2)}) collective-permute-start(bf16[1024,256]{1,0:T(8,128)(2,1)S(1)} %constant_dynamic-update-slice_fusion.points_ref), channel_id=1, source_target_pairs={{0,96},{1,25},{2,98},{3,27},{4,100},{5,29},{6,102},{7,31},{8,104},... | collective-permute-start | bytes 1572872 | tf_op jit(solution)/shard_map/ppermute | solution.py:385
  12.5 13.5 %collective-permute-start.5 = (bf16[1024,256]{1,0:T(8,128)(2,1)S(1)}, bf16[1024,256]{1,0:T(8,128)(2,1)S(1)}, u32[]{:S(2)}, u32[]{:S(2)}) collective-permute-start(bf16[1024,256]{1,0:T(8,128)(2,1)S(1)} %constant_dynamic-update-slice_fusion.points_ref), channel_id=1, source_target_pairs={{0,64},{1,17},{2,66},{3,19},{4,68},{5,21},{6,70},{7,23},{8,72},{9,... | collective-permute-start | bytes 1572872 | tf_op jit(solution)/shard_map/ppermute | solution.py:385
  14.1 1.0 copy-start
  21.2 18.7 %copy-start.2 = (f32[1024]{0:T(1024)S(1)}, f32[1024]{0:T(1024)}, u32[]{:S(2)}) copy-start(f32[1024]{0:T(1024)} %param.6) | copy-start | bytes 12292
  27.9 3.9 %collective-permute-start.6 = (f32[8,128]{1,0:T(8,128)S(1)}, f32[8,128]{1,0:T(8,128)S(1)}, u32[]{:S(2)}, u32[]{:S(2)}) collective-permute-start(f32[8,128]{1,0:T(8,128)S(1)} %get-tuple-element.31), channel_id=1, source_target_pairs={{0,1},{1,0},{2,3},{3,2},{4,5},{5,4},{6,7},{7,6},{8,9},{9,8},{10,11... | collective-permute-start | bytes 12296 | tf_op jit(solution)/shard_map/ppermute | solution.py:415
  31.8 6.9 %collective-permute-start.7 = (f32[8,128]{1,0:T(8,128)S(1)}, f32[8,128]{1,0:T(8,128)S(1)}, u32[]{:S(2)}, u32[]{:S(2)}) collective-permute-start(f32[8,128]{1,0:T(8,128)S(1)} %log_add_fusion.refs_0_), channel_id=1, source_target_pairs={{0,5},{1,4},{2,7},{3,6},{4,1},{5,0},{6,3},{7,2},{8,13},{9,12},{10,... | collective-permute-start | bytes 12296 | tf_op jit(solution)/shard_map/ppermute | solution.py:393
  35.7 4.2 %collective-permute-start.8 = (f32[8,128]{1,0:T(8,128)S(1)}, f32[8,128]{1,0:T(8,128)S(1)}, u32[]{:S(2)}, u32[]{:S(2)}) collective-permute-start(f32[8,128]{1,0:T(8,128)S(1)} %log_add_fusion.refs_0_), channel_id=1, source_target_pairs={{0,3},{1,2},{2,5},{3,4},{4,7},{5,6},{6,1},{7,0},{8,11},{9,10},{10,... | collective-permute-start | bytes 12296 | tf_op jit(solution)/shard_map/ppermute | solution.py:393
  36.5 3.5 %collective-permute-start.9 = (f32[8,128]{1,0:T(8,128)S(1)}, f32[8,128]{1,0:T(8,128)S(1)}, u32[]{:S(2)}, u32[]{:S(2)}) collective-permute-start(f32[8,128]{1,0:T(8,128)S(1)} %log_add_fusion.refs_0_), channel_id=1, source_target_pairs={{0,7},{1,6},{2,1},{3,0},{4,3},{5,2},{6,5},{7,4},{8,15},{9,14},{10,... | collective-permute-start | bytes 12296 | tf_op jit(solution)/shard_map/ppermute | solution.py:393
  64.0 2.2 %collective-permute-start.10 = (f32[8,128]{1,0:T(8,128)S(1)}, f32[8,128]{1,0:T(8,128)S(1)}, u32[]{:S(2)}, u32[]{:S(2)}) collective-permute-start(f32[8,128]{1,0:T(8,128)S(1)} %get-tuple-element.35), channel_id=1, source_target_pairs={{0,1},{1,0},{2,3},{3,2},{4,5},{5,4},{6,7},{7,6},{8,9},{9,8},{10,11... | collective-permute-start | bytes 12296 | tf_op jit(solution)/shard_map/ppermute | solution.py:415
  66.2 4.5 %collective-permute-start.11 = (f32[8,128]{1,0:T(8,128)S(1)}, f32[8,128]{1,0:T(8,128)S(1)}, u32[]{:S(2)}, u32[]{:S(2)}) collective-permute-start(f32[8,128]{1,0:T(8,128)S(1)} %add.29.refs_0_), channel_id=1, source_target_pairs={{0,5},{1,4},{2,7},{3,6},{4,1},{5,0},{6,3},{7,2},{8,13},{9,12},{10,... | collective-permute-start | bytes 12296 | tf_op jit(solution)/shard_map/ppermute | solution.py:393
  67.6 4.2 %collective-permute-start.12 = (f32[8,128]{1,0:T(8,128)S(1)}, f32[8,128]{1,0:T(8,128)S(1)}, u32[]{:S(2)}, u32[]{:S(2)}) collective-permute-start(f32[8,128]{1,0:T(8,128)S(1)} %add.29.refs_0_), channel_id=1, source_target_pairs={{0,3},{1,2},{2,5},{3,4},{4,7},{5,6},{6,1},{7,0},{8,11},{9,10},{10,... | collective-permute-start | bytes 12296 | tf_op jit(solution)/shard_map/ppermute | solution.py:393
  69.8 3.0 %collective-permute-start.13 = (f32[8,128]{1,0:T(8,128)S(1)}, f32[8,128]{1,0:T(8,128)S(1)}, u32[]{:S(2)}, u32[]{:S(2)}) collective-permute-start(f32[8,128]{1,0:T(8,128)S(1)} %add.29.refs_0_), channel_id=1, source_target_pairs={{0,7},{1,6},{2,1},{3,0},{4,3},{5,2},{6,5},{7,4},{8,15},{9,14},{10,... | collective-permute-start | bytes 12296 | tf_op jit(solution)/shard_map/ppermute | solution.py:393
  87.7 2.2 %collective-permute-start.14 = (f32[8,128]{1,0:T(8,128)S(1)}, f32[8,128]{1,0:T(8,128)S(1)}, u32[]{:S(2)}, u32[]{:S(2)}) collective-permute-start(f32[8,128]{1,0:T(8,128)S(1)} %shard_map.74), channel_id=1, source_target_pairs={{0,1},{1,0},{2,3},{3,2},{4,5},{5,4},{6,7},{7,6},{8,9},{9,8},{10,11... | collective-permute-start | bytes 12296 | tf_op jit(solution)/shard_map/ppermute | solution.py:415
  89.9 4.5 %collective-permute-start.15 = (f32[8,128]{1,0:T(8,128)S(1)}, f32[8,128]{1,0:T(8,128)S(1)}, u32[]{:S(2)}, u32[]{:S(2)}) collective-permute-start(f32[8,128]{1,0:T(8,128)S(1)} %add.30.refs_0_), channel_id=1, source_target_pairs={{0,5},{1,4},{2,7},{3,6},{4,1},{5,0},{6,3},{7,2},{8,13},{9,12},{10,... | collective-permute-start | bytes 12296 | tf_op jit(solution)/shard_map/ppermute | solution.py:393
  90.7 4.2 %collective-permute-start.16 = (f32[8,128]{1,0:T(8,128)S(1)}, f32[8,128]{1,0:T(8,128)S(1)}, u32[]{:S(2)}, u32[]{:S(2)}) collective-permute-start(f32[8,128]{1,0:T(8,128)S(1)} %add.30.refs_0_), channel_id=1, source_target_pairs={{0,3},{1,2},{2,5},{3,4},{4,7},{5,6},{6,1},{7,0},{8,11},{9,10},{10,... | collective-permute-start | bytes 12296 | tf_op jit(solution)/shard_map/ppermute | solution.py:393
  92.5 3.0 %collective-permute-start.17 = (f32[8,128]{1,0:T(8,128)S(1)}, f32[8,128]{1,0:T(8,128)S(1)}, u32[]{:S(2)}, u32[]{:S(2)}) collective-permute-start(f32[8,128]{1,0:T(8,128)S(1)} %add.30.refs_0_), channel_id=1, source_target_pairs={{0,7},{1,6},{2,1},{3,0},{4,3},{5,2},{6,5},{7,4},{8,15},{9,14},{10,... | collective-permute-start | bytes 12296 | tf_op jit(solution)/shard_map/ppermute | solution.py:393
  109.9 2.3 %collective-permute-start.18 = (f32[8,128]{1,0:T(8,128)S(1)}, f32[8,128]{1,0:T(8,128)S(1)}, u32[]{:S(2)}, u32[]{:S(2)}) collective-permute-start(f32[8,128]{1,0:T(8,128)S(1)} %get-tuple-element.42), channel_id=1, source_target_pairs={{0,1},{1,0},{2,3},{3,2},{4,5},{5,4},{6,7},{7,6},{8,9},{9,8},{10,11... | collective-permute-start | bytes 12296 | tf_op jit(solution)/shard_map/ppermute | solution.py:415
  112.2 4.5 %collective-permute-start.19 = (f32[8,128]{1,0:T(8,128)S(1)}, f32[8,128]{1,0:T(8,128)S(1)}, u32[]{:S(2)}, u32[]{:S(2)}) collective-permute-start(f32[8,128]{1,0:T(8,128)S(1)} %add.31), channel_id=1, source_target_pairs={{0,5},{1,4},{2,7},{3,6},{4,1},{5,0},{6,3},{7,2},{8,13},{9,12},{10,... | collective-permute-start | bytes 12296 | tf_op jit(solution)/shard_map/ppermute | solution.py:393
  113.6 4.2 %collective-permute-start.20 = (f32[8,128]{1,0:T(8,128)S(1)}, f32[8,128]{1,0:T(8,128)S(1)}, u32[]{:S(2)}, u32[]{:S(2)}) collective-permute-start(f32[8,128]{1,0:T(8,128)S(1)} %add.31), channel_id=1, source_target_pairs={{0,3},{1,2},{2,5},{3,4},{4,7},{5,6},{6,1},{7,0},{8,11},{9,10},{10,... | collective-permute-start | bytes 12296 | tf_op jit(solution)/shard_map/ppermute | solution.py:393
  115.2 3.0 %collective-permute-start.21 = (f32[8,128]{1,0:T(8,128)S(1)}, f32[8,128]{1,0:T(8,128)S(1)}, u32[]{:S(2)}, u32[]{:S(2)}) collective-permute-start(f32[8,128]{1,0:T(8,128)S(1)} %add.31), channel_id=1, source_target_pairs={{0,7},{1,6},{2,1},{3,0},{4,3},{5,2},{6,5},{7,4},{8,15},{9,14},{10,... | collective-permute-start | bytes 12296 | tf_op jit(solution)/shard_map/ppermute | solution.py:393
  (1 other events, 0.7 us)

commit v6 on v5

--- a/solution.py
+++ b/solution.py
@@ -130,67 +130,52 @@
     )
 
 
-def piece_blocks(k, place, points_ref, mass_ref):
-    blocks = [target_block(place, k, m) for m in range(4)]
-    biases = [
-        chunk_biases(points_ref[m * 256 : (m + 1) * 256, :], mass_ref, blocks[m]) for m in range(4)
-    ]
-    return blocks, biases
-
-
-def first_terms_kernel(place, x_ref, points_ref, mass_ref, t_ref, top_ref, sum_ref, squares_ref):
+def own_terms_kernel(place, x_ref, points_ref, mass_ref, t_ref, top_ref, sum_ref, squares_ref):
     rows = x_ref.shape[0]
     squares = x_ref[...].astype(jnp.float32) ** 2
     sum_ref[...] = squares[:, :LANES] + squares[:, LANES:]
     squares_ref[...] = collapse(sum_ref)
-    blocks, biases = piece_blocks(0, place, points_ref, mass_ref)
+    block = target_block(place, 0, 0)
+    biases = chunk_biases(points_ref[...], mass_ref, block)
     for r in range(0, rows, ROWS):
-        top = None
-        for m in range(4):
-            product = piece_product(x_ref, points_ref, r, m)
-            for side in range(2):
-                terms = product[:, lane_tile(side)] * BITS + biases[m][side]
-                t_ref[2 * blocks[m] + side, r : r + ROWS, :] = terms
-                top = terms if top is None else jnp.maximum(top, terms)
-        top_ref[r : r + ROWS, :] = top
-
-    def rows_step(r, unused):
-        at = at_rows(r)
-        top = jnp.max(top_ref[at, :], axis=1, keepdims=True)
-        total = jnp.zeros((STEP, LANES), jnp.float32)
-        for m in range(4):
-            for side in range(2):
-                total += jnp.exp2(t_ref[2 * blocks[m] + side, at, :] - top)
-        top_ref[at, :] = jnp.broadcast_to(top, (STEP, LANES))
-        sum_ref[at, :] = total
-        return unused
-
-    lax.fori_loop(0, rows // STEP, rows_step, 0)
-
-
-def piece_steps(k, place, x_ref, points_ref, mass_ref, top_ref, old_sum_ref, t_ref, sum_ref):
-    blocks, biases = piece_blocks(k, place, points_ref, mass_ref)
+        at = slice(r, r + ROWS)
+        product = piece_product(x_ref, points_ref, r, 0)
+        both = [product[:, lane_tile(side)] * BITS + biases[side] for side in range(2)]
+        for side in range(2):
+            t_ref[2 * block + side, at, :] = both[side]
+        top = jnp.max(jnp.maximum(both[0], both[1]), axis=1, keepdims=True)
+        top_ref[at, :] = jnp.broadcast_to(top, (ROWS, LANES))
+        sum_ref[at, :] = jnp.exp2(both[0] - top) + jnp.exp2(both[1] - top)
+
+
+def piece_steps(spots, place, x_ref, points_ref, mass_ref, top_ref, old_sum_ref, t_ref, sum_ref):
+    blocks = [target_block(place, k, m) for k, m in spots]
+    first = points_ref.shape[0] // 256 - len(spots)
+    biases = [
+        chunk_biases(points_ref[(first + i) * 256 : (first + i + 1) * 256, :], mass_ref, block)
+        for i, block in enumerate(blocks)
+    ]
     for r in range(0, x_ref.shape[0], ROWS):
         top = top_ref[r : r + ROWS, :]
         total = old_sum_ref[r : r + ROWS, :]
-        for m in range(4):
-            product = piece_product(x_ref, points_ref, r, m)
+        for i, block in enumerate(blocks):
+            product = piece_product(x_ref, points_ref, r, first + i)
             for side in range(2):
-                terms = product[:, lane_tile(side)] * BITS + biases[m][side]
-                t_ref[2 * blocks[m] + side, r : r + ROWS, :] = terms
+                terms = product[:, lane_tile(side)] * BITS + biases[i][side]
+                t_ref[2 * block + side, r : r + ROWS, :] = terms
                 total += jnp.exp2(terms - top)
         sum_ref[r : r + ROWS, :] = total
 
 
-def more_terms_kernel(k, place, x_ref, old_ref, old_sum_ref, top_ref, points_ref, mass_ref, *refs):
+def more_terms_kernel(spots, place, x_ref, old_ref, old_sum_ref, top_ref, points_ref, mass_ref, *refs):
     t_ref, sum_ref = refs
-    piece_steps(k, place, x_ref, points_ref, mass_ref, top_ref, old_sum_ref, t_ref, sum_ref)
-
-
-def last_terms_kernel(k, place, x_ref, old_ref, old_sum_ref, old_top_ref, points_ref, mass_ref, *refs):
+    piece_steps(spots, place, x_ref, points_ref, mass_ref, top_ref, old_sum_ref, t_ref, sum_ref)
+
+
+def last_terms_kernel(spots, place, x_ref, old_ref, old_sum_ref, old_top_ref, points_ref, mass_ref, *refs):
     t_ref, sum_ref, out_ref, top_ref = refs
     tiles, rows, _ = t_ref.shape
-    piece_steps(k, place, x_ref, points_ref, mass_ref, old_top_ref, old_sum_ref, t_ref, sum_ref)
+    piece_steps(spots, place, x_ref, points_ref, mass_ref, old_top_ref, old_sum_ref, t_ref, sum_ref)
     total = collapse(sum_ref)
     out_ref[...] = collapse_top(old_top_ref) * LN2 + jnp.log(total)
 
@@ -374,9 +359,9 @@
     return ((y % 4 * 4 + x % 4) * 4 + z) * 2 + core
 
 
-def turned(value, stage):
+def turned(value, stage, order):
     found = {0: value}
-    for k in (2, 1, 3):
+    for k in order:
         pairs = []
         for y, x, z, core in itertools.product(*map(range, SIZES)):
             along_y = (core + stage) % 2
@@ -418,22 +403,31 @@
     def over_row(value):
         return lax.all_to_all(value, ROW, 0, 0, tiled=True)
 
-    first = jnp.concatenate(turned(tgt_points, 0))
-    pieces = turned(first, 1)
+    found = turned(tgt_points, 0, (1, 2, 3))
+    halves = [jnp.concatenate(found[:2]), jnp.concatenate(found[2:])]
+    pieces = [(halves[0], [(0, 1)]), (halves[1], [(0, 2), (0, 3)])]
+    for q in range(2):
+        found = turned(halves[q], 1, (1, 2, 3))
+        pieces += [(found[k], [(k, 2 * q), (k, 2 * q + 1)]) for k in (1, 2, 3)]
     terms, top, sums, squares = call(
-        first_terms_kernel, (big, wide, wide, by_row), [SMEM] + [VMEM] * 3, []
-    )(place, src_points, first, tgt_mass)
-    for k in (1, 3):
+        own_terms_kernel, (big, wide, wide, by_row), [SMEM] + [VMEM] * 3, []
+    )(place, src_points, tgt_points, tgt_mass)
+    for piece, spots in pieces[:-1]:
         terms, sums = call(
-            functools.partial(more_terms_kernel, k), (big, wide), [SMEM] + [VMEM] * 6, [], {2: 0, 3: 1}
-        )(place, src_points, resident(terms), resident(sums), resident(top), pieces[k], tgt_mass)
+            functools.partial(more_terms_kernel, spots),
+            (big, wide),
+            [SMEM] + [VMEM] * 6,
+            [],
+            {2: 0, 3: 1},
+        )(place, src_points, resident(terms), resident(sums), resident(top), piece, tgt_mass)
+    piece, spots = pieces[-1]
     terms, sums, lse = call(
-        functools.partial(last_terms_kernel, 2),
+        functools.partial(last_terms_kernel, spots),
         (big, wide, by_row),
         [SMEM] + [VMEM] * 6,
         [wide],
         {2: 0, 3: 1},
-    )(place, src_points, resident(terms), resident(sums), resident(top), pieces[2], tgt_mass)
+    )(place, src_points, resident(terms), resident(sums), resident(top), piece, tgt_mass)
     lse, src_lse = call(column_kernel, (columns_out, by_row), [VMEM] * 6, [wide, line])(
         resident(terms), *over_col(lse, lse_all), src_mass
     )

time: 119 us -> 123 us (1.034)
  starting transfers between devices: 36.8 us -> 44 us
  waiting for transfers between devices: 15.7 us -> 11.1 us
  Pallas kernels: 24 us -> 26.8 us
  blocking collectives: 38.1 us -> 35.7 us
    ppermute x6 -> x9, waiting for transfers between devices: 5.34 us -> 0.75 us  [turned(): found[k] = lax.ppermute(value, ALL, pairs)]
    ppermute x6 -> x9, starting transfers between devices: 10.2 us -> 14.7 us  [turned(): found[k] = lax.ppermute(value, ALL, pairs)]
    ppermute x4, starting transfers between devices: 7.33 us -> 10 us  [over_col(): both = combine([value, lax.ppermute(value, 'col_1', [(0, 1), (1, 0)])])]
    pallas_call x4 -> x9, Pallas kernels: 8.87 us -> 11.5 us  [the longest x7 8.84 us: body(): call(functools.partial(more_terms_kernel, spots), (big, wide), [SMEM] + [...]
    all_to_all x3, blocking collectives: 38.1 us -> 35.7 us  [over_row(): return lax.all_to_all(value, ROW, 0, 0, tiled=True)]
    unnamed x9 -> x10, local copies, waits for them, and re-layouts: 2.73 us -> 3.63 us
  transfers between devices with their start and end apart: 22 -> 25, of which waited for: 16 -> 15; matrix products, arithmetic and copies ran while one was open for 1% -> 1% of each run, Pallas kernels for 6% -> 8%
where the time goes in v6:
time: 123 us
  starting transfers between devices  44 us (36%)
  blocking collectives  35.7 us (29%)
  Pallas kernels  26.8 us (22%)
  waiting for transfers between devices  11.1 us (9%)
  local copies, waits for them, and re-layouts  4.16 us (3%)
    all_to_all x3, blocking collectives, over_row(): return lax.all_to_all(value, ROW, 0, 0, tiled=True)  35.7 us
    ppermute x12, starting transfers between devices, crossed(): return lax.ppermute(value, ALL, pairs)  19.3 us
    ppermute x9, starting transfers between devices, turned(): found[k] = lax.ppermute(value, ALL, pairs)  14.7 us
    ppermute x4, starting transfers between devices, over_col(): both = combine([value, lax.ppermute(value, 'col_1', [(0, 1), (1, 0)])])  10 us
    pallas_call x7, Pallas kernels, body(): call(functools.partial(more_terms_kernel, spots), (big, wide), [SMEM] + [...  8.84 us
    ppermute x12, waiting for transfers between devices, crossed(): return lax.ppermute(value, ALL, pairs)  7.07 us
    pallas_call x1, Pallas kernels, body(): call(column_kernel, (columns_out, by_row), [VMEM] * 6, [wide, line])  4.91 us
    pallas_call x1, Pallas kernels, body(): call(plan_kernel, (big, by_row, by_column), [VMEM] * 5, [wide, wide, line...  3.77 us
  transfers between devices with their start and end apart: 25, of which 15 were waited for; matrix products, arithmetic and copies ran while one was open for 1% of the time, Pallas kernels for 8%

profile of v6, /device:TPU:1, one launch (start us, length us, event | category | flops | bytes accessed | tf_op | source)
XLA Modules:
  0.0 122.8 jit_solution(7029170712372049148)
XLA Ops:
  0.6 2.2 %collective-permute-start = (bf16[256,256]{1,0:T(8,128)(2,1)}, bf16[256,256]{1,0:T(8,128)(2,1)S(1)}, u32[]{:S(2)}, u32[]{:S(2)}) collective-permute-start(bf16[256,256]{1,0:T(8,128)(2,1)} %points_ref.1), channel_id=1, source_target_pairs={{0,8},{1,33},{2,10},{3,35},{4,12},{5,37},{6,14},{7,39},{8,16},{9,4... | collective-permute-start | bytes 393224 | tf_op jit(solution)/shard_map/ppermute | solution.py:370
  2.8 2.6 %collective-permute-start.1 = (bf16[256,256]{1,0:T(8,128)(2,1)}, bf16[256,256]{1,0:T(8,128)(2,1)S(1)}, u32[]{:S(2)}, u32[]{:S(2)}) collective-permute-start(bf16[256,256]{1,0:T(8,128)(2,1)} %points_ref.1), channel_id=1, source_target_pairs={{0,16},{1,65},{2,18},{3,67},{4,20},{5,69},{6,22},{7,71},{8,24},{9,... | collective-permute-start | bytes 393224 | tf_op jit(solution)/shard_map/ppermute | solution.py:370
  8.1 1.8 %collective-permute-start.2 = (bf16[256,256]{1,0:T(8,128)(2,1)}, bf16[256,256]{1,0:T(8,128)(2,1)S(1)}, u32[]{:S(2)}, u32[]{:S(2)}) collective-permute-start(bf16[256,256]{1,0:T(8,128)(2,1)} %points_ref.1), channel_id=1, source_target_pairs={{0,24},{1,97},{2,26},{3,99},{4,28},{5,101},{6,30},{7,103},{8,0},{9... | collective-permute-start | bytes 393224 | tf_op jit(solution)/shard_map/ppermute | solution.py:370
  9.9 2.5 %collective-permute-start.4 = (bf16[512,256]{1,0:T(8,128)(2,1)S(1)}, bf16[512,256]{1,0:T(8,128)(2,1)S(1)}, u32[]{:S(2)}, u32[]{:S(2)}) collective-permute-start(bf16[512,256]{1,0:T(8,128)(2,1)S(1)} %constant_dynamic-update-slice_fusion.points_ref), channel_id=1, source_target_pairs={{0,64},{1,17},{2,66},{3,19},{4,68},{5,21},{6,70},{7,23},{8,72},{9,... | collective-permute-start | bytes 786440 | tf_op jit(solution)/shard_map/ppermute | solution.py:370
  15.2 1.9 %collective-permute-start.8 = (bf16[512,256]{1,0:T(8,128)(2,1)S(1)}, bf16[512,256]{1,0:T(8,128)(2,1)S(1)}, u32[]{:S(2)}, u32[]{:S(2)}) collective-permute-start(bf16[512,256]{1,0:T(8,128)(2,1)S(1)} %constant_dynamic-update-slice_fusion.2.points_ref), channel_id=1, source_target_pairs={{0,96},{1,25},{2,98},{3,27},{4,100},{5,29},{6,102},{7,31},{8,104},... | collective-permute-start | bytes 786440 | tf_op jit(solution)/shard_map/ppermute | solution.py:370
  29.9 1.5 %shard_map.75 = (f32[32,1024,128]{2,1,0:T(8,128)S(1)}, f32[1024,128]{1,0:T(8,128)S(1)}, f32[8,128]{1,0:T(8,128)S(1)}) custom-call(s32[3]{0:T(128)S(1)} %pad_add_fusion.place, bf16[1024,256]{1,0:T(8,128)(2,1)S(1)} %copy-done, f32[32,1024,128]{2,1,0:T(8,128)S(1)} %get-tuple-element.48.old_ref, ...), custom_call_target="tpu_custom_call", output_to_operand_aliasing={{0}: (2, {}), {1}: (3, {})} | custom-call | tf_op jit(solution)/shard_map/pallas_call | solution.py:424
  31.4 5.5 %collective-permute-start.9 = (f32[8,128]{1,0:T(8,128)S(1)}, f32[8,128]{1,0:T(8,128)S(1)}, u32[]{:S(2)}, u32[]{:S(2)}) collective-permute-start(f32[8,128]{1,0:T(8,128)S(1)} %get-tuple-element.51), channel_id=1, source_target_pairs={{0,1},{1,0},{2,3},{3,2},{4,5},{5,4},{6,7},{7,6},{8,9},{9,8},{10,11... | collective-permute-start | bytes 12296 | tf_op jit(solution)/shard_map/ppermute | solution.py:400
  37.8 3.9 %collective-permute-start.10 = (f32[8,128]{1,0:T(8,128)S(1)}, f32[8,128]{1,0:T(8,128)S(1)}, u32[]{:S(2)}, u32[]{:S(2)}) collective-permute-start(f32[8,128]{1,0:T(8,128)S(1)} %log_add_fusion.refs_0_), channel_id=1, source_target_pairs={{0,5},{1,4},{2,7},{3,6},{4,1},{5,0},{6,3},{7,2},{8,13},{9,12},{10,... | collective-permute-start | bytes 12296 | tf_op jit(solution)/shard_map/ppermute | solution.py:378
  42.5 2.2 %collective-permute-start.12 = (f32[8,128]{1,0:T(8,128)S(1)}, f32[8,128]{1,0:T(8,128)S(1)}, u32[]{:S(2)}, u32[]{:S(2)}) collective-permute-start(f32[8,128]{1,0:T(8,128)S(1)} %log_add_fusion.refs_0_), channel_id=1, source_target_pairs={{0,7},{1,6},{2,1},{3,0},{4,3},{5,2},{6,5},{7,4},{8,15},{9,14},{10,... | collective-permute-start | bytes 12296 | tf_op jit(solution)/shard_map/ppermute | solution.py:378
  45.9 4.9 %shard_map.76 = (f32[16,32,128]{2,1,0:T(8,128)S(1)}, f32[8,128]{1,0:T(8,128)S(1)}) custom-call(f32[32,1024,128]{2,1,0:T(8,128)S(1)} %get-tuple-element.50.t_ref, f32[8,128]{1,0:T(8,128)S(1)} %log_add_fusion.refs_0_, f32[8,128]{1,0:T(8,128)S(1)} %collective-permute-done.10.refs_1_, f32[8,128]{1,0:T(8,128)S(1)} %collective-permute-done.11.refs_2_, ...), custom_call_target="tpu_custom_call" | custom-call | tf_op jit(solution)/shard_map/pallas_call | solution.py:431
  50.9 13.5 %all_to_all.15.parts_ref = f32[16,32,128]{2,1,0:T(8,128)S(1)} all-to-all(f32[16,32,128]{2,1,0:T(8,128)S(1)} %get-tuple-element.52), channel_id=1, replica_groups=mesh['row_0'=4,'row_1'=4,'col_0'=4,'col_1'=2] {'row_0','row_1'}, dimensions={0} | all-to-all | bytes 524288 | tf_op jit(solution)/shard_map/all_to_all | solution.py:404
  64.4 3.8 %shard_map.77 = (f32[32,1024,128]{2,1,0:T(8,128)S(1)}, f32[8,128]{1,0:T(8,128)S(1)}, f32[32,128]{1,0:T(8,128)S(1)}) custom-call(f32[32,1024,128]{2,1,0:T(8,128)S(1)} %get-tuple-element.50.t_ref, f32[16,32,128]{2,1,0:T(8,128)S(1)} %all_to_all.15.parts_ref, f32[32,128]{1,0:T(8,128)S(1)} %bitcast.17, ...), custom_call_target="tpu_custom_call", output_to_operand_aliasing={{0}: (0, {})} | custom-call | tf_op jit(solution)/shard_map/pallas_call | solution.py:434
  68.1 1.4 %collective-permute-start.13 = (f32[8,128]{1,0:T(8,128)S(1)}, f32[8,128]{1,0:T(8,128)S(1)}, u32[]{:S(2)}, u32[]{:S(2)}) collective-permute-start(f32[8,128]{1,0:T(8,128)S(1)} %get-tuple-element.55), channel_id=1, source_target_pairs={{0,1},{1,0},{2,3},{3,2},{4,5},{5,4},{6,7},{7,6},{8,9},{9,8},{10,11... | collective-permute-start | bytes 12296 | tf_op jit(solution)/shard_map/ppermute | solution.py:400
  70.4 1.4 %collective-permute-start.14 = (f32[8,128]{1,0:T(8,128)S(1)}, f32[8,128]{1,0:T(8,128)S(1)}, u32[]{:S(2)}, u32[]{:S(2)}) collective-permute-start(f32[8,128]{1,0:T(8,128)S(1)} %add.29.refs_0_), channel_id=1, source_target_pairs={{0,5},{1,4},{2,7},{3,6},{4,1},{5,0},{6,3},{7,2},{8,13},{9,12},{10,... | collective-permute-start | bytes 12296 | tf_op jit(solution)/shard_map/ppermute | solution.py:378
  71.8 2.2 %collective-permute-start.15 = (f32[8,128]{1,0:T(8,128)S(1)}, f32[8,128]{1,0:T(8,128)S(1)}, u32[]{:S(2)}, u32[]{:S(2)}) collective-permute-start(f32[8,128]{1,0:T(8,128)S(1)} %add.29.refs_0_), channel_id=1, source_target_pairs={{0,3},{1,2},{2,5},{3,4},{4,7},{5,6},{6,1},{7,0},{8,11},{9,10},{10,... | collective-permute-start | bytes 12296 | tf_op jit(solution)/shard_map/ppermute | solution.py:378
  77.0 1.7 %shard_map.78 = f32[16,32,128]{2,1,0:T(8,128)S(1)} custom-call(f32[32,1024,128]{2,1,0:T(8,128)S(1)} %get-tuple-element.54.plan_ref, f32[8,128]{1,0:T(8,128)S(1)} %add.29.refs_0_, f32[8,128]{1,0:T(8,128)S(1)} %collective-permute-done.14.refs_1_, f32[8,128]{1,0:T(8,128)S(1)} %collective-permute-done.15.refs_2_, f32[8,128]{1,0:T(8,128)S(1)} %collective-permute-done.16.refs_3_, ...), custom_call_target="tpu_custom_call" | custom-call | tf_op jit(solution)/shard_map/pallas_call | solution.py:438
  78.7 10.8 %all_to_all.16.parts_ref = f32[16,32,128]{2,1,0:T(8,128)S(1)} all-to-all(f32[16,32,128]{2,1,0:T(8,128)S(1)} %shard_map.78), channel_id=1, replica_groups=mesh['row_0'=4,'row_1'=4,'col_0'=4,'col_1'=2] {'row_0','row_1'}, dimensions={0} | all-to-all | bytes 524288 | tf_op jit(solution)/shard_map/all_to_all | solution.py:404
  89.4 2.1 %shard_map.79 = f32[8,128]{1,0:T(8,128)S(1)} custom-call(f32[32,1024,128]{2,1,0:T(8,128)S(1)} %get-tuple-element.54.plan_ref, f32[16,32,128]{2,1,0:T(8,128)S(1)} %all_to_all.16.parts_ref, f32[32,128]{1,0:T(8,128)S(1)} %bitcast.18), custom_call_target="tpu_custom_call" | custom-call | tf_op jit(solution)/shard_map/pallas_call | solution.py:441
  91.5 1.6 %collective-permute-start.17 = (f32[8,128]{1,0:T(8,128)S(1)}, f32[8,128]{1,0:T(8,128)S(1)}, u32[]{:S(2)}, u32[]{:S(2)}) collective-permute-start(f32[8,128]{1,0:T(8,128)S(1)} %shard_map.79), channel_id=1, source_target_pairs={{0,1},{1,0},{2,3},{3,2},{4,5},{5,4},{6,7},{7,6},{8,9},{9,8},{10,11... | collective-permute-start | bytes 12296 | tf_op jit(solution)/shard_map/ppermute | solution.py:400
  94.7 1.8 %collective-permute-start.19 = (f32[8,128]{1,0:T(8,128)S(1)}, f32[8,128]{1,0:T(8,128)S(1)}, u32[]{:S(2)}, u32[]{:S(2)}) collective-permute-start(f32[8,128]{1,0:T(8,128)S(1)} %add.30.refs_0_), channel_id=1, source_target_pairs={{0,3},{1,2},{2,5},{3,4},{4,7},{5,6},{6,1},{7,0},{8,11},{9,10},{10,... | collective-permute-start | bytes 12296 | tf_op jit(solution)/shard_map/ppermute | solution.py:378
  99.6 2.3 %shard_map.80 = (f32[16,40,128]{2,1,0:T(8,128)S(1)}, f32[8,128]{1,0:T(8,128)}) custom-call(f32[32,1024,128]{2,1,0:T(8,128)S(1)} %get-tuple-element.54.plan_ref, f32[8,128]{1,0:T(8,128)S(1)} %add.30.refs_0_, f32[8,128]{1,0:T(8,128)S(1)} %collective-permute-done.18.refs_1_, f32[8,128]{1,0:T(8,128)S(1)} %collective-permute-done.19.refs_2_, ...), custom_call_target="tpu_custom_call" | custom-call | tf_op jit(solution)/shard_map/pallas_call | solution.py:442
  101.8 11.5 %all_to_all.17.parts_ref = f32[16,40,128]{2,1,0:T(8,128)S(1)} all-to-all(f32[16,40,128]{2,1,0:T(8,128)S(1)} %get-tuple-element.58), channel_id=1, replica_groups=mesh['row_0'=4,'row_1'=4,'col_0'=4,'col_1'=2] {'row_0','row_1'}, dimensions={0} | all-to-all | bytes 655360 | tf_op jit(solution)/shard_map/all_to_all | solution.py:404
  113.9 1.5 %collective-permute-start.21 = (f32[8,128]{1,0:T(8,128)S(1)}, f32[8,128]{1,0:T(8,128)S(1)}, u32[]{:S(2)}, u32[]{:S(2)}) collective-permute-start(f32[8,128]{1,0:T(8,128)S(1)} %get-tuple-element.62), channel_id=1, source_target_pairs={{0,1},{1,0},{2,3},{3,2},{4,5},{5,4},{6,7},{7,6},{8,9},{9,8},{10,11... | collective-permute-start | bytes 12296 | tf_op jit(solution)/shard_map/ppermute | solution.py:400
  117.7 1.5 %collective-permute-start.23 = (f32[8,128]{1,0:T(8,128)S(1)}, f32[8,128]{1,0:T(8,128)S(1)}, u32[]{:S(2)}, u32[]{:S(2)}) collective-permute-start(f32[8,128]{1,0:T(8,128)S(1)} %add.31), channel_id=1, source_target_pairs={{0,3},{1,2},{2,5},{3,4},{4,7},{5,6},{6,1},{7,0},{8,11},{9,10},{10,... | collective-permute-start | bytes 12296 | tf_op jit(solution)/shard_map/ppermute | solution.py:378
  (63 shorter events, 36.0 us)
Async XLA Ops:
  0.6 6.5 %collective-permute-start = (bf16[256,256]{1,0:T(8,128)(2,1)}, bf16[256,256]{1,0:T(8,128)(2,1)S(1)}, u32[]{:S(2)}, u32[]{:S(2)}) collective-permute-start(bf16[256,256]{1,0:T(8,128)(2,1)} %points_ref.1), channel_id=1, source_target_pairs={{0,8},{1,33},{2,10},{3,35},{4,12},{5,37},{6,14},{7,39},{8,16},{9,4... | collective-permute-start | bytes 393224 | tf_op jit(solution)/shard_map/ppermute | solution.py:370
  2.8 10.7 %collective-permute-start.1 = (bf16[256,256]{1,0:T(8,128)(2,1)}, bf16[256,256]{1,0:T(8,128)(2,1)S(1)}, u32[]{:S(2)}, u32[]{:S(2)}) collective-permute-start(bf16[256,256]{1,0:T(8,128)(2,1)} %points_ref.1), channel_id=1, source_target_pairs={{0,16},{1,65},{2,18},{3,67},{4,20},{5,69},{6,22},{7,71},{8,24},{9,... | collective-permute-start | bytes 393224 | tf_op jit(solution)/shard_map/ppermute | solution.py:370
  7.1 8.0 %collective-permute-start.3 = (bf16[512,256]{1,0:T(8,128)(2,1)S(1)}, bf16[512,256]{1,0:T(8,128)(2,1)S(1)}, u32[]{:S(2)}, u32[]{:S(2)}) collective-permute-start(bf16[512,256]{1,0:T(8,128)(2,1)S(1)} %constant_dynamic-update-slice_fusion.points_ref), channel_id=1, source_target_pairs={{0,32},{1,9},{2,34},{3,11},{4,36},{5,13},{6,38},{7,15},{8,40},{9,1... | collective-permute-start | bytes 786440 | tf_op jit(solution)/shard_map/ppermute | solution.py:370
  8.1 5.4 %collective-permute-start.2 = (bf16[256,256]{1,0:T(8,128)(2,1)}, bf16[256,256]{1,0:T(8,128)(2,1)S(1)}, u32[]{:S(2)}, u32[]{:S(2)}) collective-permute-start(bf16[256,256]{1,0:T(8,128)(2,1)} %points_ref.1), channel_id=1, source_target_pairs={{0,24},{1,97},{2,26},{3,99},{4,28},{5,101},{6,30},{7,103},{8,0},{9... | collective-permute-start | bytes 393224 | tf_op jit(solution)/shard_map/ppermute | solution.py:370
  9.9 14.7 %collective-permute-start.4 = (bf16[512,256]{1,0:T(8,128)(2,1)S(1)}, bf16[512,256]{1,0:T(8,128)(2,1)S(1)}, u32[]{:S(2)}, u32[]{:S(2)}) collective-permute-start(bf16[512,256]{1,0:T(8,128)(2,1)S(1)} %constant_dynamic-update-slice_fusion.points_ref), channel_id=1, source_target_pairs={{0,64},{1,17},{2,66},{3,19},{4,68},{5,21},{6,70},{7,23},{8,72},{9,... | collective-permute-start | bytes 786440 | tf_op jit(solution)/shard_map/ppermute | solution.py:370
  12.3 13.6 %collective-permute-start.5 = (bf16[512,256]{1,0:T(8,128)(2,1)S(1)}, bf16[512,256]{1,0:T(8,128)(2,1)S(1)}, u32[]{:S(2)}, u32[]{:S(2)}) collective-permute-start(bf16[512,256]{1,0:T(8,128)(2,1)S(1)} %constant_dynamic-update-slice_fusion.points_ref), channel_id=1, source_target_pairs={{0,96},{1,25},{2,98},{3,27},{4,100},{5,29},{6,102},{7,31},{8,104},... | collective-permute-start | bytes 786440 | tf_op jit(solution)/shard_map/ppermute | solution.py:370
  13.5 13.7 %collective-permute-start.6 = (bf16[512,256]{1,0:T(8,128)(2,1)S(1)}, bf16[512,256]{1,0:T(8,128)(2,1)S(1)}, u32[]{:S(2)}, u32[]{:S(2)}) collective-permute-start(bf16[512,256]{1,0:T(8,128)(2,1)S(1)} %constant_dynamic-update-slice_fusion.2.points_ref), channel_id=1, source_target_pairs={{0,32},{1,9},{2,34},{3,11},{4,36},{5,13},{6,38},{7,15},{8,40},{9,1... | collective-permute-start | bytes 786440 | tf_op jit(solution)/shard_map/ppermute | solution.py:370
  13.9 14.6 %collective-permute-start.7 = (bf16[512,256]{1,0:T(8,128)(2,1)S(1)}, bf16[512,256]{1,0:T(8,128)(2,1)S(1)}, u32[]{:S(2)}, u32[]{:S(2)}) collective-permute-start(bf16[512,256]{1,0:T(8,128)(2,1)S(1)} %constant_dynamic-update-slice_fusion.2.points_ref), channel_id=1, source_target_pairs={{0,64},{1,17},{2,66},{3,19},{4,68},{5,21},{6,70},{7,23},{8,72},{9,... | collective-permute-start | bytes 786440 | tf_op jit(solution)/shard_map/ppermute | solution.py:370
  15.2 14.7 %collective-permute-start.8 = (bf16[512,256]{1,0:T(8,128)(2,1)S(1)}, bf16[512,256]{1,0:T(8,128)(2,1)S(1)}, u32[]{:S(2)}, u32[]{:S(2)}) collective-permute-start(bf16[512,256]{1,0:T(8,128)(2,1)S(1)} %constant_dynamic-update-slice_fusion.2.points_ref), channel_id=1, source_target_pairs={{0,96},{1,25},{2,98},{3,27},{4,100},{5,29},{6,102},{7,31},{8,104},... | collective-permute-start | bytes 786440 | tf_op jit(solution)/shard_map/ppermute | solution.py:370
  31.4 6.4 %collective-permute-start.9 = (f32[8,128]{1,0:T(8,128)S(1)}, f32[8,128]{1,0:T(8,128)S(1)}, u32[]{:S(2)}, u32[]{:S(2)}) collective-permute-start(f32[8,128]{1,0:T(8,128)S(1)} %get-tuple-element.51), channel_id=1, source_target_pairs={{0,1},{1,0},{2,3},{3,2},{4,5},{5,4},{6,7},{7,6},{8,9},{9,8},{10,11... | collective-permute-start | bytes 12296 | tf_op jit(solution)/shard_map/ppermute | solution.py:400
  37.8 6.9 %collective-permute-start.10 = (f32[8,128]{1,0:T(8,128)S(1)}, f32[8,128]{1,0:T(8,128)S(1)}, u32[]{:S(2)}, u32[]{:S(2)}) collective-permute-start(f32[8,128]{1,0:T(8,128)S(1)} %log_add_fusion.refs_0_), channel_id=1, source_target_pairs={{0,5},{1,4},{2,7},{3,6},{4,1},{5,0},{6,3},{7,2},{8,13},{9,12},{10,... | collective-permute-start | bytes 12296 | tf_op jit(solution)/shard_map/ppermute | solution.py:378
  41.7 4.2 %collective-permute-start.11 = (f32[8,128]{1,0:T(8,128)S(1)}, f32[8,128]{1,0:T(8,128)S(1)}, u32[]{:S(2)}, u32[]{:S(2)}) collective-permute-start(f32[8,128]{1,0:T(8,128)S(1)} %log_add_fusion.refs_0_), channel_id=1, source_target_pairs={{0,3},{1,2},{2,5},{3,4},{4,7},{5,6},{6,1},{7,0},{8,11},{9,10},{10,... | collective-permute-start | bytes 12296 | tf_op jit(solution)/shard_map/ppermute | solution.py:378
  42.5 3.5 %collective-permute-start.12 = (f32[8,128]{1,0:T(8,128)S(1)}, f32[8,128]{1,0:T(8,128)S(1)}, u32[]{:S(2)}, u32[]{:S(2)}) collective-permute-start(f32[8,128]{1,0:T(8,128)S(1)} %log_add_fusion.refs_0_), channel_id=1, source_target_pairs={{0,7},{1,6},{2,1},{3,0},{4,3},{5,2},{6,5},{7,4},{8,15},{9,14},{10,... | collective-permute-start | bytes 12296 | tf_op jit(solution)/shard_map/ppermute | solution.py:378
  70.4 4.5 %collective-permute-start.14 = (f32[8,128]{1,0:T(8,128)S(1)}, f32[8,128]{1,0:T(8,128)S(1)}, u32[]{:S(2)}, u32[]{:S(2)}) collective-permute-start(f32[8,128]{1,0:T(8,128)S(1)} %add.29.refs_0_), channel_id=1, source_target_pairs={{0,5},{1,4},{2,7},{3,6},{4,1},{5,0},{6,3},{7,2},{8,13},{9,12},{10,... | collective-permute-start | bytes 12296 | tf_op jit(solution)/shard_map/ppermute | solution.py:378
  71.8 4.2 %collective-permute-start.15 = (f32[8,128]{1,0:T(8,128)S(1)}, f32[8,128]{1,0:T(8,128)S(1)}, u32[]{:S(2)}, u32[]{:S(2)}) collective-permute-start(f32[8,128]{1,0:T(8,128)S(1)} %add.29.refs_0_), channel_id=1, source_target_pairs={{0,3},{1,2},{2,5},{3,4},{4,7},{5,6},{6,1},{7,0},{8,11},{9,10},{10,... | collective-permute-start | bytes 12296 | tf_op jit(solution)/shard_map/ppermute | solution.py:378
  74.0 3.0 %collective-permute-start.16 = (f32[8,128]{1,0:T(8,128)S(1)}, f32[8,128]{1,0:T(8,128)S(1)}, u32[]{:S(2)}, u32[]{:S(2)}) collective-permute-start(f32[8,128]{1,0:T(8,128)S(1)} %add.29.refs_0_), channel_id=1, source_target_pairs={{0,7},{1,6},{2,1},{3,0},{4,3},{5,2},{6,5},{7,4},{8,15},{9,14},{10,... | collective-permute-start | bytes 12296 | tf_op jit(solution)/shard_map/ppermute | solution.py:378
  91.5 2.4 %collective-permute-start.17 = (f32[8,128]{1,0:T(8,128)S(1)}, f32[8,128]{1,0:T(8,128)S(1)}, u32[]{:S(2)}, u32[]{:S(2)}) collective-permute-start(f32[8,128]{1,0:T(8,128)S(1)} %shard_map.79), channel_id=1, source_target_pairs={{0,1},{1,0},{2,3},{3,2},{4,5},{5,4},{6,7},{7,6},{8,9},{9,8},{10,11... | collective-permute-start | bytes 12296 | tf_op jit(solution)/shard_map/ppermute | solution.py:400
  93.9 4.5 %collective-permute-start.18 = (f32[8,128]{1,0:T(8,128)S(1)}, f32[8,128]{1,0:T(8,128)S(1)}, u32[]{:S(2)}, u32[]{:S(2)}) collective-permute-start(f32[8,128]{1,0:T(8,128)S(1)} %add.30.refs_0_), channel_id=1, source_target_pairs={{0,5},{1,4},{2,7},{3,6},{4,1},{5,0},{6,3},{7,2},{8,13},{9,12},{10,... | collective-permute-start | bytes 12296 | tf_op jit(solution)/shard_map/ppermute | solution.py:378
  94.7 4.2 %collective-permute-start.19 = (f32[8,128]{1,0:T(8,128)S(1)}, f32[8,128]{1,0:T(8,128)S(1)}, u32[]{:S(2)}, u32[]{:S(2)}) collective-permute-start(f32[8,128]{1,0:T(8,128)S(1)} %add.30.refs_0_), channel_id=1, source_target_pairs={{0,3},{1,2},{2,5},{3,4},{4,7},{5,6},{6,1},{7,0},{8,11},{9,10},{10,... | collective-permute-start | bytes 12296 | tf_op jit(solution)/shard_map/ppermute | solution.py:378
  96.5 3.0 %collective-permute-start.20 = (f32[8,128]{1,0:T(8,128)S(1)}, f32[8,128]{1,0:T(8,128)S(1)}, u32[]{:S(2)}, u32[]{:S(2)}) collective-permute-start(f32[8,128]{1,0:T(8,128)S(1)} %add.30.refs_0_), channel_id=1, source_target_pairs={{0,7},{1,6},{2,1},{3,0},{4,3},{5,2},{6,5},{7,4},{8,15},{9,14},{10,... | collective-permute-start | bytes 12296 | tf_op jit(solution)/shard_map/ppermute | solution.py:378
  113.9 2.3 %collective-permute-start.21 = (f32[8,128]{1,0:T(8,128)S(1)}, f32[8,128]{1,0:T(8,128)S(1)}, u32[]{:S(2)}, u32[]{:S(2)}) collective-permute-start(f32[8,128]{1,0:T(8,128)S(1)} %get-tuple-element.62), channel_id=1, source_target_pairs={{0,1},{1,0},{2,3},{3,2},{4,5},{5,4},{6,7},{7,6},{8,9},{9,8},{10,11... | collective-permute-start | bytes 12296 | tf_op jit(solution)/shard_map/ppermute | solution.py:400
  116.2 4.5 %collective-permute-start.22 = (f32[8,128]{1,0:T(8,128)S(1)}, f32[8,128]{1,0:T(8,128)S(1)}, u32[]{:S(2)}, u32[]{:S(2)}) collective-permute-start(f32[8,128]{1,0:T(8,128)S(1)} %add.31), channel_id=1, source_target_pairs={{0,5},{1,4},{2,7},{3,6},{4,1},{5,0},{6,3},{7,2},{8,13},{9,12},{10,... | collective-permute-start | bytes 12296 | tf_op jit(solution)/shard_map/ppermute | solution.py:378
  117.7 4.2 %collective-permute-start.23 = (f32[8,128]{1,0:T(8,128)S(1)}, f32[8,128]{1,0:T(8,128)S(1)}, u32[]{:S(2)}, u32[]{:S(2)}) collective-permute-start(f32[8,128]{1,0:T(8,128)S(1)} %add.31), channel_id=1, source_target_pairs={{0,3},{1,2},{2,5},{3,4},{4,7},{5,6},{6,1},{7,0},{8,11},{9,10},{10,... | collective-permute-start | bytes 12296 | tf_op jit(solution)/shard_map/ppermute | solution.py:378
  119.2 3.0 %collective-permute-start.24 = (f32[8,128]{1,0:T(8,128)S(1)}, f32[8,128]{1,0:T(8,128)S(1)}, u32[]{:S(2)}, u32[]{:S(2)}) collective-permute-start(f32[8,128]{1,0:T(8,128)S(1)} %add.31), channel_id=1, source_target_pairs={{0,7},{1,6},{2,1},{3,0},{4,3},{5,2},{6,5},{7,4},{8,15},{9,14},{10,... | collective-permute-start | bytes 12296 | tf_op jit(solution)/shard_map/ppermute | solution.py:378
  (5 other events, 22.3 us)

commit v7 on v5

--- a/solution.py
+++ b/solution.py
@@ -95,8 +95,8 @@
     return [ref[...] for ref in refs]
 
 
-def at_rows(r):
-    return pl.ds(pl.multiple_of(r * STEP, STEP), STEP)
+def at_rows(r, step=STEP):
+    return pl.ds(pl.multiple_of(r * step, step), step)
 
 
 def lane_tile(t):
@@ -219,16 +219,16 @@
     lse = lse_all(values(parts))
     lse_ref[...] = lse
     spread((mass_ref[...] - lse) * LOG2E, wide_ref)
-    per = 4
+    per, step = 32, 128
 
     def group(value):
-        return value.reshape(STEP // 8, 8, LANES)
+        return value.reshape(step // 8, 8, LANES)
 
     def sums(c, tops):
-        wide = [jnp.broadcast_to(top, (STEP, LANES)) for top in tops]
+        wide = [jnp.broadcast_to(top, (step, LANES)) for top in tops]
 
         def sum_step(r, totals):
-            at = at_rows(r)
+            at = at_rows(r, step)
             own = wide_ref[at, :]
             return tuple(
                 total
@@ -239,14 +239,14 @@
             )
 
         start = tuple(jnp.zeros((8, LANES), jnp.float32) for _ in range(per))
-        totals = lax.fori_loop(0, rows // STEP, sum_step, start)
+        totals = lax.fori_loop(0, rows // step, sum_step, start)
         for t in range(per):
             total = jnp.sum(totals[t], axis=0, keepdims=True)
             line_ref[c + t : c + t + 1, :] = tops[t] * LN2 + jnp.log(total)
 
     for c in range(0, tiles, per):
         tops = [
-            jnp.max(t_ref[c + t, :STEP, :] + wide_ref[:STEP, :], axis=0, keepdims=True)
+            jnp.max(t_ref[c + t, :step, :] + wide_ref[:step, :], axis=0, keepdims=True)
             for t in range(per)
         ]
         sums(c, tops)
@@ -256,14 +256,14 @@
         for c in range(0, tiles, per):
 
             def top_step(r, tops):
-                at = at_rows(r)
+                at = at_rows(r, step)
                 return tuple(
                     jnp.maximum(top, jnp.max(group(t_ref[c + t, at, :] + wide_ref[at, :]), axis=0))
                     for t, top in enumerate(tops)
                 )
 
             start = tuple(jnp.full((8, LANES), -jnp.inf, jnp.float32) for _ in range(per))
-            tops = lax.fori_loop(0, rows // STEP, top_step, start)
+            tops = lax.fori_loop(0, rows // step, top_step, start)
             sums(c, [jnp.max(top, axis=0, keepdims=True) for top in tops])
 
     copies(out_ref, line_ref[...])
@@ -276,11 +276,11 @@
     lse_ref[...] = lse
     line_ref[...] = (tgt_mass_ref[...] - lse) * LOG2E
     spread((src_mass_ref[...] - src_lse_ref[...]) * LOG2E, wide_ref)
-    per = 4
+    per, step = 4, 128
 
     def rows_step(r, unused):
-        at = at_rows(r)
-        total = jnp.zeros((STEP, LANES), jnp.float32)
+        at = at_rows(r, step)
+        total = jnp.zeros((step, LANES), jnp.float32)
         own = wide_ref[at, :]
         for c in range(0, tiles, per):
             terms = [t_ref[c + t, at, :] for t in range(per)]
@@ -293,30 +293,31 @@
         sum_ref[at, :] = total
         return unused
 
-    lax.fori_loop(0, rows // STEP, rows_step, 0)
+    lax.fori_loop(0, rows // step, rows_step, 0)
     out_ref[...] = collapse(sum_ref)
 
 
 def row_sums_kernel(plan_ref, parts_ref, mass_ref, out_ref, sum_ref, line_ref):
     tiles, rows, _ = plan_ref.shape
+    step = 512
     line_ref[...] = jnp.exp(mass_ref[...]) / combined(parts_ref, add_all)
 
     def rows_step(r, unused):
-        at = at_rows(r)
-        total = jnp.zeros((STEP, LANES), jnp.float32)
+        at = at_rows(r, step)
+        total = jnp.zeros((step, LANES), jnp.float32)
         for t in range(tiles):
             total += plan_ref[t, at, :] * line_ref[t : t + 1, :]
         sum_ref[at, :] = total
         return unused
 
-    lax.fori_loop(0, rows // STEP, rows_step, 0)
+    lax.fori_loop(0, rows // step, rows_step, 0)
     out_ref[...] = collapse(sum_ref)
 
 
 def column_sums(plan_ref, scale, line_ref, wide_ref):
     tiles, rows, _ = plan_ref.shape
     spread(scale, wide_ref)
-    per = 16
+    per = tiles
     for c in range(0, tiles, per):
 
         def rows_step(r, totals):

time: 119 us -> 117 us (0.983)
  Pallas kernels: 24 us -> 21.4 us
  starting transfers between devices: 36.8 us -> 38.8 us
    ppermute x12, starting transfers between devices: 19.3 us -> 21 us  [crossed(): return lax.ppermute(value, ALL, pairs)]
    pallas_call x1, Pallas kernels: 4.73 us -> 3.11 us  [body(): call(column_kernel, (columns_out, by_row), [VMEM] * 6, [wide, line])]
  transfers between devices with their start and end apart: 22 -> 22, of which waited for: 16 -> 13; matrix products, arithmetic and copies ran while one was open for 1% -> 1% of each run, Pallas kernels for 6% -> 6%
where the time goes in v7:
time: 117 us; the launch traced here: 118 us
  starting transfers between devices  38.8 us (33%)
  blocking collectives  38 us (32%)
  Pallas kernels  21.4 us (18%)
  waiting for transfers between devices  15.2 us (13%)
  local copies, waits for them, and re-layouts  3.26 us (3%)
    all_to_all x3, blocking collectives, over_row(): return lax.all_to_all(value, ROW, 0, 0, tiled=True)  38 us
    ppermute x12, starting transfers between devices, crossed(): return lax.ppermute(value, ALL, pairs)  21 us
    ppermute x6, starting transfers between devices, turned(): found[k] = lax.ppermute(value, ALL, pairs)  10.2 us
    ppermute x4, starting transfers between devices, over_col(): both = combine([value, lax.ppermute(value, 'col_1', [(0, 1), (1, 0)])])  7.67 us
    ppermute x12, waiting for transfers between devices, crossed(): return lax.ppermute(value, ALL, pairs)  6.52 us
    ppermute x6, waiting for transfers between devices, turned(): found[k] = lax.ppermute(value, ALL, pairs)  5.34 us
    pallas_call x1, Pallas kernels, body(): call(first_terms_kernel, (big, wide, wide, by_row), [SMEM] + [VMEM] * 3, [])  3.53 us
    pallas_call x1, Pallas kernels, body(): call(plan_kernel, (big, by_row, by_column), [VMEM] * 5, [wide, wide, line...  3.46 us
  transfers between devices with their start and end apart: 22, of which 13 were waited for; matrix products, arithmetic and copies ran while one was open for 1% of the time, Pallas kernels for 6%

profile of v7, /device:TPU:1, one launch (start us, length us, event | category | flops | bytes accessed | tf_op | source)
XLA Modules:
  0.0 117.5 jit_solution(7107534058397128627)
XLA Ops:
  0.6 2.2 %collective-permute-start = (bf16[256,256]{1,0:T(8,128)(2,1)}, bf16[256,256]{1,0:T(8,128)(2,1)S(1)}, u32[]{:S(2)}, u32[]{:S(2)}) collective-permute-start(bf16[256,256]{1,0:T(8,128)(2,1)} %param.5), channel_id=1, source_target_pairs={{0,8},{1,33},{2,10},{3,35},{4,12},{5,37},{6,14},{7,39},{8,16},{9,4... | collective-permute-start | bytes 393224 | tf_op jit(solution)/shard_map/ppermute | solution.py:386
  2.8 2.6 %collective-permute-start.1 = (bf16[256,256]{1,0:T(8,128)(2,1)}, bf16[256,256]{1,0:T(8,128)(2,1)S(1)}, u32[]{:S(2)}, u32[]{:S(2)}) collective-permute-start(bf16[256,256]{1,0:T(8,128)(2,1)} %param.5), channel_id=1, source_target_pairs={{0,16},{1,65},{2,18},{3,67},{4,20},{5,69},{6,22},{7,71},{8,24},{9,... | collective-permute-start | bytes 393224 | tf_op jit(solution)/shard_map/ppermute | solution.py:386
  7.5 2.2 %collective-permute-done.1 = bf16[256,256]{1,0:T(8,128)(2,1)S(1)} collective-permute-done((bf16[256,256]{1,0:T(8,128)(2,1)}, bf16[256,256]{1,0:T(8,128)(2,1)S(1)}, u32[]{:S(2)}, u32[]{:S(2)}) %collective-permute-start.1) | collective-permute-done | bytes 131104 | tf_op jit(solution)/shard_map/ppermute | solution.py:386
  15.9 3.5 %shard_map.67 = (f32[32,1024,128]{2,1,0:T(8,128)S(1)}, f32[1024,128]{1,0:T(8,128)S(1)}, f32[1024,128]{1,0:T(8,128)S(1)}, f32[8,128]{1,0:T(8,128)S(1)}) custom-call(s32[3]{0:T(128)S(1)} %pad_add_fusion.place, bf16[1024,256]{1,0:T(8,128)(2,1)S(1)} %copy-done, bf16[1024,256]{1,0:T(8,128)(2,1)S(1)} %constant_dynamic-update-slice_fusion.points_ref, ...), custom_call_target="tpu_custom_call" | custom-call | tf_op jit(solution)/shard_map/pallas_call | solution.py:424
  19.4 1.7 %shard_map.68 = (f32[32,1024,128]{2,1,0:T(8,128)S(1)}, f32[1024,128]{1,0:T(8,128)S(1)}) custom-call(s32[3]{0:T(128)S(1)} %pad_add_fusion.place, bf16[1024,256]{1,0:T(8,128)(2,1)S(1)} %copy-done, f32[32,1024,128]{2,1,0:T(8,128)S(1)} %get-tuple-element.23.old_ref, ...), custom_call_target="tpu_custom_call", output_to_operand_aliasing={{0}: (2, {}), {1}: (3, {})} | custom-call | tf_op jit(solution)/shard_map/pallas_call | solution.py:428
  21.2 1.7 %shard_map.69 = (f32[32,1024,128]{2,1,0:T(8,128)S(1)}, f32[1024,128]{1,0:T(8,128)S(1)}) custom-call(s32[3]{0:T(128)S(1)} %pad_add_fusion.place, bf16[1024,256]{1,0:T(8,128)(2,1)S(1)} %copy-done, f32[32,1024,128]{2,1,0:T(8,128)S(1)} %get-tuple-element.26.old_ref, ...), custom_call_target="tpu_custom_call", output_to_operand_aliasing={{0}: (2, {}), {1}: (3, {})} | custom-call | tf_op jit(solution)/shard_map/pallas_call | solution.py:428
  22.9 3.1 %collective-permute-done.5.points_ref = bf16[1024,256]{1,0:T(8,128)(2,1)S(1)} collective-permute-done((bf16[1024,256]{1,0:T(8,128)(2,1)S(1)}, bf16[1024,256]{1,0:T(8,128)(2,1)S(1)}, u32[]{:S(2)}, u32[]{:S(2)}) %collective-permute-start.5) | collective-permute-done | bytes 524320 | tf_op jit(solution)/shard_map/ppermute | solution.py:386
  26.0 1.9 %shard_map.70 = (f32[32,1024,128]{2,1,0:T(8,128)S(1)}, f32[1024,128]{1,0:T(8,128)S(1)}, f32[8,128]{1,0:T(8,128)S(1)}) custom-call(s32[3]{0:T(128)S(1)} %pad_add_fusion.place, bf16[1024,256]{1,0:T(8,128)(2,1)S(1)} %copy-done, f32[32,1024,128]{2,1,0:T(8,128)S(1)} %get-tuple-element.28.old_ref, ...), custom_call_target="tpu_custom_call", output_to_operand_aliasing={{0}: (2, {}), {1}: (3, {})} | custom-call | tf_op jit(solution)/shard_map/pallas_call | solution.py:431
  27.9 3.0 %collective-permute-start.6 = (f32[8,128]{1,0:T(8,128)S(1)}, f32[8,128]{1,0:T(8,128)S(1)}, u32[]{:S(2)}, u32[]{:S(2)}) collective-permute-start(f32[8,128]{1,0:T(8,128)S(1)} %get-tuple-element.31), channel_id=1, source_target_pairs={{0,1},{1,0},{2,3},{3,2},{4,5},{5,4},{6,7},{7,6},{8,9},{9,8},{10,11... | collective-permute-start | bytes 12296 | tf_op jit(solution)/shard_map/ppermute | solution.py:416
  31.8 3.9 %collective-permute-start.7 = (f32[8,128]{1,0:T(8,128)S(1)}, f32[8,128]{1,0:T(8,128)S(1)}, u32[]{:S(2)}, u32[]{:S(2)}) collective-permute-start(f32[8,128]{1,0:T(8,128)S(1)} %log_add_fusion.refs_0_), channel_id=1, source_target_pairs={{0,5},{1,4},{2,7},{3,6},{4,1},{5,0},{6,3},{7,2},{8,13},{9,12},{10,... | collective-permute-start | bytes 12296 | tf_op jit(solution)/shard_map/ppermute | solution.py:394
  36.5 2.2 %collective-permute-start.9 = (f32[8,128]{1,0:T(8,128)S(1)}, f32[8,128]{1,0:T(8,128)S(1)}, u32[]{:S(2)}, u32[]{:S(2)}) collective-permute-start(f32[8,128]{1,0:T(8,128)S(1)} %log_add_fusion.refs_0_), channel_id=1, source_target_pairs={{0,7},{1,6},{2,1},{3,0},{4,3},{5,2},{6,5},{7,4},{8,15},{9,14},{10,... | collective-permute-start | bytes 12296 | tf_op jit(solution)/shard_map/ppermute | solution.py:394
  39.9 3.1 %shard_map.71 = (f32[16,32,128]{2,1,0:T(8,128)S(1)}, f32[8,128]{1,0:T(8,128)S(1)}) custom-call(f32[32,1024,128]{2,1,0:T(8,128)S(1)} %get-tuple-element.30.t_ref, f32[8,128]{1,0:T(8,128)S(1)} %log_add_fusion.refs_0_, f32[8,128]{1,0:T(8,128)S(1)} %collective-permute-done.7.refs_1_, f32[8,128]{1,0:T(8,128)S(1)} %collective-permute-done.8.refs_2_, ...), custom_call_target="tpu_custom_call" | custom-call | tf_op jit(solution)/shard_map/pallas_call | solution.py:438
  43.0 15.7 %all_to_all.15.parts_ref = f32[16,32,128]{2,1,0:T(8,128)S(1)} all-to-all(f32[16,32,128]{2,1,0:T(8,128)S(1)} %get-tuple-element.32), channel_id=1, replica_groups=mesh['row_0'=4,'row_1'=4,'col_0'=4,'col_1'=2] {'row_0','row_1'}, dimensions={0} | all-to-all | bytes 524288 | tf_op jit(solution)/shard_map/all_to_all | solution.py:420
  58.8 3.5 %shard_map.72 = (f32[32,1024,128]{2,1,0:T(8,128)S(1)}, f32[8,128]{1,0:T(8,128)S(1)}, f32[32,128]{1,0:T(8,128)S(1)}) custom-call(f32[32,1024,128]{2,1,0:T(8,128)S(1)} %get-tuple-element.30.t_ref, f32[16,32,128]{2,1,0:T(8,128)S(1)} %all_to_all.15.parts_ref, f32[32,128]{1,0:T(8,128)S(1)} %bitcast.12, ...), custom_call_target="tpu_custom_call", output_to_operand_aliasing={{0}: (0, {})} | custom-call | tf_op jit(solution)/shard_map/pallas_call | solution.py:441
  62.3 1.6 %collective-permute-start.10 = (f32[8,128]{1,0:T(8,128)S(1)}, f32[8,128]{1,0:T(8,128)S(1)}, u32[]{:S(2)}, u32[]{:S(2)}) collective-permute-start(f32[8,128]{1,0:T(8,128)S(1)} %get-tuple-element.35), channel_id=1, source_target_pairs={{0,1},{1,0},{2,3},{3,2},{4,5},{5,4},{6,7},{7,6},{8,9},{9,8},{10,11... | collective-permute-start | bytes 12296 | tf_op jit(solution)/shard_map/ppermute | solution.py:416
  64.7 1.9 %collective-permute-start.11 = (f32[8,128]{1,0:T(8,128)S(1)}, f32[8,128]{1,0:T(8,128)S(1)}, u32[]{:S(2)}, u32[]{:S(2)}) collective-permute-start(f32[8,128]{1,0:T(8,128)S(1)} %add.29.refs_0_), channel_id=1, source_target_pairs={{0,5},{1,4},{2,7},{3,6},{4,1},{5,0},{6,3},{7,2},{8,13},{9,12},{10,... | collective-permute-start | bytes 12296 | tf_op jit(solution)/shard_map/ppermute | solution.py:394
  66.6 1.6 %collective-permute-start.12 = (f32[8,128]{1,0:T(8,128)S(1)}, f32[8,128]{1,0:T(8,128)S(1)}, u32[]{:S(2)}, u32[]{:S(2)}) collective-permute-start(f32[8,128]{1,0:T(8,128)S(1)} %add.29.refs_0_), channel_id=1, source_target_pairs={{0,3},{1,2},{2,5},{3,4},{4,7},{5,6},{6,1},{7,0},{8,11},{9,10},{10,... | collective-permute-start | bytes 12296 | tf_op jit(solution)/shard_map/ppermute | solution.py:394
  71.2 1.6 %shard_map.73 = f32[16,32,128]{2,1,0:T(8,128)S(1)} custom-call(f32[32,1024,128]{2,1,0:T(8,128)S(1)} %get-tuple-element.34.plan_ref, f32[8,128]{1,0:T(8,128)S(1)} %add.29.refs_0_, f32[8,128]{1,0:T(8,128)S(1)} %collective-permute-done.11.refs_1_, f32[8,128]{1,0:T(8,128)S(1)} %collective-permute-done.12.refs_2_, f32[8,128]{1,0:T(8,128)S(1)} %collective-permute-done.13.refs_3_, ...), custom_call_target="tpu_custom_call" | custom-call | tf_op jit(solution)/shard_map/pallas_call | solution.py:445
  72.8 10.8 %all_to_all.16.parts_ref = f32[16,32,128]{2,1,0:T(8,128)S(1)} all-to-all(f32[16,32,128]{2,1,0:T(8,128)S(1)} %shard_map.73), channel_id=1, replica_groups=mesh['row_0'=4,'row_1'=4,'col_0'=4,'col_1'=2] {'row_0','row_1'}, dimensions={0} | all-to-all | bytes 524288 | tf_op jit(solution)/shard_map/all_to_all | solution.py:420
  87.6 2.0 %collective-permute-start.15 = (f32[8,128]{1,0:T(8,128)S(1)}, f32[8,128]{1,0:T(8,128)S(1)}, u32[]{:S(2)}, u32[]{:S(2)}) collective-permute-start(f32[8,128]{1,0:T(8,128)S(1)} %add.30.refs_0_), channel_id=1, source_target_pairs={{0,5},{1,4},{2,7},{3,6},{4,1},{5,0},{6,3},{7,2},{8,13},{9,12},{10,... | collective-permute-start | bytes 12296 | tf_op jit(solution)/shard_map/ppermute | solution.py:394
  90.8 1.7 %collective-permute-start.17 = (f32[8,128]{1,0:T(8,128)S(1)}, f32[8,128]{1,0:T(8,128)S(1)}, u32[]{:S(2)}, u32[]{:S(2)}) collective-permute-start(f32[8,128]{1,0:T(8,128)S(1)} %add.30.refs_0_), channel_id=1, source_target_pairs={{0,7},{1,6},{2,1},{3,0},{4,3},{5,2},{6,5},{7,4},{8,15},{9,14},{10,... | collective-permute-start | bytes 12296 | tf_op jit(solution)/shard_map/ppermute | solution.py:394
  93.8 2.2 %shard_map.75 = (f32[16,40,128]{2,1,0:T(8,128)S(1)}, f32[8,128]{1,0:T(8,128)}) custom-call(f32[32,1024,128]{2,1,0:T(8,128)S(1)} %get-tuple-element.34.plan_ref, f32[8,128]{1,0:T(8,128)S(1)} %add.30.refs_0_, f32[8,128]{1,0:T(8,128)S(1)} %collective-permute-done.15.refs_1_, f32[8,128]{1,0:T(8,128)S(1)} %collective-permute-done.16.refs_2_, ...), custom_call_target="tpu_custom_call" | custom-call | tf_op jit(solution)/shard_map/pallas_call | solution.py:449
  96.0 11.5 %all_to_all.17.parts_ref = f32[16,40,128]{2,1,0:T(8,128)S(1)} all-to-all(f32[16,40,128]{2,1,0:T(8,128)S(1)} %get-tuple-element.38), channel_id=1, replica_groups=mesh['row_0'=4,'row_1'=4,'col_0'=4,'col_1'=2] {'row_0','row_1'}, dimensions={0} | all-to-all | bytes 655360 | tf_op jit(solution)/shard_map/all_to_all | solution.py:420
  111.8 2.2 %collective-permute-start.20 = (f32[8,128]{1,0:T(8,128)S(1)}, f32[8,128]{1,0:T(8,128)S(1)}, u32[]{:S(2)}, u32[]{:S(2)}) collective-permute-start(f32[8,128]{1,0:T(8,128)S(1)} %add.31), channel_id=1, source_target_pairs={{0,3},{1,2},{2,5},{3,4},{4,7},{5,6},{6,1},{7,0},{8,11},{9,10},{10,... | collective-permute-start | bytes 12296 | tf_op jit(solution)/shard_map/ppermute | solution.py:394
  (50 shorter events, 29.4 us)
Async XLA Ops:
  0.6 6.8 %collective-permute-start = (bf16[256,256]{1,0:T(8,128)(2,1)}, bf16[256,256]{1,0:T(8,128)(2,1)S(1)}, u32[]{:S(2)}, u32[]{:S(2)}) collective-permute-start(bf16[256,256]{1,0:T(8,128)(2,1)} %param.5), channel_id=1, source_target_pairs={{0,8},{1,33},{2,10},{3,35},{4,12},{5,37},{6,14},{7,39},{8,16},{9,4... | collective-permute-start | bytes 393224 | tf_op jit(solution)/shard_map/ppermute | solution.py:386
  2.8 6.9 %collective-permute-start.1 = (bf16[256,256]{1,0:T(8,128)(2,1)}, bf16[256,256]{1,0:T(8,128)(2,1)S(1)}, u32[]{:S(2)}, u32[]{:S(2)}) collective-permute-start(bf16[256,256]{1,0:T(8,128)(2,1)} %param.5), channel_id=1, source_target_pairs={{0,16},{1,65},{2,18},{3,67},{4,20},{5,69},{6,22},{7,71},{8,24},{9,... | collective-permute-start | bytes 393224 | tf_op jit(solution)/shard_map/ppermute | solution.py:386
  5.4 4.3 %collective-permute-start.2 = (bf16[256,256]{1,0:T(8,128)(2,1)}, bf16[256,256]{1,0:T(8,128)(2,1)S(1)}, u32[]{:S(2)}, u32[]{:S(2)}) collective-permute-start(bf16[256,256]{1,0:T(8,128)(2,1)} %param.5), channel_id=1, source_target_pairs={{0,24},{1,97},{2,26},{3,99},{4,28},{5,101},{6,30},{7,103},{8,0},{9... | collective-permute-start | bytes 393224 | tf_op jit(solution)/shard_map/ppermute | solution.py:386
  9.8 9.7 %collective-permute-start.3 = (bf16[1024,256]{1,0:T(8,128)(2,1)S(1)}, bf16[1024,256]{1,0:T(8,128)(2,1)S(1)}, u32[]{:S(2)}, u32[]{:S(2)}) collective-permute-start(bf16[1024,256]{1,0:T(8,128)(2,1)S(1)} %constant_dynamic-update-slice_fusion.points_ref), channel_id=1, source_target_pairs={{0,32},{1,9},{2,34},{3,11},{4,36},{5,13},{6,38},{7,15},{8,40},{9,1... | collective-permute-start | bytes 1572872 | tf_op jit(solution)/shard_map/ppermute | solution.py:386
  11.1 10.1 %collective-permute-start.4 = (bf16[1024,256]{1,0:T(8,128)(2,1)S(1)}, bf16[1024,256]{1,0:T(8,128)(2,1)S(1)}, u32[]{:S(2)}, u32[]{:S(2)}) collective-permute-start(bf16[1024,256]{1,0:T(8,128)(2,1)S(1)} %constant_dynamic-update-slice_fusion.points_ref), channel_id=1, source_target_pairs={{0,96},{1,25},{2,98},{3,27},{4,100},{5,29},{6,102},{7,31},{8,104},... | collective-permute-start | bytes 1572872 | tf_op jit(solution)/shard_map/ppermute | solution.py:386
  12.5 13.5 %collective-permute-start.5 = (bf16[1024,256]{1,0:T(8,128)(2,1)S(1)}, bf16[1024,256]{1,0:T(8,128)(2,1)S(1)}, u32[]{:S(2)}, u32[]{:S(2)}) collective-permute-start(bf16[1024,256]{1,0:T(8,128)(2,1)S(1)} %constant_dynamic-update-slice_fusion.points_ref), channel_id=1, source_target_pairs={{0,64},{1,17},{2,66},{3,19},{4,68},{5,21},{6,70},{7,23},{8,72},{9,... | collective-permute-start | bytes 1572872 | tf_op jit(solution)/shard_map/ppermute | solution.py:386
  14.1 1.0 copy-start
  21.2 18.7 %copy-start.2 = (f32[1024]{0:T(1024)S(1)}, f32[1024]{0:T(1024)}, u32[]{:S(2)}) copy-start(f32[1024]{0:T(1024)} %param.6) | copy-start | bytes 12292
  27.9 3.9 %collective-permute-start.6 = (f32[8,128]{1,0:T(8,128)S(1)}, f32[8,128]{1,0:T(8,128)S(1)}, u32[]{:S(2)}, u32[]{:S(2)}) collective-permute-start(f32[8,128]{1,0:T(8,128)S(1)} %get-tuple-element.31), channel_id=1, source_target_pairs={{0,1},{1,0},{2,3},{3,2},{4,5},{5,4},{6,7},{7,6},{8,9},{9,8},{10,11... | collective-permute-start | bytes 12296 | tf_op jit(solution)/shard_map/ppermute | solution.py:416
  31.8 6.9 %collective-permute-start.7 = (f32[8,128]{1,0:T(8,128)S(1)}, f32[8,128]{1,0:T(8,128)S(1)}, u32[]{:S(2)}, u32[]{:S(2)}) collective-permute-start(f32[8,128]{1,0:T(8,128)S(1)} %log_add_fusion.refs_0_), channel_id=1, source_target_pairs={{0,5},{1,4},{2,7},{3,6},{4,1},{5,0},{6,3},{7,2},{8,13},{9,12},{10,... | collective-permute-start | bytes 12296 | tf_op jit(solution)/shard_map/ppermute | solution.py:394
  35.7 4.2 %collective-permute-start.8 = (f32[8,128]{1,0:T(8,128)S(1)}, f32[8,128]{1,0:T(8,128)S(1)}, u32[]{:S(2)}, u32[]{:S(2)}) collective-permute-start(f32[8,128]{1,0:T(8,128)S(1)} %log_add_fusion.refs_0_), channel_id=1, source_target_pairs={{0,3},{1,2},{2,5},{3,4},{4,7},{5,6},{6,1},{7,0},{8,11},{9,10},{10,... | collective-permute-start | bytes 12296 | tf_op jit(solution)/shard_map/ppermute | solution.py:394
  36.5 3.5 %collective-permute-start.9 = (f32[8,128]{1,0:T(8,128)S(1)}, f32[8,128]{1,0:T(8,128)S(1)}, u32[]{:S(2)}, u32[]{:S(2)}) collective-permute-start(f32[8,128]{1,0:T(8,128)S(1)} %log_add_fusion.refs_0_), channel_id=1, source_target_pairs={{0,7},{1,6},{2,1},{3,0},{4,3},{5,2},{6,5},{7,4},{8,15},{9,14},{10,... | collective-permute-start | bytes 12296 | tf_op jit(solution)/shard_map/ppermute | solution.py:394
  62.3 2.4 %collective-permute-start.10 = (f32[8,128]{1,0:T(8,128)S(1)}, f32[8,128]{1,0:T(8,128)S(1)}, u32[]{:S(2)}, u32[]{:S(2)}) collective-permute-start(f32[8,128]{1,0:T(8,128)S(1)} %get-tuple-element.35), channel_id=1, source_target_pairs={{0,1},{1,0},{2,3},{3,2},{4,5},{5,4},{6,7},{7,6},{8,9},{9,8},{10,11... | collective-permute-start | bytes 12296 | tf_op jit(solution)/shard_map/ppermute | solution.py:416
  64.7 4.9 %collective-permute-start.11 = (f32[8,128]{1,0:T(8,128)S(1)}, f32[8,128]{1,0:T(8,128)S(1)}, u32[]{:S(2)}, u32[]{:S(2)}) collective-permute-start(f32[8,128]{1,0:T(8,128)S(1)} %add.29.refs_0_), channel_id=1, source_target_pairs={{0,5},{1,4},{2,7},{3,6},{4,1},{5,0},{6,3},{7,2},{8,13},{9,12},{10,... | collective-permute-start | bytes 12296 | tf_op jit(solution)/shard_map/ppermute | solution.py:394
  66.6 4.2 %collective-permute-start.12 = (f32[8,128]{1,0:T(8,128)S(1)}, f32[8,128]{1,0:T(8,128)S(1)}, u32[]{:S(2)}, u32[]{:S(2)}) collective-permute-start(f32[8,128]{1,0:T(8,128)S(1)} %add.29.refs_0_), channel_id=1, source_target_pairs={{0,3},{1,2},{2,5},{3,4},{4,7},{5,6},{6,1},{7,0},{8,11},{9,10},{10,... | collective-permute-start | bytes 12296 | tf_op jit(solution)/shard_map/ppermute | solution.py:394
  68.2 3.0 %collective-permute-start.13 = (f32[8,128]{1,0:T(8,128)S(1)}, f32[8,128]{1,0:T(8,128)S(1)}, u32[]{:S(2)}, u32[]{:S(2)}) collective-permute-start(f32[8,128]{1,0:T(8,128)S(1)} %add.29.refs_0_), channel_id=1, source_target_pairs={{0,7},{1,6},{2,1},{3,0},{4,3},{5,2},{6,5},{7,4},{8,15},{9,14},{10,... | collective-permute-start | bytes 12296 | tf_op jit(solution)/shard_map/ppermute | solution.py:394
  85.2 2.4 %collective-permute-start.14 = (f32[8,128]{1,0:T(8,128)S(1)}, f32[8,128]{1,0:T(8,128)S(1)}, u32[]{:S(2)}, u32[]{:S(2)}) collective-permute-start(f32[8,128]{1,0:T(8,128)S(1)} %shard_map.74), channel_id=1, source_target_pairs={{0,1},{1,0},{2,3},{3,2},{4,5},{5,4},{6,7},{7,6},{8,9},{9,8},{10,11... | collective-permute-start | bytes 12296 | tf_op jit(solution)/shard_map/ppermute | solution.py:416
  87.6 4.9 %collective-permute-start.15 = (f32[8,128]{1,0:T(8,128)S(1)}, f32[8,128]{1,0:T(8,128)S(1)}, u32[]{:S(2)}, u32[]{:S(2)}) collective-permute-start(f32[8,128]{1,0:T(8,128)S(1)} %add.30.refs_0_), channel_id=1, source_target_pairs={{0,5},{1,4},{2,7},{3,6},{4,1},{5,0},{6,3},{7,2},{8,13},{9,12},{10,... | collective-permute-start | bytes 12296 | tf_op jit(solution)/shard_map/ppermute | solution.py:394
  89.5 4.2 %collective-permute-start.16 = (f32[8,128]{1,0:T(8,128)S(1)}, f32[8,128]{1,0:T(8,128)S(1)}, u32[]{:S(2)}, u32[]{:S(2)}) collective-permute-start(f32[8,128]{1,0:T(8,128)S(1)} %add.30.refs_0_), channel_id=1, source_target_pairs={{0,3},{1,2},{2,5},{3,4},{4,7},{5,6},{6,1},{7,0},{8,11},{9,10},{10,... | collective-permute-start | bytes 12296 | tf_op jit(solution)/shard_map/ppermute | solution.py:394
  90.8 3.0 %collective-permute-start.17 = (f32[8,128]{1,0:T(8,128)S(1)}, f32[8,128]{1,0:T(8,128)S(1)}, u32[]{:S(2)}, u32[]{:S(2)}) collective-permute-start(f32[8,128]{1,0:T(8,128)S(1)} %add.30.refs_0_), channel_id=1, source_target_pairs={{0,7},{1,6},{2,1},{3,0},{4,3},{5,2},{6,5},{7,4},{8,15},{9,14},{10,... | collective-permute-start | bytes 12296 | tf_op jit(solution)/shard_map/ppermute | solution.py:394
  108.0 2.3 %collective-permute-start.18 = (f32[8,128]{1,0:T(8,128)S(1)}, f32[8,128]{1,0:T(8,128)S(1)}, u32[]{:S(2)}, u32[]{:S(2)}) collective-permute-start(f32[8,128]{1,0:T(8,128)S(1)} %get-tuple-element.42), channel_id=1, source_target_pairs={{0,1},{1,0},{2,3},{3,2},{4,5},{5,4},{6,7},{7,6},{8,9},{9,8},{10,11... | collective-permute-start | bytes 12296 | tf_op jit(solution)/shard_map/ppermute | solution.py:416
  110.4 4.5 %collective-permute-start.19 = (f32[8,128]{1,0:T(8,128)S(1)}, f32[8,128]{1,0:T(8,128)S(1)}, u32[]{:S(2)}, u32[]{:S(2)}) collective-permute-start(f32[8,128]{1,0:T(8,128)S(1)} %add.31), channel_id=1, source_target_pairs={{0,5},{1,4},{2,7},{3,6},{4,1},{5,0},{6,3},{7,2},{8,13},{9,12},{10,... | collective-permute-start | bytes 12296 | tf_op jit(solution)/shard_map/ppermute | solution.py:394
  111.8 4.2 %collective-permute-start.20 = (f32[8,128]{1,0:T(8,128)S(1)}, f32[8,128]{1,0:T(8,128)S(1)}, u32[]{:S(2)}, u32[]{:S(2)}) collective-permute-start(f32[8,128]{1,0:T(8,128)S(1)} %add.31), channel_id=1, source_target_pairs={{0,3},{1,2},{2,5},{3,4},{4,7},{5,6},{6,1},{7,0},{8,11},{9,10},{10,... | collective-permute-start | bytes 12296 | tf_op jit(solution)/shard_map/ppermute | solution.py:394
  114.0 3.0 %collective-permute-start.21 = (f32[8,128]{1,0:T(8,128)S(1)}, f32[8,128]{1,0:T(8,128)S(1)}, u32[]{:S(2)}, u32[]{:S(2)}) collective-permute-start(f32[8,128]{1,0:T(8,128)S(1)} %add.31), channel_id=1, source_target_pairs={{0,7},{1,6},{2,1},{3,0},{4,3},{5,2},{6,5},{7,4},{8,15},{9,14},{10,... | collective-permute-start | bytes 12296 | tf_op jit(solution)/shard_map/ppermute | solution.py:394
  (1 other events, 0.7 us)

commit v8 on v7

--- a/solution.py
+++ b/solution.py
@@ -10,9 +10,9 @@
 from jax.sharding import Mesh
 from jax.sharding import PartitionSpec as P
 
-ROW = ("row_0", "row_1")
+ROW = ("y_high", "y_low", "x_high", "x_low")
 COL = ("col_0", "col_1")
-COL_ROW = ("col_0", "col_1", "row_0", "row_1")
+ROW_PEERS = ("x_low", "x_high", "y_high", "y_low")
 
 EPS = 0.1
 WIDTH = 256
@@ -367,7 +367,7 @@
     other_ref[...] = sums[tiles:]
 
 
-ALL = ("row_0", "row_1", "col_0", "col_1")
+ALL = (*ROW, *COL)
 SIZES = (4, 4, 4, 2)
 
 
@@ -399,7 +399,7 @@
     row_tiles, column_tiles = rows // LANES, columns // LANES
     src_mass = log_src_mass.reshape(row_tiles, LANES)
     tgt_mass = log_tgt_mass.reshape(column_tiles, LANES)
-    place = jnp.stack([lax.axis_index(name) for name in ("row_0", "row_1", "col_1")])
+    place = jnp.stack([lax.axis_index(name) for name in (ROW[:2], ROW[2:], "col_1")])
     place = place.astype(jnp.int32)
     wide = pltpu.VMEM((rows, LANES), jnp.float32)
     big = pltpu.VMEM((column_tiles, rows, LANES), jnp.float32)
@@ -417,7 +417,7 @@
         return [both] + [crossed(both, k) for k in (2, 1, 3)]
 
     def over_row(value):
-        return lax.all_to_all(value, ROW, 0, 0, tiled=True)
+        return lax.all_to_all(value, ROW_PEERS, 0, 0, tiled=True)
 
     first = jnp.concatenate(turned(tgt_points, 0))
     pieces = turned(first, 1)
@@ -462,8 +462,8 @@
 
 
 def solution(mesh):
-    finer = Mesh(mesh.devices.reshape(4, 4, 4, 2), ("row_0", "row_1", "col_0", "col_1"))
-    placed = (P(ROW, None), P(COL_ROW, None), P(ROW), P(COL))
+    finer = Mesh(mesh.devices.reshape(2, 2, 2, 2, 4, 2), ALL)
+    placed = (P(ROW, None), P((*COL, *ROW), None), P(ROW), P(COL))
     return jax.shard_map(
         body, mesh=finer, in_specs=placed, out_specs=(P(ROW), P(COL), P()), check_vma=False
     )

time: 117 us -> 116 us (level)
  blocking collectives: 38 us -> 36.3 us
    ppermute x12, starting transfers between devices: 21 us -> 19.3 us  [crossed(): return lax.ppermute(value, ALL, pairs)]
    all_to_all x3, blocking collectives: 38 us -> 36.3 us  [over_row(): return lax.all_to_all(value, ROW_PEERS, 0, 0, tiled=True)]
  transfers between devices with their start and end apart: 22 -> 22, of which waited for: 13 -> 16; matrix products, arithmetic and copies ran while one was open for 1% -> 1% of each run, Pallas kernels for 6% -> 6%
where the time goes in v8:
time: 116 us
  starting transfers between devices  38.2 us (33%)
  blocking collectives  36.3 us (31%)
  Pallas kernels  21.4 us (18%)
  waiting for transfers between devices  15.8 us (14%)
  local copies, waits for them, and re-layouts  3.26 us (3%)
    all_to_all x3, blocking collectives, over_row(): return lax.all_to_all(value, ROW_PEERS, 0, 0, tiled=True)  36.3 us
    ppermute x12, starting transfers between devices, crossed(): return lax.ppermute(value, ALL, pairs)  19.3 us
    ppermute x6, starting transfers between devices, turned(): found[k] = lax.ppermute(value, ALL, pairs)  10.2 us
    ppermute x4, starting transfers between devices, over_col(): both = combine([value, lax.ppermute(value, 'col_1', [(0, 1), (1, 0)])])  8.73 us
    ppermute x12, waiting for transfers between devices, crossed(): return lax.ppermute(value, ALL, pairs)  7.13 us
    ppermute x6, waiting for transfers between devices, turned(): found[k] = lax.ppermute(value, ALL, pairs)  5.34 us
    pallas_call x1, Pallas kernels, body(): call(first_terms_kernel, (big, wide, wide, by_row), [SMEM] + [VMEM] * 3, [])  3.53 us
    pallas_call x1, Pallas kernels, body(): call(plan_kernel, (big, by_row, by_column), [VMEM] * 5, [wide, wide, line...  3.46 us
  transfers between devices with their start and end apart: 22, of which 16 were waited for; matrix products, arithmetic and copies ran while one was open for 1% of the time, Pallas kernels for 6%

profile of v8, /device:TPU:1, one launch (start us, length us, event | category | flops | bytes accessed | tf_op | source)
XLA Modules:
  0.0 115.8 jit_solution(7469242291997726457)
XLA Ops:
  0.6 2.2 %collective-permute-start = (bf16[256,256]{1,0:T(8,128)(2,1)}, bf16[256,256]{1,0:T(8,128)(2,1)S(1)}, u32[]{:S(2)}, u32[]{:S(2)}) collective-permute-start(bf16[256,256]{1,0:T(8,128)(2,1)} %param.5), channel_id=1, source_target_pairs={{0,8},{1,33},{2,10},{3,35},{4,12},{5,37},{6,14},{7,39},{8,16},{9,4... | collective-permute-start | bytes 393224 | tf_op jit(solution)/shard_map/ppermute | solution.py:386
  2.8 2.6 %collective-permute-start.1 = (bf16[256,256]{1,0:T(8,128)(2,1)}, bf16[256,256]{1,0:T(8,128)(2,1)S(1)}, u32[]{:S(2)}, u32[]{:S(2)}) collective-permute-start(bf16[256,256]{1,0:T(8,128)(2,1)} %param.5), channel_id=1, source_target_pairs={{0,16},{1,65},{2,18},{3,67},{4,20},{5,69},{6,22},{7,71},{8,24},{9,... | collective-permute-start | bytes 393224 | tf_op jit(solution)/shard_map/ppermute | solution.py:386
  7.5 2.2 %collective-permute-done.1 = bf16[256,256]{1,0:T(8,128)(2,1)S(1)} collective-permute-done((bf16[256,256]{1,0:T(8,128)(2,1)}, bf16[256,256]{1,0:T(8,128)(2,1)S(1)}, u32[]{:S(2)}, u32[]{:S(2)}) %collective-permute-start.1) | collective-permute-done | bytes 131104 | tf_op jit(solution)/shard_map/ppermute | solution.py:386
  15.9 3.5 %shard_map.67 = (f32[32,1024,128]{2,1,0:T(8,128)S(1)}, f32[1024,128]{1,0:T(8,128)S(1)}, f32[1024,128]{1,0:T(8,128)S(1)}, f32[8,128]{1,0:T(8,128)S(1)}) custom-call(s32[3]{0:T(128)S(1)} %pad_add_fusion.place, bf16[1024,256]{1,0:T(8,128)(2,1)S(1)} %copy-done, bf16[1024,256]{1,0:T(8,128)(2,1)S(1)} %constant_dynamic-update-slice_fusion.points_ref, ...), custom_call_target="tpu_custom_call" | custom-call | tf_op jit(solution)/shard_map/pallas_call | solution.py:424
  19.4 1.7 %shard_map.68 = (f32[32,1024,128]{2,1,0:T(8,128)S(1)}, f32[1024,128]{1,0:T(8,128)S(1)}) custom-call(s32[3]{0:T(128)S(1)} %pad_add_fusion.place, bf16[1024,256]{1,0:T(8,128)(2,1)S(1)} %copy-done, f32[32,1024,128]{2,1,0:T(8,128)S(1)} %get-tuple-element.23.old_ref, ...), custom_call_target="tpu_custom_call", output_to_operand_aliasing={{0}: (2, {}), {1}: (3, {})} | custom-call | tf_op jit(solution)/shard_map/pallas_call | solution.py:428
  21.2 1.7 %shard_map.69 = (f32[32,1024,128]{2,1,0:T(8,128)S(1)}, f32[1024,128]{1,0:T(8,128)S(1)}) custom-call(s32[3]{0:T(128)S(1)} %pad_add_fusion.place, bf16[1024,256]{1,0:T(8,128)(2,1)S(1)} %copy-done, f32[32,1024,128]{2,1,0:T(8,128)S(1)} %get-tuple-element.26.old_ref, ...), custom_call_target="tpu_custom_call", output_to_operand_aliasing={{0}: (2, {}), {1}: (3, {})} | custom-call | tf_op jit(solution)/shard_map/pallas_call | solution.py:428
  22.9 3.1 %collective-permute-done.5.points_ref = bf16[1024,256]{1,0:T(8,128)(2,1)S(1)} collective-permute-done((bf16[1024,256]{1,0:T(8,128)(2,1)S(1)}, bf16[1024,256]{1,0:T(8,128)(2,1)S(1)}, u32[]{:S(2)}, u32[]{:S(2)}) %collective-permute-start.5) | collective-permute-done | bytes 524320 | tf_op jit(solution)/shard_map/ppermute | solution.py:386
  26.0 1.9 %shard_map.70 = (f32[32,1024,128]{2,1,0:T(8,128)S(1)}, f32[1024,128]{1,0:T(8,128)S(1)}, f32[8,128]{1,0:T(8,128)S(1)}) custom-call(s32[3]{0:T(128)S(1)} %pad_add_fusion.place, bf16[1024,256]{1,0:T(8,128)(2,1)S(1)} %copy-done, f32[32,1024,128]{2,1,0:T(8,128)S(1)} %get-tuple-element.28.old_ref, ...), custom_call_target="tpu_custom_call", output_to_operand_aliasing={{0}: (2, {}), {1}: (3, {})} | custom-call | tf_op jit(solution)/shard_map/pallas_call | solution.py:431
  27.9 3.0 %collective-permute-start.6 = (f32[8,128]{1,0:T(8,128)S(1)}, f32[8,128]{1,0:T(8,128)S(1)}, u32[]{:S(2)}, u32[]{:S(2)}) collective-permute-start(f32[8,128]{1,0:T(8,128)S(1)} %get-tuple-element.31), channel_id=1, source_target_pairs={{0,1},{1,0},{2,3},{3,2},{4,5},{5,4},{6,7},{7,6},{8,9},{9,8},{10,11... | collective-permute-start | bytes 12296 | tf_op jit(solution)/shard_map/ppermute | solution.py:416
  31.8 3.9 %collective-permute-start.7 = (f32[8,128]{1,0:T(8,128)S(1)}, f32[8,128]{1,0:T(8,128)S(1)}, u32[]{:S(2)}, u32[]{:S(2)}) collective-permute-start(f32[8,128]{1,0:T(8,128)S(1)} %log_add_fusion.refs_0_), channel_id=1, source_target_pairs={{0,5},{1,4},{2,7},{3,6},{4,1},{5,0},{6,3},{7,2},{8,13},{9,12},{10,... | collective-permute-start | bytes 12296 | tf_op jit(solution)/shard_map/ppermute | solution.py:394
  36.5 2.2 %collective-permute-start.9 = (f32[8,128]{1,0:T(8,128)S(1)}, f32[8,128]{1,0:T(8,128)S(1)}, u32[]{:S(2)}, u32[]{:S(2)}) collective-permute-start(f32[8,128]{1,0:T(8,128)S(1)} %log_add_fusion.refs_0_), channel_id=1, source_target_pairs={{0,7},{1,6},{2,1},{3,0},{4,3},{5,2},{6,5},{7,4},{8,15},{9,14},{10,... | collective-permute-start | bytes 12296 | tf_op jit(solution)/shard_map/ppermute | solution.py:394
  39.9 3.1 %shard_map.71 = (f32[16,32,128]{2,1,0:T(8,128)S(1)}, f32[8,128]{1,0:T(8,128)S(1)}) custom-call(f32[32,1024,128]{2,1,0:T(8,128)S(1)} %get-tuple-element.30.t_ref, f32[8,128]{1,0:T(8,128)S(1)} %log_add_fusion.refs_0_, f32[8,128]{1,0:T(8,128)S(1)} %collective-permute-done.7.refs_1_, f32[8,128]{1,0:T(8,128)S(1)} %collective-permute-done.8.refs_2_, ...), custom_call_target="tpu_custom_call" | custom-call | tf_op jit(solution)/shard_map/pallas_call | solution.py:438
  43.0 14.9 %all_to_all.15.parts_ref = f32[16,32,128]{2,1,0:T(8,128)S(1)} all-to-all(f32[16,32,128]{2,1,0:T(8,128)S(1)} %get-tuple-element.32), channel_id=1, replica_groups=mesh['y_high'=2,'y_low'=2,'x_high'=2,'x_low'=2,'col_0'=4,'col_1'=2] {'x_..., dimensions={0} | all-to-all | bytes 524288 | tf_op jit(solution)/shard_map/all_to_all | solution.py:420
  57.9 3.5 %shard_map.72 = (f32[32,1024,128]{2,1,0:T(8,128)S(1)}, f32[8,128]{1,0:T(8,128)S(1)}, f32[32,128]{1,0:T(8,128)S(1)}) custom-call(f32[32,1024,128]{2,1,0:T(8,128)S(1)} %get-tuple-element.30.t_ref, f32[16,32,128]{2,1,0:T(8,128)S(1)} %all_to_all.15.parts_ref, f32[32,128]{1,0:T(8,128)S(1)} %bitcast.12, ...), custom_call_target="tpu_custom_call", output_to_operand_aliasing={{0}: (0, {})} | custom-call | tf_op jit(solution)/shard_map/pallas_call | solution.py:441
  61.4 1.9 %collective-permute-start.10 = (f32[8,128]{1,0:T(8,128)S(1)}, f32[8,128]{1,0:T(8,128)S(1)}, u32[]{:S(2)}, u32[]{:S(2)}) collective-permute-start(f32[8,128]{1,0:T(8,128)S(1)} %get-tuple-element.35), channel_id=1, source_target_pairs={{0,1},{1,0},{2,3},{3,2},{4,5},{5,4},{6,7},{7,6},{8,9},{9,8},{10,11... | collective-permute-start | bytes 12296 | tf_op jit(solution)/shard_map/ppermute | solution.py:416
  65.5 2.2 %collective-permute-start.12 = (f32[8,128]{1,0:T(8,128)S(1)}, f32[8,128]{1,0:T(8,128)S(1)}, u32[]{:S(2)}, u32[]{:S(2)}) collective-permute-start(f32[8,128]{1,0:T(8,128)S(1)} %add.37.refs_0_), channel_id=1, source_target_pairs={{0,3},{1,2},{2,5},{3,4},{4,7},{5,6},{6,1},{7,0},{8,11},{9,10},{10,... | collective-permute-start | bytes 12296 | tf_op jit(solution)/shard_map/ppermute | solution.py:394
  70.7 1.6 %shard_map.73 = f32[16,32,128]{2,1,0:T(8,128)S(1)} custom-call(f32[32,1024,128]{2,1,0:T(8,128)S(1)} %get-tuple-element.34.plan_ref, f32[8,128]{1,0:T(8,128)S(1)} %add.37.refs_0_, f32[8,128]{1,0:T(8,128)S(1)} %collective-permute-done.11.refs_1_, f32[8,128]{1,0:T(8,128)S(1)} %collective-permute-done.12.refs_2_, f32[8,128]{1,0:T(8,128)S(1)} %collective-permute-done.13.refs_3_, ...), custom_call_target="tpu_custom_call" | custom-call | tf_op jit(solution)/shard_map/pallas_call | solution.py:445
  72.3 10.4 %all_to_all.16.parts_ref = f32[16,32,128]{2,1,0:T(8,128)S(1)} all-to-all(f32[16,32,128]{2,1,0:T(8,128)S(1)} %shard_map.73), channel_id=1, replica_groups=mesh['y_high'=2,'y_low'=2,'x_high'=2,'x_low'=2,'col_0'=4,'col_1'=2] {'x_..., dimensions={0} | all-to-all | bytes 524288 | tf_op jit(solution)/shard_map/all_to_all | solution.py:420
  82.8 1.6 %shard_map.74 = f32[8,128]{1,0:T(8,128)S(1)} custom-call(f32[32,1024,128]{2,1,0:T(8,128)S(1)} %get-tuple-element.34.plan_ref, f32[16,32,128]{2,1,0:T(8,128)S(1)} %all_to_all.16.parts_ref, f32[32,128]{1,0:T(8,128)S(1)} %bitcast.13), custom_call_target="tpu_custom_call" | custom-call | tf_op jit(solution)/shard_map/pallas_call | solution.py:448
  84.3 1.9 %collective-permute-start.14 = (f32[8,128]{1,0:T(8,128)S(1)}, f32[8,128]{1,0:T(8,128)S(1)}, u32[]{:S(2)}, u32[]{:S(2)}) collective-permute-start(f32[8,128]{1,0:T(8,128)S(1)} %shard_map.74), channel_id=1, source_target_pairs={{0,1},{1,0},{2,3},{3,2},{4,5},{5,4},{6,7},{7,6},{8,9},{9,8},{10,11... | collective-permute-start | bytes 12296 | tf_op jit(solution)/shard_map/ppermute | solution.py:416
  87.8 1.9 %collective-permute-start.16 = (f32[8,128]{1,0:T(8,128)S(1)}, f32[8,128]{1,0:T(8,128)S(1)}, u32[]{:S(2)}, u32[]{:S(2)}) collective-permute-start(f32[8,128]{1,0:T(8,128)S(1)} %add.38.refs_0_), channel_id=1, source_target_pairs={{0,3},{1,2},{2,5},{3,4},{4,7},{5,6},{6,1},{7,0},{8,11},{9,10},{10,... | collective-permute-start | bytes 12296 | tf_op jit(solution)/shard_map/ppermute | solution.py:394
  92.7 2.2 %shard_map.75 = (f32[16,40,128]{2,1,0:T(8,128)S(1)}, f32[8,128]{1,0:T(8,128)}) custom-call(f32[32,1024,128]{2,1,0:T(8,128)S(1)} %get-tuple-element.34.plan_ref, f32[8,128]{1,0:T(8,128)S(1)} %add.38.refs_0_, f32[8,128]{1,0:T(8,128)S(1)} %collective-permute-done.15.refs_1_, f32[8,128]{1,0:T(8,128)S(1)} %collective-permute-done.16.refs_2_, ...), custom_call_target="tpu_custom_call" | custom-call | tf_op jit(solution)/shard_map/pallas_call | solution.py:449
  94.9 11.0 %all_to_all.17.parts_ref = f32[16,40,128]{2,1,0:T(8,128)S(1)} all-to-all(f32[16,40,128]{2,1,0:T(8,128)S(1)} %get-tuple-element.38), channel_id=1, replica_groups=mesh['y_high'=2,'y_low'=2,'x_high'=2,'x_low'=2,'col_0'=4,'col_1'=2] {'x_..., dimensions={0} | all-to-all | bytes 655360 | tf_op jit(solution)/shard_map/all_to_all | solution.py:420
  106.5 1.9 %collective-permute-start.18 = (f32[8,128]{1,0:T(8,128)S(1)}, f32[8,128]{1,0:T(8,128)S(1)}, u32[]{:S(2)}, u32[]{:S(2)}) collective-permute-start(f32[8,128]{1,0:T(8,128)S(1)} %get-tuple-element.42), channel_id=1, source_target_pairs={{0,1},{1,0},{2,3},{3,2},{4,5},{5,4},{6,7},{7,6},{8,9},{9,8},{10,11... | collective-permute-start | bytes 12296 | tf_op jit(solution)/shard_map/ppermute | solution.py:416
  (50 shorter events, 29.0 us)
Async XLA Ops:
  0.6 6.8 %collective-permute-start = (bf16[256,256]{1,0:T(8,128)(2,1)}, bf16[256,256]{1,0:T(8,128)(2,1)S(1)}, u32[]{:S(2)}, u32[]{:S(2)}) collective-permute-start(bf16[256,256]{1,0:T(8,128)(2,1)} %param.5), channel_id=1, source_target_pairs={{0,8},{1,33},{2,10},{3,35},{4,12},{5,37},{6,14},{7,39},{8,16},{9,4... | collective-permute-start | bytes 393224 | tf_op jit(solution)/shard_map/ppermute | solution.py:386
  2.8 6.9 %collective-permute-start.1 = (bf16[256,256]{1,0:T(8,128)(2,1)}, bf16[256,256]{1,0:T(8,128)(2,1)S(1)}, u32[]{:S(2)}, u32[]{:S(2)}) collective-permute-start(bf16[256,256]{1,0:T(8,128)(2,1)} %param.5), channel_id=1, source_target_pairs={{0,16},{1,65},{2,18},{3,67},{4,20},{5,69},{6,22},{7,71},{8,24},{9,... | collective-permute-start | bytes 393224 | tf_op jit(solution)/shard_map/ppermute | solution.py:386
  5.4 4.3 %collective-permute-start.2 = (bf16[256,256]{1,0:T(8,128)(2,1)}, bf16[256,256]{1,0:T(8,128)(2,1)S(1)}, u32[]{:S(2)}, u32[]{:S(2)}) collective-permute-start(bf16[256,256]{1,0:T(8,128)(2,1)} %param.5), channel_id=1, source_target_pairs={{0,24},{1,97},{2,26},{3,99},{4,28},{5,101},{6,30},{7,103},{8,0},{9... | collective-permute-start | bytes 393224 | tf_op jit(solution)/shard_map/ppermute | solution.py:386
  9.8 9.7 %collective-permute-start.3 = (bf16[1024,256]{1,0:T(8,128)(2,1)S(1)}, bf16[1024,256]{1,0:T(8,128)(2,1)S(1)}, u32[]{:S(2)}, u32[]{:S(2)}) collective-permute-start(bf16[1024,256]{1,0:T(8,128)(2,1)S(1)} %constant_dynamic-update-slice_fusion.points_ref), channel_id=1, source_target_pairs={{0,32},{1,9},{2,34},{3,11},{4,36},{5,13},{6,38},{7,15},{8,40},{9,1... | collective-permute-start | bytes 1572872 | tf_op jit(solution)/shard_map/ppermute | solution.py:386
  11.1 10.1 %collective-permute-start.4 = (bf16[1024,256]{1,0:T(8,128)(2,1)S(1)}, bf16[1024,256]{1,0:T(8,128)(2,1)S(1)}, u32[]{:S(2)}, u32[]{:S(2)}) collective-permute-start(bf16[1024,256]{1,0:T(8,128)(2,1)S(1)} %constant_dynamic-update-slice_fusion.points_ref), channel_id=1, source_target_pairs={{0,96},{1,25},{2,98},{3,27},{4,100},{5,29},{6,102},{7,31},{8,104},... | collective-permute-start | bytes 1572872 | tf_op jit(solution)/shard_map/ppermute | solution.py:386
  12.5 13.5 %collective-permute-start.5 = (bf16[1024,256]{1,0:T(8,128)(2,1)S(1)}, bf16[1024,256]{1,0:T(8,128)(2,1)S(1)}, u32[]{:S(2)}, u32[]{:S(2)}) collective-permute-start(bf16[1024,256]{1,0:T(8,128)(2,1)S(1)} %constant_dynamic-update-slice_fusion.points_ref), channel_id=1, source_target_pairs={{0,64},{1,17},{2,66},{3,19},{4,68},{5,21},{6,70},{7,23},{8,72},{9,... | collective-permute-start | bytes 1572872 | tf_op jit(solution)/shard_map/ppermute | solution.py:386
  14.1 1.0 copy-start
  21.2 18.7 %copy-start.2 = (f32[1024]{0:T(1024)S(1)}, f32[1024]{0:T(1024)}, u32[]{:S(2)}) copy-start(f32[1024]{0:T(1024)} %param.6) | copy-start | bytes 12292
  27.9 3.9 %collective-permute-start.6 = (f32[8,128]{1,0:T(8,128)S(1)}, f32[8,128]{1,0:T(8,128)S(1)}, u32[]{:S(2)}, u32[]{:S(2)}) collective-permute-start(f32[8,128]{1,0:T(8,128)S(1)} %get-tuple-element.31), channel_id=1, source_target_pairs={{0,1},{1,0},{2,3},{3,2},{4,5},{5,4},{6,7},{7,6},{8,9},{9,8},{10,11... | collective-permute-start | bytes 12296 | tf_op jit(solution)/shard_map/ppermute | solution.py:416
  31.8 6.9 %collective-permute-start.7 = (f32[8,128]{1,0:T(8,128)S(1)}, f32[8,128]{1,0:T(8,128)S(1)}, u32[]{:S(2)}, u32[]{:S(2)}) collective-permute-start(f32[8,128]{1,0:T(8,128)S(1)} %log_add_fusion.refs_0_), channel_id=1, source_target_pairs={{0,5},{1,4},{2,7},{3,6},{4,1},{5,0},{6,3},{7,2},{8,13},{9,12},{10,... | collective-permute-start | bytes 12296 | tf_op jit(solution)/shard_map/ppermute | solution.py:394
  35.7 4.2 %collective-permute-start.8 = (f32[8,128]{1,0:T(8,128)S(1)}, f32[8,128]{1,0:T(8,128)S(1)}, u32[]{:S(2)}, u32[]{:S(2)}) collective-permute-start(f32[8,128]{1,0:T(8,128)S(1)} %log_add_fusion.refs_0_), channel_id=1, source_target_pairs={{0,3},{1,2},{2,5},{3,4},{4,7},{5,6},{6,1},{7,0},{8,11},{9,10},{10,... | collective-permute-start | bytes 12296 | tf_op jit(solution)/shard_map/ppermute | solution.py:394
  36.5 3.5 %collective-permute-start.9 = (f32[8,128]{1,0:T(8,128)S(1)}, f32[8,128]{1,0:T(8,128)S(1)}, u32[]{:S(2)}, u32[]{:S(2)}) collective-permute-start(f32[8,128]{1,0:T(8,128)S(1)} %log_add_fusion.refs_0_), channel_id=1, source_target_pairs={{0,7},{1,6},{2,1},{3,0},{4,3},{5,2},{6,5},{7,4},{8,15},{9,14},{10,... | collective-permute-start | bytes 12296 | tf_op jit(solution)/shard_map/ppermute | solution.py:394
  61.4 2.7 %collective-permute-start.10 = (f32[8,128]{1,0:T(8,128)S(1)}, f32[8,128]{1,0:T(8,128)S(1)}, u32[]{:S(2)}, u32[]{:S(2)}) collective-permute-start(f32[8,128]{1,0:T(8,128)S(1)} %get-tuple-element.35), channel_id=1, source_target_pairs={{0,1},{1,0},{2,3},{3,2},{4,5},{5,4},{6,7},{7,6},{8,9},{9,8},{10,11... | collective-permute-start | bytes 12296 | tf_op jit(solution)/shard_map/ppermute | solution.py:416
  64.1 4.5 %collective-permute-start.11 = (f32[8,128]{1,0:T(8,128)S(1)}, f32[8,128]{1,0:T(8,128)S(1)}, u32[]{:S(2)}, u32[]{:S(2)}) collective-permute-start(f32[8,128]{1,0:T(8,128)S(1)} %add.37.refs_0_), channel_id=1, source_target_pairs={{0,5},{1,4},{2,7},{3,6},{4,1},{5,0},{6,3},{7,2},{8,13},{9,12},{10,... | collective-permute-start | bytes 12296 | tf_op jit(solution)/shard_map/ppermute | solution.py:394
  65.5 4.2 %collective-permute-start.12 = (f32[8,128]{1,0:T(8,128)S(1)}, f32[8,128]{1,0:T(8,128)S(1)}, u32[]{:S(2)}, u32[]{:S(2)}) collective-permute-start(f32[8,128]{1,0:T(8,128)S(1)} %add.37.refs_0_), channel_id=1, source_target_pairs={{0,3},{1,2},{2,5},{3,4},{4,7},{5,6},{6,1},{7,0},{8,11},{9,10},{10,... | collective-permute-start | bytes 12296 | tf_op jit(solution)/shard_map/ppermute | solution.py:394
  67.7 3.0 %collective-permute-start.13 = (f32[8,128]{1,0:T(8,128)S(1)}, f32[8,128]{1,0:T(8,128)S(1)}, u32[]{:S(2)}, u32[]{:S(2)}) collective-permute-start(f32[8,128]{1,0:T(8,128)S(1)} %add.37.refs_0_), channel_id=1, source_target_pairs={{0,7},{1,6},{2,1},{3,0},{4,3},{5,2},{6,5},{7,4},{8,15},{9,14},{10,... | collective-permute-start | bytes 12296 | tf_op jit(solution)/shard_map/ppermute | solution.py:394
  84.3 2.7 %collective-permute-start.14 = (f32[8,128]{1,0:T(8,128)S(1)}, f32[8,128]{1,0:T(8,128)S(1)}, u32[]{:S(2)}, u32[]{:S(2)}) collective-permute-start(f32[8,128]{1,0:T(8,128)S(1)} %shard_map.74), channel_id=1, source_target_pairs={{0,1},{1,0},{2,3},{3,2},{4,5},{5,4},{6,7},{7,6},{8,9},{9,8},{10,11... | collective-permute-start | bytes 12296 | tf_op jit(solution)/shard_map/ppermute | solution.py:416
  87.1 4.5 %collective-permute-start.15 = (f32[8,128]{1,0:T(8,128)S(1)}, f32[8,128]{1,0:T(8,128)S(1)}, u32[]{:S(2)}, u32[]{:S(2)}) collective-permute-start(f32[8,128]{1,0:T(8,128)S(1)} %add.38.refs_0_), channel_id=1, source_target_pairs={{0,5},{1,4},{2,7},{3,6},{4,1},{5,0},{6,3},{7,2},{8,13},{9,12},{10,... | collective-permute-start | bytes 12296 | tf_op jit(solution)/shard_map/ppermute | solution.py:394
  87.8 4.2 %collective-permute-start.16 = (f32[8,128]{1,0:T(8,128)S(1)}, f32[8,128]{1,0:T(8,128)S(1)}, u32[]{:S(2)}, u32[]{:S(2)}) collective-permute-start(f32[8,128]{1,0:T(8,128)S(1)} %add.38.refs_0_), channel_id=1, source_target_pairs={{0,3},{1,2},{2,5},{3,4},{4,7},{5,6},{6,1},{7,0},{8,11},{9,10},{10,... | collective-permute-start | bytes 12296 | tf_op jit(solution)/shard_map/ppermute | solution.py:394
  89.7 3.0 %collective-permute-start.17 = (f32[8,128]{1,0:T(8,128)S(1)}, f32[8,128]{1,0:T(8,128)S(1)}, u32[]{:S(2)}, u32[]{:S(2)}) collective-permute-start(f32[8,128]{1,0:T(8,128)S(1)} %add.38.refs_0_), channel_id=1, source_target_pairs={{0,7},{1,6},{2,1},{3,0},{4,3},{5,2},{6,5},{7,4},{8,15},{9,14},{10,... | collective-permute-start | bytes 12296 | tf_op jit(solution)/shard_map/ppermute | solution.py:394
  106.5 2.7 %collective-permute-start.18 = (f32[8,128]{1,0:T(8,128)S(1)}, f32[8,128]{1,0:T(8,128)S(1)}, u32[]{:S(2)}, u32[]{:S(2)}) collective-permute-start(f32[8,128]{1,0:T(8,128)S(1)} %get-tuple-element.42), channel_id=1, source_target_pairs={{0,1},{1,0},{2,3},{3,2},{4,5},{5,4},{6,7},{7,6},{8,9},{9,8},{10,11... | collective-permute-start | bytes 12296 | tf_op jit(solution)/shard_map/ppermute | solution.py:416
  109.3 4.5 %collective-permute-start.19 = (f32[8,128]{1,0:T(8,128)S(1)}, f32[8,128]{1,0:T(8,128)S(1)}, u32[]{:S(2)}, u32[]{:S(2)}) collective-permute-start(f32[8,128]{1,0:T(8,128)S(1)} %add.39), channel_id=1, source_target_pairs={{0,5},{1,4},{2,7},{3,6},{4,1},{5,0},{6,3},{7,2},{8,13},{9,12},{10,... | collective-permute-start | bytes 12296 | tf_op jit(solution)/shard_map/ppermute | solution.py:394
  110.7 4.2 %collective-permute-start.20 = (f32[8,128]{1,0:T(8,128)S(1)}, f32[8,128]{1,0:T(8,128)S(1)}, u32[]{:S(2)}, u32[]{:S(2)}) collective-permute-start(f32[8,128]{1,0:T(8,128)S(1)} %add.39), channel_id=1, source_target_pairs={{0,3},{1,2},{2,5},{3,4},{4,7},{5,6},{6,1},{7,0},{8,11},{9,10},{10,... | collective-permute-start | bytes 12296 | tf_op jit(solution)/shard_map/ppermute | solution.py:394
  112.2 3.0 %collective-permute-start.21 = (f32[8,128]{1,0:T(8,128)S(1)}, f32[8,128]{1,0:T(8,128)S(1)}, u32[]{:S(2)}, u32[]{:S(2)}) collective-permute-start(f32[8,128]{1,0:T(8,128)S(1)} %add.39), channel_id=1, source_target_pairs={{0,7},{1,6},{2,1},{3,0},{4,3},{5,2},{6,5},{7,4},{8,15},{9,14},{10,... | collective-permute-start | bytes 12296 | tf_op jit(solution)/shard_map/ppermute | solution.py:394
  (1 other events, 0.7 us)

commit v9 on v7

--- a/solution.py
+++ b/solution.py
@@ -349,12 +349,12 @@
     out_ref, potential_ref, wide_ref, line_ref = refs[7:]
     sums = add_all(values(parts))
     mass = mass_ref[...]
-    column_sums(plan_ref, jnp.exp(mass) / sums, line_ref, wide_ref)
     squares = squares_ref[...] / (WIDTH * EPS)
     potential = -EPS * (lse_ref[...] + jnp.log(sums) - mass - squares)
     potential_ref[...] = potential
     tiles = plan_ref.shape[0]
     line_ref[tiles:, :] = jnp.broadcast_to(jnp.sum(potential), (8, LANES))
+    column_sums(plan_ref, jnp.exp(mass) / sums, line_ref, wide_ref)
     copies(out_ref, line_ref[...])
 
 
@@ -424,17 +424,17 @@
     terms, top, sums, squares = call(
         first_terms_kernel, (big, wide, wide, by_row), [SMEM] + [VMEM] * 3, []
     )(place, src_points, first, tgt_mass)
-    for k in (1, 3):
+    for k in (1, 2):
         terms, sums = call(
             functools.partial(more_terms_kernel, k), (big, wide), [SMEM] + [VMEM] * 6, [], {2: 0, 3: 1}
         )(place, src_points, resident(terms), resident(sums), resident(top), pieces[k], tgt_mass)
     terms, sums, lse = call(
-        functools.partial(last_terms_kernel, 2),
+        functools.partial(last_terms_kernel, 3),
         (big, wide, by_row),
         [SMEM] + [VMEM] * 6,
         [wide],
         {2: 0, 3: 1},
-    )(place, src_points, resident(terms), resident(sums), resident(top), pieces[2], tgt_mass)
+    )(place, src_points, resident(terms), resident(sums), resident(top), pieces[3], tgt_mass)
     lse, src_lse = call(column_kernel, (columns_out, by_row), [VMEM] * 6, [wide, line])(
         resident(terms), *over_col(lse, lse_all), src_mass
     )

time: 117 us -> 116 us (level)
  blocking collectives: 38 us -> 36 us
  waiting for transfers between devices: 15.2 us -> 16.8 us
  starting transfers between devices: 38.8 us -> 37.6 us
    all_to_all x3, blocking collectives: 38 us -> 36 us  [over_row(): return lax.all_to_all(value, ROW, 0, 0, tiled=True)]
    ppermute x12, starting transfers between devices: 21 us -> 19.3 us  [crossed(): return lax.ppermute(value, ALL, pairs)]
  transfers between devices with their start and end apart: 22 -> 22, of which waited for: 13 -> 16; matrix products, arithmetic and copies ran while one was open for 1% -> 1% of each run, Pallas kernels for 6% -> 6%
where the time goes in v9:
time: 116 us
  starting transfers between devices  37.6 us (32%)
  blocking collectives  36 us (31%)
  Pallas kernels  21.3 us (18%)
  waiting for transfers between devices  16.8 us (14%)
  local copies, waits for them, and re-layouts  3.25 us (3%)
    all_to_all x3, blocking collectives, over_row(): return lax.all_to_all(value, ROW, 0, 0, tiled=True)  36 us
    ppermute x12, starting transfers between devices, crossed(): return lax.ppermute(value, ALL, pairs)  19.3 us
    ppermute x6, starting transfers between devices, turned(): found[k] = lax.ppermute(value, ALL, pairs)  10.8 us
    ppermute x4, starting transfers between devices, over_col(): both = combine([value, lax.ppermute(value, 'col_1', [(0, 1), (1, 0)])])  7.49 us
    ppermute x12, waiting for transfers between devices, crossed(): return lax.ppermute(value, ALL, pairs)  7.07 us
    ppermute x6, waiting for transfers between devices, turned(): found[k] = lax.ppermute(value, ALL, pairs)  6.48 us
    pallas_call x1, Pallas kernels, body(): call(first_terms_kernel, (big, wide, wide, by_row), [SMEM] + [VMEM] * 3, [])  3.53 us
    pallas_call x1, Pallas kernels, body(): call(plan_kernel, (big, by_row, by_column), [VMEM] * 5, [wide, wide, line...  3.46 us
  transfers between devices with their start and end apart: 22, of which 16 were waited for; matrix products, arithmetic and copies ran while one was open for 1% of the time, Pallas kernels for 6%

profile of v9, /device:TPU:1, one launch (start us, length us, event | category | flops | bytes accessed | tf_op | source)
XLA Modules:
  0.0 115.9 jit_solution(16696819073186388411)
XLA Ops:
  0.6 2.2 %collective-permute-start = (bf16[256,256]{1,0:T(8,128)(2,1)}, bf16[256,256]{1,0:T(8,128)(2,1)S(1)}, u32[]{:S(2)}, u32[]{:S(2)}) collective-permute-start(bf16[256,256]{1,0:T(8,128)(2,1)} %param.5), channel_id=1, source_target_pairs={{0,8},{1,33},{2,10},{3,35},{4,12},{5,37},{6,14},{7,39},{8,16},{9,4... | collective-permute-start | bytes 393224 | tf_op jit(solution)/shard_map/ppermute | solution.py:386
  2.8 2.6 %collective-permute-start.1 = (bf16[256,256]{1,0:T(8,128)(2,1)}, bf16[256,256]{1,0:T(8,128)(2,1)S(1)}, u32[]{:S(2)}, u32[]{:S(2)}) collective-permute-start(bf16[256,256]{1,0:T(8,128)(2,1)} %param.5), channel_id=1, source_target_pairs={{0,16},{1,65},{2,18},{3,67},{4,20},{5,69},{6,22},{7,71},{8,24},{9,... | collective-permute-start | bytes 393224 | tf_op jit(solution)/shard_map/ppermute | solution.py:386
  7.5 2.2 %collective-permute-done.1 = bf16[256,256]{1,0:T(8,128)(2,1)S(1)} collective-permute-done((bf16[256,256]{1,0:T(8,128)(2,1)}, bf16[256,256]{1,0:T(8,128)(2,1)S(1)}, u32[]{:S(2)}, u32[]{:S(2)}) %collective-permute-start.1) | collective-permute-done | bytes 131104 | tf_op jit(solution)/shard_map/ppermute | solution.py:386
  11.1 2.5 %collective-permute-start.4 = (bf16[1024,256]{1,0:T(8,128)(2,1)S(1)}, bf16[1024,256]{1,0:T(8,128)(2,1)S(1)}, u32[]{:S(2)}, u32[]{:S(2)}) collective-permute-start(bf16[1024,256]{1,0:T(8,128)(2,1)S(1)} %constant_dynamic-update-slice_fusion.points_ref), channel_id=1, source_target_pairs={{0,64},{1,17},{2,66},{3,19},{4,68},{5,21},{6,70},{7,23},{8,72},{9,... | collective-permute-start | bytes 1572872 | tf_op jit(solution)/shard_map/ppermute | solution.py:386
  16.5 3.5 %shard_map.67 = (f32[32,1024,128]{2,1,0:T(8,128)S(1)}, f32[1024,128]{1,0:T(8,128)S(1)}, f32[1024,128]{1,0:T(8,128)S(1)}, f32[8,128]{1,0:T(8,128)S(1)}) custom-call(s32[3]{0:T(128)S(1)} %pad_add_fusion.place, bf16[1024,256]{1,0:T(8,128)(2,1)S(1)} %copy-done, bf16[1024,256]{1,0:T(8,128)(2,1)S(1)} %constant_dynamic-update-slice_fusion.points_ref, ...), custom_call_target="tpu_custom_call" | custom-call | tf_op jit(solution)/shard_map/pallas_call | solution.py:424
  20.1 1.7 %shard_map.68 = (f32[32,1024,128]{2,1,0:T(8,128)S(1)}, f32[1024,128]{1,0:T(8,128)S(1)}) custom-call(s32[3]{0:T(128)S(1)} %pad_add_fusion.place, bf16[1024,256]{1,0:T(8,128)(2,1)S(1)} %copy-done, f32[32,1024,128]{2,1,0:T(8,128)S(1)} %get-tuple-element.23.old_ref, ...), custom_call_target="tpu_custom_call", output_to_operand_aliasing={{0}: (2, {}), {1}: (3, {})} | custom-call | tf_op jit(solution)/shard_map/pallas_call | solution.py:428
  21.8 4.2 %collective-permute-done.4.points_ref = bf16[1024,256]{1,0:T(8,128)(2,1)S(1)} collective-permute-done((bf16[1024,256]{1,0:T(8,128)(2,1)S(1)}, bf16[1024,256]{1,0:T(8,128)(2,1)S(1)}, u32[]{:S(2)}, u32[]{:S(2)}) %collective-permute-start.4) | collective-permute-done | bytes 524320 | tf_op jit(solution)/shard_map/ppermute | solution.py:386
  26.0 1.7 %shard_map.69 = (f32[32,1024,128]{2,1,0:T(8,128)S(1)}, f32[1024,128]{1,0:T(8,128)S(1)}) custom-call(s32[3]{0:T(128)S(1)} %pad_add_fusion.place, bf16[1024,256]{1,0:T(8,128)(2,1)S(1)} %copy-done, f32[32,1024,128]{2,1,0:T(8,128)S(1)} %get-tuple-element.26.old_ref, ...), custom_call_target="tpu_custom_call", output_to_operand_aliasing={{0}: (2, {}), {1}: (3, {})} | custom-call | tf_op jit(solution)/shard_map/pallas_call | solution.py:428
  27.7 1.9 %shard_map.70 = (f32[32,1024,128]{2,1,0:T(8,128)S(1)}, f32[1024,128]{1,0:T(8,128)S(1)}, f32[8,128]{1,0:T(8,128)S(1)}) custom-call(s32[3]{0:T(128)S(1)} %pad_add_fusion.place, bf16[1024,256]{1,0:T(8,128)(2,1)S(1)} %copy-done, f32[32,1024,128]{2,1,0:T(8,128)S(1)} %get-tuple-element.28.old_ref, ...), custom_call_target="tpu_custom_call", output_to_operand_aliasing={{0}: (2, {}), {1}: (3, {})} | custom-call | tf_op jit(solution)/shard_map/pallas_call | solution.py:431
  29.6 3.0 %collective-permute-start.6 = (f32[8,128]{1,0:T(8,128)S(1)}, f32[8,128]{1,0:T(8,128)S(1)}, u32[]{:S(2)}, u32[]{:S(2)}) collective-permute-start(f32[8,128]{1,0:T(8,128)S(1)} %get-tuple-element.31), channel_id=1, source_target_pairs={{0,1},{1,0},{2,3},{3,2},{4,5},{5,4},{6,7},{7,6},{8,9},{9,8},{10,11... | collective-permute-start | bytes 12296 | tf_op jit(solution)/shard_map/ppermute | solution.py:416
  33.5 3.9 %collective-permute-start.7 = (f32[8,128]{1,0:T(8,128)S(1)}, f32[8,128]{1,0:T(8,128)S(1)}, u32[]{:S(2)}, u32[]{:S(2)}) collective-permute-start(f32[8,128]{1,0:T(8,128)S(1)} %log_add_fusion.refs_0_), channel_id=1, source_target_pairs={{0,5},{1,4},{2,7},{3,6},{4,1},{5,0},{6,3},{7,2},{8,13},{9,12},{10,... | collective-permute-start | bytes 12296 | tf_op jit(solution)/shard_map/ppermute | solution.py:394
  38.2 2.2 %collective-permute-start.9 = (f32[8,128]{1,0:T(8,128)S(1)}, f32[8,128]{1,0:T(8,128)S(1)}, u32[]{:S(2)}, u32[]{:S(2)}) collective-permute-start(f32[8,128]{1,0:T(8,128)S(1)} %log_add_fusion.refs_0_), channel_id=1, source_target_pairs={{0,7},{1,6},{2,1},{3,0},{4,3},{5,2},{6,5},{7,4},{8,15},{9,14},{10,... | collective-permute-start | bytes 12296 | tf_op jit(solution)/shard_map/ppermute | solution.py:394
  41.6 3.1 %shard_map.71 = (f32[16,32,128]{2,1,0:T(8,128)S(1)}, f32[8,128]{1,0:T(8,128)S(1)}) custom-call(f32[32,1024,128]{2,1,0:T(8,128)S(1)} %get-tuple-element.30.t_ref, f32[8,128]{1,0:T(8,128)S(1)} %log_add_fusion.refs_0_, f32[8,128]{1,0:T(8,128)S(1)} %collective-permute-done.7.refs_1_, f32[8,128]{1,0:T(8,128)S(1)} %collective-permute-done.8.refs_2_, ...), custom_call_target="tpu_custom_call" | custom-call | tf_op jit(solution)/shard_map/pallas_call | solution.py:438
  44.8 13.8 %all_to_all.15.parts_ref = f32[16,32,128]{2,1,0:T(8,128)S(1)} all-to-all(f32[16,32,128]{2,1,0:T(8,128)S(1)} %get-tuple-element.32), channel_id=1, replica_groups=mesh['row_0'=4,'row_1'=4,'col_0'=4,'col_1'=2] {'row_0','row_1'}, dimensions={0} | all-to-all | bytes 524288 | tf_op jit(solution)/shard_map/all_to_all | solution.py:420
  58.5 3.5 %shard_map.72 = (f32[32,1024,128]{2,1,0:T(8,128)S(1)}, f32[8,128]{1,0:T(8,128)S(1)}, f32[32,128]{1,0:T(8,128)S(1)}) custom-call(f32[32,1024,128]{2,1,0:T(8,128)S(1)} %get-tuple-element.30.t_ref, f32[16,32,128]{2,1,0:T(8,128)S(1)} %all_to_all.15.parts_ref, f32[32,128]{1,0:T(8,128)S(1)} %bitcast.12, ...), custom_call_target="tpu_custom_call", output_to_operand_aliasing={{0}: (0, {})} | custom-call | tf_op jit(solution)/shard_map/pallas_call | solution.py:441
  65.7 2.2 %collective-permute-start.12 = (f32[8,128]{1,0:T(8,128)S(1)}, f32[8,128]{1,0:T(8,128)S(1)}, u32[]{:S(2)}, u32[]{:S(2)}) collective-permute-start(f32[8,128]{1,0:T(8,128)S(1)} %add.29.refs_0_), channel_id=1, source_target_pairs={{0,3},{1,2},{2,5},{3,4},{4,7},{5,6},{6,1},{7,0},{8,11},{9,10},{10,... | collective-permute-start | bytes 12296 | tf_op jit(solution)/shard_map/ppermute | solution.py:394
  70.9 1.6 %shard_map.73 = f32[16,32,128]{2,1,0:T(8,128)S(1)} custom-call(f32[32,1024,128]{2,1,0:T(8,128)S(1)} %get-tuple-element.34.plan_ref, f32[8,128]{1,0:T(8,128)S(1)} %add.29.refs_0_, f32[8,128]{1,0:T(8,128)S(1)} %collective-permute-done.11.refs_1_, f32[8,128]{1,0:T(8,128)S(1)} %collective-permute-done.12.refs_2_, f32[8,128]{1,0:T(8,128)S(1)} %collective-permute-done.13.refs_3_, ...), custom_call_target="tpu_custom_call" | custom-call | tf_op jit(solution)/shard_map/pallas_call | solution.py:445
  72.5 10.8 %all_to_all.16.parts_ref = f32[16,32,128]{2,1,0:T(8,128)S(1)} all-to-all(f32[16,32,128]{2,1,0:T(8,128)S(1)} %shard_map.73), channel_id=1, replica_groups=mesh['row_0'=4,'row_1'=4,'col_0'=4,'col_1'=2] {'row_0','row_1'}, dimensions={0} | all-to-all | bytes 524288 | tf_op jit(solution)/shard_map/all_to_all | solution.py:420
  83.2 1.6 %shard_map.74 = f32[8,128]{1,0:T(8,128)S(1)} custom-call(f32[32,1024,128]{2,1,0:T(8,128)S(1)} %get-tuple-element.34.plan_ref, f32[16,32,128]{2,1,0:T(8,128)S(1)} %all_to_all.16.parts_ref, f32[32,128]{1,0:T(8,128)S(1)} %bitcast.13), custom_call_target="tpu_custom_call" | custom-call | tf_op jit(solution)/shard_map/pallas_call | solution.py:448
  84.8 1.6 %collective-permute-start.14 = (f32[8,128]{1,0:T(8,128)S(1)}, f32[8,128]{1,0:T(8,128)S(1)}, u32[]{:S(2)}, u32[]{:S(2)}) collective-permute-start(f32[8,128]{1,0:T(8,128)S(1)} %shard_map.74), channel_id=1, source_target_pairs={{0,1},{1,0},{2,3},{3,2},{4,5},{5,4},{6,7},{7,6},{8,9},{9,8},{10,11... | collective-permute-start | bytes 12296 | tf_op jit(solution)/shard_map/ppermute | solution.py:416
  88.0 1.8 %collective-permute-start.16 = (f32[8,128]{1,0:T(8,128)S(1)}, f32[8,128]{1,0:T(8,128)S(1)}, u32[]{:S(2)}, u32[]{:S(2)}) collective-permute-start(f32[8,128]{1,0:T(8,128)S(1)} %add.30.refs_0_), channel_id=1, source_target_pairs={{0,3},{1,2},{2,5},{3,4},{4,7},{5,6},{6,1},{7,0},{8,11},{9,10},{10,... | collective-permute-start | bytes 12296 | tf_op jit(solution)/shard_map/ppermute | solution.py:394
  92.9 2.1 %shard_map.75 = (f32[16,40,128]{2,1,0:T(8,128)S(1)}, f32[8,128]{1,0:T(8,128)}) custom-call(f32[32,1024,128]{2,1,0:T(8,128)S(1)} %get-tuple-element.34.plan_ref, f32[8,128]{1,0:T(8,128)S(1)} %add.30.refs_0_, f32[8,128]{1,0:T(8,128)S(1)} %collective-permute-done.15.refs_1_, f32[8,128]{1,0:T(8,128)S(1)} %collective-permute-done.16.refs_2_, ...), custom_call_target="tpu_custom_call" | custom-call | tf_op jit(solution)/shard_map/pallas_call | solution.py:449
  95.0 11.5 %all_to_all.17.parts_ref = f32[16,40,128]{2,1,0:T(8,128)S(1)} all-to-all(f32[16,40,128]{2,1,0:T(8,128)S(1)} %get-tuple-element.38), channel_id=1, replica_groups=mesh['row_0'=4,'row_1'=4,'col_0'=4,'col_1'=2] {'row_0','row_1'}, dimensions={0} | all-to-all | bytes 655360 | tf_op jit(solution)/shard_map/all_to_all | solution.py:420
  110.8 1.5 %collective-permute-start.20 = (f32[8,128]{1,0:T(8,128)S(1)}, f32[8,128]{1,0:T(8,128)S(1)}, u32[]{:S(2)}, u32[]{:S(2)}) collective-permute-start(f32[8,128]{1,0:T(8,128)S(1)} %add.31), channel_id=1, source_target_pairs={{0,3},{1,2},{2,5},{3,4},{4,7},{5,6},{6,1},{7,0},{8,11},{9,10},{10,... | collective-permute-start | bytes 12296 | tf_op jit(solution)/shard_map/ppermute | solution.py:394
  (50 shorter events, 28.5 us)
Async XLA Ops:
  0.6 6.8 %collective-permute-start = (bf16[256,256]{1,0:T(8,128)(2,1)}, bf16[256,256]{1,0:T(8,128)(2,1)S(1)}, u32[]{:S(2)}, u32[]{:S(2)}) collective-permute-start(bf16[256,256]{1,0:T(8,128)(2,1)} %param.5), channel_id=1, source_target_pairs={{0,8},{1,33},{2,10},{3,35},{4,12},{5,37},{6,14},{7,39},{8,16},{9,4... | collective-permute-start | bytes 393224 | tf_op jit(solution)/shard_map/ppermute | solution.py:386
  2.8 6.9 %collective-permute-start.1 = (bf16[256,256]{1,0:T(8,128)(2,1)}, bf16[256,256]{1,0:T(8,128)(2,1)S(1)}, u32[]{:S(2)}, u32[]{:S(2)}) collective-permute-start(bf16[256,256]{1,0:T(8,128)(2,1)} %param.5), channel_id=1, source_target_pairs={{0,16},{1,65},{2,18},{3,67},{4,20},{5,69},{6,22},{7,71},{8,24},{9,... | collective-permute-start | bytes 393224 | tf_op jit(solution)/shard_map/ppermute | solution.py:386
  5.4 4.3 %collective-permute-start.2 = (bf16[256,256]{1,0:T(8,128)(2,1)}, bf16[256,256]{1,0:T(8,128)(2,1)S(1)}, u32[]{:S(2)}, u32[]{:S(2)}) collective-permute-start(bf16[256,256]{1,0:T(8,128)(2,1)} %param.5), channel_id=1, source_target_pairs={{0,24},{1,97},{2,26},{3,99},{4,28},{5,101},{6,30},{7,103},{8,0},{9... | collective-permute-start | bytes 393224 | tf_op jit(solution)/shard_map/ppermute | solution.py:386
  9.8 10.3 %collective-permute-start.3 = (bf16[1024,256]{1,0:T(8,128)(2,1)S(1)}, bf16[1024,256]{1,0:T(8,128)(2,1)S(1)}, u32[]{:S(2)}, u32[]{:S(2)}) collective-permute-start(bf16[1024,256]{1,0:T(8,128)(2,1)S(1)} %constant_dynamic-update-slice_fusion.points_ref), channel_id=1, source_target_pairs={{0,32},{1,9},{2,34},{3,11},{4,36},{5,13},{6,38},{7,15},{8,40},{9,1... | collective-permute-start | bytes 1572872 | tf_op jit(solution)/shard_map/ppermute | solution.py:386
  11.1 14.9 %collective-permute-start.4 = (bf16[1024,256]{1,0:T(8,128)(2,1)S(1)}, bf16[1024,256]{1,0:T(8,128)(2,1)S(1)}, u32[]{:S(2)}, u32[]{:S(2)}) collective-permute-start(bf16[1024,256]{1,0:T(8,128)(2,1)S(1)} %constant_dynamic-update-slice_fusion.points_ref), channel_id=1, source_target_pairs={{0,64},{1,17},{2,66},{3,19},{4,68},{5,21},{6,70},{7,23},{8,72},{9,... | collective-permute-start | bytes 1572872 | tf_op jit(solution)/shard_map/ppermute | solution.py:386
  13.5 14.2 %collective-permute-start.5 = (bf16[1024,256]{1,0:T(8,128)(2,1)S(1)}, bf16[1024,256]{1,0:T(8,128)(2,1)S(1)}, u32[]{:S(2)}, u32[]{:S(2)}) collective-permute-start(bf16[1024,256]{1,0:T(8,128)(2,1)S(1)} %constant_dynamic-update-slice_fusion.points_ref), channel_id=1, source_target_pairs={{0,96},{1,25},{2,98},{3,27},{4,100},{5,29},{6,102},{7,31},{8,104},... | collective-permute-start | bytes 1572872 | tf_op jit(solution)/shard_map/ppermute | solution.py:386
  14.7 1.0 copy-start
  26.0 15.6 %copy-start.2 = (f32[1024]{0:T(1024)S(1)}, f32[1024]{0:T(1024)}, u32[]{:S(2)}) copy-start(f32[1024]{0:T(1024)} %param.6) | copy-start | bytes 12292
  29.6 3.8 %collective-permute-start.6 = (f32[8,128]{1,0:T(8,128)S(1)}, f32[8,128]{1,0:T(8,128)S(1)}, u32[]{:S(2)}, u32[]{:S(2)}) collective-permute-start(f32[8,128]{1,0:T(8,128)S(1)} %get-tuple-element.31), channel_id=1, source_target_pairs={{0,1},{1,0},{2,3},{3,2},{4,5},{5,4},{6,7},{7,6},{8,9},{9,8},{10,11... | collective-permute-start | bytes 12296 | tf_op jit(solution)/shard_map/ppermute | solution.py:416
  33.5 6.9 %collective-permute-start.7 = (f32[8,128]{1,0:T(8,128)S(1)}, f32[8,128]{1,0:T(8,128)S(1)}, u32[]{:S(2)}, u32[]{:S(2)}) collective-permute-start(f32[8,128]{1,0:T(8,128)S(1)} %log_add_fusion.refs_0_), channel_id=1, source_target_pairs={{0,5},{1,4},{2,7},{3,6},{4,1},{5,0},{6,3},{7,2},{8,13},{9,12},{10,... | collective-permute-start | bytes 12296 | tf_op jit(solution)/shard_map/ppermute | solution.py:394
  37.4 4.2 %collective-permute-start.8 = (f32[8,128]{1,0:T(8,128)S(1)}, f32[8,128]{1,0:T(8,128)S(1)}, u32[]{:S(2)}, u32[]{:S(2)}) collective-permute-start(f32[8,128]{1,0:T(8,128)S(1)} %log_add_fusion.refs_0_), channel_id=1, source_target_pairs={{0,3},{1,2},{2,5},{3,4},{4,7},{5,6},{6,1},{7,0},{8,11},{9,10},{10,... | collective-permute-start | bytes 12296 | tf_op jit(solution)/shard_map/ppermute | solution.py:394
  38.2 3.5 %collective-permute-start.9 = (f32[8,128]{1,0:T(8,128)S(1)}, f32[8,128]{1,0:T(8,128)S(1)}, u32[]{:S(2)}, u32[]{:S(2)}) collective-permute-start(f32[8,128]{1,0:T(8,128)S(1)} %log_add_fusion.refs_0_), channel_id=1, source_target_pairs={{0,7},{1,6},{2,1},{3,0},{4,3},{5,2},{6,5},{7,4},{8,15},{9,14},{10,... | collective-permute-start | bytes 12296 | tf_op jit(solution)/shard_map/ppermute | solution.py:394
  62.0 2.2 %collective-permute-start.10 = (f32[8,128]{1,0:T(8,128)S(1)}, f32[8,128]{1,0:T(8,128)S(1)}, u32[]{:S(2)}, u32[]{:S(2)}) collective-permute-start(f32[8,128]{1,0:T(8,128)S(1)} %get-tuple-element.35), channel_id=1, source_target_pairs={{0,1},{1,0},{2,3},{3,2},{4,5},{5,4},{6,7},{7,6},{8,9},{9,8},{10,11... | collective-permute-start | bytes 12296 | tf_op jit(solution)/shard_map/ppermute | solution.py:416
  64.2 4.5 %collective-permute-start.11 = (f32[8,128]{1,0:T(8,128)S(1)}, f32[8,128]{1,0:T(8,128)S(1)}, u32[]{:S(2)}, u32[]{:S(2)}) collective-permute-start(f32[8,128]{1,0:T(8,128)S(1)} %add.29.refs_0_), channel_id=1, source_target_pairs={{0,5},{1,4},{2,7},{3,6},{4,1},{5,0},{6,3},{7,2},{8,13},{9,12},{10,... | collective-permute-start | bytes 12296 | tf_op jit(solution)/shard_map/ppermute | solution.py:394
  65.7 4.2 %collective-permute-start.12 = (f32[8,128]{1,0:T(8,128)S(1)}, f32[8,128]{1,0:T(8,128)S(1)}, u32[]{:S(2)}, u32[]{:S(2)}) collective-permute-start(f32[8,128]{1,0:T(8,128)S(1)} %add.29.refs_0_), channel_id=1, source_target_pairs={{0,3},{1,2},{2,5},{3,4},{4,7},{5,6},{6,1},{7,0},{8,11},{9,10},{10,... | collective-permute-start | bytes 12296 | tf_op jit(solution)/shard_map/ppermute | solution.py:394
  67.8 3.0 %collective-permute-start.13 = (f32[8,128]{1,0:T(8,128)S(1)}, f32[8,128]{1,0:T(8,128)S(1)}, u32[]{:S(2)}, u32[]{:S(2)}) collective-permute-start(f32[8,128]{1,0:T(8,128)S(1)} %add.29.refs_0_), channel_id=1, source_target_pairs={{0,7},{1,6},{2,1},{3,0},{4,3},{5,2},{6,5},{7,4},{8,15},{9,14},{10,... | collective-permute-start | bytes 12296 | tf_op jit(solution)/shard_map/ppermute | solution.py:394
  84.8 2.4 %collective-permute-start.14 = (f32[8,128]{1,0:T(8,128)S(1)}, f32[8,128]{1,0:T(8,128)S(1)}, u32[]{:S(2)}, u32[]{:S(2)}) collective-permute-start(f32[8,128]{1,0:T(8,128)S(1)} %shard_map.74), channel_id=1, source_target_pairs={{0,1},{1,0},{2,3},{3,2},{4,5},{5,4},{6,7},{7,6},{8,9},{9,8},{10,11... | collective-permute-start | bytes 12296 | tf_op jit(solution)/shard_map/ppermute | solution.py:416
  87.2 4.5 %collective-permute-start.15 = (f32[8,128]{1,0:T(8,128)S(1)}, f32[8,128]{1,0:T(8,128)S(1)}, u32[]{:S(2)}, u32[]{:S(2)}) collective-permute-start(f32[8,128]{1,0:T(8,128)S(1)} %add.30.refs_0_), channel_id=1, source_target_pairs={{0,5},{1,4},{2,7},{3,6},{4,1},{5,0},{6,3},{7,2},{8,13},{9,12},{10,... | collective-permute-start | bytes 12296 | tf_op jit(solution)/shard_map/ppermute | solution.py:394
  88.0 4.2 %collective-permute-start.16 = (f32[8,128]{1,0:T(8,128)S(1)}, f32[8,128]{1,0:T(8,128)S(1)}, u32[]{:S(2)}, u32[]{:S(2)}) collective-permute-start(f32[8,128]{1,0:T(8,128)S(1)} %add.30.refs_0_), channel_id=1, source_target_pairs={{0,3},{1,2},{2,5},{3,4},{4,7},{5,6},{6,1},{7,0},{8,11},{9,10},{10,... | collective-permute-start | bytes 12296 | tf_op jit(solution)/shard_map/ppermute | solution.py:394
  89.8 3.0 %collective-permute-start.17 = (f32[8,128]{1,0:T(8,128)S(1)}, f32[8,128]{1,0:T(8,128)S(1)}, u32[]{:S(2)}, u32[]{:S(2)}) collective-permute-start(f32[8,128]{1,0:T(8,128)S(1)} %add.30.refs_0_), channel_id=1, source_target_pairs={{0,7},{1,6},{2,1},{3,0},{4,3},{5,2},{6,5},{7,4},{8,15},{9,14},{10,... | collective-permute-start | bytes 12296 | tf_op jit(solution)/shard_map/ppermute | solution.py:394
  107.0 2.3 %collective-permute-start.18 = (f32[8,128]{1,0:T(8,128)S(1)}, f32[8,128]{1,0:T(8,128)S(1)}, u32[]{:S(2)}, u32[]{:S(2)}) collective-permute-start(f32[8,128]{1,0:T(8,128)S(1)} %get-tuple-element.42), channel_id=1, source_target_pairs={{0,1},{1,0},{2,3},{3,2},{4,5},{5,4},{6,7},{7,6},{8,9},{9,8},{10,11... | collective-permute-start | bytes 12296 | tf_op jit(solution)/shard_map/ppermute | solution.py:416
  109.4 4.5 %collective-permute-start.19 = (f32[8,128]{1,0:T(8,128)S(1)}, f32[8,128]{1,0:T(8,128)S(1)}, u32[]{:S(2)}, u32[]{:S(2)}) collective-permute-start(f32[8,128]{1,0:T(8,128)S(1)} %add.31), channel_id=1, source_target_pairs={{0,5},{1,4},{2,7},{3,6},{4,1},{5,0},{6,3},{7,2},{8,13},{9,12},{10,... | collective-permute-start | bytes 12296 | tf_op jit(solution)/shard_map/ppermute | solution.py:394
  110.8 4.2 %collective-permute-start.20 = (f32[8,128]{1,0:T(8,128)S(1)}, f32[8,128]{1,0:T(8,128)S(1)}, u32[]{:S(2)}, u32[]{:S(2)}) collective-permute-start(f32[8,128]{1,0:T(8,128)S(1)} %add.31), channel_id=1, source_target_pairs={{0,3},{1,2},{2,5},{3,4},{4,7},{5,6},{6,1},{7,0},{8,11},{9,10},{10,... | collective-permute-start | bytes 12296 | tf_op jit(solution)/shard_map/ppermute | solution.py:394
  112.3 3.0 %collective-permute-start.21 = (f32[8,128]{1,0:T(8,128)S(1)}, f32[8,128]{1,0:T(8,128)S(1)}, u32[]{:S(2)}, u32[]{:S(2)}) collective-permute-start(f32[8,128]{1,0:T(8,128)S(1)} %add.31), channel_id=1, source_target_pairs={{0,7},{1,6},{2,1},{3,0},{4,3},{5,2},{6,5},{7,4},{8,15},{9,14},{10,... | collective-permute-start | bytes 12296 | tf_op jit(solution)/shard_map/ppermute | solution.py:394
  (1 other events, 0.7 us)

commit v10 on v7

--- a/solution.py
+++ b/solution.py
@@ -349,12 +349,12 @@
     out_ref, potential_ref, wide_ref, line_ref = refs[7:]
     sums = add_all(values(parts))
     mass = mass_ref[...]
-    column_sums(plan_ref, jnp.exp(mass) / sums, line_ref, wide_ref)
     squares = squares_ref[...] / (WIDTH * EPS)
     potential = -EPS * (lse_ref[...] + jnp.log(sums) - mass - squares)
     potential_ref[...] = potential
     tiles = plan_ref.shape[0]
     line_ref[tiles:, :] = jnp.broadcast_to(jnp.sum(potential), (8, LANES))
+    column_sums(plan_ref, jnp.exp(mass) / sums, line_ref, wide_ref)
     copies(out_ref, line_ref[...])
 
 
@@ -375,9 +375,9 @@
     return ((y % 4 * 4 + x % 4) * 4 + z) * 2 + core
 
 
-def turned(value, stage):
+def turned(value, stage, order):
     found = {0: value}
-    for k in (2, 1, 3):
+    for k in order:
         pairs = []
         for y, x, z, core in itertools.product(*map(range, SIZES)):
             along_y = (core + stage) % 2
@@ -419,8 +419,8 @@
     def over_row(value):
         return lax.all_to_all(value, ROW, 0, 0, tiled=True)
 
-    first = jnp.concatenate(turned(tgt_points, 0))
-    pieces = turned(first, 1)
+    first = jnp.concatenate(turned(tgt_points, 0, (2, 1, 3)))
+    pieces = turned(first, 1, (1, 3, 2))
     terms, top, sums, squares = call(
         first_terms_kernel, (big, wide, wide, by_row), [SMEM] + [VMEM] * 3, []
     )(place, src_points, first, tgt_mass)

time: 117 us -> 116 us (level)
  starting transfers between devices: 38.8 us -> 37 us
    ppermute x12, starting transfers between devices: 21 us -> 19.3 us  [crossed(): return lax.ppermute(value, ALL, pairs)]
  transfers between devices with their start and end apart: 22 -> 22, of which waited for: 13 -> 16; matrix products, arithmetic and copies ran while one was open for 1% -> 1% of each run, Pallas kernels for 6% -> 6%
where the time goes in v10:
time: 116 us
  blocking collectives  37.7 us (33%)
  starting transfers between devices  37 us (32%)
  Pallas kernels  21.3 us (18%)
  waiting for transfers between devices  15.7 us (14%)
  local copies, waits for them, and re-layouts  3.26 us (3%)
    all_to_all x3, blocking collectives, over_row(): return lax.all_to_all(value, ROW, 0, 0, tiled=True)  37.7 us
    ppermute x12, starting transfers between devices, crossed(): return lax.ppermute(value, ALL, pairs)  19.3 us
    ppermute x6, starting transfers between devices, turned(): found[k] = lax.ppermute(value, ALL, pairs)  10.2 us
    ppermute x4, starting transfers between devices, over_col(): both = combine([value, lax.ppermute(value, 'col_1', [(0, 1), (1, 0)])])  7.51 us
    ppermute x12, waiting for transfers between devices, crossed(): return lax.ppermute(value, ALL, pairs)  7.07 us
    ppermute x6, waiting for transfers between devices, turned(): found[k] = lax.ppermute(value, ALL, pairs)  5.34 us
    pallas_call x1, Pallas kernels, body(): call(first_terms_kernel, (big, wide, wide, by_row), [SMEM] + [VMEM] * 3, [])  3.53 us
    pallas_call x1, Pallas kernels, body(): call(plan_kernel, (big, by_row, by_column), [VMEM] * 5, [wide, wide, line...  3.46 us
  transfers between devices with their start and end apart: 22, of which 16 were waited for; matrix products, arithmetic and copies ran while one was open for 1% of the time, Pallas kernels for 6%

profile of v10, /device:TPU:1, one launch (start us, length us, event | category | flops | bytes accessed | tf_op | source)
XLA Modules:
  0.0 115.9 jit_solution(17897103073311113949)
XLA Ops:
  0.6 2.2 %collective-permute-start = (bf16[256,256]{1,0:T(8,128)(2,1)}, bf16[256,256]{1,0:T(8,128)(2,1)S(1)}, u32[]{:S(2)}, u32[]{:S(2)}) collective-permute-start(bf16[256,256]{1,0:T(8,128)(2,1)} %param.5), channel_id=1, source_target_pairs={{0,8},{1,33},{2,10},{3,35},{4,12},{5,37},{6,14},{7,39},{8,16},{9,4... | collective-permute-start | bytes 393224 | tf_op jit(solution)/shard_map/ppermute | solution.py:386
  2.8 2.6 %collective-permute-start.1 = (bf16[256,256]{1,0:T(8,128)(2,1)}, bf16[256,256]{1,0:T(8,128)(2,1)S(1)}, u32[]{:S(2)}, u32[]{:S(2)}) collective-permute-start(bf16[256,256]{1,0:T(8,128)(2,1)} %param.5), channel_id=1, source_target_pairs={{0,16},{1,65},{2,18},{3,67},{4,20},{5,69},{6,22},{7,71},{8,24},{9,... | collective-permute-start | bytes 393224 | tf_op jit(solution)/shard_map/ppermute | solution.py:386
  7.5 2.2 %collective-permute-done.1 = bf16[256,256]{1,0:T(8,128)(2,1)S(1)} collective-permute-done((bf16[256,256]{1,0:T(8,128)(2,1)}, bf16[256,256]{1,0:T(8,128)(2,1)S(1)}, u32[]{:S(2)}, u32[]{:S(2)}) %collective-permute-start.1) | collective-permute-done | bytes 131104 | tf_op jit(solution)/shard_map/ppermute | solution.py:386
  12.5 1.5 %collective-permute-start.5 = (bf16[1024,256]{1,0:T(8,128)(2,1)S(1)}, bf16[1024,256]{1,0:T(8,128)(2,1)S(1)}, u32[]{:S(2)}, u32[]{:S(2)}) collective-permute-start(bf16[1024,256]{1,0:T(8,128)(2,1)S(1)} %constant_dynamic-update-slice_fusion.points_ref), channel_id=1, source_target_pairs={{0,64},{1,17},{2,66},{3,19},{4,68},{5,21},{6,70},{7,23},{8,72},{9,... | collective-permute-start | bytes 1572872 | tf_op jit(solution)/shard_map/ppermute | solution.py:386
  15.9 3.5 %shard_map.67 = (f32[32,1024,128]{2,1,0:T(8,128)S(1)}, f32[1024,128]{1,0:T(8,128)S(1)}, f32[1024,128]{1,0:T(8,128)S(1)}, f32[8,128]{1,0:T(8,128)S(1)}) custom-call(s32[3]{0:T(128)S(1)} %pad_add_fusion.place, bf16[1024,256]{1,0:T(8,128)(2,1)S(1)} %copy-done, bf16[1024,256]{1,0:T(8,128)(2,1)S(1)} %constant_dynamic-update-slice_fusion.points_ref, ...), custom_call_target="tpu_custom_call" | custom-call | tf_op jit(solution)/shard_map/pallas_call | solution.py:424
  19.4 1.7 %shard_map.68 = (f32[32,1024,128]{2,1,0:T(8,128)S(1)}, f32[1024,128]{1,0:T(8,128)S(1)}) custom-call(s32[3]{0:T(128)S(1)} %pad_add_fusion.place, bf16[1024,256]{1,0:T(8,128)(2,1)S(1)} %copy-done, f32[32,1024,128]{2,1,0:T(8,128)S(1)} %get-tuple-element.23.old_ref, ...), custom_call_target="tpu_custom_call", output_to_operand_aliasing={{0}: (2, {}), {1}: (3, {})} | custom-call | tf_op jit(solution)/shard_map/pallas_call | solution.py:428
  21.2 1.7 %shard_map.69 = (f32[32,1024,128]{2,1,0:T(8,128)S(1)}, f32[1024,128]{1,0:T(8,128)S(1)}) custom-call(s32[3]{0:T(128)S(1)} %pad_add_fusion.place, bf16[1024,256]{1,0:T(8,128)(2,1)S(1)} %copy-done, f32[32,1024,128]{2,1,0:T(8,128)S(1)} %get-tuple-element.26.old_ref, ...), custom_call_target="tpu_custom_call", output_to_operand_aliasing={{0}: (2, {}), {1}: (3, {})} | custom-call | tf_op jit(solution)/shard_map/pallas_call | solution.py:428
  22.9 3.1 %collective-permute-done.5.points_ref = bf16[1024,256]{1,0:T(8,128)(2,1)S(1)} collective-permute-done((bf16[1024,256]{1,0:T(8,128)(2,1)S(1)}, bf16[1024,256]{1,0:T(8,128)(2,1)S(1)}, u32[]{:S(2)}, u32[]{:S(2)}) %collective-permute-start.5) | collective-permute-done | bytes 524320 | tf_op jit(solution)/shard_map/ppermute | solution.py:386
  26.0 1.9 %shard_map.70 = (f32[32,1024,128]{2,1,0:T(8,128)S(1)}, f32[1024,128]{1,0:T(8,128)S(1)}, f32[8,128]{1,0:T(8,128)S(1)}) custom-call(s32[3]{0:T(128)S(1)} %pad_add_fusion.place, bf16[1024,256]{1,0:T(8,128)(2,1)S(1)} %copy-done, f32[32,1024,128]{2,1,0:T(8,128)S(1)} %get-tuple-element.28.old_ref, ...), custom_call_target="tpu_custom_call", output_to_operand_aliasing={{0}: (2, {}), {1}: (3, {})} | custom-call | tf_op jit(solution)/shard_map/pallas_call | solution.py:431
  27.9 3.0 %collective-permute-start.6 = (f32[8,128]{1,0:T(8,128)S(1)}, f32[8,128]{1,0:T(8,128)S(1)}, u32[]{:S(2)}, u32[]{:S(2)}) collective-permute-start(f32[8,128]{1,0:T(8,128)S(1)} %get-tuple-element.31), channel_id=1, source_target_pairs={{0,1},{1,0},{2,3},{3,2},{4,5},{5,4},{6,7},{7,6},{8,9},{9,8},{10,11... | collective-permute-start | bytes 12296 | tf_op jit(solution)/shard_map/ppermute | solution.py:416
  31.8 3.9 %collective-permute-start.7 = (f32[8,128]{1,0:T(8,128)S(1)}, f32[8,128]{1,0:T(8,128)S(1)}, u32[]{:S(2)}, u32[]{:S(2)}) collective-permute-start(f32[8,128]{1,0:T(8,128)S(1)} %log_add_fusion.refs_0_), channel_id=1, source_target_pairs={{0,5},{1,4},{2,7},{3,6},{4,1},{5,0},{6,3},{7,2},{8,13},{9,12},{10,... | collective-permute-start | bytes 12296 | tf_op jit(solution)/shard_map/ppermute | solution.py:394
  36.5 2.2 %collective-permute-start.9 = (f32[8,128]{1,0:T(8,128)S(1)}, f32[8,128]{1,0:T(8,128)S(1)}, u32[]{:S(2)}, u32[]{:S(2)}) collective-permute-start(f32[8,128]{1,0:T(8,128)S(1)} %log_add_fusion.refs_0_), channel_id=1, source_target_pairs={{0,7},{1,6},{2,1},{3,0},{4,3},{5,2},{6,5},{7,4},{8,15},{9,14},{10,... | collective-permute-start | bytes 12296 | tf_op jit(solution)/shard_map/ppermute | solution.py:394
  39.9 3.1 %shard_map.71 = (f32[16,32,128]{2,1,0:T(8,128)S(1)}, f32[8,128]{1,0:T(8,128)S(1)}) custom-call(f32[32,1024,128]{2,1,0:T(8,128)S(1)} %get-tuple-element.30.t_ref, f32[8,128]{1,0:T(8,128)S(1)} %log_add_fusion.refs_0_, f32[8,128]{1,0:T(8,128)S(1)} %collective-permute-done.7.refs_1_, f32[8,128]{1,0:T(8,128)S(1)} %collective-permute-done.8.refs_2_, ...), custom_call_target="tpu_custom_call" | custom-call | tf_op jit(solution)/shard_map/pallas_call | solution.py:438
  43.0 15.5 %all_to_all.15.parts_ref = f32[16,32,128]{2,1,0:T(8,128)S(1)} all-to-all(f32[16,32,128]{2,1,0:T(8,128)S(1)} %get-tuple-element.32), channel_id=1, replica_groups=mesh['row_0'=4,'row_1'=4,'col_0'=4,'col_1'=2] {'row_0','row_1'}, dimensions={0} | all-to-all | bytes 524288 | tf_op jit(solution)/shard_map/all_to_all | solution.py:420
  58.6 3.5 %shard_map.72 = (f32[32,1024,128]{2,1,0:T(8,128)S(1)}, f32[8,128]{1,0:T(8,128)S(1)}, f32[32,128]{1,0:T(8,128)S(1)}) custom-call(f32[32,1024,128]{2,1,0:T(8,128)S(1)} %get-tuple-element.30.t_ref, f32[16,32,128]{2,1,0:T(8,128)S(1)} %all_to_all.15.parts_ref, f32[32,128]{1,0:T(8,128)S(1)} %bitcast.12, ...), custom_call_target="tpu_custom_call", output_to_operand_aliasing={{0}: (0, {})} | custom-call | tf_op jit(solution)/shard_map/pallas_call | solution.py:441
  65.7 2.2 %collective-permute-start.12 = (f32[8,128]{1,0:T(8,128)S(1)}, f32[8,128]{1,0:T(8,128)S(1)}, u32[]{:S(2)}, u32[]{:S(2)}) collective-permute-start(f32[8,128]{1,0:T(8,128)S(1)} %add.29.refs_0_), channel_id=1, source_target_pairs={{0,3},{1,2},{2,5},{3,4},{4,7},{5,6},{6,1},{7,0},{8,11},{9,10},{10,... | collective-permute-start | bytes 12296 | tf_op jit(solution)/shard_map/ppermute | solution.py:394
  70.9 1.6 %shard_map.73 = f32[16,32,128]{2,1,0:T(8,128)S(1)} custom-call(f32[32,1024,128]{2,1,0:T(8,128)S(1)} %get-tuple-element.34.plan_ref, f32[8,128]{1,0:T(8,128)S(1)} %add.29.refs_0_, f32[8,128]{1,0:T(8,128)S(1)} %collective-permute-done.11.refs_1_, f32[8,128]{1,0:T(8,128)S(1)} %collective-permute-done.12.refs_2_, f32[8,128]{1,0:T(8,128)S(1)} %collective-permute-done.13.refs_3_, ...), custom_call_target="tpu_custom_call" | custom-call | tf_op jit(solution)/shard_map/pallas_call | solution.py:445
  72.5 10.8 %all_to_all.16.parts_ref = f32[16,32,128]{2,1,0:T(8,128)S(1)} all-to-all(f32[16,32,128]{2,1,0:T(8,128)S(1)} %shard_map.73), channel_id=1, replica_groups=mesh['row_0'=4,'row_1'=4,'col_0'=4,'col_1'=2] {'row_0','row_1'}, dimensions={0} | all-to-all | bytes 524288 | tf_op jit(solution)/shard_map/all_to_all | solution.py:420
  83.3 1.6 %shard_map.74 = f32[8,128]{1,0:T(8,128)S(1)} custom-call(f32[32,1024,128]{2,1,0:T(8,128)S(1)} %get-tuple-element.34.plan_ref, f32[16,32,128]{2,1,0:T(8,128)S(1)} %all_to_all.16.parts_ref, f32[32,128]{1,0:T(8,128)S(1)} %bitcast.13), custom_call_target="tpu_custom_call" | custom-call | tf_op jit(solution)/shard_map/pallas_call | solution.py:448
  84.8 1.6 %collective-permute-start.14 = (f32[8,128]{1,0:T(8,128)S(1)}, f32[8,128]{1,0:T(8,128)S(1)}, u32[]{:S(2)}, u32[]{:S(2)}) collective-permute-start(f32[8,128]{1,0:T(8,128)S(1)} %shard_map.74), channel_id=1, source_target_pairs={{0,1},{1,0},{2,3},{3,2},{4,5},{5,4},{6,7},{7,6},{8,9},{9,8},{10,11... | collective-permute-start | bytes 12296 | tf_op jit(solution)/shard_map/ppermute | solution.py:416
  88.0 1.8 %collective-permute-start.16 = (f32[8,128]{1,0:T(8,128)S(1)}, f32[8,128]{1,0:T(8,128)S(1)}, u32[]{:S(2)}, u32[]{:S(2)}) collective-permute-start(f32[8,128]{1,0:T(8,128)S(1)} %add.30.refs_0_), channel_id=1, source_target_pairs={{0,3},{1,2},{2,5},{3,4},{4,7},{5,6},{6,1},{7,0},{8,11},{9,10},{10,... | collective-permute-start | bytes 12296 | tf_op jit(solution)/shard_map/ppermute | solution.py:394
  92.9 2.1 %shard_map.75 = (f32[16,40,128]{2,1,0:T(8,128)S(1)}, f32[8,128]{1,0:T(8,128)}) custom-call(f32[32,1024,128]{2,1,0:T(8,128)S(1)} %get-tuple-element.34.plan_ref, f32[8,128]{1,0:T(8,128)S(1)} %add.30.refs_0_, f32[8,128]{1,0:T(8,128)S(1)} %collective-permute-done.15.refs_1_, f32[8,128]{1,0:T(8,128)S(1)} %collective-permute-done.16.refs_2_, ...), custom_call_target="tpu_custom_call" | custom-call | tf_op jit(solution)/shard_map/pallas_call | solution.py:449
  95.0 11.5 %all_to_all.17.parts_ref = f32[16,40,128]{2,1,0:T(8,128)S(1)} all-to-all(f32[16,40,128]{2,1,0:T(8,128)S(1)} %get-tuple-element.38), channel_id=1, replica_groups=mesh['row_0'=4,'row_1'=4,'col_0'=4,'col_1'=2] {'row_0','row_1'}, dimensions={0} | all-to-all | bytes 655360 | tf_op jit(solution)/shard_map/all_to_all | solution.py:420
  110.8 1.5 %collective-permute-start.20 = (f32[8,128]{1,0:T(8,128)S(1)}, f32[8,128]{1,0:T(8,128)S(1)}, u32[]{:S(2)}, u32[]{:S(2)}) collective-permute-start(f32[8,128]{1,0:T(8,128)S(1)} %add.31), channel_id=1, source_target_pairs={{0,3},{1,2},{2,5},{3,4},{4,7},{5,6},{6,1},{7,0},{8,11},{9,10},{10,... | collective-permute-start | bytes 12296 | tf_op jit(solution)/shard_map/ppermute | solution.py:394
  (50 shorter events, 28.8 us)
Async XLA Ops:
  0.6 6.8 %collective-permute-start = (bf16[256,256]{1,0:T(8,128)(2,1)}, bf16[256,256]{1,0:T(8,128)(2,1)S(1)}, u32[]{:S(2)}, u32[]{:S(2)}) collective-permute-start(bf16[256,256]{1,0:T(8,128)(2,1)} %param.5), channel_id=1, source_target_pairs={{0,8},{1,33},{2,10},{3,35},{4,12},{5,37},{6,14},{7,39},{8,16},{9,4... | collective-permute-start | bytes 393224 | tf_op jit(solution)/shard_map/ppermute | solution.py:386
  2.8 6.9 %collective-permute-start.1 = (bf16[256,256]{1,0:T(8,128)(2,1)}, bf16[256,256]{1,0:T(8,128)(2,1)S(1)}, u32[]{:S(2)}, u32[]{:S(2)}) collective-permute-start(bf16[256,256]{1,0:T(8,128)(2,1)} %param.5), channel_id=1, source_target_pairs={{0,16},{1,65},{2,18},{3,67},{4,20},{5,69},{6,22},{7,71},{8,24},{9,... | collective-permute-start | bytes 393224 | tf_op jit(solution)/shard_map/ppermute | solution.py:386
  5.4 4.3 %collective-permute-start.2 = (bf16[256,256]{1,0:T(8,128)(2,1)}, bf16[256,256]{1,0:T(8,128)(2,1)S(1)}, u32[]{:S(2)}, u32[]{:S(2)}) collective-permute-start(bf16[256,256]{1,0:T(8,128)(2,1)} %param.5), channel_id=1, source_target_pairs={{0,24},{1,97},{2,26},{3,99},{4,28},{5,101},{6,30},{7,103},{8,0},{9... | collective-permute-start | bytes 393224 | tf_op jit(solution)/shard_map/ppermute | solution.py:386
  9.8 9.7 %collective-permute-start.3 = (bf16[1024,256]{1,0:T(8,128)(2,1)S(1)}, bf16[1024,256]{1,0:T(8,128)(2,1)S(1)}, u32[]{:S(2)}, u32[]{:S(2)}) collective-permute-start(bf16[1024,256]{1,0:T(8,128)(2,1)S(1)} %constant_dynamic-update-slice_fusion.points_ref), channel_id=1, source_target_pairs={{0,32},{1,9},{2,34},{3,11},{4,36},{5,13},{6,38},{7,15},{8,40},{9,1... | collective-permute-start | bytes 1572872 | tf_op jit(solution)/shard_map/ppermute | solution.py:386
  11.1 10.1 %collective-permute-start.4 = (bf16[1024,256]{1,0:T(8,128)(2,1)S(1)}, bf16[1024,256]{1,0:T(8,128)(2,1)S(1)}, u32[]{:S(2)}, u32[]{:S(2)}) collective-permute-start(bf16[1024,256]{1,0:T(8,128)(2,1)S(1)} %constant_dynamic-update-slice_fusion.points_ref), channel_id=1, source_target_pairs={{0,96},{1,25},{2,98},{3,27},{4,100},{5,29},{6,102},{7,31},{8,104},... | collective-permute-start | bytes 1572872 | tf_op jit(solution)/shard_map/ppermute | solution.py:386
  12.5 13.5 %collective-permute-start.5 = (bf16[1024,256]{1,0:T(8,128)(2,1)S(1)}, bf16[1024,256]{1,0:T(8,128)(2,1)S(1)}, u32[]{:S(2)}, u32[]{:S(2)}) collective-permute-start(bf16[1024,256]{1,0:T(8,128)(2,1)S(1)} %constant_dynamic-update-slice_fusion.points_ref), channel_id=1, source_target_pairs={{0,64},{1,17},{2,66},{3,19},{4,68},{5,21},{6,70},{7,23},{8,72},{9,... | collective-permute-start | bytes 1572872 | tf_op jit(solution)/shard_map/ppermute | solution.py:386
  14.1 1.0 copy-start
  21.2 18.7 %copy-start.2 = (f32[1024]{0:T(1024)S(1)}, f32[1024]{0:T(1024)}, u32[]{:S(2)}) copy-start(f32[1024]{0:T(1024)} %param.6) | copy-start | bytes 12292
  27.9 3.9 %collective-permute-start.6 = (f32[8,128]{1,0:T(8,128)S(1)}, f32[8,128]{1,0:T(8,128)S(1)}, u32[]{:S(2)}, u32[]{:S(2)}) collective-permute-start(f32[8,128]{1,0:T(8,128)S(1)} %get-tuple-element.31), channel_id=1, source_target_pairs={{0,1},{1,0},{2,3},{3,2},{4,5},{5,4},{6,7},{7,6},{8,9},{9,8},{10,11... | collective-permute-start | bytes 12296 | tf_op jit(solution)/shard_map/ppermute | solution.py:416
  31.8 6.9 %collective-permute-start.7 = (f32[8,128]{1,0:T(8,128)S(1)}, f32[8,128]{1,0:T(8,128)S(1)}, u32[]{:S(2)}, u32[]{:S(2)}) collective-permute-start(f32[8,128]{1,0:T(8,128)S(1)} %log_add_fusion.refs_0_), channel_id=1, source_target_pairs={{0,5},{1,4},{2,7},{3,6},{4,1},{5,0},{6,3},{7,2},{8,13},{9,12},{10,... | collective-permute-start | bytes 12296 | tf_op jit(solution)/shard_map/ppermute | solution.py:394
  35.7 4.2 %collective-permute-start.8 = (f32[8,128]{1,0:T(8,128)S(1)}, f32[8,128]{1,0:T(8,128)S(1)}, u32[]{:S(2)}, u32[]{:S(2)}) collective-permute-start(f32[8,128]{1,0:T(8,128)S(1)} %log_add_fusion.refs_0_), channel_id=1, source_target_pairs={{0,3},{1,2},{2,5},{3,4},{4,7},{5,6},{6,1},{7,0},{8,11},{9,10},{10,... | collective-permute-start | bytes 12296 | tf_op jit(solution)/shard_map/ppermute | solution.py:394
  36.5 3.5 %collective-permute-start.9 = (f32[8,128]{1,0:T(8,128)S(1)}, f32[8,128]{1,0:T(8,128)S(1)}, u32[]{:S(2)}, u32[]{:S(2)}) collective-permute-start(f32[8,128]{1,0:T(8,128)S(1)} %log_add_fusion.refs_0_), channel_id=1, source_target_pairs={{0,7},{1,6},{2,1},{3,0},{4,3},{5,2},{6,5},{7,4},{8,15},{9,14},{10,... | collective-permute-start | bytes 12296 | tf_op jit(solution)/shard_map/ppermute | solution.py:394
  62.0 2.2 %collective-permute-start.10 = (f32[8,128]{1,0:T(8,128)S(1)}, f32[8,128]{1,0:T(8,128)S(1)}, u32[]{:S(2)}, u32[]{:S(2)}) collective-permute-start(f32[8,128]{1,0:T(8,128)S(1)} %get-tuple-element.35), channel_id=1, source_target_pairs={{0,1},{1,0},{2,3},{3,2},{4,5},{5,4},{6,7},{7,6},{8,9},{9,8},{10,11... | collective-permute-start | bytes 12296 | tf_op jit(solution)/shard_map/ppermute | solution.py:416
  64.3 4.5 %collective-permute-start.11 = (f32[8,128]{1,0:T(8,128)S(1)}, f32[8,128]{1,0:T(8,128)S(1)}, u32[]{:S(2)}, u32[]{:S(2)}) collective-permute-start(f32[8,128]{1,0:T(8,128)S(1)} %add.29.refs_0_), channel_id=1, source_target_pairs={{0,5},{1,4},{2,7},{3,6},{4,1},{5,0},{6,3},{7,2},{8,13},{9,12},{10,... | collective-permute-start | bytes 12296 | tf_op jit(solution)/shard_map/ppermute | solution.py:394
  65.7 4.2 %collective-permute-start.12 = (f32[8,128]{1,0:T(8,128)S(1)}, f32[8,128]{1,0:T(8,128)S(1)}, u32[]{:S(2)}, u32[]{:S(2)}) collective-permute-start(f32[8,128]{1,0:T(8,128)S(1)} %add.29.refs_0_), channel_id=1, source_target_pairs={{0,3},{1,2},{2,5},{3,4},{4,7},{5,6},{6,1},{7,0},{8,11},{9,10},{10,... | collective-permute-start | bytes 12296 | tf_op jit(solution)/shard_map/ppermute | solution.py:394
  67.9 3.0 %collective-permute-start.13 = (f32[8,128]{1,0:T(8,128)S(1)}, f32[8,128]{1,0:T(8,128)S(1)}, u32[]{:S(2)}, u32[]{:S(2)}) collective-permute-start(f32[8,128]{1,0:T(8,128)S(1)} %add.29.refs_0_), channel_id=1, source_target_pairs={{0,7},{1,6},{2,1},{3,0},{4,3},{5,2},{6,5},{7,4},{8,15},{9,14},{10,... | collective-permute-start | bytes 12296 | tf_op jit(solution)/shard_map/ppermute | solution.py:394
  84.8 2.4 %collective-permute-start.14 = (f32[8,128]{1,0:T(8,128)S(1)}, f32[8,128]{1,0:T(8,128)S(1)}, u32[]{:S(2)}, u32[]{:S(2)}) collective-permute-start(f32[8,128]{1,0:T(8,128)S(1)} %shard_map.74), channel_id=1, source_target_pairs={{0,1},{1,0},{2,3},{3,2},{4,5},{5,4},{6,7},{7,6},{8,9},{9,8},{10,11... | collective-permute-start | bytes 12296 | tf_op jit(solution)/shard_map/ppermute | solution.py:416
  87.2 4.5 %collective-permute-start.15 = (f32[8,128]{1,0:T(8,128)S(1)}, f32[8,128]{1,0:T(8,128)S(1)}, u32[]{:S(2)}, u32[]{:S(2)}) collective-permute-start(f32[8,128]{1,0:T(8,128)S(1)} %add.30.refs_0_), channel_id=1, source_target_pairs={{0,5},{1,4},{2,7},{3,6},{4,1},{5,0},{6,3},{7,2},{8,13},{9,12},{10,... | collective-permute-start | bytes 12296 | tf_op jit(solution)/shard_map/ppermute | solution.py:394
  88.0 4.2 %collective-permute-start.16 = (f32[8,128]{1,0:T(8,128)S(1)}, f32[8,128]{1,0:T(8,128)S(1)}, u32[]{:S(2)}, u32[]{:S(2)}) collective-permute-start(f32[8,128]{1,0:T(8,128)S(1)} %add.30.refs_0_), channel_id=1, source_target_pairs={{0,3},{1,2},{2,5},{3,4},{4,7},{5,6},{6,1},{7,0},{8,11},{9,10},{10,... | collective-permute-start | bytes 12296 | tf_op jit(solution)/shard_map/ppermute | solution.py:394
  89.9 3.0 %collective-permute-start.17 = (f32[8,128]{1,0:T(8,128)S(1)}, f32[8,128]{1,0:T(8,128)S(1)}, u32[]{:S(2)}, u32[]{:S(2)}) collective-permute-start(f32[8,128]{1,0:T(8,128)S(1)} %add.30.refs_0_), channel_id=1, source_target_pairs={{0,7},{1,6},{2,1},{3,0},{4,3},{5,2},{6,5},{7,4},{8,15},{9,14},{10,... | collective-permute-start | bytes 12296 | tf_op jit(solution)/shard_map/ppermute | solution.py:394
  107.1 2.3 %collective-permute-start.18 = (f32[8,128]{1,0:T(8,128)S(1)}, f32[8,128]{1,0:T(8,128)S(1)}, u32[]{:S(2)}, u32[]{:S(2)}) collective-permute-start(f32[8,128]{1,0:T(8,128)S(1)} %get-tuple-element.42), channel_id=1, source_target_pairs={{0,1},{1,0},{2,3},{3,2},{4,5},{5,4},{6,7},{7,6},{8,9},{9,8},{10,11... | collective-permute-start | bytes 12296 | tf_op jit(solution)/shard_map/ppermute | solution.py:416
  109.4 4.5 %collective-permute-start.19 = (f32[8,128]{1,0:T(8,128)S(1)}, f32[8,128]{1,0:T(8,128)S(1)}, u32[]{:S(2)}, u32[]{:S(2)}) collective-permute-start(f32[8,128]{1,0:T(8,128)S(1)} %add.31), channel_id=1, source_target_pairs={{0,5},{1,4},{2,7},{3,6},{4,1},{5,0},{6,3},{7,2},{8,13},{9,12},{10,... | collective-permute-start | bytes 12296 | tf_op jit(solution)/shard_map/ppermute | solution.py:394
  110.8 4.2 %collective-permute-start.20 = (f32[8,128]{1,0:T(8,128)S(1)}, f32[8,128]{1,0:T(8,128)S(1)}, u32[]{:S(2)}, u32[]{:S(2)}) collective-permute-start(f32[8,128]{1,0:T(8,128)S(1)} %add.31), channel_id=1, source_target_pairs={{0,3},{1,2},{2,5},{3,4},{4,7},{5,6},{6,1},{7,0},{8,11},{9,10},{10,... | collective-permute-start | bytes 12296 | tf_op jit(solution)/shard_map/ppermute | solution.py:394
  112.4 3.0 %collective-permute-start.21 = (f32[8,128]{1,0:T(8,128)S(1)}, f32[8,128]{1,0:T(8,128)S(1)}, u32[]{:S(2)}, u32[]{:S(2)}) collective-permute-start(f32[8,128]{1,0:T(8,128)S(1)} %add.31), channel_id=1, source_target_pairs={{0,7},{1,6},{2,1},{3,0},{4,3},{5,2},{6,5},{7,4},{8,15},{9,14},{10,... | collective-permute-start | bytes 12296 | tf_op jit(solution)/shard_map/ppermute | solution.py:394
  (1 other events, 0.7 us)

commit v11 on v10

--- a/solution.py
+++ b/solution.py
@@ -168,29 +168,34 @@
     lax.fori_loop(0, rows // STEP, rows_step, 0)
 
 
-def piece_steps(k, place, x_ref, points_ref, mass_ref, top_ref, old_sum_ref, t_ref, sum_ref):
-    blocks, biases = piece_blocks(k, place, points_ref, mass_ref)
+def piece_steps(pieces, place, x_ref, mass_ref, top_ref, old_sum_ref, t_ref, sum_ref):
+    chunks = []
+    for k, points_ref in pieces:
+        blocks, biases = piece_blocks(k, place, points_ref, mass_ref)
+        chunks += [(points_ref, m, blocks[m], biases[m]) for m in range(4)]
     for r in range(0, x_ref.shape[0], ROWS):
         top = top_ref[r : r + ROWS, :]
         total = old_sum_ref[r : r + ROWS, :]
-        for m in range(4):
+        for points_ref, m, block, bias in chunks:
             product = piece_product(x_ref, points_ref, r, m)
             for side in range(2):
-                terms = product[:, lane_tile(side)] * BITS + biases[m][side]
-                t_ref[2 * blocks[m] + side, r : r + ROWS, :] = terms
+                terms = product[:, lane_tile(side)] * BITS + bias[side]
+                t_ref[2 * block + side, r : r + ROWS, :] = terms
                 total += jnp.exp2(terms - top)
         sum_ref[r : r + ROWS, :] = total
 
 
 def more_terms_kernel(k, place, x_ref, old_ref, old_sum_ref, top_ref, points_ref, mass_ref, *refs):
     t_ref, sum_ref = refs
-    piece_steps(k, place, x_ref, points_ref, mass_ref, top_ref, old_sum_ref, t_ref, sum_ref)
-
-
-def last_terms_kernel(k, place, x_ref, old_ref, old_sum_ref, old_top_ref, points_ref, mass_ref, *refs):
-    t_ref, sum_ref, out_ref, top_ref = refs
+    pieces = [(k, points_ref)]
+    piece_steps(pieces, place, x_ref, mass_ref, top_ref, old_sum_ref, t_ref, sum_ref)
+
+
+def last_terms_kernel(shifts, place, x_ref, old_ref, old_sum_ref, old_top_ref, *refs):
+    points_ref, more_ref, mass_ref, t_ref, sum_ref, out_ref, top_ref = refs
     tiles, rows, _ = t_ref.shape
-    piece_steps(k, place, x_ref, points_ref, mass_ref, old_top_ref, old_sum_ref, t_ref, sum_ref)
+    pieces = list(zip(shifts, (points_ref, more_ref)))
+    piece_steps(pieces, place, x_ref, mass_ref, old_top_ref, old_sum_ref, t_ref, sum_ref)
     total = collapse(sum_ref)
     out_ref[...] = collapse_top(old_top_ref) * LN2 + jnp.log(total)
 
@@ -424,17 +429,17 @@
     terms, top, sums, squares = call(
         first_terms_kernel, (big, wide, wide, by_row), [SMEM] + [VMEM] * 3, []
     )(place, src_points, first, tgt_mass)
-    for k in (1, 3):
+    for k in (1,):
         terms, sums = call(
             functools.partial(more_terms_kernel, k), (big, wide), [SMEM] + [VMEM] * 6, [], {2: 0, 3: 1}
         )(place, src_points, resident(terms), resident(sums), resident(top), pieces[k], tgt_mass)
     terms, sums, lse = call(
-        functools.partial(last_terms_kernel, 2),
+        functools.partial(last_terms_kernel, (3, 2)),
         (big, wide, by_row),
-        [SMEM] + [VMEM] * 6,
+        [SMEM] + [VMEM] * 7,
         [wide],
         {2: 0, 3: 1},
-    )(place, src_points, resident(terms), resident(sums), resident(top), pieces[2], tgt_mass)
+    )(place, src_points, resident(terms), resident(sums), resident(top), pieces[3], pieces[2], tgt_mass)
     lse, src_lse = call(column_kernel, (columns_out, by_row), [VMEM] * 6, [wide, line])(
         resident(terms), *over_col(lse, lse_all), src_mass
     )

time: 116 us -> 116 us (level)
  blocking collectives: 37.7 us -> 36 us
  waiting for transfers between devices: 15.7 us -> 17.4 us
    all_to_all x3, blocking collectives: 37.7 us -> 36 us  [over_row(): return lax.all_to_all(value, ROW, 0, 0, tiled=True)]
    ppermute x6, waiting for transfers between devices: 5.34 us -> 7.06 us  [turned(): found[k] = lax.ppermute(value, ALL, pairs)]
    pallas_call x2 -> x1, Pallas kernels: 3.44 us -> 1.72 us  [body(): call(functools.partial(more_terms_kernel, k), (big, wide), [SMEM] + [VMEM...]
    unnamed x9 -> x11, local copies, waits for them, and re-layouts: 2.73 us -> 2.74 us
  transfers between devices with their start and end apart: 22 -> 22, of which waited for: 16 -> 16; matrix products, arithmetic and copies ran while one was open for 1% -> 1% of each run, Pallas kernels for 6% -> 5%
where the time goes in v11:
time: 116 us; the launch traced here: 115 us
  starting transfers between devices  37 us (32%)
  blocking collectives  36 us (31%)
  Pallas kernels  20.7 us (18%)
  waiting for transfers between devices  17.4 us (15%)
  local copies, waits for them, and re-layouts  3.26 us (3%)
    all_to_all x3, blocking collectives, over_row(): return lax.all_to_all(value, ROW, 0, 0, tiled=True)  36 us
    ppermute x12, starting transfers between devices, crossed(): return lax.ppermute(value, ALL, pairs)  19.3 us
    ppermute x6, starting transfers between devices, turned(): found[k] = lax.ppermute(value, ALL, pairs)  10.2 us
    ppermute x4, starting transfers between devices, over_col(): both = combine([value, lax.ppermute(value, 'col_1', [(0, 1), (1, 0)])])  7.5 us
    ppermute x12, waiting for transfers between devices, crossed(): return lax.ppermute(value, ALL, pairs)  7.07 us
    ppermute x6, waiting for transfers between devices, turned(): found[k] = lax.ppermute(value, ALL, pairs)  7.06 us
    pallas_call x1, Pallas kernels, body(): call(first_terms_kernel, (big, wide, wide, by_row), [SMEM] + [VMEM] * 3, [])  3.53 us
    pallas_call x1, Pallas kernels, body(): call(plan_kernel, (big, by_row, by_column), [VMEM] * 5, [wide, wide, line...  3.46 us
  transfers between devices with their start and end apart: 22, of which 16 were waited for; matrix products, arithmetic and copies ran while one was open for 1% of the time, Pallas kernels for 5%

profile of v11, /device:TPU:1, one launch (start us, length us, event | category | flops | bytes accessed | tf_op | source)
XLA Modules:
  0.0 115.2 jit_solution(9375588539852774241)
XLA Ops:
  0.6 2.2 %collective-permute-start = (bf16[256,256]{1,0:T(8,128)(2,1)}, bf16[256,256]{1,0:T(8,128)(2,1)S(1)}, u32[]{:S(2)}, u32[]{:S(2)}) collective-permute-start(bf16[256,256]{1,0:T(8,128)(2,1)} %param.5), channel_id=1, source_target_pairs={{0,8},{1,33},{2,10},{3,35},{4,12},{5,37},{6,14},{7,39},{8,16},{9,4... | collective-permute-start | bytes 393224 | tf_op jit(solution)/shard_map/ppermute | solution.py:391
  2.8 2.6 %collective-permute-start.1 = (bf16[256,256]{1,0:T(8,128)(2,1)}, bf16[256,256]{1,0:T(8,128)(2,1)S(1)}, u32[]{:S(2)}, u32[]{:S(2)}) collective-permute-start(bf16[256,256]{1,0:T(8,128)(2,1)} %param.5), channel_id=1, source_target_pairs={{0,16},{1,65},{2,18},{3,67},{4,20},{5,69},{6,22},{7,71},{8,24},{9,... | collective-permute-start | bytes 393224 | tf_op jit(solution)/shard_map/ppermute | solution.py:391
  7.5 2.2 %collective-permute-done.1 = bf16[256,256]{1,0:T(8,128)(2,1)S(1)} collective-permute-done((bf16[256,256]{1,0:T(8,128)(2,1)}, bf16[256,256]{1,0:T(8,128)(2,1)S(1)}, u32[]{:S(2)}, u32[]{:S(2)}) %collective-permute-start.1) | collective-permute-done | bytes 131104 | tf_op jit(solution)/shard_map/ppermute | solution.py:391
  12.5 1.5 %collective-permute-start.5 = (bf16[1024,256]{1,0:T(8,128)(2,1)S(1)}, bf16[1024,256]{1,0:T(8,128)(2,1)S(1)}, u32[]{:S(2)}, u32[]{:S(2)}) collective-permute-start(bf16[1024,256]{1,0:T(8,128)(2,1)S(1)} %constant_dynamic-update-slice_fusion.points_ref), channel_id=1, source_target_pairs={{0,64},{1,17},{2,66},{3,19},{4,68},{5,21},{6,70},{7,23},{8,72},{9,... | collective-permute-start | bytes 1572872 | tf_op jit(solution)/shard_map/ppermute | solution.py:391
  15.9 3.5 %shard_map.67 = (f32[32,1024,128]{2,1,0:T(8,128)S(1)}, f32[1024,128]{1,0:T(8,128)S(1)}, f32[1024,128]{1,0:T(8,128)S(1)}, f32[8,128]{1,0:T(8,128)S(1)}) custom-call(s32[3]{0:T(128)S(1)} %pad_add_fusion.place, bf16[1024,256]{1,0:T(8,128)(2,1)S(1)} %copy-done, bf16[1024,256]{1,0:T(8,128)(2,1)S(1)} %constant_dynamic-update-slice_fusion.points_ref, ...), custom_call_target="tpu_custom_call" | custom-call | tf_op jit(solution)/shard_map/pallas_call | solution.py:429
  19.5 1.7 %shard_map.68 = (f32[32,1024,128]{2,1,0:T(8,128)S(1)}, f32[1024,128]{1,0:T(8,128)S(1)}) custom-call(s32[3]{0:T(128)S(1)} %pad_add_fusion.place, bf16[1024,256]{1,0:T(8,128)(2,1)S(1)} %copy-done, f32[32,1024,128]{2,1,0:T(8,128)S(1)} %get-tuple-element.21.old_ref, ...), custom_call_target="tpu_custom_call", output_to_operand_aliasing={{0}: (2, {}), {1}: (3, {})} | custom-call | tf_op jit(solution)/shard_map/pallas_call | solution.py:433
  21.2 4.8 %collective-permute-done.5.refs_1_ = bf16[1024,256]{1,0:T(8,128)(2,1)S(1)} collective-permute-done((bf16[1024,256]{1,0:T(8,128)(2,1)S(1)}, bf16[1024,256]{1,0:T(8,128)(2,1)S(1)}, u32[]{:S(2)}, u32[]{:S(2)}) %collective-permute-start.5) | collective-permute-done | bytes 524320 | tf_op jit(solution)/shard_map/ppermute | solution.py:391
  26.0 3.0 %shard_map.69 = (f32[32,1024,128]{2,1,0:T(8,128)S(1)}, f32[1024,128]{1,0:T(8,128)S(1)}, f32[8,128]{1,0:T(8,128)S(1)}) custom-call(s32[3]{0:T(128)S(1)} %pad_add_fusion.place, bf16[1024,256]{1,0:T(8,128)(2,1)S(1)} %copy-done, f32[32,1024,128]{2,1,0:T(8,128)S(1)} %get-tuple-element.24.old_ref, ...), custom_call_target="tpu_custom_call", output_to_operand_aliasing={{0}: (2, {}), {1}: (3, {})} | custom-call | tf_op jit(solution)/shard_map/pallas_call | solution.py:436
  29.0 3.0 %collective-permute-start.6 = (f32[8,128]{1,0:T(8,128)S(1)}, f32[8,128]{1,0:T(8,128)S(1)}, u32[]{:S(2)}, u32[]{:S(2)}) collective-permute-start(f32[8,128]{1,0:T(8,128)S(1)} %get-tuple-element.27), channel_id=1, source_target_pairs={{0,1},{1,0},{2,3},{3,2},{4,5},{5,4},{6,7},{7,6},{8,9},{9,8},{10,11... | collective-permute-start | bytes 12296 | tf_op jit(solution)/shard_map/ppermute | solution.py:421
  32.8 3.9 %collective-permute-start.7 = (f32[8,128]{1,0:T(8,128)S(1)}, f32[8,128]{1,0:T(8,128)S(1)}, u32[]{:S(2)}, u32[]{:S(2)}) collective-permute-start(f32[8,128]{1,0:T(8,128)S(1)} %log_add_fusion.refs_0_), channel_id=1, source_target_pairs={{0,5},{1,4},{2,7},{3,6},{4,1},{5,0},{6,3},{7,2},{8,13},{9,12},{10,... | collective-permute-start | bytes 12296 | tf_op jit(solution)/shard_map/ppermute | solution.py:399
  37.5 2.2 %collective-permute-start.9 = (f32[8,128]{1,0:T(8,128)S(1)}, f32[8,128]{1,0:T(8,128)S(1)}, u32[]{:S(2)}, u32[]{:S(2)}) collective-permute-start(f32[8,128]{1,0:T(8,128)S(1)} %log_add_fusion.refs_0_), channel_id=1, source_target_pairs={{0,7},{1,6},{2,1},{3,0},{4,3},{5,2},{6,5},{7,4},{8,15},{9,14},{10,... | collective-permute-start | bytes 12296 | tf_op jit(solution)/shard_map/ppermute | solution.py:399
  41.0 3.1 %shard_map.70 = (f32[16,32,128]{2,1,0:T(8,128)S(1)}, f32[8,128]{1,0:T(8,128)S(1)}) custom-call(f32[32,1024,128]{2,1,0:T(8,128)S(1)} %get-tuple-element.26.t_ref, f32[8,128]{1,0:T(8,128)S(1)} %log_add_fusion.refs_0_, f32[8,128]{1,0:T(8,128)S(1)} %collective-permute-done.7.refs_1_, f32[8,128]{1,0:T(8,128)S(1)} %collective-permute-done.8.refs_2_, ...), custom_call_target="tpu_custom_call" | custom-call | tf_op jit(solution)/shard_map/pallas_call | solution.py:443
  44.1 13.8 %all_to_all.15.parts_ref = f32[16,32,128]{2,1,0:T(8,128)S(1)} all-to-all(f32[16,32,128]{2,1,0:T(8,128)S(1)} %get-tuple-element.28), channel_id=1, replica_groups=mesh['row_0'=4,'row_1'=4,'col_0'=4,'col_1'=2] {'row_0','row_1'}, dimensions={0} | all-to-all | bytes 524288 | tf_op jit(solution)/shard_map/all_to_all | solution.py:425
  57.9 3.5 %shard_map.71 = (f32[32,1024,128]{2,1,0:T(8,128)S(1)}, f32[8,128]{1,0:T(8,128)S(1)}, f32[32,128]{1,0:T(8,128)S(1)}) custom-call(f32[32,1024,128]{2,1,0:T(8,128)S(1)} %get-tuple-element.26.t_ref, f32[16,32,128]{2,1,0:T(8,128)S(1)} %all_to_all.15.parts_ref, f32[32,128]{1,0:T(8,128)S(1)} %bitcast.11, ...), custom_call_target="tpu_custom_call", output_to_operand_aliasing={{0}: (0, {})} | custom-call | tf_op jit(solution)/shard_map/pallas_call | solution.py:446
  65.0 2.2 %collective-permute-start.12 = (f32[8,128]{1,0:T(8,128)S(1)}, f32[8,128]{1,0:T(8,128)S(1)}, u32[]{:S(2)}, u32[]{:S(2)}) collective-permute-start(f32[8,128]{1,0:T(8,128)S(1)} %add.29.refs_0_), channel_id=1, source_target_pairs={{0,3},{1,2},{2,5},{3,4},{4,7},{5,6},{6,1},{7,0},{8,11},{9,10},{10,... | collective-permute-start | bytes 12296 | tf_op jit(solution)/shard_map/ppermute | solution.py:399
  70.2 1.6 %shard_map.72 = f32[16,32,128]{2,1,0:T(8,128)S(1)} custom-call(f32[32,1024,128]{2,1,0:T(8,128)S(1)} %get-tuple-element.30.plan_ref, f32[8,128]{1,0:T(8,128)S(1)} %add.29.refs_0_, f32[8,128]{1,0:T(8,128)S(1)} %collective-permute-done.11.refs_1_, f32[8,128]{1,0:T(8,128)S(1)} %collective-permute-done.12.refs_2_, f32[8,128]{1,0:T(8,128)S(1)} %collective-permute-done.13.refs_3_, ...), custom_call_target="tpu_custom_call" | custom-call | tf_op jit(solution)/shard_map/pallas_call | solution.py:450
  71.8 10.8 %all_to_all.16.parts_ref = f32[16,32,128]{2,1,0:T(8,128)S(1)} all-to-all(f32[16,32,128]{2,1,0:T(8,128)S(1)} %shard_map.72), channel_id=1, replica_groups=mesh['row_0'=4,'row_1'=4,'col_0'=4,'col_1'=2] {'row_0','row_1'}, dimensions={0} | all-to-all | bytes 524288 | tf_op jit(solution)/shard_map/all_to_all | solution.py:425
  82.6 1.6 %shard_map.73 = f32[8,128]{1,0:T(8,128)S(1)} custom-call(f32[32,1024,128]{2,1,0:T(8,128)S(1)} %get-tuple-element.30.plan_ref, f32[16,32,128]{2,1,0:T(8,128)S(1)} %all_to_all.16.parts_ref, f32[32,128]{1,0:T(8,128)S(1)} %bitcast.12), custom_call_target="tpu_custom_call" | custom-call | tf_op jit(solution)/shard_map/pallas_call | solution.py:453
  84.2 1.6 %collective-permute-start.14 = (f32[8,128]{1,0:T(8,128)S(1)}, f32[8,128]{1,0:T(8,128)S(1)}, u32[]{:S(2)}, u32[]{:S(2)}) collective-permute-start(f32[8,128]{1,0:T(8,128)S(1)} %shard_map.73), channel_id=1, source_target_pairs={{0,1},{1,0},{2,3},{3,2},{4,5},{5,4},{6,7},{7,6},{8,9},{9,8},{10,11... | collective-permute-start | bytes 12296 | tf_op jit(solution)/shard_map/ppermute | solution.py:421
  87.3 1.8 %collective-permute-start.16 = (f32[8,128]{1,0:T(8,128)S(1)}, f32[8,128]{1,0:T(8,128)S(1)}, u32[]{:S(2)}, u32[]{:S(2)}) collective-permute-start(f32[8,128]{1,0:T(8,128)S(1)} %add.30.refs_0_), channel_id=1, source_target_pairs={{0,3},{1,2},{2,5},{3,4},{4,7},{5,6},{6,1},{7,0},{8,11},{9,10},{10,... | collective-permute-start | bytes 12296 | tf_op jit(solution)/shard_map/ppermute | solution.py:399
  92.2 2.1 %shard_map.74 = (f32[16,40,128]{2,1,0:T(8,128)S(1)}, f32[8,128]{1,0:T(8,128)}) custom-call(f32[32,1024,128]{2,1,0:T(8,128)S(1)} %get-tuple-element.30.plan_ref, f32[8,128]{1,0:T(8,128)S(1)} %add.30.refs_0_, f32[8,128]{1,0:T(8,128)S(1)} %collective-permute-done.15.refs_1_, f32[8,128]{1,0:T(8,128)S(1)} %collective-permute-done.16.refs_2_, ...), custom_call_target="tpu_custom_call" | custom-call | tf_op jit(solution)/shard_map/pallas_call | solution.py:454
  94.3 11.5 %all_to_all.17.parts_ref = f32[16,40,128]{2,1,0:T(8,128)S(1)} all-to-all(f32[16,40,128]{2,1,0:T(8,128)S(1)} %get-tuple-element.34), channel_id=1, replica_groups=mesh['row_0'=4,'row_1'=4,'col_0'=4,'col_1'=2] {'row_0','row_1'}, dimensions={0} | all-to-all | bytes 655360 | tf_op jit(solution)/shard_map/all_to_all | solution.py:425
  106.4 1.5 %collective-permute-start.18 = (f32[8,128]{1,0:T(8,128)S(1)}, f32[8,128]{1,0:T(8,128)S(1)}, u32[]{:S(2)}, u32[]{:S(2)}) collective-permute-start(f32[8,128]{1,0:T(8,128)S(1)} %get-tuple-element.38), channel_id=1, source_target_pairs={{0,1},{1,0},{2,3},{3,2},{4,5},{5,4},{6,7},{7,6},{8,9},{9,8},{10,11... | collective-permute-start | bytes 12296 | tf_op jit(solution)/shard_map/ppermute | solution.py:421
  110.1 1.5 %collective-permute-start.20 = (f32[8,128]{1,0:T(8,128)S(1)}, f32[8,128]{1,0:T(8,128)S(1)}, u32[]{:S(2)}, u32[]{:S(2)}) collective-permute-start(f32[8,128]{1,0:T(8,128)S(1)} %add.31), channel_id=1, source_target_pairs={{0,3},{1,2},{2,5},{3,4},{4,7},{5,6},{6,1},{7,0},{8,11},{9,10},{10,... | collective-permute-start | bytes 12296 | tf_op jit(solution)/shard_map/ppermute | solution.py:399
  (51 shorter events, 27.4 us)
Async XLA Ops:
  0.6 25.4 %copy-start.2 = (f32[4096]{0:T(1024)S(1)}, f32[4096]{0:T(1024)}, u32[]{:S(2)}) copy-start(f32[4096]{0:T(1024)} %param.7) | copy-start | bytes 49156
  0.6 6.8 %collective-permute-start = (bf16[256,256]{1,0:T(8,128)(2,1)}, bf16[256,256]{1,0:T(8,128)(2,1)S(1)}, u32[]{:S(2)}, u32[]{:S(2)}) collective-permute-start(bf16[256,256]{1,0:T(8,128)(2,1)} %param.5), channel_id=1, source_target_pairs={{0,8},{1,33},{2,10},{3,35},{4,12},{5,37},{6,14},{7,39},{8,16},{9,4... | collective-permute-start | bytes 393224 | tf_op jit(solution)/shard_map/ppermute | solution.py:391
  2.8 6.9 %collective-permute-start.1 = (bf16[256,256]{1,0:T(8,128)(2,1)}, bf16[256,256]{1,0:T(8,128)(2,1)S(1)}, u32[]{:S(2)}, u32[]{:S(2)}) collective-permute-start(bf16[256,256]{1,0:T(8,128)(2,1)} %param.5), channel_id=1, source_target_pairs={{0,16},{1,65},{2,18},{3,67},{4,20},{5,69},{6,22},{7,71},{8,24},{9,... | collective-permute-start | bytes 393224 | tf_op jit(solution)/shard_map/ppermute | solution.py:391
  5.5 4.3 %collective-permute-start.2 = (bf16[256,256]{1,0:T(8,128)(2,1)}, bf16[256,256]{1,0:T(8,128)(2,1)S(1)}, u32[]{:S(2)}, u32[]{:S(2)}) collective-permute-start(bf16[256,256]{1,0:T(8,128)(2,1)} %param.5), channel_id=1, source_target_pairs={{0,24},{1,97},{2,26},{3,99},{4,28},{5,101},{6,30},{7,103},{8,0},{9... | collective-permute-start | bytes 393224 | tf_op jit(solution)/shard_map/ppermute | solution.py:391
  9.8 9.7 %collective-permute-start.3 = (bf16[1024,256]{1,0:T(8,128)(2,1)S(1)}, bf16[1024,256]{1,0:T(8,128)(2,1)S(1)}, u32[]{:S(2)}, u32[]{:S(2)}) collective-permute-start(bf16[1024,256]{1,0:T(8,128)(2,1)S(1)} %constant_dynamic-update-slice_fusion.points_ref), channel_id=1, source_target_pairs={{0,32},{1,9},{2,34},{3,11},{4,36},{5,13},{6,38},{7,15},{8,40},{9,1... | collective-permute-start | bytes 1572872 | tf_op jit(solution)/shard_map/ppermute | solution.py:391
  11.1 10.1 %collective-permute-start.4 = (bf16[1024,256]{1,0:T(8,128)(2,1)S(1)}, bf16[1024,256]{1,0:T(8,128)(2,1)S(1)}, u32[]{:S(2)}, u32[]{:S(2)}) collective-permute-start(bf16[1024,256]{1,0:T(8,128)(2,1)S(1)} %constant_dynamic-update-slice_fusion.points_ref), channel_id=1, source_target_pairs={{0,96},{1,25},{2,98},{3,27},{4,100},{5,29},{6,102},{7,31},{8,104},... | collective-permute-start | bytes 1572872 | tf_op jit(solution)/shard_map/ppermute | solution.py:391
  12.5 13.5 %collective-permute-start.5 = (bf16[1024,256]{1,0:T(8,128)(2,1)S(1)}, bf16[1024,256]{1,0:T(8,128)(2,1)S(1)}, u32[]{:S(2)}, u32[]{:S(2)}) collective-permute-start(bf16[1024,256]{1,0:T(8,128)(2,1)S(1)} %constant_dynamic-update-slice_fusion.points_ref), channel_id=1, source_target_pairs={{0,64},{1,17},{2,66},{3,19},{4,68},{5,21},{6,70},{7,23},{8,72},{9,... | collective-permute-start | bytes 1572872 | tf_op jit(solution)/shard_map/ppermute | solution.py:391
  19.5 21.5 %copy-start.3 = (f32[1024]{0:T(1024)S(1)}, f32[1024]{0:T(1024)}, u32[]{:S(2)}) copy-start(f32[1024]{0:T(1024)} %param.6) | copy-start | bytes 12292
  29.0 3.8 %collective-permute-start.6 = (f32[8,128]{1,0:T(8,128)S(1)}, f32[8,128]{1,0:T(8,128)S(1)}, u32[]{:S(2)}, u32[]{:S(2)}) collective-permute-start(f32[8,128]{1,0:T(8,128)S(1)} %get-tuple-element.27), channel_id=1, source_target_pairs={{0,1},{1,0},{2,3},{3,2},{4,5},{5,4},{6,7},{7,6},{8,9},{9,8},{10,11... | collective-permute-start | bytes 12296 | tf_op jit(solution)/shard_map/ppermute | solution.py:421
  32.8 6.9 %collective-permute-start.7 = (f32[8,128]{1,0:T(8,128)S(1)}, f32[8,128]{1,0:T(8,128)S(1)}, u32[]{:S(2)}, u32[]{:S(2)}) collective-permute-start(f32[8,128]{1,0:T(8,128)S(1)} %log_add_fusion.refs_0_), channel_id=1, source_target_pairs={{0,5},{1,4},{2,7},{3,6},{4,1},{5,0},{6,3},{7,2},{8,13},{9,12},{10,... | collective-permute-start | bytes 12296 | tf_op jit(solution)/shard_map/ppermute | solution.py:399
  36.7 4.2 %collective-permute-start.8 = (f32[8,128]{1,0:T(8,128)S(1)}, f32[8,128]{1,0:T(8,128)S(1)}, u32[]{:S(2)}, u32[]{:S(2)}) collective-permute-start(f32[8,128]{1,0:T(8,128)S(1)} %log_add_fusion.refs_0_), channel_id=1, source_target_pairs={{0,3},{1,2},{2,5},{3,4},{4,7},{5,6},{6,1},{7,0},{8,11},{9,10},{10,... | collective-permute-start | bytes 12296 | tf_op jit(solution)/shard_map/ppermute | solution.py:399
  37.5 3.5 %collective-permute-start.9 = (f32[8,128]{1,0:T(8,128)S(1)}, f32[8,128]{1,0:T(8,128)S(1)}, u32[]{:S(2)}, u32[]{:S(2)}) collective-permute-start(f32[8,128]{1,0:T(8,128)S(1)} %log_add_fusion.refs_0_), channel_id=1, source_target_pairs={{0,7},{1,6},{2,1},{3,0},{4,3},{5,2},{6,5},{7,4},{8,15},{9,14},{10,... | collective-permute-start | bytes 12296 | tf_op jit(solution)/shard_map/ppermute | solution.py:399
  61.4 2.2 %collective-permute-start.10 = (f32[8,128]{1,0:T(8,128)S(1)}, f32[8,128]{1,0:T(8,128)S(1)}, u32[]{:S(2)}, u32[]{:S(2)}) collective-permute-start(f32[8,128]{1,0:T(8,128)S(1)} %get-tuple-element.31), channel_id=1, source_target_pairs={{0,1},{1,0},{2,3},{3,2},{4,5},{5,4},{6,7},{7,6},{8,9},{9,8},{10,11... | collective-permute-start | bytes 12296 | tf_op jit(solution)/shard_map/ppermute | solution.py:421
  63.6 4.5 %collective-permute-start.11 = (f32[8,128]{1,0:T(8,128)S(1)}, f32[8,128]{1,0:T(8,128)S(1)}, u32[]{:S(2)}, u32[]{:S(2)}) collective-permute-start(f32[8,128]{1,0:T(8,128)S(1)} %add.29.refs_0_), channel_id=1, source_target_pairs={{0,5},{1,4},{2,7},{3,6},{4,1},{5,0},{6,3},{7,2},{8,13},{9,12},{10,... | collective-permute-start | bytes 12296 | tf_op jit(solution)/shard_map/ppermute | solution.py:399
  65.0 4.2 %collective-permute-start.12 = (f32[8,128]{1,0:T(8,128)S(1)}, f32[8,128]{1,0:T(8,128)S(1)}, u32[]{:S(2)}, u32[]{:S(2)}) collective-permute-start(f32[8,128]{1,0:T(8,128)S(1)} %add.29.refs_0_), channel_id=1, source_target_pairs={{0,3},{1,2},{2,5},{3,4},{4,7},{5,6},{6,1},{7,0},{8,11},{9,10},{10,... | collective-permute-start | bytes 12296 | tf_op jit(solution)/shard_map/ppermute | solution.py:399
  67.2 3.0 %collective-permute-start.13 = (f32[8,128]{1,0:T(8,128)S(1)}, f32[8,128]{1,0:T(8,128)S(1)}, u32[]{:S(2)}, u32[]{:S(2)}) collective-permute-start(f32[8,128]{1,0:T(8,128)S(1)} %add.29.refs_0_), channel_id=1, source_target_pairs={{0,7},{1,6},{2,1},{3,0},{4,3},{5,2},{6,5},{7,4},{8,15},{9,14},{10,... | collective-permute-start | bytes 12296 | tf_op jit(solution)/shard_map/ppermute | solution.py:399
  84.2 2.4 %collective-permute-start.14 = (f32[8,128]{1,0:T(8,128)S(1)}, f32[8,128]{1,0:T(8,128)S(1)}, u32[]{:S(2)}, u32[]{:S(2)}) collective-permute-start(f32[8,128]{1,0:T(8,128)S(1)} %shard_map.73), channel_id=1, source_target_pairs={{0,1},{1,0},{2,3},{3,2},{4,5},{5,4},{6,7},{7,6},{8,9},{9,8},{10,11... | collective-permute-start | bytes 12296 | tf_op jit(solution)/shard_map/ppermute | solution.py:421
  86.6 4.5 %collective-permute-start.15 = (f32[8,128]{1,0:T(8,128)S(1)}, f32[8,128]{1,0:T(8,128)S(1)}, u32[]{:S(2)}, u32[]{:S(2)}) collective-permute-start(f32[8,128]{1,0:T(8,128)S(1)} %add.30.refs_0_), channel_id=1, source_target_pairs={{0,5},{1,4},{2,7},{3,6},{4,1},{5,0},{6,3},{7,2},{8,13},{9,12},{10,... | collective-permute-start | bytes 12296 | tf_op jit(solution)/shard_map/ppermute | solution.py:399
  87.3 4.2 %collective-permute-start.16 = (f32[8,128]{1,0:T(8,128)S(1)}, f32[8,128]{1,0:T(8,128)S(1)}, u32[]{:S(2)}, u32[]{:S(2)}) collective-permute-start(f32[8,128]{1,0:T(8,128)S(1)} %add.30.refs_0_), channel_id=1, source_target_pairs={{0,3},{1,2},{2,5},{3,4},{4,7},{5,6},{6,1},{7,0},{8,11},{9,10},{10,... | collective-permute-start | bytes 12296 | tf_op jit(solution)/shard_map/ppermute | solution.py:399
  89.2 3.0 %collective-permute-start.17 = (f32[8,128]{1,0:T(8,128)S(1)}, f32[8,128]{1,0:T(8,128)S(1)}, u32[]{:S(2)}, u32[]{:S(2)}) collective-permute-start(f32[8,128]{1,0:T(8,128)S(1)} %add.30.refs_0_), channel_id=1, source_target_pairs={{0,7},{1,6},{2,1},{3,0},{4,3},{5,2},{6,5},{7,4},{8,15},{9,14},{10,... | collective-permute-start | bytes 12296 | tf_op jit(solution)/shard_map/ppermute | solution.py:399
  106.4 2.3 %collective-permute-start.18 = (f32[8,128]{1,0:T(8,128)S(1)}, f32[8,128]{1,0:T(8,128)S(1)}, u32[]{:S(2)}, u32[]{:S(2)}) collective-permute-start(f32[8,128]{1,0:T(8,128)S(1)} %get-tuple-element.38), channel_id=1, source_target_pairs={{0,1},{1,0},{2,3},{3,2},{4,5},{5,4},{6,7},{7,6},{8,9},{9,8},{10,11... | collective-permute-start | bytes 12296 | tf_op jit(solution)/shard_map/ppermute | solution.py:421
  108.7 4.5 %collective-permute-start.19 = (f32[8,128]{1,0:T(8,128)S(1)}, f32[8,128]{1,0:T(8,128)S(1)}, u32[]{:S(2)}, u32[]{:S(2)}) collective-permute-start(f32[8,128]{1,0:T(8,128)S(1)} %add.31), channel_id=1, source_target_pairs={{0,5},{1,4},{2,7},{3,6},{4,1},{5,0},{6,3},{7,2},{8,13},{9,12},{10,... | collective-permute-start | bytes 12296 | tf_op jit(solution)/shard_map/ppermute | solution.py:399
  110.1 4.2 %collective-permute-start.20 = (f32[8,128]{1,0:T(8,128)S(1)}, f32[8,128]{1,0:T(8,128)S(1)}, u32[]{:S(2)}, u32[]{:S(2)}) collective-permute-start(f32[8,128]{1,0:T(8,128)S(1)} %add.31), channel_id=1, source_target_pairs={{0,3},{1,2},{2,5},{3,4},{4,7},{5,6},{6,1},{7,0},{8,11},{9,10},{10,... | collective-permute-start | bytes 12296 | tf_op jit(solution)/shard_map/ppermute | solution.py:399
  111.7 3.0 %collective-permute-start.21 = (f32[8,128]{1,0:T(8,128)S(1)}, f32[8,128]{1,0:T(8,128)S(1)}, u32[]{:S(2)}, u32[]{:S(2)}) collective-permute-start(f32[8,128]{1,0:T(8,128)S(1)} %add.31), channel_id=1, source_target_pairs={{0,7},{1,6},{2,1},{3,0},{4,3},{5,2},{6,5},{7,4},{8,15},{9,14},{10,... | collective-permute-start | bytes 12296 | tf_op jit(solution)/shard_map/ppermute | solution.py:399
  (2 other events, 1.8 us)

commit v12 on v11

--- a/solution.py
+++ b/solution.py
@@ -138,7 +138,8 @@
     return blocks, biases
 
 
-def first_terms_kernel(place, x_ref, points_ref, mass_ref, t_ref, top_ref, sum_ref, squares_ref):
+def first_terms_kernel(place, x_ref, points_ref, mass_ref, t_ref, top_ref, sum_ref, *refs):
+    squares_ref, top_line_ref = refs
     rows = x_ref.shape[0]
     squares = x_ref[...].astype(jnp.float32) ** 2
     sum_ref[...] = squares[:, :LANES] + squares[:, LANES:]
@@ -166,6 +167,7 @@
         return unused
 
     lax.fori_loop(0, rows // STEP, rows_step, 0)
+    top_line_ref[...] = collapse_top(top_ref)
 
 
 def piece_steps(pieces, place, x_ref, mass_ref, top_ref, old_sum_ref, t_ref, sum_ref):
@@ -192,12 +194,12 @@
 
 
 def last_terms_kernel(shifts, place, x_ref, old_ref, old_sum_ref, old_top_ref, *refs):
-    points_ref, more_ref, mass_ref, t_ref, sum_ref, out_ref, top_ref = refs
+    points_ref, more_ref, mass_ref, top_line_ref, t_ref, sum_ref, out_ref, top_ref = refs
     tiles, rows, _ = t_ref.shape
     pieces = list(zip(shifts, (points_ref, more_ref)))
     piece_steps(pieces, place, x_ref, mass_ref, old_top_ref, old_sum_ref, t_ref, sum_ref)
     total = collapse(sum_ref)
-    out_ref[...] = collapse_top(old_top_ref) * LN2 + jnp.log(total)
+    out_ref[...] = top_line_ref[...] * LN2 + jnp.log(total)
 
     @pl.when(jnp.logical_not(jnp.max(total) < HUGE))
     def exact():
@@ -251,7 +253,7 @@
 
     for c in range(0, tiles, per):
         tops = [
-            jnp.max(t_ref[c + t, :step, :] + wide_ref[:step, :], axis=0, keepdims=True)
+            jnp.max(t_ref[c + t, :32, :] + wide_ref[:32, :], axis=0, keepdims=True)
             for t in range(per)
         ]
         sums(c, tops)
@@ -426,8 +428,8 @@
 
     first = jnp.concatenate(turned(tgt_points, 0, (2, 1, 3)))
     pieces = turned(first, 1, (1, 3, 2))
-    terms, top, sums, squares = call(
-        first_terms_kernel, (big, wide, wide, by_row), [SMEM] + [VMEM] * 3, []
+    terms, top, sums, squares, top_line = call(
+        first_terms_kernel, (big, wide, wide, by_row, by_row), [SMEM] + [VMEM] * 3, []
     )(place, src_points, first, tgt_mass)
     for k in (1,):
         terms, sums = call(
@@ -436,10 +438,10 @@
     terms, sums, lse = call(
         functools.partial(last_terms_kernel, (3, 2)),
         (big, wide, by_row),
-        [SMEM] + [VMEM] * 7,
+        [SMEM] + [VMEM] * 8,
         [wide],
         {2: 0, 3: 1},
-    )(place, src_points, resident(terms), resident(sums), resident(top), pieces[3], pieces[2], tgt_mass)
+    )(place, src_points, resident(terms), resident(sums), resident(top), pieces[3], pieces[2], tgt_mass, top_line)
     lse, src_lse = call(column_kernel, (columns_out, by_row), [VMEM] * 6, [wide, line])(
         resident(terms), *over_col(lse, lse_all), src_mass
     )

time: 116 us -> 116 us (level)
  no operation moved by 1% of the time
where the time goes in v12:
time: 116 us; the launch traced here: 115 us
  starting transfers between devices  37 us (32%)
  blocking collectives  36 us (31%)
  Pallas kernels  20.7 us (18%)
  waiting for transfers between devices  17.3 us (15%)
  local copies, waits for them, and re-layouts  3.26 us (3%)
    all_to_all x3, blocking collectives, over_row(): return lax.all_to_all(value, ROW, 0, 0, tiled=True)  36 us
    ppermute x12, starting transfers between devices, crossed(): return lax.ppermute(value, ALL, pairs)  19.3 us
    ppermute x6, starting transfers between devices, turned(): found[k] = lax.ppermute(value, ALL, pairs)  10.2 us
    ppermute x4, starting transfers between devices, over_col(): both = combine([value, lax.ppermute(value, 'col_1', [(0, 1), (1, 0)])])  7.5 us
    ppermute x12, waiting for transfers between devices, crossed(): return lax.ppermute(value, ALL, pairs)  7.07 us
    ppermute x6, waiting for transfers between devices, turned(): found[k] = lax.ppermute(value, ALL, pairs)  6.92 us
    pallas_call x1, Pallas kernels, body(): call(first_terms_kernel, (big, wide, wide, by_row, by_row), [SMEM] + [VME...  3.68 us
    pallas_call x1, Pallas kernels, body(): call(plan_kernel, (big, by_row, by_column), [VMEM] * 5, [wide, wide, line...  3.5 us
  transfers between devices with their start and end apart: 22, of which 16 were waited for; matrix products, arithmetic and copies ran while one was open for 1% of the time, Pallas kernels for 5%

profile of v12, /device:TPU:1, one launch (start us, length us, event | category | flops | bytes accessed | tf_op | source)
XLA Modules:
  0.0 115.1 jit_solution(7617735894797777632)
XLA Ops:
  0.6 2.2 %collective-permute-start = (bf16[256,256]{1,0:T(8,128)(2,1)}, bf16[256,256]{1,0:T(8,128)(2,1)S(1)}, u32[]{:S(2)}, u32[]{:S(2)}) collective-permute-start(bf16[256,256]{1,0:T(8,128)(2,1)} %param.5), channel_id=1, source_target_pairs={{0,8},{1,33},{2,10},{3,35},{4,12},{5,37},{6,14},{7,39},{8,16},{9,4... | collective-permute-start | bytes 393224 | tf_op jit(solution)/shard_map/ppermute | solution.py:393
  2.8 2.6 %collective-permute-start.1 = (bf16[256,256]{1,0:T(8,128)(2,1)}, bf16[256,256]{1,0:T(8,128)(2,1)S(1)}, u32[]{:S(2)}, u32[]{:S(2)}) collective-permute-start(bf16[256,256]{1,0:T(8,128)(2,1)} %param.5), channel_id=1, source_target_pairs={{0,16},{1,65},{2,18},{3,67},{4,20},{5,69},{6,22},{7,71},{8,24},{9,... | collective-permute-start | bytes 393224 | tf_op jit(solution)/shard_map/ppermute | solution.py:393
  7.5 2.2 %collective-permute-done.1 = bf16[256,256]{1,0:T(8,128)(2,1)S(1)} collective-permute-done((bf16[256,256]{1,0:T(8,128)(2,1)}, bf16[256,256]{1,0:T(8,128)(2,1)S(1)}, u32[]{:S(2)}, u32[]{:S(2)}) %collective-permute-start.1) | collective-permute-done | bytes 131104 | tf_op jit(solution)/shard_map/ppermute | solution.py:393
  12.5 1.5 %collective-permute-start.5 = (bf16[1024,256]{1,0:T(8,128)(2,1)S(1)}, bf16[1024,256]{1,0:T(8,128)(2,1)S(1)}, u32[]{:S(2)}, u32[]{:S(2)}) collective-permute-start(bf16[1024,256]{1,0:T(8,128)(2,1)S(1)} %constant_dynamic-update-slice_fusion.points_ref), channel_id=1, source_target_pairs={{0,64},{1,17},{2,66},{3,19},{4,68},{5,21},{6,70},{7,23},{8,72},{9,... | collective-permute-start | bytes 1572872 | tf_op jit(solution)/shard_map/ppermute | solution.py:393
  15.9 3.7 %shard_map.67 = (f32[32,1024,128]{2,1,0:T(8,128)S(1)}, f32[1024,128]{1,0:T(8,128)S(1)}, f32[1024,128]{1,0:T(8,128)S(1)}, f32[8,128]{1,0:T(8,128)S(1)}, f32[8,128]{1,0:T(8,128)S(1)}) custom-call(s32[3]{0:T(128)S(1)} %pad_add_fusion.place, bf16[1024,256]{1,0:T(8,128)(2,1)S(1)} %copy-done, bf16[1024,256]{1,0:T(8,128)(2,1)S(1)} %constant_dynamic-update-slice_fusion.points_ref, ...), custom_call_target="tpu_custom_call" | custom-call | tf_op jit(solution)/shard_map/pallas_call | solution.py:431
  19.6 1.7 %shard_map.68 = (f32[32,1024,128]{2,1,0:T(8,128)S(1)}, f32[1024,128]{1,0:T(8,128)S(1)}) custom-call(s32[3]{0:T(128)S(1)} %pad_add_fusion.place, bf16[1024,256]{1,0:T(8,128)(2,1)S(1)} %copy-done, f32[32,1024,128]{2,1,0:T(8,128)S(1)} %get-tuple-element.22.old_ref, ...), custom_call_target="tpu_custom_call", output_to_operand_aliasing={{0}: (2, {}), {1}: (3, {})} | custom-call | tf_op jit(solution)/shard_map/pallas_call | solution.py:435
  21.3 4.7 %collective-permute-done.5.refs_1_ = bf16[1024,256]{1,0:T(8,128)(2,1)S(1)} collective-permute-done((bf16[1024,256]{1,0:T(8,128)(2,1)S(1)}, bf16[1024,256]{1,0:T(8,128)(2,1)S(1)}, u32[]{:S(2)}, u32[]{:S(2)}) %collective-permute-start.5) | collective-permute-done | bytes 524320 | tf_op jit(solution)/shard_map/ppermute | solution.py:393
  26.0 3.0 %shard_map.69 = (f32[32,1024,128]{2,1,0:T(8,128)S(1)}, f32[1024,128]{1,0:T(8,128)S(1)}, f32[8,128]{1,0:T(8,128)S(1)}) custom-call(s32[3]{0:T(128)S(1)} %pad_add_fusion.place, bf16[1024,256]{1,0:T(8,128)(2,1)S(1)} %copy-done, f32[32,1024,128]{2,1,0:T(8,128)S(1)} %get-tuple-element.25.old_ref, ...), custom_call_target="tpu_custom_call", output_to_operand_aliasing={{0}: (2, {}), {1}: (3, {})} | custom-call | tf_op jit(solution)/shard_map/pallas_call | solution.py:438
  29.0 3.0 %collective-permute-start.6 = (f32[8,128]{1,0:T(8,128)S(1)}, f32[8,128]{1,0:T(8,128)S(1)}, u32[]{:S(2)}, u32[]{:S(2)}) collective-permute-start(f32[8,128]{1,0:T(8,128)S(1)} %get-tuple-element.29), channel_id=1, source_target_pairs={{0,1},{1,0},{2,3},{3,2},{4,5},{5,4},{6,7},{7,6},{8,9},{9,8},{10,11... | collective-permute-start | bytes 12296 | tf_op jit(solution)/shard_map/ppermute | solution.py:423
  32.9 3.9 %collective-permute-start.7 = (f32[8,128]{1,0:T(8,128)S(1)}, f32[8,128]{1,0:T(8,128)S(1)}, u32[]{:S(2)}, u32[]{:S(2)}) collective-permute-start(f32[8,128]{1,0:T(8,128)S(1)} %log_add_fusion.refs_0_), channel_id=1, source_target_pairs={{0,5},{1,4},{2,7},{3,6},{4,1},{5,0},{6,3},{7,2},{8,13},{9,12},{10,... | collective-permute-start | bytes 12296 | tf_op jit(solution)/shard_map/ppermute | solution.py:401
  37.6 2.2 %collective-permute-start.9 = (f32[8,128]{1,0:T(8,128)S(1)}, f32[8,128]{1,0:T(8,128)S(1)}, u32[]{:S(2)}, u32[]{:S(2)}) collective-permute-start(f32[8,128]{1,0:T(8,128)S(1)} %log_add_fusion.refs_0_), channel_id=1, source_target_pairs={{0,7},{1,6},{2,1},{3,0},{4,3},{5,2},{6,5},{7,4},{8,15},{9,14},{10,... | collective-permute-start | bytes 12296 | tf_op jit(solution)/shard_map/ppermute | solution.py:401
  41.0 2.9 %shard_map.70 = (f32[16,32,128]{2,1,0:T(8,128)S(1)}, f32[8,128]{1,0:T(8,128)S(1)}) custom-call(f32[32,1024,128]{2,1,0:T(8,128)S(1)} %get-tuple-element.28.t_ref, f32[8,128]{1,0:T(8,128)S(1)} %log_add_fusion.refs_0_, f32[8,128]{1,0:T(8,128)S(1)} %collective-permute-done.7.refs_1_, f32[8,128]{1,0:T(8,128)S(1)} %collective-permute-done.8.refs_2_, ...), custom_call_target="tpu_custom_call" | custom-call | tf_op jit(solution)/shard_map/pallas_call | solution.py:445
  43.9 13.8 %all_to_all.15.parts_ref = f32[16,32,128]{2,1,0:T(8,128)S(1)} all-to-all(f32[16,32,128]{2,1,0:T(8,128)S(1)} %get-tuple-element.30), channel_id=1, replica_groups=mesh['row_0'=4,'row_1'=4,'col_0'=4,'col_1'=2] {'row_0','row_1'}, dimensions={0} | all-to-all | bytes 524288 | tf_op jit(solution)/shard_map/all_to_all | solution.py:427
  57.7 3.5 %shard_map.71 = (f32[32,1024,128]{2,1,0:T(8,128)S(1)}, f32[8,128]{1,0:T(8,128)S(1)}, f32[32,128]{1,0:T(8,128)S(1)}) custom-call(f32[32,1024,128]{2,1,0:T(8,128)S(1)} %get-tuple-element.28.t_ref, f32[16,32,128]{2,1,0:T(8,128)S(1)} %all_to_all.15.parts_ref, f32[32,128]{1,0:T(8,128)S(1)} %bitcast.11, ...), custom_call_target="tpu_custom_call", output_to_operand_aliasing={{0}: (0, {})} | custom-call | tf_op jit(solution)/shard_map/pallas_call | solution.py:448
  64.8 2.2 %collective-permute-start.12 = (f32[8,128]{1,0:T(8,128)S(1)}, f32[8,128]{1,0:T(8,128)S(1)}, u32[]{:S(2)}, u32[]{:S(2)}) collective-permute-start(f32[8,128]{1,0:T(8,128)S(1)} %add.29.refs_0_), channel_id=1, source_target_pairs={{0,3},{1,2},{2,5},{3,4},{4,7},{5,6},{6,1},{7,0},{8,11},{9,10},{10,... | collective-permute-start | bytes 12296 | tf_op jit(solution)/shard_map/ppermute | solution.py:401
  70.1 1.6 %shard_map.72 = f32[16,32,128]{2,1,0:T(8,128)S(1)} custom-call(f32[32,1024,128]{2,1,0:T(8,128)S(1)} %get-tuple-element.32.plan_ref, f32[8,128]{1,0:T(8,128)S(1)} %add.29.refs_0_, f32[8,128]{1,0:T(8,128)S(1)} %collective-permute-done.11.refs_1_, f32[8,128]{1,0:T(8,128)S(1)} %collective-permute-done.12.refs_2_, f32[8,128]{1,0:T(8,128)S(1)} %collective-permute-done.13.refs_3_, ...), custom_call_target="tpu_custom_call" | custom-call | tf_op jit(solution)/shard_map/pallas_call | solution.py:452
  71.7 10.8 %all_to_all.16.parts_ref = f32[16,32,128]{2,1,0:T(8,128)S(1)} all-to-all(f32[16,32,128]{2,1,0:T(8,128)S(1)} %shard_map.72), channel_id=1, replica_groups=mesh['row_0'=4,'row_1'=4,'col_0'=4,'col_1'=2] {'row_0','row_1'}, dimensions={0} | all-to-all | bytes 524288 | tf_op jit(solution)/shard_map/all_to_all | solution.py:427
  82.4 1.6 %shard_map.73 = f32[8,128]{1,0:T(8,128)S(1)} custom-call(f32[32,1024,128]{2,1,0:T(8,128)S(1)} %get-tuple-element.32.plan_ref, f32[16,32,128]{2,1,0:T(8,128)S(1)} %all_to_all.16.parts_ref, f32[32,128]{1,0:T(8,128)S(1)} %bitcast.12), custom_call_target="tpu_custom_call" | custom-call | tf_op jit(solution)/shard_map/pallas_call | solution.py:455
  84.0 1.6 %collective-permute-start.14 = (f32[8,128]{1,0:T(8,128)S(1)}, f32[8,128]{1,0:T(8,128)S(1)}, u32[]{:S(2)}, u32[]{:S(2)}) collective-permute-start(f32[8,128]{1,0:T(8,128)S(1)} %shard_map.73), channel_id=1, source_target_pairs={{0,1},{1,0},{2,3},{3,2},{4,5},{5,4},{6,7},{7,6},{8,9},{9,8},{10,11... | collective-permute-start | bytes 12296 | tf_op jit(solution)/shard_map/ppermute | solution.py:423
  87.2 1.8 %collective-permute-start.16 = (f32[8,128]{1,0:T(8,128)S(1)}, f32[8,128]{1,0:T(8,128)S(1)}, u32[]{:S(2)}, u32[]{:S(2)}) collective-permute-start(f32[8,128]{1,0:T(8,128)S(1)} %add.30.refs_0_), channel_id=1, source_target_pairs={{0,3},{1,2},{2,5},{3,4},{4,7},{5,6},{6,1},{7,0},{8,11},{9,10},{10,... | collective-permute-start | bytes 12296 | tf_op jit(solution)/shard_map/ppermute | solution.py:401
  92.1 2.1 %shard_map.74 = (f32[16,40,128]{2,1,0:T(8,128)S(1)}, f32[8,128]{1,0:T(8,128)}) custom-call(f32[32,1024,128]{2,1,0:T(8,128)S(1)} %get-tuple-element.32.plan_ref, f32[8,128]{1,0:T(8,128)S(1)} %add.30.refs_0_, f32[8,128]{1,0:T(8,128)S(1)} %collective-permute-done.15.refs_1_, f32[8,128]{1,0:T(8,128)S(1)} %collective-permute-done.16.refs_2_, ...), custom_call_target="tpu_custom_call" | custom-call | tf_op jit(solution)/shard_map/pallas_call | solution.py:456
  94.2 11.5 %all_to_all.17.parts_ref = f32[16,40,128]{2,1,0:T(8,128)S(1)} all-to-all(f32[16,40,128]{2,1,0:T(8,128)S(1)} %get-tuple-element.36), channel_id=1, replica_groups=mesh['row_0'=4,'row_1'=4,'col_0'=4,'col_1'=2] {'row_0','row_1'}, dimensions={0} | all-to-all | bytes 655360 | tf_op jit(solution)/shard_map/all_to_all | solution.py:427
  106.3 1.5 %collective-permute-start.18 = (f32[8,128]{1,0:T(8,128)S(1)}, f32[8,128]{1,0:T(8,128)S(1)}, u32[]{:S(2)}, u32[]{:S(2)}) collective-permute-start(f32[8,128]{1,0:T(8,128)S(1)} %get-tuple-element.40), channel_id=1, source_target_pairs={{0,1},{1,0},{2,3},{3,2},{4,5},{5,4},{6,7},{7,6},{8,9},{9,8},{10,11... | collective-permute-start | bytes 12296 | tf_op jit(solution)/shard_map/ppermute | solution.py:423
  110.0 1.5 %collective-permute-start.20 = (f32[8,128]{1,0:T(8,128)S(1)}, f32[8,128]{1,0:T(8,128)S(1)}, u32[]{:S(2)}, u32[]{:S(2)}) collective-permute-start(f32[8,128]{1,0:T(8,128)S(1)} %add.31), channel_id=1, source_target_pairs={{0,3},{1,2},{2,5},{3,4},{4,7},{5,6},{6,1},{7,0},{8,11},{9,10},{10,... | collective-permute-start | bytes 12296 | tf_op jit(solution)/shard_map/ppermute | solution.py:401
  (51 shorter events, 27.4 us)
Async XLA Ops:
  0.6 25.4 %copy-start.2 = (f32[4096]{0:T(1024)S(1)}, f32[4096]{0:T(1024)}, u32[]{:S(2)}) copy-start(f32[4096]{0:T(1024)} %param.7) | copy-start | bytes 49156
  0.6 6.8 %collective-permute-start = (bf16[256,256]{1,0:T(8,128)(2,1)}, bf16[256,256]{1,0:T(8,128)(2,1)S(1)}, u32[]{:S(2)}, u32[]{:S(2)}) collective-permute-start(bf16[256,256]{1,0:T(8,128)(2,1)} %param.5), channel_id=1, source_target_pairs={{0,8},{1,33},{2,10},{3,35},{4,12},{5,37},{6,14},{7,39},{8,16},{9,4... | collective-permute-start | bytes 393224 | tf_op jit(solution)/shard_map/ppermute | solution.py:393
  2.8 6.9 %collective-permute-start.1 = (bf16[256,256]{1,0:T(8,128)(2,1)}, bf16[256,256]{1,0:T(8,128)(2,1)S(1)}, u32[]{:S(2)}, u32[]{:S(2)}) collective-permute-start(bf16[256,256]{1,0:T(8,128)(2,1)} %param.5), channel_id=1, source_target_pairs={{0,16},{1,65},{2,18},{3,67},{4,20},{5,69},{6,22},{7,71},{8,24},{9,... | collective-permute-start | bytes 393224 | tf_op jit(solution)/shard_map/ppermute | solution.py:393
  5.5 4.3 %collective-permute-start.2 = (bf16[256,256]{1,0:T(8,128)(2,1)}, bf16[256,256]{1,0:T(8,128)(2,1)S(1)}, u32[]{:S(2)}, u32[]{:S(2)}) collective-permute-start(bf16[256,256]{1,0:T(8,128)(2,1)} %param.5), channel_id=1, source_target_pairs={{0,24},{1,97},{2,26},{3,99},{4,28},{5,101},{6,30},{7,103},{8,0},{9... | collective-permute-start | bytes 393224 | tf_op jit(solution)/shard_map/ppermute | solution.py:393
  9.8 9.8 %collective-permute-start.3 = (bf16[1024,256]{1,0:T(8,128)(2,1)S(1)}, bf16[1024,256]{1,0:T(8,128)(2,1)S(1)}, u32[]{:S(2)}, u32[]{:S(2)}) collective-permute-start(bf16[1024,256]{1,0:T(8,128)(2,1)S(1)} %constant_dynamic-update-slice_fusion.points_ref), channel_id=1, source_target_pairs={{0,32},{1,9},{2,34},{3,11},{4,36},{5,13},{6,38},{7,15},{8,40},{9,1... | collective-permute-start | bytes 1572872 | tf_op jit(solution)/shard_map/ppermute | solution.py:393
  11.1 10.3 %collective-permute-start.4 = (bf16[1024,256]{1,0:T(8,128)(2,1)S(1)}, bf16[1024,256]{1,0:T(8,128)(2,1)S(1)}, u32[]{:S(2)}, u32[]{:S(2)}) collective-permute-start(bf16[1024,256]{1,0:T(8,128)(2,1)S(1)} %constant_dynamic-update-slice_fusion.points_ref), channel_id=1, source_target_pairs={{0,96},{1,25},{2,98},{3,27},{4,100},{5,29},{6,102},{7,31},{8,104},... | collective-permute-start | bytes 1572872 | tf_op jit(solution)/shard_map/ppermute | solution.py:393
  12.5 13.5 %collective-permute-start.5 = (bf16[1024,256]{1,0:T(8,128)(2,1)S(1)}, bf16[1024,256]{1,0:T(8,128)(2,1)S(1)}, u32[]{:S(2)}, u32[]{:S(2)}) collective-permute-start(bf16[1024,256]{1,0:T(8,128)(2,1)S(1)} %constant_dynamic-update-slice_fusion.points_ref), channel_id=1, source_target_pairs={{0,64},{1,17},{2,66},{3,19},{4,68},{5,21},{6,70},{7,23},{8,72},{9,... | collective-permute-start | bytes 1572872 | tf_op jit(solution)/shard_map/ppermute | solution.py:393
  19.6 21.4 %copy-start.3 = (f32[1024]{0:T(1024)S(1)}, f32[1024]{0:T(1024)}, u32[]{:S(2)}) copy-start(f32[1024]{0:T(1024)} %param.6) | copy-start | bytes 12292
  29.0 3.8 %collective-permute-start.6 = (f32[8,128]{1,0:T(8,128)S(1)}, f32[8,128]{1,0:T(8,128)S(1)}, u32[]{:S(2)}, u32[]{:S(2)}) collective-permute-start(f32[8,128]{1,0:T(8,128)S(1)} %get-tuple-element.29), channel_id=1, source_target_pairs={{0,1},{1,0},{2,3},{3,2},{4,5},{5,4},{6,7},{7,6},{8,9},{9,8},{10,11... | collective-permute-start | bytes 12296 | tf_op jit(solution)/shard_map/ppermute | solution.py:423
  32.9 6.9 %collective-permute-start.7 = (f32[8,128]{1,0:T(8,128)S(1)}, f32[8,128]{1,0:T(8,128)S(1)}, u32[]{:S(2)}, u32[]{:S(2)}) collective-permute-start(f32[8,128]{1,0:T(8,128)S(1)} %log_add_fusion.refs_0_), channel_id=1, source_target_pairs={{0,5},{1,4},{2,7},{3,6},{4,1},{5,0},{6,3},{7,2},{8,13},{9,12},{10,... | collective-permute-start | bytes 12296 | tf_op jit(solution)/shard_map/ppermute | solution.py:401
  36.8 4.2 %collective-permute-start.8 = (f32[8,128]{1,0:T(8,128)S(1)}, f32[8,128]{1,0:T(8,128)S(1)}, u32[]{:S(2)}, u32[]{:S(2)}) collective-permute-start(f32[8,128]{1,0:T(8,128)S(1)} %log_add_fusion.refs_0_), channel_id=1, source_target_pairs={{0,3},{1,2},{2,5},{3,4},{4,7},{5,6},{6,1},{7,0},{8,11},{9,10},{10,... | collective-permute-start | bytes 12296 | tf_op jit(solution)/shard_map/ppermute | solution.py:401
  37.6 3.5 %collective-permute-start.9 = (f32[8,128]{1,0:T(8,128)S(1)}, f32[8,128]{1,0:T(8,128)S(1)}, u32[]{:S(2)}, u32[]{:S(2)}) collective-permute-start(f32[8,128]{1,0:T(8,128)S(1)} %log_add_fusion.refs_0_), channel_id=1, source_target_pairs={{0,7},{1,6},{2,1},{3,0},{4,3},{5,2},{6,5},{7,4},{8,15},{9,14},{10,... | collective-permute-start | bytes 12296 | tf_op jit(solution)/shard_map/ppermute | solution.py:401
  61.2 2.2 %collective-permute-start.10 = (f32[8,128]{1,0:T(8,128)S(1)}, f32[8,128]{1,0:T(8,128)S(1)}, u32[]{:S(2)}, u32[]{:S(2)}) collective-permute-start(f32[8,128]{1,0:T(8,128)S(1)} %get-tuple-element.33), channel_id=1, source_target_pairs={{0,1},{1,0},{2,3},{3,2},{4,5},{5,4},{6,7},{7,6},{8,9},{9,8},{10,11... | collective-permute-start | bytes 12296 | tf_op jit(solution)/shard_map/ppermute | solution.py:423
  63.4 4.5 %collective-permute-start.11 = (f32[8,128]{1,0:T(8,128)S(1)}, f32[8,128]{1,0:T(8,128)S(1)}, u32[]{:S(2)}, u32[]{:S(2)}) collective-permute-start(f32[8,128]{1,0:T(8,128)S(1)} %add.29.refs_0_), channel_id=1, source_target_pairs={{0,5},{1,4},{2,7},{3,6},{4,1},{5,0},{6,3},{7,2},{8,13},{9,12},{10,... | collective-permute-start | bytes 12296 | tf_op jit(solution)/shard_map/ppermute | solution.py:401
  64.8 4.2 %collective-permute-start.12 = (f32[8,128]{1,0:T(8,128)S(1)}, f32[8,128]{1,0:T(8,128)S(1)}, u32[]{:S(2)}, u32[]{:S(2)}) collective-permute-start(f32[8,128]{1,0:T(8,128)S(1)} %add.29.refs_0_), channel_id=1, source_target_pairs={{0,3},{1,2},{2,5},{3,4},{4,7},{5,6},{6,1},{7,0},{8,11},{9,10},{10,... | collective-permute-start | bytes 12296 | tf_op jit(solution)/shard_map/ppermute | solution.py:401
  67.0 3.0 %collective-permute-start.13 = (f32[8,128]{1,0:T(8,128)S(1)}, f32[8,128]{1,0:T(8,128)S(1)}, u32[]{:S(2)}, u32[]{:S(2)}) collective-permute-start(f32[8,128]{1,0:T(8,128)S(1)} %add.29.refs_0_), channel_id=1, source_target_pairs={{0,7},{1,6},{2,1},{3,0},{4,3},{5,2},{6,5},{7,4},{8,15},{9,14},{10,... | collective-permute-start | bytes 12296 | tf_op jit(solution)/shard_map/ppermute | solution.py:401
  84.0 2.4 %collective-permute-start.14 = (f32[8,128]{1,0:T(8,128)S(1)}, f32[8,128]{1,0:T(8,128)S(1)}, u32[]{:S(2)}, u32[]{:S(2)}) collective-permute-start(f32[8,128]{1,0:T(8,128)S(1)} %shard_map.73), channel_id=1, source_target_pairs={{0,1},{1,0},{2,3},{3,2},{4,5},{5,4},{6,7},{7,6},{8,9},{9,8},{10,11... | collective-permute-start | bytes 12296 | tf_op jit(solution)/shard_map/ppermute | solution.py:423
  86.4 4.5 %collective-permute-start.15 = (f32[8,128]{1,0:T(8,128)S(1)}, f32[8,128]{1,0:T(8,128)S(1)}, u32[]{:S(2)}, u32[]{:S(2)}) collective-permute-start(f32[8,128]{1,0:T(8,128)S(1)} %add.30.refs_0_), channel_id=1, source_target_pairs={{0,5},{1,4},{2,7},{3,6},{4,1},{5,0},{6,3},{7,2},{8,13},{9,12},{10,... | collective-permute-start | bytes 12296 | tf_op jit(solution)/shard_map/ppermute | solution.py:401
  87.2 4.2 %collective-permute-start.16 = (f32[8,128]{1,0:T(8,128)S(1)}, f32[8,128]{1,0:T(8,128)S(1)}, u32[]{:S(2)}, u32[]{:S(2)}) collective-permute-start(f32[8,128]{1,0:T(8,128)S(1)} %add.30.refs_0_), channel_id=1, source_target_pairs={{0,3},{1,2},{2,5},{3,4},{4,7},{5,6},{6,1},{7,0},{8,11},{9,10},{10,... | collective-permute-start | bytes 12296 | tf_op jit(solution)/shard_map/ppermute | solution.py:401
  89.0 3.0 %collective-permute-start.17 = (f32[8,128]{1,0:T(8,128)S(1)}, f32[8,128]{1,0:T(8,128)S(1)}, u32[]{:S(2)}, u32[]{:S(2)}) collective-permute-start(f32[8,128]{1,0:T(8,128)S(1)} %add.30.refs_0_), channel_id=1, source_target_pairs={{0,7},{1,6},{2,1},{3,0},{4,3},{5,2},{6,5},{7,4},{8,15},{9,14},{10,... | collective-permute-start | bytes 12296 | tf_op jit(solution)/shard_map/ppermute | solution.py:401
  106.3 2.3 %collective-permute-start.18 = (f32[8,128]{1,0:T(8,128)S(1)}, f32[8,128]{1,0:T(8,128)S(1)}, u32[]{:S(2)}, u32[]{:S(2)}) collective-permute-start(f32[8,128]{1,0:T(8,128)S(1)} %get-tuple-element.40), channel_id=1, source_target_pairs={{0,1},{1,0},{2,3},{3,2},{4,5},{5,4},{6,7},{7,6},{8,9},{9,8},{10,11... | collective-permute-start | bytes 12296 | tf_op jit(solution)/shard_map/ppermute | solution.py:423
  108.6 4.5 %collective-permute-start.19 = (f32[8,128]{1,0:T(8,128)S(1)}, f32[8,128]{1,0:T(8,128)S(1)}, u32[]{:S(2)}, u32[]{:S(2)}) collective-permute-start(f32[8,128]{1,0:T(8,128)S(1)} %add.31), channel_id=1, source_target_pairs={{0,5},{1,4},{2,7},{3,6},{4,1},{5,0},{6,3},{7,2},{8,13},{9,12},{10,... | collective-permute-start | bytes 12296 | tf_op jit(solution)/shard_map/ppermute | solution.py:401
  110.0 4.2 %collective-permute-start.20 = (f32[8,128]{1,0:T(8,128)S(1)}, f32[8,128]{1,0:T(8,128)S(1)}, u32[]{:S(2)}, u32[]{:S(2)}) collective-permute-start(f32[8,128]{1,0:T(8,128)S(1)} %add.31), channel_id=1, source_target_pairs={{0,3},{1,2},{2,5},{3,4},{4,7},{5,6},{6,1},{7,0},{8,11},{9,10},{10,... | collective-permute-start | bytes 12296 | tf_op jit(solution)/shard_map/ppermute | solution.py:401
  111.5 3.0 %collective-permute-start.21 = (f32[8,128]{1,0:T(8,128)S(1)}, f32[8,128]{1,0:T(8,128)S(1)}, u32[]{:S(2)}, u32[]{:S(2)}) collective-permute-start(f32[8,128]{1,0:T(8,128)S(1)} %add.31), channel_id=1, source_target_pairs={{0,7},{1,6},{2,1},{3,0},{4,3},{5,2},{6,5},{7,4},{8,15},{9,14},{10,... | collective-permute-start | bytes 12296 | tf_op jit(solution)/shard_map/ppermute | solution.py:401
  (2 other events, 1.8 us)

commit v13 on v11

--- a/solution.py
+++ b/solution.py
@@ -251,7 +251,7 @@
 
     for c in range(0, tiles, per):
         tops = [
-            jnp.max(t_ref[c + t, :step, :] + wide_ref[:step, :], axis=0, keepdims=True)
+            jnp.max(t_ref[c + t, :32, :] + wide_ref[:32, :], axis=0, keepdims=True)
             for t in range(per)
         ]
         sums(c, tops)

time: 116 us -> 116 us (level)
  no operation moved by 1% of the time
where the time goes in v13:
time: 116 us; the launch traced here: 115 us
  starting transfers between devices  37 us (32%)
  blocking collectives  36 us (31%)
  Pallas kernels  20.5 us (18%)
  waiting for transfers between devices  17.4 us (15%)
  local copies, waits for them, and re-layouts  3.26 us (3%)
    all_to_all x3, blocking collectives, over_row(): return lax.all_to_all(value, ROW, 0, 0, tiled=True)  36 us
    ppermute x12, starting transfers between devices, crossed(): return lax.ppermute(value, ALL, pairs)  19.3 us
    ppermute x6, starting transfers between devices, turned(): found[k] = lax.ppermute(value, ALL, pairs)  10.2 us
    ppermute x4, starting transfers between devices, over_col(): both = combine([value, lax.ppermute(value, 'col_1', [(0, 1), (1, 0)])])  7.5 us
    ppermute x12, waiting for transfers between devices, crossed(): return lax.ppermute(value, ALL, pairs)  7.07 us
    ppermute x6, waiting for transfers between devices, turned(): found[k] = lax.ppermute(value, ALL, pairs)  7.06 us
    pallas_call x1, Pallas kernels, body(): call(first_terms_kernel, (big, wide, wide, by_row), [SMEM] + [VMEM] * 3, [])  3.53 us
    pallas_call x1, Pallas kernels, body(): call(plan_kernel, (big, by_row, by_column), [VMEM] * 5, [wide, wide, line...  3.46 us
  transfers between devices with their start and end apart: 22, of which 16 were waited for; matrix products, arithmetic and copies ran while one was open for 1% of the time, Pallas kernels for 5%

profile of v13, /device:TPU:1, one launch (start us, length us, event | category | flops | bytes accessed | tf_op | source)
XLA Modules:
  0.0 115.0 jit_solution(6925142143341830684)
XLA Ops:
  0.6 2.2 %collective-permute-start = (bf16[256,256]{1,0:T(8,128)(2,1)}, bf16[256,256]{1,0:T(8,128)(2,1)S(1)}, u32[]{:S(2)}, u32[]{:S(2)}) collective-permute-start(bf16[256,256]{1,0:T(8,128)(2,1)} %param.5), channel_id=1, source_target_pairs={{0,8},{1,33},{2,10},{3,35},{4,12},{5,37},{6,14},{7,39},{8,16},{9,4... | collective-permute-start | bytes 393224 | tf_op jit(solution)/shard_map/ppermute | solution.py:391
  2.8 2.6 %collective-permute-start.1 = (bf16[256,256]{1,0:T(8,128)(2,1)}, bf16[256,256]{1,0:T(8,128)(2,1)S(1)}, u32[]{:S(2)}, u32[]{:S(2)}) collective-permute-start(bf16[256,256]{1,0:T(8,128)(2,1)} %param.5), channel_id=1, source_target_pairs={{0,16},{1,65},{2,18},{3,67},{4,20},{5,69},{6,22},{7,71},{8,24},{9,... | collective-permute-start | bytes 393224 | tf_op jit(solution)/shard_map/ppermute | solution.py:391
  7.5 2.2 %collective-permute-done.1 = bf16[256,256]{1,0:T(8,128)(2,1)S(1)} collective-permute-done((bf16[256,256]{1,0:T(8,128)(2,1)}, bf16[256,256]{1,0:T(8,128)(2,1)S(1)}, u32[]{:S(2)}, u32[]{:S(2)}) %collective-permute-start.1) | collective-permute-done | bytes 131104 | tf_op jit(solution)/shard_map/ppermute | solution.py:391
  12.5 1.5 %collective-permute-start.5 = (bf16[1024,256]{1,0:T(8,128)(2,1)S(1)}, bf16[1024,256]{1,0:T(8,128)(2,1)S(1)}, u32[]{:S(2)}, u32[]{:S(2)}) collective-permute-start(bf16[1024,256]{1,0:T(8,128)(2,1)S(1)} %constant_dynamic-update-slice_fusion.points_ref), channel_id=1, source_target_pairs={{0,64},{1,17},{2,66},{3,19},{4,68},{5,21},{6,70},{7,23},{8,72},{9,... | collective-permute-start | bytes 1572872 | tf_op jit(solution)/shard_map/ppermute | solution.py:391
  15.9 3.5 %shard_map.67 = (f32[32,1024,128]{2,1,0:T(8,128)S(1)}, f32[1024,128]{1,0:T(8,128)S(1)}, f32[1024,128]{1,0:T(8,128)S(1)}, f32[8,128]{1,0:T(8,128)S(1)}) custom-call(s32[3]{0:T(128)S(1)} %pad_add_fusion.place, bf16[1024,256]{1,0:T(8,128)(2,1)S(1)} %copy-done, bf16[1024,256]{1,0:T(8,128)(2,1)S(1)} %constant_dynamic-update-slice_fusion.points_ref, ...), custom_call_target="tpu_custom_call" | custom-call | tf_op jit(solution)/shard_map/pallas_call | solution.py:429
  19.5 1.7 %shard_map.68 = (f32[32,1024,128]{2,1,0:T(8,128)S(1)}, f32[1024,128]{1,0:T(8,128)S(1)}) custom-call(s32[3]{0:T(128)S(1)} %pad_add_fusion.place, bf16[1024,256]{1,0:T(8,128)(2,1)S(1)} %copy-done, f32[32,1024,128]{2,1,0:T(8,128)S(1)} %get-tuple-element.21.old_ref, ...), custom_call_target="tpu_custom_call", output_to_operand_aliasing={{0}: (2, {}), {1}: (3, {})} | custom-call | tf_op jit(solution)/shard_map/pallas_call | solution.py:433
  21.2 4.8 %collective-permute-done.5.refs_1_ = bf16[1024,256]{1,0:T(8,128)(2,1)S(1)} collective-permute-done((bf16[1024,256]{1,0:T(8,128)(2,1)S(1)}, bf16[1024,256]{1,0:T(8,128)(2,1)S(1)}, u32[]{:S(2)}, u32[]{:S(2)}) %collective-permute-start.5) | collective-permute-done | bytes 524320 | tf_op jit(solution)/shard_map/ppermute | solution.py:391
  26.0 3.0 %shard_map.69 = (f32[32,1024,128]{2,1,0:T(8,128)S(1)}, f32[1024,128]{1,0:T(8,128)S(1)}, f32[8,128]{1,0:T(8,128)S(1)}) custom-call(s32[3]{0:T(128)S(1)} %pad_add_fusion.place, bf16[1024,256]{1,0:T(8,128)(2,1)S(1)} %copy-done, f32[32,1024,128]{2,1,0:T(8,128)S(1)} %get-tuple-element.24.old_ref, ...), custom_call_target="tpu_custom_call", output_to_operand_aliasing={{0}: (2, {}), {1}: (3, {})} | custom-call | tf_op jit(solution)/shard_map/pallas_call | solution.py:436
  29.0 3.0 %collective-permute-start.6 = (f32[8,128]{1,0:T(8,128)S(1)}, f32[8,128]{1,0:T(8,128)S(1)}, u32[]{:S(2)}, u32[]{:S(2)}) collective-permute-start(f32[8,128]{1,0:T(8,128)S(1)} %get-tuple-element.27), channel_id=1, source_target_pairs={{0,1},{1,0},{2,3},{3,2},{4,5},{5,4},{6,7},{7,6},{8,9},{9,8},{10,11... | collective-permute-start | bytes 12296 | tf_op jit(solution)/shard_map/ppermute | solution.py:421
  32.8 3.9 %collective-permute-start.7 = (f32[8,128]{1,0:T(8,128)S(1)}, f32[8,128]{1,0:T(8,128)S(1)}, u32[]{:S(2)}, u32[]{:S(2)}) collective-permute-start(f32[8,128]{1,0:T(8,128)S(1)} %log_add_fusion.refs_0_), channel_id=1, source_target_pairs={{0,5},{1,4},{2,7},{3,6},{4,1},{5,0},{6,3},{7,2},{8,13},{9,12},{10,... | collective-permute-start | bytes 12296 | tf_op jit(solution)/shard_map/ppermute | solution.py:399
  37.5 2.2 %collective-permute-start.9 = (f32[8,128]{1,0:T(8,128)S(1)}, f32[8,128]{1,0:T(8,128)S(1)}, u32[]{:S(2)}, u32[]{:S(2)}) collective-permute-start(f32[8,128]{1,0:T(8,128)S(1)} %log_add_fusion.refs_0_), channel_id=1, source_target_pairs={{0,7},{1,6},{2,1},{3,0},{4,3},{5,2},{6,5},{7,4},{8,15},{9,14},{10,... | collective-permute-start | bytes 12296 | tf_op jit(solution)/shard_map/ppermute | solution.py:399
  41.0 2.9 %shard_map.70 = (f32[16,32,128]{2,1,0:T(8,128)S(1)}, f32[8,128]{1,0:T(8,128)S(1)}) custom-call(f32[32,1024,128]{2,1,0:T(8,128)S(1)} %get-tuple-element.26.t_ref, f32[8,128]{1,0:T(8,128)S(1)} %log_add_fusion.refs_0_, f32[8,128]{1,0:T(8,128)S(1)} %collective-permute-done.7.refs_1_, f32[8,128]{1,0:T(8,128)S(1)} %collective-permute-done.8.refs_2_, ...), custom_call_target="tpu_custom_call" | custom-call | tf_op jit(solution)/shard_map/pallas_call | solution.py:443
  43.9 13.8 %all_to_all.15.parts_ref = f32[16,32,128]{2,1,0:T(8,128)S(1)} all-to-all(f32[16,32,128]{2,1,0:T(8,128)S(1)} %get-tuple-element.28), channel_id=1, replica_groups=mesh['row_0'=4,'row_1'=4,'col_0'=4,'col_1'=2] {'row_0','row_1'}, dimensions={0} | all-to-all | bytes 524288 | tf_op jit(solution)/shard_map/all_to_all | solution.py:425
  57.7 3.5 %shard_map.71 = (f32[32,1024,128]{2,1,0:T(8,128)S(1)}, f32[8,128]{1,0:T(8,128)S(1)}, f32[32,128]{1,0:T(8,128)S(1)}) custom-call(f32[32,1024,128]{2,1,0:T(8,128)S(1)} %get-tuple-element.26.t_ref, f32[16,32,128]{2,1,0:T(8,128)S(1)} %all_to_all.15.parts_ref, f32[32,128]{1,0:T(8,128)S(1)} %bitcast.11, ...), custom_call_target="tpu_custom_call", output_to_operand_aliasing={{0}: (0, {})} | custom-call | tf_op jit(solution)/shard_map/pallas_call | solution.py:446
  64.8 2.2 %collective-permute-start.12 = (f32[8,128]{1,0:T(8,128)S(1)}, f32[8,128]{1,0:T(8,128)S(1)}, u32[]{:S(2)}, u32[]{:S(2)}) collective-permute-start(f32[8,128]{1,0:T(8,128)S(1)} %add.29.refs_0_), channel_id=1, source_target_pairs={{0,3},{1,2},{2,5},{3,4},{4,7},{5,6},{6,1},{7,0},{8,11},{9,10},{10,... | collective-permute-start | bytes 12296 | tf_op jit(solution)/shard_map/ppermute | solution.py:399
  70.0 1.6 %shard_map.72 = f32[16,32,128]{2,1,0:T(8,128)S(1)} custom-call(f32[32,1024,128]{2,1,0:T(8,128)S(1)} %get-tuple-element.30.plan_ref, f32[8,128]{1,0:T(8,128)S(1)} %add.29.refs_0_, f32[8,128]{1,0:T(8,128)S(1)} %collective-permute-done.11.refs_1_, f32[8,128]{1,0:T(8,128)S(1)} %collective-permute-done.12.refs_2_, f32[8,128]{1,0:T(8,128)S(1)} %collective-permute-done.13.refs_3_, ...), custom_call_target="tpu_custom_call" | custom-call | tf_op jit(solution)/shard_map/pallas_call | solution.py:450
  71.6 10.8 %all_to_all.16.parts_ref = f32[16,32,128]{2,1,0:T(8,128)S(1)} all-to-all(f32[16,32,128]{2,1,0:T(8,128)S(1)} %shard_map.72), channel_id=1, replica_groups=mesh['row_0'=4,'row_1'=4,'col_0'=4,'col_1'=2] {'row_0','row_1'}, dimensions={0} | all-to-all | bytes 524288 | tf_op jit(solution)/shard_map/all_to_all | solution.py:425
  82.3 1.6 %shard_map.73 = f32[8,128]{1,0:T(8,128)S(1)} custom-call(f32[32,1024,128]{2,1,0:T(8,128)S(1)} %get-tuple-element.30.plan_ref, f32[16,32,128]{2,1,0:T(8,128)S(1)} %all_to_all.16.parts_ref, f32[32,128]{1,0:T(8,128)S(1)} %bitcast.12), custom_call_target="tpu_custom_call" | custom-call | tf_op jit(solution)/shard_map/pallas_call | solution.py:453
  83.9 1.6 %collective-permute-start.14 = (f32[8,128]{1,0:T(8,128)S(1)}, f32[8,128]{1,0:T(8,128)S(1)}, u32[]{:S(2)}, u32[]{:S(2)}) collective-permute-start(f32[8,128]{1,0:T(8,128)S(1)} %shard_map.73), channel_id=1, source_target_pairs={{0,1},{1,0},{2,3},{3,2},{4,5},{5,4},{6,7},{7,6},{8,9},{9,8},{10,11... | collective-permute-start | bytes 12296 | tf_op jit(solution)/shard_map/ppermute | solution.py:421
  87.1 1.8 %collective-permute-start.16 = (f32[8,128]{1,0:T(8,128)S(1)}, f32[8,128]{1,0:T(8,128)S(1)}, u32[]{:S(2)}, u32[]{:S(2)}) collective-permute-start(f32[8,128]{1,0:T(8,128)S(1)} %add.30.refs_0_), channel_id=1, source_target_pairs={{0,3},{1,2},{2,5},{3,4},{4,7},{5,6},{6,1},{7,0},{8,11},{9,10},{10,... | collective-permute-start | bytes 12296 | tf_op jit(solution)/shard_map/ppermute | solution.py:399
  92.0 2.1 %shard_map.74 = (f32[16,40,128]{2,1,0:T(8,128)S(1)}, f32[8,128]{1,0:T(8,128)}) custom-call(f32[32,1024,128]{2,1,0:T(8,128)S(1)} %get-tuple-element.30.plan_ref, f32[8,128]{1,0:T(8,128)S(1)} %add.30.refs_0_, f32[8,128]{1,0:T(8,128)S(1)} %collective-permute-done.15.refs_1_, f32[8,128]{1,0:T(8,128)S(1)} %collective-permute-done.16.refs_2_, ...), custom_call_target="tpu_custom_call" | custom-call | tf_op jit(solution)/shard_map/pallas_call | solution.py:454
  94.1 11.5 %all_to_all.17.parts_ref = f32[16,40,128]{2,1,0:T(8,128)S(1)} all-to-all(f32[16,40,128]{2,1,0:T(8,128)S(1)} %get-tuple-element.34), channel_id=1, replica_groups=mesh['row_0'=4,'row_1'=4,'col_0'=4,'col_1'=2] {'row_0','row_1'}, dimensions={0} | all-to-all | bytes 655360 | tf_op jit(solution)/shard_map/all_to_all | solution.py:425
  106.2 1.5 %collective-permute-start.18 = (f32[8,128]{1,0:T(8,128)S(1)}, f32[8,128]{1,0:T(8,128)S(1)}, u32[]{:S(2)}, u32[]{:S(2)}) collective-permute-start(f32[8,128]{1,0:T(8,128)S(1)} %get-tuple-element.38), channel_id=1, source_target_pairs={{0,1},{1,0},{2,3},{3,2},{4,5},{5,4},{6,7},{7,6},{8,9},{9,8},{10,11... | collective-permute-start | bytes 12296 | tf_op jit(solution)/shard_map/ppermute | solution.py:421
  109.9 1.5 %collective-permute-start.20 = (f32[8,128]{1,0:T(8,128)S(1)}, f32[8,128]{1,0:T(8,128)S(1)}, u32[]{:S(2)}, u32[]{:S(2)}) collective-permute-start(f32[8,128]{1,0:T(8,128)S(1)} %add.31), channel_id=1, source_target_pairs={{0,3},{1,2},{2,5},{3,4},{4,7},{5,6},{6,1},{7,0},{8,11},{9,10},{10,... | collective-permute-start | bytes 12296 | tf_op jit(solution)/shard_map/ppermute | solution.py:399
  (51 shorter events, 27.4 us)
Async XLA Ops:
  0.6 25.4 %copy-start.2 = (f32[4096]{0:T(1024)S(1)}, f32[4096]{0:T(1024)}, u32[]{:S(2)}) copy-start(f32[4096]{0:T(1024)} %param.7) | copy-start | bytes 49156
  0.6 6.8 %collective-permute-start = (bf16[256,256]{1,0:T(8,128)(2,1)}, bf16[256,256]{1,0:T(8,128)(2,1)S(1)}, u32[]{:S(2)}, u32[]{:S(2)}) collective-permute-start(bf16[256,256]{1,0:T(8,128)(2,1)} %param.5), channel_id=1, source_target_pairs={{0,8},{1,33},{2,10},{3,35},{4,12},{5,37},{6,14},{7,39},{8,16},{9,4... | collective-permute-start | bytes 393224 | tf_op jit(solution)/shard_map/ppermute | solution.py:391
  2.8 6.9 %collective-permute-start.1 = (bf16[256,256]{1,0:T(8,128)(2,1)}, bf16[256,256]{1,0:T(8,128)(2,1)S(1)}, u32[]{:S(2)}, u32[]{:S(2)}) collective-permute-start(bf16[256,256]{1,0:T(8,128)(2,1)} %param.5), channel_id=1, source_target_pairs={{0,16},{1,65},{2,18},{3,67},{4,20},{5,69},{6,22},{7,71},{8,24},{9,... | collective-permute-start | bytes 393224 | tf_op jit(solution)/shard_map/ppermute | solution.py:391
  5.5 4.3 %collective-permute-start.2 = (bf16[256,256]{1,0:T(8,128)(2,1)}, bf16[256,256]{1,0:T(8,128)(2,1)S(1)}, u32[]{:S(2)}, u32[]{:S(2)}) collective-permute-start(bf16[256,256]{1,0:T(8,128)(2,1)} %param.5), channel_id=1, source_target_pairs={{0,24},{1,97},{2,26},{3,99},{4,28},{5,101},{6,30},{7,103},{8,0},{9... | collective-permute-start | bytes 393224 | tf_op jit(solution)/shard_map/ppermute | solution.py:391
  9.8 9.7 %collective-permute-start.3 = (bf16[1024,256]{1,0:T(8,128)(2,1)S(1)}, bf16[1024,256]{1,0:T(8,128)(2,1)S(1)}, u32[]{:S(2)}, u32[]{:S(2)}) collective-permute-start(bf16[1024,256]{1,0:T(8,128)(2,1)S(1)} %constant_dynamic-update-slice_fusion.points_ref), channel_id=1, source_target_pairs={{0,32},{1,9},{2,34},{3,11},{4,36},{5,13},{6,38},{7,15},{8,40},{9,1... | collective-permute-start | bytes 1572872 | tf_op jit(solution)/shard_map/ppermute | solution.py:391
  11.1 10.1 %collective-permute-start.4 = (bf16[1024,256]{1,0:T(8,128)(2,1)S(1)}, bf16[1024,256]{1,0:T(8,128)(2,1)S(1)}, u32[]{:S(2)}, u32[]{:S(2)}) collective-permute-start(bf16[1024,256]{1,0:T(8,128)(2,1)S(1)} %constant_dynamic-update-slice_fusion.points_ref), channel_id=1, source_target_pairs={{0,96},{1,25},{2,98},{3,27},{4,100},{5,29},{6,102},{7,31},{8,104},... | collective-permute-start | bytes 1572872 | tf_op jit(solution)/shard_map/ppermute | solution.py:391
  12.5 13.5 %collective-permute-start.5 = (bf16[1024,256]{1,0:T(8,128)(2,1)S(1)}, bf16[1024,256]{1,0:T(8,128)(2,1)S(1)}, u32[]{:S(2)}, u32[]{:S(2)}) collective-permute-start(bf16[1024,256]{1,0:T(8,128)(2,1)S(1)} %constant_dynamic-update-slice_fusion.points_ref), channel_id=1, source_target_pairs={{0,64},{1,17},{2,66},{3,19},{4,68},{5,21},{6,70},{7,23},{8,72},{9,... | collective-permute-start | bytes 1572872 | tf_op jit(solution)/shard_map/ppermute | solution.py:391
  19.5 21.5 %copy-start.3 = (f32[1024]{0:T(1024)S(1)}, f32[1024]{0:T(1024)}, u32[]{:S(2)}) copy-start(f32[1024]{0:T(1024)} %param.6) | copy-start | bytes 12292
  29.0 3.8 %collective-permute-start.6 = (f32[8,128]{1,0:T(8,128)S(1)}, f32[8,128]{1,0:T(8,128)S(1)}, u32[]{:S(2)}, u32[]{:S(2)}) collective-permute-start(f32[8,128]{1,0:T(8,128)S(1)} %get-tuple-element.27), channel_id=1, source_target_pairs={{0,1},{1,0},{2,3},{3,2},{4,5},{5,4},{6,7},{7,6},{8,9},{9,8},{10,11... | collective-permute-start | bytes 12296 | tf_op jit(solution)/shard_map/ppermute | solution.py:421
  32.8 6.9 %collective-permute-start.7 = (f32[8,128]{1,0:T(8,128)S(1)}, f32[8,128]{1,0:T(8,128)S(1)}, u32[]{:S(2)}, u32[]{:S(2)}) collective-permute-start(f32[8,128]{1,0:T(8,128)S(1)} %log_add_fusion.refs_0_), channel_id=1, source_target_pairs={{0,5},{1,4},{2,7},{3,6},{4,1},{5,0},{6,3},{7,2},{8,13},{9,12},{10,... | collective-permute-start | bytes 12296 | tf_op jit(solution)/shard_map/ppermute | solution.py:399
  36.7 4.2 %collective-permute-start.8 = (f32[8,128]{1,0:T(8,128)S(1)}, f32[8,128]{1,0:T(8,128)S(1)}, u32[]{:S(2)}, u32[]{:S(2)}) collective-permute-start(f32[8,128]{1,0:T(8,128)S(1)} %log_add_fusion.refs_0_), channel_id=1, source_target_pairs={{0,3},{1,2},{2,5},{3,4},{4,7},{5,6},{6,1},{7,0},{8,11},{9,10},{10,... | collective-permute-start | bytes 12296 | tf_op jit(solution)/shard_map/ppermute | solution.py:399
  37.5 3.5 %collective-permute-start.9 = (f32[8,128]{1,0:T(8,128)S(1)}, f32[8,128]{1,0:T(8,128)S(1)}, u32[]{:S(2)}, u32[]{:S(2)}) collective-permute-start(f32[8,128]{1,0:T(8,128)S(1)} %log_add_fusion.refs_0_), channel_id=1, source_target_pairs={{0,7},{1,6},{2,1},{3,0},{4,3},{5,2},{6,5},{7,4},{8,15},{9,14},{10,... | collective-permute-start | bytes 12296 | tf_op jit(solution)/shard_map/ppermute | solution.py:399
  61.1 2.2 %collective-permute-start.10 = (f32[8,128]{1,0:T(8,128)S(1)}, f32[8,128]{1,0:T(8,128)S(1)}, u32[]{:S(2)}, u32[]{:S(2)}) collective-permute-start(f32[8,128]{1,0:T(8,128)S(1)} %get-tuple-element.31), channel_id=1, source_target_pairs={{0,1},{1,0},{2,3},{3,2},{4,5},{5,4},{6,7},{7,6},{8,9},{9,8},{10,11... | collective-permute-start | bytes 12296 | tf_op jit(solution)/shard_map/ppermute | solution.py:421
  63.4 4.5 %collective-permute-start.11 = (f32[8,128]{1,0:T(8,128)S(1)}, f32[8,128]{1,0:T(8,128)S(1)}, u32[]{:S(2)}, u32[]{:S(2)}) collective-permute-start(f32[8,128]{1,0:T(8,128)S(1)} %add.29.refs_0_), channel_id=1, source_target_pairs={{0,5},{1,4},{2,7},{3,6},{4,1},{5,0},{6,3},{7,2},{8,13},{9,12},{10,... | collective-permute-start | bytes 12296 | tf_op jit(solution)/shard_map/ppermute | solution.py:399
  64.8 4.2 %collective-permute-start.12 = (f32[8,128]{1,0:T(8,128)S(1)}, f32[8,128]{1,0:T(8,128)S(1)}, u32[]{:S(2)}, u32[]{:S(2)}) collective-permute-start(f32[8,128]{1,0:T(8,128)S(1)} %add.29.refs_0_), channel_id=1, source_target_pairs={{0,3},{1,2},{2,5},{3,4},{4,7},{5,6},{6,1},{7,0},{8,11},{9,10},{10,... | collective-permute-start | bytes 12296 | tf_op jit(solution)/shard_map/ppermute | solution.py:399
  66.9 3.0 %collective-permute-start.13 = (f32[8,128]{1,0:T(8,128)S(1)}, f32[8,128]{1,0:T(8,128)S(1)}, u32[]{:S(2)}, u32[]{:S(2)}) collective-permute-start(f32[8,128]{1,0:T(8,128)S(1)} %add.29.refs_0_), channel_id=1, source_target_pairs={{0,7},{1,6},{2,1},{3,0},{4,3},{5,2},{6,5},{7,4},{8,15},{9,14},{10,... | collective-permute-start | bytes 12296 | tf_op jit(solution)/shard_map/ppermute | solution.py:399
  83.9 2.4 %collective-permute-start.14 = (f32[8,128]{1,0:T(8,128)S(1)}, f32[8,128]{1,0:T(8,128)S(1)}, u32[]{:S(2)}, u32[]{:S(2)}) collective-permute-start(f32[8,128]{1,0:T(8,128)S(1)} %shard_map.73), channel_id=1, source_target_pairs={{0,1},{1,0},{2,3},{3,2},{4,5},{5,4},{6,7},{7,6},{8,9},{9,8},{10,11... | collective-permute-start | bytes 12296 | tf_op jit(solution)/shard_map/ppermute | solution.py:421
  86.3 4.5 %collective-permute-start.15 = (f32[8,128]{1,0:T(8,128)S(1)}, f32[8,128]{1,0:T(8,128)S(1)}, u32[]{:S(2)}, u32[]{:S(2)}) collective-permute-start(f32[8,128]{1,0:T(8,128)S(1)} %add.30.refs_0_), channel_id=1, source_target_pairs={{0,5},{1,4},{2,7},{3,6},{4,1},{5,0},{6,3},{7,2},{8,13},{9,12},{10,... | collective-permute-start | bytes 12296 | tf_op jit(solution)/shard_map/ppermute | solution.py:399
  87.1 4.2 %collective-permute-start.16 = (f32[8,128]{1,0:T(8,128)S(1)}, f32[8,128]{1,0:T(8,128)S(1)}, u32[]{:S(2)}, u32[]{:S(2)}) collective-permute-start(f32[8,128]{1,0:T(8,128)S(1)} %add.30.refs_0_), channel_id=1, source_target_pairs={{0,3},{1,2},{2,5},{3,4},{4,7},{5,6},{6,1},{7,0},{8,11},{9,10},{10,... | collective-permute-start | bytes 12296 | tf_op jit(solution)/shard_map/ppermute | solution.py:399
  89.0 3.0 %collective-permute-start.17 = (f32[8,128]{1,0:T(8,128)S(1)}, f32[8,128]{1,0:T(8,128)S(1)}, u32[]{:S(2)}, u32[]{:S(2)}) collective-permute-start(f32[8,128]{1,0:T(8,128)S(1)} %add.30.refs_0_), channel_id=1, source_target_pairs={{0,7},{1,6},{2,1},{3,0},{4,3},{5,2},{6,5},{7,4},{8,15},{9,14},{10,... | collective-permute-start | bytes 12296 | tf_op jit(solution)/shard_map/ppermute | solution.py:399
  106.2 2.3 %collective-permute-start.18 = (f32[8,128]{1,0:T(8,128)S(1)}, f32[8,128]{1,0:T(8,128)S(1)}, u32[]{:S(2)}, u32[]{:S(2)}) collective-permute-start(f32[8,128]{1,0:T(8,128)S(1)} %get-tuple-element.38), channel_id=1, source_target_pairs={{0,1},{1,0},{2,3},{3,2},{4,5},{5,4},{6,7},{7,6},{8,9},{9,8},{10,11... | collective-permute-start | bytes 12296 | tf_op jit(solution)/shard_map/ppermute | solution.py:421
  108.5 4.5 %collective-permute-start.19 = (f32[8,128]{1,0:T(8,128)S(1)}, f32[8,128]{1,0:T(8,128)S(1)}, u32[]{:S(2)}, u32[]{:S(2)}) collective-permute-start(f32[8,128]{1,0:T(8,128)S(1)} %add.31), channel_id=1, source_target_pairs={{0,5},{1,4},{2,7},{3,6},{4,1},{5,0},{6,3},{7,2},{8,13},{9,12},{10,... | collective-permute-start | bytes 12296 | tf_op jit(solution)/shard_map/ppermute | solution.py:399
  109.9 4.2 %collective-permute-start.20 = (f32[8,128]{1,0:T(8,128)S(1)}, f32[8,128]{1,0:T(8,128)S(1)}, u32[]{:S(2)}, u32[]{:S(2)}) collective-permute-start(f32[8,128]{1,0:T(8,128)S(1)} %add.31), channel_id=1, source_target_pairs={{0,3},{1,2},{2,5},{3,4},{4,7},{5,6},{6,1},{7,0},{8,11},{9,10},{10,... | collective-permute-start | bytes 12296 | tf_op jit(solution)/shard_map/ppermute | solution.py:399
  111.4 3.0 %collective-permute-start.21 = (f32[8,128]{1,0:T(8,128)S(1)}, f32[8,128]{1,0:T(8,128)S(1)}, u32[]{:S(2)}, u32[]{:S(2)}) collective-permute-start(f32[8,128]{1,0:T(8,128)S(1)} %add.31), channel_id=1, source_target_pairs={{0,7},{1,6},{2,1},{3,0},{4,3},{5,2},{6,5},{7,4},{8,15},{9,14},{10,... | collective-permute-start | bytes 12296 | tf_op jit(solution)/shard_map/ppermute | solution.py:399
  (2 other events, 1.8 us)
